TPU v7x, 32 devices: a whole 2x2x4 slice. The times are simulated.
32 devices in a mesh: rep: 8 (over z, y), shard: 4 (over x, core).
Axes of the slice: x: 2, y: 2, z: 4, core: 2. Of those that a mesh axis runs over, the one named last changes fastest.
Arguments:
- tokens: bfloat16 [16384, 1024], P(('rep', 'shard')), may hold values from -6 to 6
- token_ids: int32 [16384], P(('rep', 'shard')), may hold values from 0 to 8007
- hash_table: int32 [8008], replicated, may hold values from 0 to 1
- piece_starts: int32 [8, 2], P('rep'), may hold values from 0 to 1792, as said below
- valid_mask: int32 [16384], P(('rep', 'shard')), may hold values from 0 to 1, as said below
- teacher: bfloat16 [16384, 1024], P(('rep', 'shard')), may hold values from -6 to 6
- cotangent: bfloat16 [16384, 1024], P(('rep', 'shard')), may hold values from -6 to 6
- ln1_gain: bfloat16 [1024], P('shard'), may hold values from 0.5 to 1.5
- ln1_bias: bfloat16 [1024], P('shard'), may hold values from -0.59765625 to 0.59765625
- w_qkv: bfloat16 [1024, 3072], P('shard'), may hold values from -0.1875 to 0.1875
- w_out: bfloat16 [1024, 1024], P('shard'), may hold values from -3 to 3
- out_bias: bfloat16 [1024], P('shard'), may hold values from -0.59765625 to 0.59765625
- ln2_gain: bfloat16 [1024], P('shard'), may hold values from 0.5 to 1.5
- ln2_bias: bfloat16 [1024], P('shard'), may hold values from -0.59765625 to 0.59765625
- w_in: bfloat16 [2, 1024, 4096], P(None, 'shard'), may hold values from -0.1875 to 0.1875
- in_bias: bfloat16 [2, 4096], P(None, 'shard'), may hold values from -0.59765625 to 0.59765625
- w_back: bfloat16 [2, 4096, 1024], P(None, 'shard'), may hold values from -0.09375 to 0.09375
- back_bias: bfloat16 [2, 1024], P(None, 'shard'), may hold values from -0.59765625 to 0.59765625
Outputs:
- output: bfloat16 [16384, 1024], P(('rep', 'shard'))
- input_grad: float32 [16384, 1024], P(('rep', 'shard'))
- ln1_gain_grad: float32 [1024], P('shard')
- ln1_bias_grad: float32 [1024], P('shard')
- w_qkv_grad: float32 [1024, 3072], P('shard')
- w_out_grad: float32 [1024, 1024], P('shard')
- out_bias_grad: float32 [1024], P('shard')
- ln2_gain_grad: float32 [1024], P('shard')
- ln2_bias_grad: float32 [1024], P('shard')
- w_in_grad: float32 [2, 1024, 4096], P(None, 'shard')
- in_bias_grad: float32 [2, 4096], P(None, 'shard')
- w_back_grad: float32 [2, 4096, 1024], P(None, 'shard')
- back_bias_grad: float32 [2, 1024], P(None, 'shard')
Inputs may be any that keep to these rules, and one draw needn't show every extreme that they name: `piece_starts`: in each sequence the 2 pieces of 256 tokens rise, do not intersect and lie inside the sequence; piece j begins in the j-th of 2 equal spans of the sequence. In the first sequence the first piece begins at 0 and the last ends with the sequence. `valid_mask`: the last token of each aligned block of 512 tokens always counts.
All inputs are finite; a program needn't handle non-finite values.
Results may differ from a plain program's by a relative error of at most 0.013.
Values may be sent and summed in bfloat16 or wider, within the bound.
No kernel may reach another device: no remote copies, remote signals or barrier semaphores. Data moves between devices by JAX's collectives and lax.ppermute only.
A program may use at most 256 MiB of HBM per device.

v0:
```python
import math

import jax
import jax.numpy as jnp
from jax import lax
from jax.sharding import PartitionSpec as P

D = 1024
HEADS = 16
HEAD_DIM = 64
EXPERTS = 2
PIECE_LEN = 256
CAP = 320


epsilon = 1e-05


def layer_norm(tok_rows):
    row_mean = jnp.mean(tok_rows, axis=-1, keepdims=True)
    centred = tok_rows - row_mean
    variance = jnp.mean(centred * centred, axis=-1, keepdims=True)
    inverse = lax.rsqrt(variance + epsilon)
    return (centred * inverse, inverse)


def norm_back(upstream, normed, inverse, norm_gain):
    scaled = upstream * norm_gain
    first_mean = jnp.mean(scaled, axis=-1, keepdims=True)
    second_mean = jnp.mean(scaled * normed, axis=-1, keepdims=True)
    return inverse * (scaled - first_mean - normed * second_mean)


def piece_ids(positions, seq_starts):
    inside = (positions[:, None] >= seq_starts[None, :]) & (
        positions[:, None] < seq_starts[None, :] + PIECE_LEN
    )
    numbers = jnp.arange(1, seq_starts.shape[0] + 1, dtype=jnp.int32)
    return jnp.sum(jnp.where(inside, numbers[None, :], 0), axis=1) - 1


def allowed(query_pos, query_piece, key_pos, key_piece):
    causal = key_pos[None, :] <= query_pos[:, None]
    within = (query_piece[:, None] == key_piece[None, :]) & (query_piece[:, None] >= 0)
    return causal | within


def routing(expert_of):
    chosen = expert_of[:, None] == jnp.arange(EXPERTS, dtype=jnp.int32)[None, :]
    running = jnp.cumsum(chosen.astype(jnp.int32), axis=0) - 1
    slot_of = jnp.sum(jnp.where(chosen, running, 0), axis=1)
    slot_ids = jnp.arange(CAP, dtype=jnp.int32)
    dispatch = chosen.T[:, None, :] & (slot_of[None, None, :] == slot_ids[None, :, None])
    kept_rows = slot_of < CAP
    flat_index = expert_of * CAP + jnp.minimum(slot_of, CAP - 1)
    return (dispatch.astype(jnp.bfloat16), kept_rows, flat_index)


def split_keys(keys_all, values_all, key_piece):
    seq_length = keys_all.shape[0]
    block_rows = math.gcd(seq_length, 512)
    blocks = seq_length // block_rows
    key_stack = keys_all.reshape(blocks, block_rows, HEADS, HEAD_DIM)
    value_stack = values_all.reshape(blocks, block_rows, HEADS, HEAD_DIM)
    piece_stack = key_piece.reshape(blocks, block_rows)
    offsets = jnp.arange(blocks, dtype=jnp.int32) * block_rows
    return (key_stack, value_stack, piece_stack, offsets)


def score_block(queries, key_tile, query_pos, query_piece, piece_tile, offset, score_scale):
    key_pos = offset + jnp.arange(key_tile.shape[0], dtype=jnp.int32)
    visible = allowed(query_pos, query_piece, key_pos, piece_tile)[None]
    scores = (
        jnp.einsum("qhd,khd->hqk", queries, key_tile, preferred_element_type=jnp.float32)
        * score_scale
    )
    return (scores, visible)


def attend_forward(queries, keys_all, values_all, query_pos, query_piece, key_piece, score_scale):
    key_stack, value_stack, piece_stack, offsets = split_keys(keys_all, values_all, key_piece)
    local_rows = queries.shape[0]

    def sum_block(state_in, packed):
        running_max, running_sum = state_in
        key_tile, piece_tile, offset = packed
        scores, visible = score_block(
            queries, key_tile, query_pos, query_piece, piece_tile, offset, score_scale
        )
        block_max = jnp.max(jnp.where(visible, scores, -1e30), axis=-1)
        new_max = jnp.maximum(running_max, block_max)
        raised = jnp.where(visible, jnp.exp(scores - new_max[..., None]), 0.0)
        new_sum = running_sum * jnp.exp(running_max - new_max) + jnp.sum(raised, axis=-1)
        return ((new_max, new_sum), None)

    start_state = (
        jnp.full((HEADS, local_rows), -1e30, jnp.float32),
        jnp.zeros((HEADS, local_rows), jnp.float32),
    )
    (row_max, row_sum), ignored = lax.scan(
        sum_block, start_state, (key_stack, piece_stack, offsets)
    )
    log_total = row_max + jnp.log(row_sum)

    def value_block(mixed_sum, packed):
        key_tile, value_tile, piece_tile, offset = packed
        scores, visible = score_block(
            queries, key_tile, query_pos, query_piece, piece_tile, offset, score_scale
        )
        probs_low = jnp.where(visible, jnp.exp(scores - log_total[..., None]), 0.0).astype(
            jnp.bfloat16
        )
        return (
            mixed_sum
            + jnp.einsum("hqk,khd->qhd", probs_low, value_tile, preferred_element_type=jnp.float32),
            None,
        )

    mixed_sum, ignored = lax.scan(
        value_block,
        jnp.zeros((local_rows, HEADS, HEAD_DIM), jnp.float32),
        (key_stack, value_stack, piece_stack, offsets),
    )
    return (mixed_sum.reshape(local_rows, HEADS * HEAD_DIM), log_total)


def attend_back(
    queries,
    keys_all,
    values_all,
    grad_mixed,
    log_total,
    query_pos,
    query_piece,
    key_piece,
    score_scale,
):
    key_stack, value_stack, piece_stack, offsets = split_keys(keys_all, values_all, key_piece)
    local_rows = queries.shape[0]
    seq_length = keys_all.shape[0]
    grad_heads = grad_mixed.reshape(local_rows, HEADS, HEAD_DIM)

    def weights_and_grads(key_tile, value_tile, piece_tile, offset):
        scores, visible = score_block(
            queries, key_tile, query_pos, query_piece, piece_tile, offset, score_scale
        )
        attn_soft = jnp.where(visible, jnp.exp(scores - log_total[..., None]), 0.0)
        grad_probs = jnp.einsum(
            "qhd,khd->hqk", grad_heads, value_tile, preferred_element_type=jnp.float32
        )
        return (attn_soft, grad_probs)

    def delta_block(delta_sum, packed):
        key_tile, value_tile, piece_tile, offset = packed
        attn_soft, grad_probs = weights_and_grads(key_tile, value_tile, piece_tile, offset)
        return (delta_sum + jnp.sum(attn_soft * grad_probs, axis=-1), None)

    row_delta, ignored = lax.scan(
        delta_block,
        jnp.zeros((HEADS, local_rows), jnp.float32),
        (key_stack, value_stack, piece_stack, offsets),
    )

    def grad_block(grad_query, packed):
        key_tile, value_tile, piece_tile, offset = packed
        attn_soft, grad_probs = weights_and_grads(key_tile, value_tile, piece_tile, offset)
        grad_scores = (attn_soft * (grad_probs - row_delta[..., None])).astype(jnp.bfloat16)
        grad_query = (
            grad_query
            + jnp.einsum("hqk,khd->qhd", grad_scores, key_tile, preferred_element_type=jnp.float32)
            * score_scale
        )
        grad_key = (
            jnp.einsum("hqk,qhd->khd", grad_scores, queries, preferred_element_type=jnp.float32)
            * score_scale
        )
        grad_value = jnp.einsum(
            "hqk,qhd->khd",
            attn_soft.astype(jnp.bfloat16),
            grad_heads,
            preferred_element_type=jnp.float32,
        )
        return (grad_query, (grad_key, grad_value))

    grad_query, (key_grads, value_grads) = lax.scan(
        grad_block,
        jnp.zeros((local_rows, HEADS, HEAD_DIM), jnp.float32),
        (key_stack, value_stack, piece_stack, offsets),
    )
    return (
        grad_query.reshape(local_rows, HEADS * HEAD_DIM),
        key_grads.reshape(seq_length, HEADS * HEAD_DIM),
        value_grads.reshape(seq_length, HEADS * HEAD_DIM),
    )


def shards(
    tokens,
    token_ids,
    hash_table,
    piece_starts,
    valid_mask,
    teacher,
    cotangent,
    ln1_gain,
    ln1_bias,
    w_qkv,
    w_out,
    out_bias,
    ln2_gain,
    ln2_bias,
    w_in,
    in_bias,
    w_back,
    back_bias,
):
    local_rows = tokens.shape[0]
    seq_length = local_rows * lax.axis_size("shard")
    tokens_all = seq_length * lax.axis_size("rep")
    score_scale = float(HEAD_DIM) ** (-0.5)
    (
        gain_one,
        bias_one,
        qkv_weight,
        out_weight,
        out_shift,
        gain_two,
        bias_two,
        in_weight,
        in_shift,
        back_weight,
        back_shift,
    ) = (
        lax.all_gather(ln1_gain, "shard", axis=0, tiled=True),
        lax.all_gather(ln1_bias, "shard", axis=0, tiled=True),
        lax.all_gather(w_qkv, "shard", axis=0, tiled=True),
        lax.all_gather(w_out, "shard", axis=0, tiled=True),
        lax.all_gather(out_bias, "shard", axis=0, tiled=True),
        lax.all_gather(ln2_gain, "shard", axis=0, tiled=True),
        lax.all_gather(ln2_bias, "shard", axis=0, tiled=True),
        lax.all_gather(w_in, "shard", axis=1, tiled=True),
        lax.all_gather(in_bias, "shard", axis=1, tiled=True),
        lax.all_gather(w_back, "shard", axis=1, tiled=True),
        lax.all_gather(back_bias, "shard", axis=1, tiled=True),
    )
    tok_rows = tokens.astype(jnp.float32)
    normed_one, inverse_one = layer_norm(tok_rows)
    first_in = (normed_one * gain_one.astype(jnp.float32) + bias_one.astype(jnp.float32)).astype(
        jnp.bfloat16
    )
    qkv_low = jnp.dot(first_in, qkv_weight, preferred_element_type=jnp.float32).astype(jnp.bfloat16)
    queries = qkv_low[:, :D].reshape(local_rows, HEADS, HEAD_DIM)
    keys_all, values_all = (
        lax.all_gather(qkv_low[:, D : 2 * D], "shard", axis=0, tiled=True),
        lax.all_gather(qkv_low[:, 2 * D :], "shard", axis=0, tiled=True),
    )
    query_pos = lax.axis_index("shard") * local_rows + jnp.arange(local_rows, dtype=jnp.int32)
    key_pos = jnp.arange(seq_length, dtype=jnp.int32)
    seq_starts = piece_starts[0]
    query_piece = piece_ids(query_pos, seq_starts)
    key_piece = piece_ids(key_pos, seq_starts)
    attn_mixed, log_total = attend_forward(
        queries, keys_all, values_all, query_pos, query_piece, key_piece, score_scale
    )
    mixed_low = attn_mixed.astype(jnp.bfloat16)
    middle = (
        tok_rows
        + jnp.dot(mixed_low, out_weight, preferred_element_type=jnp.float32)
        + out_shift.astype(jnp.float32)
    )
    normed_two, inverse_two = layer_norm(middle)
    second_in = (normed_two * gain_two.astype(jnp.float32) + bias_two.astype(jnp.float32)).astype(
        jnp.bfloat16
    )
    expert_of = jnp.take(hash_table, token_ids)
    dispatch, kept_rows, flat_index = routing(expert_of)
    inputs = jnp.einsum(
        "ect,td->ecd", dispatch, second_in, preferred_element_type=jnp.float32
    ).astype(jnp.bfloat16)
    hidden_pre = (
        jnp.einsum("ecd,edf->ecf", inputs, in_weight, preferred_element_type=jnp.float32)
        + in_shift.astype(jnp.float32)[:, None, :]
    )
    hidden = jnp.maximum(hidden_pre, 0.0).astype(jnp.bfloat16)
    result = (
        jnp.einsum("ecf,efd->ecd", hidden, back_weight, preferred_element_type=jnp.float32)
        + back_shift.astype(jnp.float32)[:, None, :]
    )
    picked = jnp.take(result.reshape(EXPERTS * CAP, D), flat_index, axis=0)
    final = middle + jnp.where(kept_rows[:, None], picked, 0.0)
    counted = valid_mask.astype(jnp.float32)
    count_all = lax.psum(jnp.sum(counted), ("rep", "shard"))
    grad_final = cotangent.astype(jnp.float32) + tokens_all / (2.0 * count_all) * counted[
        :, None
    ] * (final - teacher.astype(jnp.float32))
    (
        back_gain_one,
        back_bias_one,
        back_qkv,
        back_out,
        back_out_shift,
        back_gain_two,
        back_bias_two,
        back_in,
        back_in_shift,
        back_second,
        back_second_shift,
    ) = (
        lax.all_gather(ln1_gain, "shard", axis=0, tiled=True),
        lax.all_gather(ln1_bias, "shard", axis=0, tiled=True),
        lax.all_gather(w_qkv, "shard", axis=0, tiled=True),
        lax.all_gather(w_out, "shard", axis=0, tiled=True),
        lax.all_gather(out_bias, "shard", axis=0, tiled=True),
        lax.all_gather(ln2_gain, "shard", axis=0, tiled=True),
        lax.all_gather(ln2_bias, "shard", axis=0, tiled=True),
        lax.all_gather(w_in, "shard", axis=1, tiled=True),
        lax.all_gather(in_bias, "shard", axis=1, tiled=True),
        lax.all_gather(w_back, "shard", axis=1, tiled=True),
        lax.all_gather(back_bias, "shard", axis=1, tiled=True),
    )
    grad_low = grad_final.astype(jnp.bfloat16)
    grad_result = jnp.einsum("ect,td->ecd", dispatch, grad_low, preferred_element_type=jnp.float32)
    result_low = grad_result.astype(jnp.bfloat16)
    grad_back_shift = jnp.sum(grad_result, axis=1)
    grad_hidden = jnp.einsum(
        "ecd,efd->ecf", result_low, back_second, preferred_element_type=jnp.float32
    )
    grad_pre = jnp.where(hidden_pre > 0, grad_hidden, 0.0).astype(jnp.bfloat16)
    grad_in_shift = jnp.sum(grad_pre.astype(jnp.float32), axis=1)
    grad_inputs = jnp.einsum(
        "ecf,edf->ecd", grad_pre, back_in, preferred_element_type=jnp.float32
    ).astype(jnp.bfloat16)
    grad_second = jnp.einsum(
        "ect,ecd->td", dispatch, grad_inputs, preferred_element_type=jnp.float32
    )
    grad_gain_two = jnp.sum(grad_second * normed_two, axis=0)
    grad_bias_two = jnp.sum(grad_second, axis=0)
    grad_middle = grad_final + norm_back(
        grad_second, normed_two, inverse_two, back_gain_two.astype(jnp.float32)
    )
    grad_branch = grad_middle.astype(jnp.bfloat16)
    grad_out_shift = jnp.sum(grad_branch.astype(jnp.float32), axis=0)
    grad_mixed = jnp.einsum(
        "te,de->td", grad_branch, back_out, preferred_element_type=jnp.float32
    ).astype(jnp.bfloat16)
    grad_query, key_grads_all, value_grads_all = attend_back(
        queries,
        keys_all,
        values_all,
        grad_mixed,
        log_total,
        query_pos,
        query_piece,
        key_piece,
        score_scale,
    )
    key_grads, value_grads = (
        lax.psum_scatter(
            key_grads_all.astype(jnp.bfloat16), "shard", scatter_dimension=0, tiled=True
        ).astype(jnp.float32),
        lax.psum_scatter(
            value_grads_all.astype(jnp.bfloat16), "shard", scatter_dimension=0, tiled=True
        ).astype(jnp.float32),
    )
    grad_qkv = jnp.concatenate([grad_query, key_grads, value_grads], axis=1).astype(jnp.bfloat16)
    grad_first = jnp.einsum("te,de->td", grad_qkv, back_qkv, preferred_element_type=jnp.float32)
    grad_gain_one = jnp.sum(grad_first * normed_one, axis=0)
    grad_bias_one = jnp.sum(grad_first, axis=0)
    input_grad = grad_middle + norm_back(
        grad_first, normed_one, inverse_one, back_gain_one.astype(jnp.float32)
    )
    grad_back_weight = jnp.einsum(
        "ecf,ecd->efd", hidden, result_low, preferred_element_type=jnp.float32
    )
    grad_in_weight = jnp.einsum(
        "ecd,ecf->edf", inputs, grad_pre, preferred_element_type=jnp.float32
    )
    grad_out_weight = jnp.einsum(
        "td,te->de", mixed_low, grad_branch, preferred_element_type=jnp.float32
    )
    grad_qkv_weight = jnp.einsum(
        "td,te->de", first_in, grad_qkv, preferred_element_type=jnp.float32
    )
    (
        owned_gain_one,
        owned_bias_one,
        owned_qkv,
        owned_out,
        owned_out_shift,
        owned_gain_two,
        owned_bias_two,
        owned_in,
        owned_in_shift,
        owned_back,
        owned_back_shift,
    ) = (
        lax.psum_scatter(
            grad_gain_one.astype(jnp.bfloat16), "shard", scatter_dimension=0, tiled=True
        ).astype(jnp.float32),
        lax.psum_scatter(
            grad_bias_one.astype(jnp.bfloat16), "shard", scatter_dimension=0, tiled=True
        ).astype(jnp.float32),
        lax.psum_scatter(
            grad_qkv_weight.astype(jnp.bfloat16), "shard", scatter_dimension=0, tiled=True
        ).astype(jnp.float32),
        lax.psum_scatter(
            grad_out_weight.astype(jnp.bfloat16), "shard", scatter_dimension=0, tiled=True
        ).astype(jnp.float32),
        lax.psum_scatter(
            grad_out_shift.astype(jnp.bfloat16), "shard", scatter_dimension=0, tiled=True
        ).astype(jnp.float32),
        lax.psum_scatter(
            grad_gain_two.astype(jnp.bfloat16), "shard", scatter_dimension=0, tiled=True
        ).astype(jnp.float32),
        lax.psum_scatter(
            grad_bias_two.astype(jnp.bfloat16), "shard", scatter_dimension=0, tiled=True
        ).astype(jnp.float32),
        lax.psum_scatter(
            grad_in_weight.astype(jnp.bfloat16), "shard", scatter_dimension=1, tiled=True
        ).astype(jnp.float32),
        lax.psum_scatter(
            grad_in_shift.astype(jnp.bfloat16), "shard", scatter_dimension=1, tiled=True
        ).astype(jnp.float32),
        lax.psum_scatter(
            grad_back_weight.astype(jnp.bfloat16), "shard", scatter_dimension=1, tiled=True
        ).astype(jnp.float32),
        lax.psum_scatter(
            grad_back_shift.astype(jnp.bfloat16), "shard", scatter_dimension=1, tiled=True
        ).astype(jnp.float32),
    )
    final_grads = (
        lax.psum(owned_gain_one.astype(jnp.bfloat16), "rep").astype(jnp.float32),
        lax.psum(owned_bias_one.astype(jnp.bfloat16), "rep").astype(jnp.float32),
        lax.psum(owned_qkv.astype(jnp.bfloat16), "rep").astype(jnp.float32),
        lax.psum(owned_out.astype(jnp.bfloat16), "rep").astype(jnp.float32),
        lax.psum(owned_out_shift.astype(jnp.bfloat16), "rep").astype(jnp.float32),
        lax.psum(owned_gain_two.astype(jnp.bfloat16), "rep").astype(jnp.float32),
        lax.psum(owned_bias_two.astype(jnp.bfloat16), "rep").astype(jnp.float32),
        lax.psum(owned_in.astype(jnp.bfloat16), "rep").astype(jnp.float32),
        lax.psum(owned_in_shift.astype(jnp.bfloat16), "rep").astype(jnp.float32),
        lax.psum(owned_back.astype(jnp.bfloat16), "rep").astype(jnp.float32),
        lax.psum(owned_back_shift.astype(jnp.bfloat16), "rep").astype(jnp.float32),
    )
    return (final.astype(jnp.bfloat16), input_grad) + tuple(final_grads)


def solution(mesh):
    in_specs = (
        P(("rep", "shard"), None),
        P(("rep", "shard")),
        P(),
        P("rep", None),
        P(("rep", "shard")),
        P(("rep", "shard"), None),
        P(("rep", "shard"), None),
        P("shard"),
        P("shard"),
        P("shard", None),
        P("shard", None),
        P("shard"),
        P("shard"),
        P("shard"),
        P(None, "shard", None),
        P(None, "shard"),
        P(None, "shard", None),
        P(None, "shard"),
    )
    out_specs = (
        P(("rep", "shard"), None),
        P(("rep", "shard"), None),
        P("shard"),
        P("shard"),
        P("shard", None),
        P("shard", None),
        P("shard"),
        P("shard"),
        P("shard"),
        P(None, "shard", None),
        P(None, "shard"),
        P(None, "shard", None),
        P(None, "shard"),
    )
    return jax.shard_map(shards, mesh=mesh, in_specs=in_specs, out_specs=out_specs, check_vma=False)
```

profile of v0, /device:TPU:0, one launch (start us, length us, event | category | flops | bytes accessed | tf_op | source)
XLA Modules:
  0.0 1523.7 jit_solution(1001879703543651700)
XLA Ops:
  22.7 36.0 %all-gather.12.cloned.1.call-done = bf16[1024,3072]{1,0:T(8,128)(2,1)} async-done(((bf16[256,3072]{1,0:T(8,128)(2,1)}), bf16[1024,3072]{1,0:T(8,128)(2,1)}) %all-gather.12.cloned.1.call-update) | async-done | bytes 6291472 | tf_op jit(solution)/shard_map/all_gather | solution.py:236
  70.3 39.7 %psum.84 = f32[]{:T(128)} all-reduce(f32[]{:T(128)} %convert_reduce_fusion.1), channel_id=1, replica_groups=mesh['rep'=8,'shard'=4] {'rep','shard'}, use_global_device_ids=true, to_apply=%region_16.17 | all-reduce | flops 1 | bytes 8 | tf_op jit(solution)/shard_map/psum | solution.py:292
  142.5 11.7 reshape.562
  154.2 9.8 copy.87
  164.0 11.8 reshape.563
  175.8 10.6 copy.88
  186.4 78.0 %while.50 = (s32[]{:T(128)}, f32[16,512]{1,0:T(8,128)S(1)}, f32[16,512]{1,0:T(8,128)S(1)}, s32[4]{0:T(128)S(1)}, s32[512]{0:T(512)S(1)}, /*index=5*/s32[4,512]{1...) while((s32[]{:T(128)}, f32[16,512]{1,0:T(8,128)S(1)}, ...), condition=%wide.region_7.8_spmd.clone, body=%wide.region_4.7_spmd.clone.sunk | while | flops 567322112 | bytes 36883608 | solution.py:100
  196.5 9.1 fusion.170
  207.4 8.7 fusion.169
  216.1 9.1 fusion.170
  226.9 8.5 fusion.169
  235.5 9.2 fusion.170
  246.4 8.6 fusion.169
  255.0 9.3 fusion.170
  264.4 41.2 %while.51 = (s32[]{:T(128)}, f32[512,16,64]{0,2,1:T(8,128)}, bf16[4,512,16,64]{1,3,2,0:T(8,128)(2,1)}, s32[4]{0:T(128)S(1)}, s32[512]{0:T(512)S(1)}, /*index=5*/...) while((s32[]{:T(128)}, f32[512,16,64]{0,2,1:T(8,128)}, ...), condition=%wide.region_9.10_spmd.clone, body=%wide.region_8.9_spmd.clone.sunk | while | flops 1092617728 | bytes 7918238 | solution.py:119
  286.0 9.6 bitcast_add_fusion.4
  314.6 17.3 %fusion.56 = (u8[320,4096]{1,0:T(8,128)(4,1)}, f32[2,320,4096]{2,1,0:T(8,128)}) fusion(f32[2,4096]{1,0:T(2,128)S(1)} %convert_element_type.206, bf16[2,320,1024]{2,1,0:T(8,128)(2,1)} %fusion.80, bf16[2,1024,4096]{2,1,0:T(8,128)(2,1)} %all-gather.20.cloned.1.call-done), kind=kOutput, calls=%fused_computation.94 | convolution fusion | flops 5383127040 | bytes 29917184 | tf_op jit(solution)/shard_map/ecd,edf->ecf/dot_general | solution.py:281
  331.9 45.9 %all-gather.22.cloned.1.call-done = bf16[2,4096,1024]{2,1,0:T(8,128)(2,1)} async-done(((bf16[2,1024,1024]{2,1,0:T(8,128)(2,1)}), bf16[2,4096,1024]{2,1,0:T(8,128)(2,1)}) %all-gather.22.cloned.1.call-update) | async-done | bytes 16777232 | tf_op jit(solution)/shard_map/all_gather | solution.py:243
  377.8 14.4 convolution_add_fusion
  401.6 12.5 fusion.115
  414.2 15.3 %fusion.72 = (bf16[1024]{0:T(1024)(128)(2,1)}, f32[512]{0:T(512)S(1)}, f32[512]{0:T(512)S(1)}, bf16[1024]{0:T(1024)(128)(2,1)}, bf16[512,1024]{1,0:T(8,128)(2,1)}, /*index=5*/f32[512,1024,1]{1,0,2:T(8,128)}) fusion(f32[512,1024]{1,0:T(8,128)S(1)} %get-tuple-element.715, f32[512]{0:T(512)S(1)} %add_rsqrt_fusion, f32[512]{0:T(512)S(1)} %broadcast_multiply_fusion.4, ...), kind=kOutput, calls=%fused_computation.113 | convolution fusion | flops 6047593472 | bytes 29542400 | tf_op jit(solution)/shard_map/ect,ecd->td/dot_general | solution.py:333
  437.7 48.3 %while.52 = (s32[]{:T(128)}, f32[16,512]{1,0:T(8,128)S(1)}, s32[4]{0:T(128)S(1)}, s32[512]{0:T(512)S(1)}, s32[4,512]{1,0:T(4,128)S(1)}, /*index=5*/bf16[4,512,16...) while((s32[]{:T(128)}, f32[16,512]{1,0:T(8,128)S(1)}, ...), condition=%wide.region_21.22_spmd.clone, body=%wide.region_19.21_spmd.clone.sunk | while | flops 1095771648 | bytes 38456492 | solution.py:158
  485.9 177.7 %while.53 = (s32[]{:T(128)}, f32[512,16,64]{0,2,1:T(8,128)S(1)}, bf16[4,512,16,64]{1,3,2,0:T(8,128)(2,1)}, bf16[4,512,16,64]{1,3,2,0:T(8,128)(2,1)}, bf16[4,512,...) while((s32[]{:T(128)}, f32[512,16,64]{0,2,1:T(8,128)S(1)}, ...), condition=%wide.region_23.24_spmd.clone, body=%wide.region_22.23_spmd.clone.sunk | while | flops 2729444864 | bytes 163433808 | solution.py:185
  486.4 9.4 fusion.191
  497.4 11.1 fusion.192
  520.4 10.3 bitcast_dynamic-update-slice_fusion.5
  530.7 9.4 fusion.191
  541.7 11.0 fusion.192
  564.7 10.3 bitcast_dynamic-update-slice_fusion.5
  574.9 9.4 fusion.191
  586.0 11.0 fusion.192
  608.9 10.3 bitcast_dynamic-update-slice_fusion.5
  619.2 9.4 fusion.191
  630.2 11.1 fusion.192
  653.2 10.3 bitcast_dynamic-update-slice_fusion.5
  689.3 28.1 %reduce-scatter.15.cloned.1.call-done = bf16[512,1024]{0,1:T(8,128)(2,1)} async-done(((bf16[2048,1024]{0,1:T(8,128)(2,1)}), bf16[512,1024]{0,1:T(8,128)(2,1)}) %reduce-scatter.15.cloned.1.call-update) | async-done | bytes 1048592 | tf_op jit(solution)/shard_map/reduce_scatter | solution.py:361
  717.4 47.2 %reduce-scatter.13.cloned.1.call-done = bf16[512,1024]{0,1:T(8,128)(2,1)} async-done(((bf16[2048,1024]{0,1:T(8,128)(2,1)}), bf16[512,1024]{0,1:T(8,128)(2,1)}) %reduce-scatter.13.cloned.1.call-update) | async-done | bytes 1048592 | tf_op jit(solution)/shard_map/reduce_scatter | solution.py:358
  774.4 15.4 %convolution_convert_fusion.1 = bf16[2,1024,4096]{2,1,0:T(8,128)(2,1)} fusion(bf16[2,320,1024]{2,1,0:T(8,128)(2,1)S(1)} %copy-done.43, bf16[2,320,4096]{2,1,0:T(8,128)(2,1)} %get-tuple-element.721), kind=kOutput, calls=%fused_computation.83 | convolution fusion | flops 5377097728 | bytes 23330816 | tf_op jit(solution)/shard_map/ecd,ecf->edf/dot_general | solution.py:375
  791.1 17.7 %convolution_convert_fusion = bf16[2,4096,1024]{2,1,0:T(8,128)(2,1)} fusion(f32[2,320,4096]{2,1,0:T(8,128)} %get-tuple-element.717, f32[2,4096]{1,0:T(2,128)S(1)} %copy-done.18, bf16[2,320,1024]{2,1,0:T(8,128)(2,1)S(1)} %copy-done.42), kind=kOutput, calls=%fused_computation.82 | convolution fusion | flops 5384962048 | bytes 28606464 | tf_op jit(solution)/shard_map/ecf,ecd->efd/dot_general | solution.py:372
  812.2 48.6 %reduce-scatter.17.cloned.1.call-done = bf16[256,3072]{1,0:T(8,128)(2,1)} async-done(((bf16[1024,3072]{1,0:T(8,128)(2,1)}), bf16[256,3072]{1,0:T(8,128)(2,1)}) %reduce-scatter.17.cloned.1.call-update) | async-done | bytes 1572880 | tf_op jit(solution)/shard_map/reduce_scatter | solution.py:403
  860.8 128.7 %reduce-scatter.21.cloned.1.call-done = bf16[2,256,4096]{2,1,0:T(8,128)(2,1)} async-done(((bf16[2,1024,4096]{2,1,0:T(8,128)(2,1)}), bf16[2,256,4096]{2,1,0:T(8,128)(2,1)}) %reduce-scatter.21.cloned.1.call-update) | async-done | bytes 4194320 | tf_op jit(solution)/shard_map/reduce_scatter | solution.py:418
  989.5 128.8 %reduce-scatter.23.cloned.1.call-done = bf16[2,1024,1024]{2,1,0:T(8,128)(2,1)} async-done(((bf16[2,4096,1024]{2,1,0:T(8,128)(2,1)}), bf16[2,1024,1024]{2,1,0:T(8,128)(2,1)}) %reduce-scatter.23.cloned.1.call-update) | async-done | bytes 4194320 | tf_op jit(solution)/shard_map/reduce_scatter | solution.py:424
  1120.2 20.6 %reduce-scatter.27.cloned.1.call-done = bf16[256,2]{1,0:T(8,128)(2,1)} async-done(((bf16[1024,2]{1,0:T(8,128)(2,1)}), bf16[256,2]{1,0:T(8,128)(2,1)}) %reduce-scatter.27.cloned.1.call-update) | async-done | bytes 1040
  1141.7 27.1 %reduce-scatter.25.cloned.1.call-done = bf16[1024,2]{1,0:T(8,128)(2,1)} async-done(((bf16[4096,2]{1,0:T(8,128)(2,1)}), bf16[1024,2]{1,0:T(8,128)(2,1)}) %reduce-scatter.25.cloned.1.call-update) | async-done | bytes 4112
  1169.9 9.2 fusion.69
  1179.1 10.9 all-reduce.7
  1190.4 23.0 %all-reduce.5 = (bf16[256]{0:T(256)(128)(2,1)S(1)}, bf16[256]{0:T(256)(128)(2,1)S(1)}, bf16[256]{0:T(256)(128)(2,1)S(1)}, bf16[256]{0:T(256)(128)(2,1)S(1)}, bf1...) all-reduce(bf16[256]{0:T(256)(128)(2,1)S(1)} %dynamic-slice.1, ...), channel_id=1, replica_groups=mesh['rep'=8,'shard'=4] {'rep'}, use_global_device_ids=true, to_apply=%region_30.31 | all-reduce | flops 3840 | bytes 15360 | tf_op jit(solution)/shard_map/psum | solution.py:432
  1221.1 282.2 %all-reduce.10.cloned.1.call-done = (bf16[256,3072]{1,0:T(8,128)(2,1)}, bf16[256,1024]{1,0:T(8,128)(2,1)}, bf16[2,256,4096]{2,1,0:T(8,128)(2,1)}, bf16[2,1024,1024]{2,1,0:T(8,128)(2,1)}) async-done(((bf16[256,3072]{1,0:T(8,128)(2,1)}, bf16[256,1024]{1,0:T(8,128)(2,1)}, bf16[2,256,4096]{2,1,0:T(8,128)(2,1)}, bf16[2,1024,1024]{2,1,0:T(8,128)(2,1)}), (bf16[256,3072]{1,0:T(8,128)(2,1)}, ...) | async-done | bytes 10485776 | tf_op jit(solution)/shard_map/psum | solution.py:434
  (365 shorter events, 297.9 us)
Async XLA Ops:
  7.2 124.1 %copy-start = (s32[8008]{0:T(1024)S(1)}, s32[8008]{0:T(1024)}, u32[]{:S(2)}) copy-start(s32[8008]{0:T(1024)} %param.28) | copy-start | bytes 96100
  7.2 15.1 copy-start.5
  7.2 51.5 %all-gather.12.cloned.1.call-start = ((), (), s32[]{:S(2)}) async-start(), calls=%async_computation.8 | async-start | bytes 7864320 | tf_op jit(solution)/shard_map/all_gather | solution.py:236
  7.9 134.6 %all-gather.14.cloned.1.call-start = ((), (), s32[]{:S(2)}) async-start(), calls=%async_computation.9 | async-start | bytes 5242880 | tf_op jit(solution)/shard_map/all_gather | solution.py:255
  14.6 44.1 %copy-start.31 = (f32[4,1,256]{2,1,0:T(1,128)}, f32[4,1,256]{2,1,0:T(1,128)S(1)}, u32[]{:S(2)}) copy-start(f32[4,1,256]{2,1,0:T(1,128)S(1)} %convert_element_type.244) | copy-start | bytes 12292
  20.6 38.1 %copy-start.22 = (f32[4,1,256]{2,1,0:T(1,128)}, f32[4,1,256]{2,1,0:T(1,128)S(1)}, u32[]{:S(2)}) copy-start(f32[4,1,256]{2,1,0:T(1,128)S(1)} %convert_element_type.243) | copy-start | bytes 12292
  22.3 36.5 %copy-start.19 = (f32[512]{0:T(512)}, f32[512]{0:T(512)S(1)}, u32[]{:S(2)}) copy-start(f32[512]{0:T(512)S(1)} %broadcast_multiply_fusion.5) | copy-start | bytes 6148
  22.7 36.0 %copy-start.27 = (f32[512]{0:T(512)}, f32[512]{0:T(512)S(1)}, u32[]{:S(2)}) copy-start(f32[512]{0:T(512)S(1)} %add_rsqrt_fusion.1) | copy-start | bytes 6148
  67.1 96.8 %all-gather.16.cloned.1.call-start = ((), (), s32[]{:S(2)}) async-start(), calls=%async_computation.10 | async-start | bytes 5242880 | tf_op jit(solution)/shard_map/all_gather | solution.py:254
  67.8 240.5 %all-gather.18.cloned.1.call-start = ((), (), s32[]{:S(2)}) async-start(), calls=%async_computation.11 | async-start | bytes 2621440 | tf_op jit(solution)/shard_map/all_gather | solution.py:237
  68.4 246.2 %all-gather.20.cloned.1.call-start = ((), (), s32[]{:S(2)}) async-start(), calls=%async_computation.12 | async-start | bytes 20971520 | tf_op jit(solution)/shard_map/all_gather | solution.py:241
  69.0 41.0 %copy-start.37 = (bf16[256]{0:T(256)(128)(2,1)S(1)}, bf16[256]{0:T(256)(128)(2,1)}, u32[]{:S(2)}) copy-start(bf16[256]{0:T(256)(128)(2,1)} %param.37) | copy-start | bytes 1540
  69.0 46.5 %copy-start.38 = (bf16[256]{0:T(256)(128)(2,1)S(1)}, bf16[256]{0:T(256)(128)(2,1)}, u32[]{:S(2)}) copy-start(bf16[256]{0:T(256)(128)(2,1)} %param.38) | copy-start | bytes 1540
  69.1 51.9 %copy-start.30 = (bf16[2,1024]{1,0:T(2,128)(2,1)S(1)}, bf16[2,1024]{1,0:T(2,128)(2,1)}, u32[]{:S(2)}) copy-start(bf16[2,1024]{1,0:T(2,128)(2,1)} %param.41) | copy-start | bytes 12292
  69.1 57.1 %copy-start.39 = (bf16[256]{0:T(256)(128)(2,1)S(1)}, bf16[256]{0:T(256)(128)(2,1)}, u32[]{:S(2)}) copy-start(bf16[256]{0:T(256)(128)(2,1)} %param.39) | copy-start | bytes 1540
  69.1 62.2 %copy-start.24 = (s32[512]{0:T(512)S(1)}, s32[512]{0:T(512)}, u32[]{:S(2)}) copy-start(s32[512]{0:T(512)} %param.27) | copy-start | bytes 6148
  69.1 66.4 %copy-start.36 = (bf16[2,256]{1,0:T(2,128)(2,1)S(1)}, bf16[2,256]{1,0:T(2,128)(2,1)}, u32[]{:S(2)}) copy-start(bf16[2,256]{1,0:T(2,128)(2,1)} %param.43) | copy-start | bytes 3076
  69.1 308.7 %all-gather.22.cloned.1.call-start = ((), (), s32[]{:S(2)}) async-start(), calls=%async_computation.13 | async-start | bytes 20971520 | tf_op jit(solution)/shard_map/all_gather | solution.py:243
  69.7 647.8 %reduce-scatter.15.cloned.1.call-start = ((), (), s32[]{:S(2)}) async-start(), calls=%async_computation.15 | async-start | bytes 5242880 | tf_op jit(solution)/shard_map/reduce_scatter | solution.py:361
  126.2 251.6 %copy-start.17 = (f32[2,4096]{1,0:T(2,128)}, f32[2,4096]{1,0:T(2,128)S(1)}, u32[]{:S(2)}) copy-start(f32[2,4096]{1,0:T(2,128)S(1)} %convert_element_type.206) | copy-start | bytes 98308
  401.6 12.5 copy-start.41
  437.6 48.3 %copy-start.3 = (f32[512,16,64]{0,2,1:T(8,128)S(1)}, f32[512,16,64]{0,2,1:T(8,128)}, u32[]{:S(2)}) copy-start(f32[512,16,64]{0,2,1:T(8,128)} %custom-call.4) | copy-start | bytes 6291460
  486.4 11.0 copy-start.4
  508.5 6.1 copy-start.2
  508.5 7.3 copy-start.11
  530.7 11.0 copy-start.4
  552.8 7.3 copy-start.11
  574.9 11.0 copy-start.4
  597.0 7.3 copy-start.11
  619.2 11.0 copy-start.4
  641.3 7.3 copy-start.11
  672.8 91.9 %reduce-scatter.13.cloned.1.call-start = ((), (), s32[]{:S(2)}) async-start(), calls=%async_computation.14 | async-start | bytes 5242880 | tf_op jit(solution)/shard_map/reduce_scatter | solution.py:358
  682.4 129.8 %reduce-scatter.19.cloned.1.call-start = ((), (), s32[]{:S(2)}) async-start(), calls=%async_computation.17 | async-start | bytes 2621440 | tf_op jit(solution)/shard_map/reduce_scatter | solution.py:406
  687.9 76.8 %copy-start.6 = (bf16[512,1024]{1,0:T(8,128)(2,1)S(1)}, bf16[512,1024]{1,0:T(8,128)(2,1)}, u32[]{:S(2)}) copy-start(bf16[512,1024]{1,0:T(8,128)(2,1)} %param.26) | copy-start | bytes 3145732
  687.9 76.8 %copy-start.20 = (f32[512]{0:T(512)S(1)}, f32[512]{0:T(512)}, u32[]{:S(2)}) copy-start(f32[512]{0:T(512)} %copy-done.19) | copy-start | bytes 6148
  687.9 76.8 %copy-start.23 = (f32[4,1,256]{2,1,0:T(1,128)S(1)}, f32[4,1,256]{2,1,0:T(1,128)}, u32[]{:S(2)}) copy-start(f32[4,1,256]{2,1,0:T(1,128)} %copy-done.22) | copy-start | bytes 12292
  687.9 76.8 %copy-start.28 = (f32[512]{0:T(512)S(1)}, f32[512]{0:T(512)}, u32[]{:S(2)}) copy-start(f32[512]{0:T(512)} %copy-done.27) | copy-start | bytes 6148
  687.9 76.8 %copy-start.32 = (f32[4,1,256]{2,1,0:T(1,128)S(1)}, f32[4,1,256]{2,1,0:T(1,128)}, u32[]{:S(2)}) copy-start(f32[4,1,256]{2,1,0:T(1,128)} %copy-done.31) | copy-start | bytes 12292
  687.9 172.8 %reduce-scatter.17.cloned.1.call-start = ((), (), s32[]{:S(2)}) async-start(), calls=%async_computation.16 | async-start | bytes 7864320 | tf_op jit(solution)/shard_map/reduce_scatter | solution.py:403
  773.1 216.4 %reduce-scatter.21.cloned.1.call-start = ((), (), s32[]{:S(2)}) async-start(), calls=%async_computation.18 | async-start | bytes 20971520 | tf_op jit(solution)/shard_map/reduce_scatter | solution.py:418
  789.8 328.5 %reduce-scatter.23.cloned.1.call-start = ((), (), s32[]{:S(2)}) async-start(), calls=%async_computation.19 | async-start | bytes 20971520 | tf_op jit(solution)/shard_map/reduce_scatter | solution.py:424
  808.8 332.0 %reduce-scatter.27.cloned.1.call-start = ((), (), s32[]{:S(2)}) async-start(), calls=%async_computation.21 | async-start | bytes 327680
  810.4 358.4 %reduce-scatter.25.cloned.1.call-start = ((), (), s32[]{:S(2)}) async-start(), calls=%async_computation.20 | async-start | bytes 1310720
  811.9 691.4 %all-reduce.10.cloned.1.call-start = ((), (), s32[]{:S(2)}) async-start(), calls=%async_computation.22 | async-start | bytes 20971520 | tf_op jit(solution)/shard_map/psum | solution.py:434
  1169.9 9.2 copy-start.26
  1169.9 9.2 copy-start.33
  1169.9 9.2 copy-start.34
  1169.9 47.5 %copy-start.8 = (f32[512,1024]{1,0:T(8,128)S(1)}, f32[512,1024]{1,0:T(8,128)}, u32[]{:S(2)}) copy-start(f32[512,1024]{1,0:T(8,128)} %copy-done.7) | copy-start | bytes 6291460
  (23 other events, 62.6 us)
Sparse Core Ops, SparseCore 0:
  9.6 49.0 all-gather.11
  67.2 35.0 all-gather.13
  104.5 34.4 all-gather.15
  140.4 22.5 all-gather.17
  164.4 105.9 all-gather.19
  271.8 105.9 all-gather.21
  672.9 44.4 reduce-scatter.14
  720.1 44.4 reduce-scatter.12
  767.8 31.4 reduce-scatter.18
  802.4 58.3 reduce-scatter.16
  863.3 126.1 reduce-scatter.20
  992.1 126.0 reduce-scatter.22
  1120.7 20.0 reduce-scatter.26
  1143.9 24.8 reduce-scatter.24
  1173.3 329.9 all-reduce.9
where the time goes:
time: 1530 us; the launch traced here: 1520 us
  waiting for transfers between devices  796 us (52%)
  matrix products  398 us (26%)
  local copies, waits for them, and re-layouts  113 us (7%)
  blocking collectives  111 us (7%)
  other arithmetic  86.4 us (6%)
  between operations  16.1 us (1%)
    psum x1, waiting for transfers between devices, shards(): lax.psum(owned_qkv.astype(jnp.bfloat16), 'rep').astype(jnp.float32)  282 us
    reduce_scatter x1, waiting for transfers between devices, shards(): lax.psum_scatter(grad_back_weight.astype(jnp.bfloat16), 'shard', scatter_...  129 us
    reduce_scatter x1, waiting for transfers between devices, shards(): lax.psum_scatter(grad_in_weight.astype(jnp.bfloat16), 'shard', scatter_di...  129 us
    dot_general x12, matrix products, score_block(): jnp.einsum('qhd,khd->hqk', queries, key_tile, preferred_element_type=jnp....  97.9 us
    dot_general x8, matrix products, weights_and_grads(): jnp.einsum('qhd,khd->hqk', grad_heads, value_tile, preferred_element_type...  60 us
    unnamed x17, waiting for transfers between devices  50.9 us
    reduce_scatter x1, waiting for transfers between devices, shards(): lax.psum_scatter(grad_qkv_weight.astype(jnp.bfloat16), 'shard', scatter_d...  48.6 us
    reduce_scatter x1, waiting for transfers between devices, shards(): lax.psum_scatter(key_grads_all.astype(jnp.bfloat16), 'shard', scatter_dim...  47.2 us
  transfers between devices with their start and end apart: 15, of which 10 were waited for; matrix products, arithmetic and copies ran while one was open for 18% of the time, Pallas kernels for 0%

commit v1 on v0

v1 whole, which is shorter than its diff:
```python
import functools

import jax
import jax.numpy as jnp
from jax import lax
from jax.experimental import pallas as pl
from jax.experimental.pallas import tpu as pltpu
from jax.sharding import PartitionSpec as P

D = 1024
HEADS = 16
HEAD_DIM = 64
EXPERTS = 2
PIECE_LEN = 256
CAP = 320
N_SHARD = 4
OWN_HEADS = HEADS // N_SHARD
OWN = OWN_HEADS * HEAD_DIM
TILE = 256
NEG = -1e30

epsilon = 1e-05
f32 = jnp.float32
bf16 = jnp.bfloat16


def layer_norm(tok_rows):
    row_mean = jnp.mean(tok_rows, axis=-1, keepdims=True)
    centred = tok_rows - row_mean
    variance = jnp.mean(centred * centred, axis=-1, keepdims=True)
    inverse = lax.rsqrt(variance + epsilon)
    return (centred * inverse, inverse)


def norm_back(upstream, normed, inverse, norm_gain):
    scaled = upstream * norm_gain
    first_mean = jnp.mean(scaled, axis=-1, keepdims=True)
    second_mean = jnp.mean(scaled * normed, axis=-1, keepdims=True)
    return inverse * (scaled - first_mean - normed * second_mean)


def dot_nn(a, b):
    return lax.dot_general(a, b, (((1,), (0,)), ((), ())), preferred_element_type=f32)


def dot_nt(a, b):
    return lax.dot_general(a, b, (((1,), (1,)), ((), ())), preferred_element_type=f32)


def dot_tn(a, b):
    return lax.dot_general(a, b, (((0,), (0,)), ((), ())), preferred_element_type=f32)


def swap(value, mask):
    return lax.ppermute(value, "shard", [(i, i ^ mask) for i in range(N_SHARD)])


def gather_blocks(value):
    far = swap(value, 2)
    near = swap(value, 1)
    return (value, near, far, swap(far, 1))


def exchange_blocks(blocks):
    return (blocks[0], swap(blocks[1], 1), swap(blocks[2], 2), swap(blocks[3], 3))


def scatter_far(block_two, block_three):
    near = swap(block_three, 1)
    return swap((block_two.astype(f32) + near.astype(f32)).astype(bf16), 2)


def scatter_near(block_zero, block_one, far):
    near = swap(block_one, 1)
    return block_zero.astype(f32) + near.astype(f32) + far.astype(f32)


def rep_masks(count):
    masks = []
    step = 1
    while step < count:
        masks.append(step)
        step *= 2
    if count == 8:
        return [(1, (1,)), (2, (2, 4)), (6, (4,))]
    return [(m, (m,)) for m in masks]


def rep_pair(value, mask, count):
    return lax.ppermute(value, "rep", [(i, i ^ mask) for i in range(count)])


def rep_side(bits):
    index = lax.axis_index("rep")
    side = jnp.zeros((), jnp.int32)
    for bit in bits:
        side = side ^ ((index & bit) // bit)
    return side


def rep_sum_part(value, turn, count):
    dims = rep_masks(count)
    turn = turn % len(dims)
    dims = dims[turn:] + dims[:turn]
    sides = [rep_side(bits) for unused, bits in dims]
    for (mask, unused), side in zip(dims, sides):
        half = value.shape[0] // 2
        split = value.reshape(2, half, value.shape[1])
        send = lax.dynamic_index_in_dim(split, 1 - side, 0, keepdims=False)
        keep = lax.dynamic_index_in_dim(split, side, 0, keepdims=False)
        other = rep_pair(send, mask, count)
        value = (keep.astype(f32) + other.astype(f32)).astype(bf16)
    for (mask, unused), side in reversed(list(zip(dims, sides))):
        other = rep_pair(value, mask, count)
        value = jnp.where(
            side == 0,
            jnp.concatenate([value, other], axis=0),
            jnp.concatenate([other, value], axis=0),
        )
    return value


def rep_sum(value, parts, count):
    if count == 1:
        return value
    if count & (count - 1) or value.shape[0] % (16 * count):
        return lax.psum(value, "rep")
    unit = 16 * count
    total = value.shape[0] // unit
    parts = min(parts, total)
    sizes = [(total // parts + (1 if p >= parts - total % parts else 0)) * unit for p in range(parts)]
    pieces, start = [], 0
    for turn, size in enumerate(sizes):
        pieces.append(rep_sum_part(value[start : start + size], turn, count))
        start += size
    return jnp.concatenate(pieces, axis=0)


def visible_tile(key_block, query_block, starts):
    key_pos = key_block * TILE + lax.broadcasted_iota(jnp.int32, (TILE, TILE), 0)
    query_pos = query_block * TILE + lax.broadcasted_iota(jnp.int32, (TILE, TILE), 1)
    seen = key_pos <= query_pos
    for start in starts:
        low = jnp.minimum(key_pos, query_pos)
        high = jnp.maximum(key_pos, query_pos)
        seen = seen | ((low >= start) & (high < start + PIECE_LEN))
    return seen


def crosses(boundary, starts):
    met = jnp.bool_(False)
    for start in starts:
        met = met | ((start < boundary) & (start + PIECE_LEN > boundary))
    return met


def head_lanes(rows):
    return lax.broadcasted_iota(jnp.int32, (rows, OWN), 1) // HEAD_DIM


def attend_kernel(blocks, facts, near, far, mixed, logs, q_own, k_own, v_turned, acc, top, total):
    me = facts[0]
    starts = [facts[1 + i] for i in range(facts.shape[0] - 1)]
    for j in range(N_SHARD):
        src = near if j < 2 else far
        base = (j % 2) * 2 * TILE
        for half in range(2):
            rows = slice(base + half * TILE, base + (half + 1) * TILE)
            at = (me ^ j) * 2 + half
            q_own[at] = src[rows, 0:OWN] * jnp.asarray(HEAD_DIM**-0.5, bf16)
            k_own[at] = src[rows, OWN : 2 * OWN]
            v_turned[at] = src[rows, 2 * OWN : 3 * OWN].astype(f32).T.astype(bf16)
    lanes = head_lanes(TILE)

    def query_block(i, unused):
        q_i = q_own[i]
        q_heads = [jnp.where(lanes == h, q_i, jnp.zeros_like(q_i)) for h in range(OWN_HEADS)]
        acc[...] = jnp.zeros_like(acc)
        top[...] = jnp.full_like(top, NEG)
        total[...] = jnp.zeros_like(total)

        def key_block(j, masked):
            k_j = k_own[j]
            v_j = v_turned[j]
            seen = visible_tile(j, i, starts) if masked else None
            for h in range(OWN_HEADS):
                scores = dot_nt(k_j, q_heads[h])
                if masked:
                    scores = jnp.where(seen, scores, NEG)
                old_top = top[h : h + 1, :]
                new_top = jnp.maximum(old_top, jnp.max(scores, axis=0, keepdims=True))
                raised = jnp.exp(scores - new_top)
                fade = jnp.exp(old_top - new_top)
                top[h : h + 1, :] = new_top
                total[h : h + 1, :] = total[h : h + 1, :] * fade + jnp.sum(
                    raised, axis=0, keepdims=True
                )
                part = dot_nn(v_j[h * HEAD_DIM : (h + 1) * HEAD_DIM, :], raised.astype(bf16))
                rows = slice(h * HEAD_DIM, (h + 1) * HEAD_DIM)
                acc[rows, :] = acc[rows, :] * fade + part

        def plain(j, unused):
            key_block(j, False)
            return unused

        lax.fori_loop(0, i, plain, 0)
        key_block(i, True)

        @pl.when((i + 1 < blocks) & crosses((i + 1) * TILE, starts))
        def _():
            key_block(i + 1, True)

        for h in range(OWN_HEADS):
            rows = slice(h * HEAD_DIM, (h + 1) * HEAD_DIM)
            acc[rows, :] = acc[rows, :] / total[h : h + 1, :]
        place = ((i // 2) ^ me) * (2 * TILE) + (i % 2) * TILE
        mixed[pl.ds(pl.multiple_of(place, TILE), TILE), :] = acc[...].T.astype(bf16)
        logs[i] = top[...] + jnp.log(jnp.maximum(total[...], 1e-30))
        return unused

    lax.fori_loop(0, blocks, query_block, 0)


def attend(facts, near, far):
    rows = near.shape[0] + far.shape[0]
    blocks = rows // TILE
    vmem = pl.BlockSpec(memory_space=pltpu.VMEM)
    return pl.pallas_call(
        functools.partial(attend_kernel, blocks),
        out_shape=(
            jax.ShapeDtypeStruct((rows, OWN), bf16),
            jax.ShapeDtypeStruct((blocks, 8, TILE), f32),
        ),
        in_specs=[pl.BlockSpec(memory_space=pltpu.SMEM), vmem, vmem],
        out_specs=(vmem, vmem),
        scratch_shapes=[
            pltpu.VMEM((blocks, TILE, OWN), bf16),
            pltpu.VMEM((blocks, TILE, OWN), bf16),
            pltpu.VMEM((blocks, OWN, TILE), bf16),
            pltpu.VMEM((OWN, TILE), f32),
            pltpu.VMEM((8, TILE), f32),
            pltpu.VMEM((8, TILE), f32),
        ],
        compiler_params=pltpu.CompilerParams(vmem_limit_bytes=48 * 2**20),
        cost_estimate=pl.CostEstimate(
            flops=rows * rows * OWN * 8, bytes_accessed=rows * OWN * 10, transcendentals=rows * rows * 2
        ),
        name="attend",
    )(facts, near, far)


def attend_back_kernel(
    blocks, facts, near, far, mixed, g0, g1, g2, g3, logs, grads,
    q_own, k_own, v_own, k_turned, g_own, q_heads, g_heads, deltas, q_grad, k_grad, v_grad, k_heads, v_heads,
):
    me = facts[0]
    starts = [facts[1 + i] for i in range(facts.shape[0] - 1)]
    lanes = head_lanes(TILE)
    pick = (
        lax.broadcasted_iota(jnp.int32, (8, OWN), 1) // HEAD_DIM
        == lax.broadcasted_iota(jnp.int32, (8, OWN), 0)
    ).astype(f32)
    for j in range(N_SHARD):
        src = near if j < 2 else far
        grad_src = (g0, g1, g2, g3)[j]
        base = (j % 2) * 2 * TILE
        for half in range(2):
            rows = slice(base + half * TILE, base + (half + 1) * TILE)
            at = (me ^ j) * 2 + half
            q_tile = src[rows, 0:OWN] * jnp.asarray(HEAD_DIM**-0.5, bf16)
            k_tile = src[rows, OWN : 2 * OWN]
            g_tile = grad_src[half * TILE : (half + 1) * TILE, :]
            o_tile = mixed[j * 2 * TILE + half * TILE : j * 2 * TILE + (half + 1) * TILE, :]
            q_own[at] = q_tile
            k_own[at] = k_tile
            v_own[at] = src[rows, 2 * OWN : 3 * OWN]
            k_turned[at] = k_tile.astype(f32).T.astype(bf16)
            g_own[at] = g_tile
            for h in range(OWN_HEADS):
                q_heads[at, h * TILE : (h + 1) * TILE, :] = jnp.where(lanes == h, q_tile, jnp.zeros_like(q_tile))
                g_heads[at, h * TILE : (h + 1) * TILE, :] = jnp.where(lanes == h, g_tile, jnp.zeros_like(g_tile))
            both = g_tile.astype(f32) * o_tile.astype(f32)
            deltas[at] = lax.dot_general(
                pick, both, (((1,), (1,)), ((), ())),
                precision=lax.Precision.HIGHEST, preferred_element_type=f32,
            )
    q_grad[...] = jnp.zeros_like(q_grad)

    def key_block(j, unused):
        k_j = k_own[j]
        v_j = v_own[j]
        for h in range(OWN_HEADS):
            k_heads[h * TILE : (h + 1) * TILE, :] = jnp.where(lanes == h, k_j, jnp.zeros_like(k_j))
            v_heads[h * TILE : (h + 1) * TILE, :] = jnp.where(lanes == h, v_j, jnp.zeros_like(v_j))
        k_grad[...] = jnp.zeros_like(k_grad)
        v_grad[...] = jnp.zeros_like(v_grad)

        def query_block(i, masked):
            q_i = q_own[i]
            g_i = g_own[i]
            kt = k_turned[j]
            seen = visible_tile(j, i, starts) if masked else None
            softs = []
            scored = []
            for h in range(OWN_HEADS):
                rows = slice(h * TILE, (h + 1) * TILE)
                scores = dot_nt(k_heads[rows, :], q_i)
                soft = jnp.exp(scores - logs[i, h : h + 1, :])
                if masked:
                    soft = jnp.where(seen, soft, 0.0)
                grad_soft = dot_nt(v_heads[rows, :], g_i)
                grad_scores = (soft * (grad_soft - deltas[i, h : h + 1, :])).astype(bf16)
                softs.append(soft.astype(bf16))
                scored.append(grad_scores)
                head = slice(h * HEAD_DIM, (h + 1) * HEAD_DIM)
                q_grad[i, head, :] += dot_nn(kt[head, :], grad_scores)
            v_grad[...] += dot_nn(jnp.concatenate(softs, axis=1), g_heads[i])
            k_grad[...] += dot_nn(jnp.concatenate(scored, axis=1), q_heads[i])

        def plain(i, unused):
            query_block(i, False)
            return unused

        @pl.when((j > 0) & crosses(j * TILE, starts))
        def _():
            query_block(j - 1, True)

        query_block(j, True)
        lax.fori_loop(j + 1, blocks, plain, 0)
        place = pl.multiple_of(((j // 2) ^ me) * (2 * TILE) + (j % 2) * TILE, TILE)
        grads[pl.ds(place, TILE), OWN : 2 * OWN] = k_grad[...].astype(bf16)
        grads[pl.ds(place, TILE), 2 * OWN : 3 * OWN] = v_grad[...].astype(bf16)
        return unused

    lax.fori_loop(0, blocks, key_block, 0)

    def write_query(i, unused):
        place = pl.multiple_of(((i // 2) ^ me) * (2 * TILE) + (i % 2) * TILE, TILE)
        grads[pl.ds(place, TILE), 0:OWN] = (q_grad[i] * HEAD_DIM**-0.5).T.astype(bf16)
        return unused

    lax.fori_loop(0, blocks, write_query, 0)


def attend_back(facts, near, far, mixed, grad_blocks, logs):
    rows = near.shape[0] + far.shape[0]
    blocks = rows // TILE
    vmem = pl.BlockSpec(memory_space=pltpu.VMEM)
    tile = lambda n, m, kind: pltpu.VMEM((n, m), kind)
    stack = lambda n, m, kind: pltpu.VMEM((blocks, n, m), kind)
    return pl.pallas_call(
        functools.partial(attend_back_kernel, blocks),
        out_shape=jax.ShapeDtypeStruct((rows, 3 * OWN), bf16),
        in_specs=[pl.BlockSpec(memory_space=pltpu.SMEM)] + [vmem] * 8,
        out_specs=vmem,
        scratch_shapes=[
            stack(TILE, OWN, bf16),
            stack(TILE, OWN, bf16),
            stack(TILE, OWN, bf16),
            stack(OWN, TILE, bf16),
            stack(TILE, OWN, bf16),
            stack(OWN_HEADS * TILE, OWN, bf16),
            stack(OWN_HEADS * TILE, OWN, bf16),
            stack(8, TILE, f32),
            stack(OWN, TILE, f32),
            tile(TILE, OWN, f32),
            tile(TILE, OWN, f32),
            tile(OWN_HEADS * TILE, OWN, bf16),
            tile(OWN_HEADS * TILE, OWN, bf16),
        ],
        compiler_params=pltpu.CompilerParams(vmem_limit_bytes=56 * 2**20),
        cost_estimate=pl.CostEstimate(
            flops=rows * rows * OWN * 20, bytes_accessed=rows * OWN * 20, transcendentals=rows * rows * 2
        ),
        name="attend_back",
    )(facts, near, far, mixed, *grad_blocks, logs)


def expert_tile(counts, step, tiles):
    block = step // tiles
    start = (step % tiles) * TILE
    border = counts[block, 0] - start
    late = lax.broadcasted_iota(jnp.int32, (TILE, 1), 0) >= border
    return border, late


def expert_kernel(tiles, counts, rows_a, rows_b, w_in, in_bias, w_back, hidden, out_a, out_b, held):
    step = pl.program_id(0)
    border, late = expert_tile(counts, step, tiles)

    def work(rows, out):
        @pl.when(border > 0)
        def _():
            held[...] = jnp.maximum(dot_nn(rows[...], w_in[0]) + in_bias[0:1, :], 0.0).astype(bf16)

        @pl.when(border < TILE)
        def _():
            one = jnp.maximum(dot_nn(rows[...], w_in[1]) + in_bias[1:2, :], 0.0).astype(bf16)
            held[...] = jnp.where(late, one, held[...])

        hidden[...] = held[...]

        @pl.when(border > 0)
        def _():
            out[...] = dot_nn(held[...], w_back[0]).astype(bf16)

        @pl.when(border < TILE)
        def _():
            out[...] = jnp.where(late, dot_nn(held[...], w_back[1]).astype(bf16), out[...])

    @pl.when(step < tiles)
    def _():
        work(rows_a, out_a)

    @pl.when(step >= tiles)
    def _():
        work(rows_b, out_b)


def expert_back_kernel(tiles, counts, rows_a, rows_b, hidden, w_in, w_back, grad_pre, out_a, out_b, held):
    step = pl.program_id(0)
    border, late = expert_tile(counts, step, tiles)

    def work(rows, out):
        alive = hidden[...] > 0

        @pl.when(border > 0)
        def _():
            held[...] = jnp.where(alive, dot_nt(rows[...], w_back[0]), 0.0).astype(bf16)

        @pl.when(border < TILE)
        def _():
            one = jnp.where(alive, dot_nt(rows[...], w_back[1]), 0.0).astype(bf16)
            held[...] = jnp.where(late, one, held[...])

        grad_pre[...] = held[...]

        @pl.when(border > 0)
        def _():
            out[...] = dot_nt(held[...], w_in[0]).astype(bf16)

        @pl.when(border < TILE)
        def _():
            out[...] = jnp.where(late, dot_nt(held[...], w_in[1]).astype(bf16), out[...])

    @pl.when(step < tiles)
    def _():
        work(rows_a, out_a)

    @pl.when(step >= tiles)
    def _():
        work(rows_b, out_b)


def expert_specs(rows, width, inner):
    tiles = rows // TILE
    first = pl.BlockSpec((TILE, width), lambda i, c: (jnp.minimum(i, tiles - 1), 0))
    second = pl.BlockSpec((TILE, width), lambda i, c: (jnp.maximum(i - tiles, 0), 0))
    both = pl.BlockSpec((TILE, inner), lambda i, c: (i, 0))
    once = pl.Buffered(1)
    w_in = pl.BlockSpec((EXPERTS, width, inner), lambda i, c: (0, 0, 0), pipeline_mode=once)
    w_back = pl.BlockSpec((EXPERTS, inner, width), lambda i, c: (0, 0, 0), pipeline_mode=once)
    bias = pl.BlockSpec((EXPERTS, inner), lambda i, c: (0, 0), pipeline_mode=once)
    return tiles, first, second, both, w_in, w_back, bias


def run_experts(counts, rows_a, rows_b, w_in, in_bias, w_back):
    rows, width = rows_a.shape
    inner = w_in.shape[2]
    tiles, first, second, both, in_spec, back_spec, bias_spec = expert_specs(rows, width, inner)
    return pl.pallas_call(
        functools.partial(expert_kernel, tiles),
        grid_spec=pltpu.PrefetchScalarGridSpec(
            num_scalar_prefetch=1,
            grid=(2 * tiles,),
            in_specs=[first, second, in_spec, bias_spec, back_spec],
            out_specs=[both, first, second],
            scratch_shapes=[pltpu.VMEM((TILE, inner), bf16)],
        ),
        out_shape=(
            jax.ShapeDtypeStruct((2 * rows, inner), bf16),
            jax.ShapeDtypeStruct((rows, width), bf16),
            jax.ShapeDtypeStruct((rows, width), bf16),
        ),
        compiler_params=pltpu.CompilerParams(vmem_limit_bytes=40 * 2**20),
        cost_estimate=pl.CostEstimate(
            flops=2 * rows * width * inner * 4, bytes_accessed=4 * width * inner * 2, transcendentals=0
        ),
        name="experts",
    )(counts, rows_a, rows_b, w_in, in_bias, w_back)


def run_experts_back(counts, rows_a, rows_b, hidden, w_in, w_back):
    rows, width = rows_a.shape
    inner = w_in.shape[2]
    tiles, first, second, both, in_spec, back_spec, bias_spec = expert_specs(rows, width, inner)
    return pl.pallas_call(
        functools.partial(expert_back_kernel, tiles),
        grid_spec=pltpu.PrefetchScalarGridSpec(
            num_scalar_prefetch=1,
            grid=(2 * tiles,),
            in_specs=[first, second, both, in_spec, back_spec],
            out_specs=[both, first, second],
            scratch_shapes=[pltpu.VMEM((TILE, inner), bf16)],
        ),
        out_shape=(
            jax.ShapeDtypeStruct((2 * rows, inner), bf16),
            jax.ShapeDtypeStruct((rows, width), bf16),
            jax.ShapeDtypeStruct((rows, width), bf16),
        ),
        compiler_params=pltpu.CompilerParams(vmem_limit_bytes=40 * 2**20),
        cost_estimate=pl.CostEstimate(
            flops=2 * rows * width * inner * 4, bytes_accessed=4 * width * inner * 2, transcendentals=0
        ),
        name="experts_back",
    )(counts, rows_a, rows_b, hidden, w_in, w_back)


def shards(
    n_rep,
    tokens,
    token_ids,
    hash_table,
    piece_starts,
    valid_mask,
    teacher,
    cotangent,
    ln1_gain,
    ln1_bias,
    w_qkv,
    w_out,
    out_bias,
    ln2_gain,
    ln2_bias,
    w_in,
    in_bias,
    w_back,
    back_bias,
):
    local_rows = tokens.shape[0]
    tokens_all = local_rows * N_SHARD * n_rep
    me = lax.axis_index("shard").astype(jnp.int32)
    rep_at = lax.axis_index("rep")
    inner = w_back.shape[1]
    facts = jnp.concatenate([me[None], piece_starts[0]])

    tok_blocks = gather_blocks(tokens)

    expert_of = jnp.take(hash_table, token_ids)
    places = jnp.arange(local_rows, dtype=jnp.int32)
    earlier = (expert_of[:, None] == expert_of[None, :]) & (places[None, :] < places[:, None])
    slot_of = jnp.sum(earlier.astype(jnp.int32), axis=1)
    kept = slot_of < CAP
    is_late = expert_of > 0
    late_count = jnp.sum(is_late.astype(jnp.int32))
    own_counts = jnp.stack(
        [jnp.minimum(local_rows - late_count, CAP), jnp.minimum(late_count, CAP)]
    )
    sorted_at = jnp.where(kept, slot_of + jnp.where(is_late, own_counts[0], 0), -1)
    sorter = (sorted_at[None, :] == places[:, None]).astype(bf16)

    counted = valid_mask.astype(f32)
    own_count = jnp.sum(counted)
    shard_width = ln1_gain.shape[0]
    lasts = jnp.zeros((1, shard_width), f32)
    lasts = lasts.at[0, 0].set(own_counts[0].astype(f32)).at[0, 1].set(own_count)
    packed = jnp.concatenate(
        [
            jnp.stack([v.astype(f32) for v in (ln1_gain, ln1_bias, out_bias, ln2_gain, ln2_bias)]),
            back_bias.astype(f32),
            lasts,
        ],
        axis=0,
    )
    everyone = lax.all_gather(packed, ("rep", "shard"), axis=0).reshape(
        n_rep, N_SHARD, 8, shard_width
    )
    count_all = jnp.sum(everyone[:, :, 7, 1])
    mine = lax.dynamic_index_in_dim(everyone, rep_at, 0, keepdims=False)
    rows_of = mine[:, :7].transpose(1, 0, 2).reshape(7, N_SHARD * shard_width)
    gain_one, bias_one, out_shift, gain_two, bias_two = [rows_of[i] for i in range(5)]
    back_shift = rows_of[5:7]
    borders = jnp.take(mine[:, 7, 0], me ^ jnp.arange(N_SHARD, dtype=jnp.int32)).astype(jnp.int32)
    counts_near, counts_far = borders[:2, None], borders[2:, None]

    heads_in = w_qkv.reshape(shard_width, 3, N_SHARD, OWN)
    qkv_weight = lax.all_to_all(heads_in, "shard", split_axis=2, concat_axis=0, tiled=True)
    qkv_weight = qkv_weight.reshape(D, 3 * OWN)
    slice_width = inner // n_rep
    thin = lax.dynamic_index_in_dim(
        w_in.reshape(EXPERTS, shard_width, N_SHARD, n_rep, slice_width), rep_at, 3, keepdims=False
    )
    thin = lax.all_to_all(thin, "shard", split_axis=2, concat_axis=1, tiled=True)
    in_weight = lax.all_gather(thin.reshape(EXPERTS, D, slice_width), "rep", axis=0)
    in_weight = in_weight.transpose(1, 2, 0, 3).reshape(EXPERTS, D, inner)
    out_blocks = gather_blocks(w_out)

    def first_rows(block):
        normed, inverse = layer_norm(block.astype(f32))
        return (normed * gain_one + bias_one).astype(bf16), normed, inverse

    first_near = jnp.concatenate([first_rows(tok_blocks[0])[0], first_rows(tok_blocks[1])[0]], axis=0)
    first_far = jnp.concatenate([first_rows(tok_blocks[2])[0], first_rows(tok_blocks[3])[0]], axis=0)
    qkv_near = dot_nn(first_near, qkv_weight).astype(bf16)
    qkv_far = dot_nn(first_far, qkv_weight).astype(bf16)

    mixed, logs = attend(facts, qkv_near, qkv_far)
    mixed_blocks = exchange_blocks(
        [mixed[j * local_rows : (j + 1) * local_rows] for j in range(N_SHARD)]
    )
    tok_rows = tokens.astype(f32)
    branch = dot_nn(mixed_blocks[0], out_blocks[0])
    for j in range(1, N_SHARD):
        branch = branch + dot_nn(mixed_blocks[j], out_blocks[j])
    middle = tok_rows + branch + out_shift
    normed_two, inverse_two = layer_norm(middle)
    second_in = (normed_two * gain_two + bias_two).astype(bf16)
    sorted_in = dot_nn(sorter, second_in).astype(bf16)
    rows_in = gather_blocks(sorted_in)
    bias_in = in_bias.astype(f32)
    hidden_near, out0, out1 = run_experts(counts_near, rows_in[0], rows_in[1], in_weight, bias_in, w_back)
    hidden_far, out2, out3 = run_experts(counts_far, rows_in[2], rows_in[3], in_weight, bias_in, w_back)
    summed = scatter_near(out0, out1, scatter_far(out2, out3))
    picked = dot_tn(sorter, summed.astype(bf16))
    picked = picked + jnp.where(is_late[:, None], back_shift[1], back_shift[0])
    final = middle + jnp.where(kept[:, None], picked, 0.0)
    grad_final = cotangent.astype(f32) + tokens_all / (2.0 * count_all) * counted[:, None] * (
        final - teacher.astype(f32)
    )
    grad_low = grad_final.astype(bf16)

    sorted_grad = dot_nn(sorter, grad_low).astype(bf16)
    rows_grad = gather_blocks(sorted_grad)
    pre_near, gin0, gin1 = run_experts_back(
        counts_near, rows_grad[0], rows_grad[1], hidden_near, in_weight, w_back
    )
    pre_far, gin2, gin3 = run_experts_back(
        counts_far, rows_grad[2], rows_grad[3], hidden_far, in_weight, w_back
    )
    summed_grad = scatter_near(gin0, gin1, scatter_far(gin2, gin3))
    grad_second = dot_tn(sorter, summed_grad.astype(bf16))

    early = (jnp.arange(local_rows, dtype=jnp.int32)[None, :] < borders[:, None]).reshape(-1)
    hidden_all = jnp.concatenate([hidden_near, hidden_far], axis=0)
    pre_all = jnp.concatenate([pre_near, pre_far], axis=0)
    in_all = jnp.concatenate(rows_in, axis=0)
    grad_all = jnp.concatenate(rows_grad, axis=0)
    masks = [early[:, None], ~early[:, None]]
    back_grad = jnp.concatenate(
        [dot_tn(jnp.where(m, hidden_all, 0), grad_all).astype(bf16) for m in masks], axis=0
    )
    in_grad = [dot_tn(in_all, jnp.where(m, pre_all, 0)).astype(bf16) for m in masks]
    in_shift_grad = jnp.stack([jnp.sum(jnp.where(m, pre_all.astype(f32), 0), axis=0) for m in masks])
    back_grad = rep_sum(back_grad, 3, n_rep)

    grad_gain_two = jnp.sum(grad_second * normed_two, axis=0)
    grad_bias_two = jnp.sum(grad_second, axis=0)
    grad_middle = grad_final + norm_back(grad_second, normed_two, inverse_two, gain_two)
    grad_branch = grad_middle.astype(bf16)
    grad_out_shift = jnp.sum(grad_branch.astype(f32), axis=0)
    grad_mixed = exchange_blocks([dot_nt(grad_branch, w).astype(bf16) for w in out_blocks])

    grad_qkv = attend_back(facts, qkv_near, qkv_far, mixed, grad_mixed, logs)

    def row_block(array, j, size):
        return lax.dynamic_slice_in_dim(array, (me ^ j) * size, size, axis=0)

    in_parts = exchange_blocks(
        [
            jnp.concatenate([row_block(g, j, shard_width) for g in in_grad], axis=0)
            for j in range(N_SHARD)
        ]
    )
    in_parts = rep_sum(jnp.concatenate(in_parts, axis=0), 3, n_rep)

    out_parts = [dot_tn(b, grad_branch).astype(bf16) for b in mixed_blocks]
    out_grad = scatter_near(
        out_parts[0], out_parts[1], scatter_far(out_parts[2], out_parts[3])
    ).astype(bf16)

    first_grads = [
        dot_nt(grad_qkv[j * local_rows : (j + 1) * local_rows], qkv_weight).astype(bf16)
        for j in range(N_SHARD)
    ]
    grad_first = scatter_near(first_grads[0], first_grads[1], scatter_far(first_grads[2], first_grads[3]))
    first_all = jnp.concatenate([first_near, first_far], axis=0)
    qkv_grad = dot_tn(first_all, grad_qkv).astype(bf16)
    qkv_parts = exchange_blocks([row_block(qkv_grad, j, shard_width) for j in range(N_SHARD)])
    qkv_parts = jnp.concatenate(qkv_parts, axis=0)
    last_rows = jnp.concatenate([qkv_parts.reshape(-1, D), out_grad], axis=0)
    last_rows = rep_sum(last_rows, 3, n_rep)
    split_at = last_rows.shape[0] - out_grad.shape[0]
    qkv_parts = last_rows[:split_at].reshape(N_SHARD, shard_width, 3, OWN)
    out_grad = last_rows[split_at:].astype(f32)

    first_in, normed_one, inverse_one = first_rows(tokens)
    grad_gain_one = jnp.sum(grad_first * normed_one, axis=0)
    grad_bias_one = jnp.sum(grad_first, axis=0)
    input_grad = grad_middle + norm_back(grad_first, normed_one, inverse_one, gain_one)

    by_expert = jnp.stack([(kept & ~is_late), (kept & is_late)]).astype(bf16)
    grad_back_shift = dot_nn(by_expert, grad_low)
    small = jnp.concatenate(
        [
            jnp.stack([grad_gain_one, grad_bias_one, grad_out_shift, grad_gain_two, grad_bias_two]),
            grad_back_shift,
        ],
        axis=0,
    )
    small = lax.psum(small, ("rep", "shard"))
    small = lax.dynamic_slice_in_dim(small, me * shard_width, shard_width, axis=1)
    in_shift_grad = lax.psum(in_shift_grad, "rep")

    order = me ^ jnp.arange(N_SHARD, dtype=jnp.int32)
    in_grad = jnp.take(in_parts.reshape(N_SHARD, EXPERTS, shard_width, inner), order, axis=0)
    in_grad = in_grad.transpose(1, 2, 0, 3).reshape(EXPERTS, shard_width, N_SHARD * inner)
    qkv_grad = jnp.take(qkv_parts, order, axis=0).transpose(1, 2, 0, 3)
    return (
        final.astype(bf16),
        input_grad,
        small[0],
        small[1],
        qkv_grad.reshape(shard_width, 3 * D).astype(f32),
        out_grad,
        small[2],
        small[3],
        small[4],
        in_grad.astype(f32),
        in_shift_grad,
        back_grad.reshape(EXPERTS, inner, D).astype(f32),
        small[5:7],
    )


def solution(mesh):
    in_specs = (
        P(("rep", "shard"), None),
        P(("rep", "shard")),
        P(),
        P("rep", None),
        P(("rep", "shard")),
        P(("rep", "shard"), None),
        P(("rep", "shard"), None),
        P("shard"),
        P("shard"),
        P("shard", None),
        P("shard", None),
        P("shard"),
        P("shard"),
        P("shard"),
        P(None, "shard", None),
        P(None, "shard"),
        P(None, "shard", None),
        P(None, "shard"),
    )
    out_specs = (
        P(("rep", "shard"), None),
        P(("rep", "shard"), None),
        P("shard"),
        P("shard"),
        P("shard", None),
        P("shard", None),
        P("shard"),
        P("shard"),
        P("shard"),
        P(None, "shard", None),
        P(None, "shard"),
        P(None, "shard", None),
        P(None, "shard"),
    )
    body = functools.partial(shards, mesh.shape["rep"])
    return jax.shard_map(body, mesh=mesh, in_specs=in_specs, out_specs=out_specs, check_vma=False)
```

time: 1530 us -> 977 us (0.64)
  waiting for transfers between devices: 796 us -> 262 us
  matrix products: 398 us -> 77 us
  Pallas kernels: 0 us -> 158 us
  starting transfers between devices: 1.07 us -> 155 us
  local copies, waits for them, and re-layouts: 113 us -> 94.2 us
    reduce_scatter x6 -> x0, waiting for transfers between devices: 381 us -> none  [the longest x1 129 us: shards(): lax.psum_scatter(grad_back_weight.astype(jnp.bfloat16), 'shard', scatter_...]
    dot_general x50 -> x28, matrix products: 398 us -> 77 us  [the longest x11 45.4 us: dot_tn(): lax.dot_general(a, b, (((0,), (0,)), ((), ())), preferred_element_type=f32)]
    psum x1 -> x0, waiting for transfers between devices: 282 us -> none  [shards(): lax.psum(owned_qkv.astype(jnp.bfloat16), 'rep').astype(jnp.float32)]
    ppermute x0 -> x90, waiting for transfers between devices: none -> 246 us  [the longest x54 155 us: rep_pair(): return lax.ppermute(value, 'rep', [(i, i ^ mask) for i in range(count)])]
    pallas_call x0 -> x6, Pallas kernels: none -> 158 us  [the longest x1 63.9 us: attend_back(): pl.pallas_call(functools.partial(attend_back_kernel, blocks), out_shape=j...]
    ppermute x0 -> x90, starting transfers between devices: none -> 146 us  [the longest x54 128 us: rep_pair(): return lax.ppermute(value, 'rep', [(i, i ^ mask) for i in range(count)])]
    all_gather x6 -> x1, waiting for transfers between devices: 81.9 us -> 0.01 us  [shards(): lax.all_gather(thin.reshape(EXPERTS, D, slice_width), 'rep', axis=0)]
    unnamed x17 -> x1, waiting for transfers between devices: 50.9 us -> 0.02 us
  transfers between devices with their start and end apart: 15 -> 93, of which waited for: 10 -> 29; matrix products, arithmetic and copies ran while one was open for 18% -> 22% of each run, Pallas kernels for 0% -> 15%
where the time goes in v1:
time: 977 us; the launch traced here: 969 us
  waiting for transfers between devices  262 us (27%)
  Pallas kernels  158 us (16%)
  starting transfers between devices  155 us (16%)
  blocking collectives  121 us (12%)
  local copies, waits for them, and re-layouts  94.2 us (10%)
  other arithmetic  83.1 us (9%)
  matrix products  77 us (8%)
  between operations  18.5 us (2%)
    ppermute x54, waiting for transfers between devices, rep_pair(): return lax.ppermute(value, 'rep', [(i, i ^ mask) for i in range(count)])  155 us
    ppermute x54, starting transfers between devices, rep_pair(): return lax.ppermute(value, 'rep', [(i, i ^ mask) for i in range(count)])  128 us
    ppermute x36, waiting for transfers between devices, swap(): return lax.ppermute(value, 'shard', [(i, i ^ mask) for i in range(N_SHARD)])  91 us
    pallas_call x1, Pallas kernels, attend_back(): pl.pallas_call(functools.partial(attend_back_kernel, blocks), out_shape=j...  63.9 us
    all_gather x1, blocking collectives, shards(): lax.all_gather(packed, ('rep', 'shard'), axis=0)  50.1 us
    dot_general x11, matrix products, dot_tn(): lax.dot_general(a, b, (((0,), (0,)), ((), ())), preferred_element_type=f32)  45.4 us
    pallas_call x1, Pallas kernels, attend(): pl.pallas_call(functools.partial(attend_kernel, blocks), out_shape=(jax.S...  41.9 us
    unnamed x186, local copies, waits for them, and re-layouts  41.1 us
  transfers between devices with their start and end apart: 93, of which 29 were waited for; matrix products, arithmetic and copies ran while one was open for 22% of the time, Pallas kernels for 15%

profile of v1, /device:TPU:0, one launch (start us, length us, event | category | flops | bytes accessed | tf_op | source)
XLA Modules:
  0.0 969.0 jit_solution(7310298329984575626)
XLA Ops:
  10.7 6.3 copy.93
  35.4 50.1 %all-gather = f32[256,256]{1,0:T(8,128)S(1)} all-gather(f32[8,256]{1,0:T(8,128)S(1)} %concatenate.235), channel_id=2, replica_groups=mesh['rep'=8,'shard'=4] {'rep','shard'}, dimensions={0}, use_global_device_ids=true | all-gather | bytes 270336 | tf_op jit(solution)/shard_map/all_gather | solution.py:575
  100.6 16.3 %all-to-all-done = bf16[256,3,4,256]{0,3,1,2:T(8,128)(2,1)} async-done(((bf16[256,3,4,256]{0,3,1,2:T(8,128)(2,1)}), bf16[256,3,4,256]{0,3,1,2:T(8,128)(2,1)}, u32[]{:S(2)}, u32[]{:S(2)}) %all-to-all-start) | async-done | bytes 1572896 | tf_op jit(solution)/shard_map/all_to_all | solution.py:587
  130.6 41.9 %attend.1 = (bf16[2048,256]{1,0:T(8,128)(2,1)S(1)}, f32[8,8,256]{2,1,0:T(8,128)S(1)}) custom-call(s32[3]{0:T(128)S(1)} %pad_add_fusion.facts, bf16[1024,768]{1,0:T(8,128)(2,1)S(1)} %fusion.82.near, bf16[1024,768]{1,0:T(8,128)(2,1)S(1)} %fusion.79.far), custom_call_target="tpu_custom_call" | custom-call | flops 8589934592 | bytes 5242880 | tf_op jit(solution)/shard_map/attend/pallas_call | solution.py:228
  174.9 11.5 %collective-permute-done.5 = bf16[512,256]{1,0:T(8,128)(2,1)S(1)} collective-permute-done((bf16[512,256]{1,0:T(8,128)(2,1)S(1)}, bf16[512,256]{1,0:T(8,128)(2,1)S(1)}, u32[]{:S(2)}, u32[]{:S(2)}) %collective-permute-start.5) | collective-permute-done | bytes 262176 | tf_op jit(solution)/shard_map/ppermute | solution.py:55
  194.7 24.5 %collective-permute-done.11.rows_a = bf16[512,1024]{1,0:T(8,128)(2,1)S(1)} collective-permute-done((bf16[512,1024]{1,0:T(8,128)(2,1)}, bf16[512,1024]{1,0:T(8,128)(2,1)S(1)}, u32[]{:S(2)}, u32[]{:S(2)}) %collective-permute-start.11) | collective-permute-done | bytes 1048608 | tf_op jit(solution)/shard_map/ppermute | solution.py:55
  227.7 12.9 %experts.3 = (bf16[1024,1024]{1,0:T(8,128)(2,1)S(1)}, bf16[512,1024]{1,0:T(8,128)(2,1)S(1)}, bf16[512,1024]{1,0:T(8,128)(2,1)}) custom-call(s32[2,1]{1,0:T(2,128)S(1)} %copy.99.counts, bf16[512,1024]{1,0:T(8,128)(2,1)S(1)} %copy-done.16, bf16[512,1024]{1,0:T(8,128)(2,1)S(1)} %copy-done.19, bf16[2,1024,1024]{2,1,0:T(8,128)(2,1)S(1)} %copy_bitcast_fusion.w_in, ...), custom_call_target="tpu_custom_call" | custom-call | flops 4294967296 | bytes 8388608 | tf_op jit(solution)/shard_map/experts/pallas_call | solution.py:471
  243.9 12.9 %experts.2 = (bf16[1024,1024]{1,0:T(8,128)(2,1)S(1)}, bf16[512,1024]{1,0:T(8,128)(2,1)S(1)}, bf16[512,1024]{1,0:T(8,128)(2,1)}) custom-call(s32[2,1]{1,0:T(2,128)S(1)} %copy.98.counts, bf16[512,1024]{1,0:T(8,128)(2,1)} %convolution_convert_fusion.5.rows_a, bf16[512,1024]{1,0:T(8,128)(2,1)} %collective-permute-done.9.rows_b, ...), custom_call_target="tpu_custom_call" | custom-call | flops 4294967296 | bytes 8388608 | tf_op jit(solution)/shard_map/experts/pallas_call | solution.py:471
  264.9 22.6 %collective-permute-done.14 = bf16[512,1024]{1,0:T(8,128)(2,1)} collective-permute-done((bf16[512,1024]{1,0:T(8,128)(2,1)}, bf16[512,1024]{1,0:T(8,128)(2,1)}, u32[]{:S(2)}, u32[]{:S(2)}) %collective-permute-start.14) | collective-permute-done | bytes 1048608 | tf_op jit(solution)/shard_map/ppermute | solution.py:55
  287.5 5.4 multiply_add_fusion.1
  296.7 23.8 %collective-permute-done.17.rows_a = bf16[512,1024]{1,0:T(8,128)(2,1)} collective-permute-done((bf16[512,1024]{1,0:T(8,128)(2,1)}, bf16[512,1024]{1,0:T(8,128)(2,1)}, u32[]{:S(2)}, u32[]{:S(2)}) %collective-permute-start.17) | collective-permute-done | bytes 1048608 | tf_op jit(solution)/shard_map/ppermute | solution.py:55
  327.6 13.0 %experts_back.2 = (bf16[1024,1024]{1,0:T(8,128)(2,1)S(1)}, bf16[512,1024]{1,0:T(8,128)(2,1)S(1)}, bf16[512,1024]{1,0:T(8,128)(2,1)S(1)}) custom-call(s32[2,1]{1,0:T(2,128)S(1)} %copy.98.counts, bf16[512,1024]{1,0:T(8,128)(2,1)} %convolution_convert_fusion.4.rows_a, bf16[512,1024]{1,0:T(8,128)(2,1)} %collective-permute-done.15.rows_b, ...), custom_call_target="tpu_custom_call" | custom-call | flops 4294967296 | bytes 8388608 | tf_op jit(solution)/shard_map/experts_back/pallas_call | solution.py:497
  342.0 13.5 %experts_back.3 = (bf16[1024,1024]{1,0:T(8,128)(2,1)S(1)}, bf16[512,1024]{1,0:T(8,128)(2,1)S(1)}, bf16[512,1024]{1,0:T(8,128)(2,1)}) custom-call(s32[2,1]{1,0:T(2,128)S(1)} %copy.99.counts, bf16[512,1024]{1,0:T(8,128)(2,1)} %collective-permute-done.17.rows_a, bf16[512,1024]{1,0:T(8,128)(2,1)S(1)} %collective-permute-done.18.rows_b, ...), custom_call_target="tpu_custom_call" | custom-call | flops 4294967296 | bytes 8388608 | tf_op jit(solution)/shard_map/experts_back/pallas_call | solution.py:497
  359.0 7.8 fusion.76
  366.9 7.8 fusion.73
  377.0 6.4 fusion.70
  383.4 6.2 fusion.67
  397.6 29.9 %psum.15 = f32[2,1024]{1,0:T(2,128)} all-reduce(f32[2,1024]{1,0:T(2,128)S(1)} %pad_maximum_fusion.20), channel_id=1, replica_groups=mesh['rep'=8,'shard'=4] {'rep'}, use_global_device_ids=true, to_apply=%region_28.29 | all-reduce | flops 2048 | bytes 16384 | tf_op jit(solution)/shard_map/psum | solution.py:712
  432.1 14.7 %collective-permute-start.79 = (bf16[160,1024]{1,0:T(8,128)(2,1)S(1)}, bf16[160,1024]{1,0:T(8,128)(2,1)S(1)}, u32[]{:S(2)}, u32[]{:S(2)}) collective-permute-start(bf16[160,1024]{1,0:T(8,128)(2,1)S(1)} %dynamic-slice_bitcast_fusion.11), channel_id=1, source_target_pairs={{0,24},{4,28},{8,16},{12,20},{16,8},{20,12},{24,0},{28,4},{1,25},{... | collective-permute-start | bytes 983048 | tf_op jit(solution)/shard_map/ppermute | solution.py:90
  448.2 7.0 collective-permute-done.79
  455.2 7.5 collective-permute-start.73
  462.8 7.8 collective-permute-done.73
  479.5 6.4 collective-permute-done.80
  494.2 6.0 collective-permute-done.86
  504.1 10.2 %collective-permute-done.87 = bf16[96,1024]{1,0:T(8,128)(2,1)S(1)} collective-permute-done((bf16[96,1024]{1,0:T(8,128)(2,1)S(1)}, bf16[96,1024]{1,0:T(8,128)(2,1)S(1)}, u32[]{:S(2)}, u32[]{:S(2)}) %collective-permute-start.87) | collective-permute-done | bytes 196640 | tf_op jit(solution)/shard_map/ppermute | solution.py:90
  515.7 5.5 collective-permute-done.76
  524.5 7.4 collective-permute-done.52
  533.6 10.0 %collective-permute-done.66 = bf16[384,1024]{1,0:T(8,128)(2,1)S(1)} collective-permute-done((bf16[384,1024]{1,0:T(8,128)(2,1)S(1)}, bf16[384,1024]{1,0:T(8,128)(2,1)S(1)}, u32[]{:S(2)}, u32[]{:S(2)}) %collective-permute-start.66) | collective-permute-done | bytes 786464 | tf_op jit(solution)/shard_map/ppermute | solution.py:90
  546.9 16.9 %collective-permute-done.60 = bf16[160,1024]{1,0:T(8,128)(2,1)S(1)} collective-permute-done((bf16[160,1024]{1,0:T(8,128)(2,1)S(1)}, bf16[160,1024]{1,0:T(8,128)(2,1)S(1)}, u32[]{:S(2)}, u32[]{:S(2)}) %collective-permute-start.60) | collective-permute-done | bytes 327712 | tf_op jit(solution)/shard_map/ppermute | solution.py:90
  563.8 7.5 collective-permute-start.53
  571.5 7.8 collective-permute-done.53
  609.3 20.1 %collective-permute-start.68 = (bf16[96,1024]{1,0:T(8,128)(2,1)S(1)}, bf16[96,1024]{1,0:T(8,128)(2,1)S(1)}, u32[]{:S(2)}, u32[]{:S(2)}) collective-permute-start(bf16[96,1024]{1,0:T(8,128)(2,1)S(1)} %dynamic-slice_bitcast_fusion.17), channel_id=1, source_target_pairs={{0,8},{4,12},{8,0},{12,4},{16,24},{20,28},{24,16},{28,20},{1,9},{5... | collective-permute-start | bytes 589832 | tf_op jit(solution)/shard_map/ppermute | solution.py:90
  631.7 63.9 %attend_back.1 = bf16[2048,768]{1,0:T(8,128)(2,1)} custom-call(s32[3]{0:T(128)} %copy-done.21, bf16[1024,768]{1,0:T(8,128)(2,1)} %copy-done.24, bf16[1024,768]{1,0:T(8,128)(2,1)} %copy-done.25, bf16[2048,256]{1,0:T(8,128)(2,1)} %copy-done.7, bf16[512,256]{1,0:T(8,128)(2,1)} %convolution_convert_fusion.13.g0, bf16[512,256]{1,0:T(8,128)(2,1)} %copy-done.75, ...), custom_call_target="tpu_custom_call" | custom-call | flops 21474836480 | bytes 10485760 | tf_op jit(solution)/shard_map/attend_back/pallas_call | solution.py:351
  698.9 6.0 fusion.85
  706.9 4.6 collective-permute-start.69
  730.3 4.4 collective-permute-done.28
  745.2 4.4 convert.64
  756.6 14.8 %collective-permute-done.31 = bf16[64,1024]{1,0:T(8,128)(2,1)S(1)} collective-permute-done((bf16[64,1024]{1,0:T(8,128)(2,1)S(1)}, bf16[64,1024]{1,0:T(8,128)(2,1)S(1)}, u32[]{:S(2)}, u32[]{:S(2)}) %collective-permute-start.31) | collective-permute-done | bytes 131104 | tf_op jit(solution)/shard_map/ppermute | solution.py:90
  789.1 24.6 %collective-permute-done.34 = bf16[64,1024]{1,0:T(8,128)(2,1)S(1)} collective-permute-done((bf16[64,1024]{1,0:T(8,128)(2,1)S(1)}, bf16[64,1024]{1,0:T(8,128)(2,1)S(1)}, u32[]{:S(2)}, u32[]{:S(2)}) %collective-permute-start.34) | collective-permute-done | bytes 131104 | tf_op jit(solution)/shard_map/ppermute | solution.py:90
  818.3 6.4 collective-permute-done.36
  830.9 13.2 %collective-permute-start.47 = (bf16[48,1024]{1,0:T(8,128)(2,1)S(1)}, bf16[48,1024]{1,0:T(8,128)(2,1)S(1)}, u32[]{:S(2)}, u32[]{:S(2)}) collective-permute-start(bf16[48,1024]{1,0:T(8,128)(2,1)S(1)} %dynamic-slice_bitcast_fusion.25), channel_id=1, source_target_pairs={{0,8},{4,12},{8,0},{12,4},{16,24},{20,28},{24,16},{28,20},{1,9},{5... | collective-permute-start | bytes 294920 | tf_op jit(solution)/shard_map/ppermute | solution.py:90
  849.2 5.2 gather_fusion.3
  856.1 5.0 collective-permute-done.48
  862.8 6.2 convert_bitcast_fusion
  869.0 8.8 copy.103
  877.8 9.0 copy.105
  890.8 5.0 fusion.40
  895.9 40.9 %psum.14 = f32[7,1024]{1,0:T(8,128)S(1)} all-reduce(f32[7,1024]{1,0:T(8,128)S(1)} %concatenate.238), channel_id=1, replica_groups=mesh['rep'=8,'shard'=4] {'rep','shard'}, use_global_device_ids=true, to_apply=%region_25.26 | all-reduce | flops 7168 | bytes 57344 | tf_op jit(solution)/shard_map/psum | solution.py:710
  (554 shorter events, 280.8 us)
Async XLA Ops:
  7.2 92.0 %collective-permute-start.1 = (bf16[512,1024]{1,0:T(8,128)(2,1)}, bf16[512,1024]{1,0:T(8,128)(2,1)S(1)}, u32[]{:S(2)}, u32[]{:S(2)}) collective-permute-start(bf16[512,1024]{1,0:T(8,128)(2,1)} %param.22), channel_id=1, source_target_pairs={{0,2},{1,3},{2,0},{3,1},{4,6},{5,7},{6,4},{7,5},{8,10},{9,11},{10,... | collective-permute-start | bytes 3145736 | tf_op jit(solution)/shard_map/ppermute | solution.py:55
  10.2 89.3 %collective-permute-start = (bf16[512,1024]{1,0:T(8,128)(2,1)}, bf16[512,1024]{1,0:T(8,128)(2,1)S(1)}, u32[]{:S(2)}, u32[]{:S(2)}) collective-permute-start(bf16[512,1024]{1,0:T(8,128)(2,1)} %param.22), channel_id=1, source_target_pairs={{0,1},{1,0},{2,3},{3,2},{4,5},{5,4},{6,7},{7,6},{8,9},{9,8},{10,11... | collective-permute-start | bytes 3145736 | tf_op jit(solution)/shard_map/ppermute | solution.py:55
  10.2 88.5 %collective-permute-start.6 = (bf16[256,1024]{1,0:T(8,128)(2,1)}, bf16[256,1024]{1,0:T(8,128)(2,1)}, u32[]{:S(2)}, u32[]{:S(2)}) collective-permute-start(bf16[256,1024]{1,0:T(8,128)(2,1)} %param.32), channel_id=1, source_target_pairs={{0,2},{1,3},{2,0},{3,1},{4,6},{5,7},{6,4},{7,5},{8,10},{9,11},{10,... | collective-permute-start | bytes 1572872 | tf_op jit(solution)/shard_map/ppermute | solution.py:55
  10.4 177.6 %collective-permute-start.4 = (bf16[256,1024]{1,0:T(8,128)(2,1)}, bf16[256,1024]{1,0:T(8,128)(2,1)}, u32[]{:S(2)}, u32[]{:S(2)}) collective-permute-start(bf16[256,1024]{1,0:T(8,128)(2,1)} %param.32), channel_id=1, source_target_pairs={{0,1},{1,0},{2,3},{3,2},{4,5},{5,4},{6,7},{7,6},{8,9},{9,8},{10,11... | collective-permute-start | bytes 1572872 | tf_op jit(solution)/shard_map/ppermute | solution.py:55
  19.2 73.1 %all-to-all-start.1 = ((bf16[2,256,4,128]{3,1,0,2:T(8,128)(2,1)}), bf16[2,256,4,128]{3,1,0,2:T(8,128)(2,1)}, u32[]{:S(2)}, u32[]{:S(2)}) async-start(bf16[2,256,4,128]{3,1,0,2:T(8,128)(2,1)} %copy.95), calls=%async_computation.1 | async-start | bytes 1048576 | tf_op jit(solution)/shard_map/all_to_all | solution.py:593
  92.4 24.5 %all-to-all-start = ((bf16[256,3,4,256]{0,3,1,2:T(8,128)(2,1)}), bf16[256,3,4,256]{0,3,1,2:T(8,128)(2,1)}, u32[]{:S(2)}, u32[]{:S(2)}) async-start(bf16[256,3,4,256]{0,3,1,2:T(8,128)(2,1)} %copy.91), calls=%async_computation | async-start | bytes 3145728 | tf_op jit(solution)/shard_map/all_to_all | solution.py:587
  96.7 123.9 %all-gather.3.cloned.1.call-start = ((), (), s32[]{:S(2)}) async-start(), calls=%async_computation.2 | async-start | bytes 4718592 | tf_op jit(solution)/shard_map/all_gather | solution.py:594
  98.7 90.8 %collective-permute-start.8 = (bf16[256,1024]{1,0:T(8,128)(2,1)}, bf16[256,1024]{1,0:T(8,128)(2,1)}, u32[]{:S(2)}, u32[]{:S(2)}) collective-permute-start(bf16[256,1024]{1,0:T(8,128)(2,1)} %collective-permute-done.6), channel_id=1, source_target_pairs={{0,1},{1,0},{2,3},{3,2},{4,5},{5,4},{6,7},{7,6},{8,9},{9,8},{10,11... | collective-permute-start | bytes 1572872 | tf_op jit(solution)/shard_map/ppermute | solution.py:55
  193.8 25.4 %collective-permute-start.11 = (bf16[512,1024]{1,0:T(8,128)(2,1)}, bf16[512,1024]{1,0:T(8,128)(2,1)S(1)}, u32[]{:S(2)}, u32[]{:S(2)}) collective-permute-start(bf16[512,1024]{1,0:T(8,128)(2,1)} %convolution_convert_fusion.5.rows_a), channel_id=1, source_target_pairs={{0,2},{1,3},{2,0},{3,1},{4,6},{5,7},{6,4},{7,5},{8,10},{9,11},{10,... | collective-permute-start | bytes 3145736 | tf_op jit(solution)/shard_map/ppermute | solution.py:55
  262.1 25.4 %collective-permute-start.14 = (bf16[512,1024]{1,0:T(8,128)(2,1)}, bf16[512,1024]{1,0:T(8,128)(2,1)}, u32[]{:S(2)}, u32[]{:S(2)}) collective-permute-start(bf16[512,1024]{1,0:T(8,128)(2,1)} %add_convert_fusion.4), channel_id=1, source_target_pairs={{0,2},{1,3},{2,0},{3,1},{4,6},{5,7},{6,4},{7,5},{8,10},{9,11},{10,... | collective-permute-start | bytes 3145736 | tf_op jit(solution)/shard_map/ppermute | solution.py:55
  296.0 24.6 %collective-permute-start.17 = (bf16[512,1024]{1,0:T(8,128)(2,1)}, bf16[512,1024]{1,0:T(8,128)(2,1)}, u32[]{:S(2)}, u32[]{:S(2)}) collective-permute-start(bf16[512,1024]{1,0:T(8,128)(2,1)} %convolution_convert_fusion.4.rows_a), channel_id=1, source_target_pairs={{0,2},{1,3},{2,0},{3,1},{4,6},{5,7},{6,4},{7,5},{8,10},{9,11},{10,... | collective-permute-start | bytes 3145736 | tf_op jit(solution)/shard_map/ppermute | solution.py:55
  296.5 29.7 %collective-permute-start.15 = (bf16[512,1024]{1,0:T(8,128)(2,1)}, bf16[512,1024]{1,0:T(8,128)(2,1)}, u32[]{:S(2)}, u32[]{:S(2)}) collective-permute-start(bf16[512,1024]{1,0:T(8,128)(2,1)} %convolution_convert_fusion.4.rows_a), channel_id=1, source_target_pairs={{0,1},{1,0},{2,3},{3,2},{4,5},{5,4},{6,7},{7,6},{8,9},{9,8},{10,11... | collective-permute-start | bytes 3145736 | tf_op jit(solution)/shard_map/ppermute | solution.py:55
  355.5 117.7 %collective-permute-start.19 = (bf16[512,1024]{1,0:T(8,128)(2,1)}, bf16[512,1024]{1,0:T(8,128)(2,1)}, u32[]{:S(2)}, u32[]{:S(2)}) collective-permute-start(bf16[512,1024]{1,0:T(8,128)(2,1)} %get-tuple-element.61), channel_id=1, source_target_pairs={{0,1},{1,0},{2,3},{3,2},{4,5},{5,4},{6,7},{7,6},{8,9},{9,8},{10,11... | collective-permute-start | bytes 3145736 | tf_op jit(solution)/shard_map/ppermute | solution.py:55
  375.8 51.6 %collective-permute-start.78 = (bf16[320,1024]{1,0:T(8,128)(2,1)}, bf16[320,1024]{1,0:T(8,128)(2,1)}, u32[]{:S(2)}, u32[]{:S(2)}) collective-permute-start(bf16[320,1024]{1,0:T(8,128)(2,1)} %dynamic-slice_bitcast_fusion.2), channel_id=1, source_target_pairs={{0,8},{4,12},{8,0},{12,4},{16,24},{20,28},{24,16},{28,20},{1,9},{5... | collective-permute-start | bytes 1966088 | tf_op jit(solution)/shard_map/ppermute | solution.py:90
  392.1 85.1 %collective-permute-start.65 = (bf16[512,1024]{1,0:T(8,128)(2,1)}, bf16[512,1024]{1,0:T(8,128)(2,1)}, u32[]{:S(2)}, u32[]{:S(2)}) collective-permute-start(bf16[512,1024]{1,0:T(8,128)(2,1)} %pad_maximum_fusion.14), channel_id=1, source_target_pairs={{0,3},{1,2},{2,1},{3,0},{4,7},{5,6},{6,5},{7,4},{8,11},{9,10},{10,... | collective-permute-start | bytes 3145736 | tf_op jit(solution)/shard_map/ppermute | solution.py:55
  393.7 38.4 %collective-permute-start.84 = (bf16[384,1024]{1,0:T(8,128)(2,1)}, bf16[384,1024]{1,0:T(8,128)(2,1)}, u32[]{:S(2)}, u32[]{:S(2)}) collective-permute-start(bf16[384,1024]{1,0:T(8,128)(2,1)} %dynamic-slice_bitcast_fusion), channel_id=1, source_target_pairs={{0,24},{4,28},{8,16},{12,20},{16,8},{20,12},{24,0},{28,4},{1,25},{... | collective-permute-start | bytes 2359304 | tf_op jit(solution)/shard_map/ppermute | solution.py:90
  394.5 36.0 %collective-permute-start.72 = (bf16[320,1024]{1,0:T(8,128)(2,1)}, bf16[320,1024]{1,0:T(8,128)(2,1)}, u32[]{:S(2)}, u32[]{:S(2)}) collective-permute-start(bf16[320,1024]{1,0:T(8,128)(2,1)} %dynamic-slice_bitcast_fusion.3), channel_id=1, source_target_pairs={{0,4},{4,0},{8,12},{12,8},{16,20},{20,16},{24,28},{28,24},{1,5},{5... | collective-permute-start | bytes 1966088 | tf_op jit(solution)/shard_map/ppermute | solution.py:90
  427.5 43.3 %collective-permute-start.58 = (bf16[512,1024]{1,0:T(8,128)(2,1)}, bf16[512,1024]{1,0:T(8,128)(2,1)S(1)}, u32[]{:S(2)}, u32[]{:S(2)}) collective-permute-start(bf16[512,1024]{1,0:T(8,128)(2,1)} %pad_maximum_fusion.13), channel_id=1, source_target_pairs={{0,2},{1,3},{2,0},{3,1},{4,6},{5,7},{6,4},{7,5},{8,10},{9,11},{10,... | collective-permute-start | bytes 3145736 | tf_op jit(solution)/shard_map/ppermute | solution.py:55
  430.6 40.3 %collective-permute-start.51 = (bf16[512,1024]{1,0:T(8,128)(2,1)S(1)}, bf16[512,1024]{1,0:T(8,128)(2,1)S(1)}, u32[]{:S(2)}, u32[]{:S(2)}) collective-permute-start(bf16[512,1024]{1,0:T(8,128)(2,1)S(1)} %copy-done.55), channel_id=1, source_target_pairs={{0,1},{1,0},{2,3},{3,2},{4,5},{5,4},{6,7},{7,6},{8,9},{9,8},{10,11... | collective-permute-start | bytes 3145736 | tf_op jit(solution)/shard_map/ppermute | solution.py:55
  432.1 23.1 %collective-permute-start.79 = (bf16[160,1024]{1,0:T(8,128)(2,1)S(1)}, bf16[160,1024]{1,0:T(8,128)(2,1)S(1)}, u32[]{:S(2)}, u32[]{:S(2)}) collective-permute-start(bf16[160,1024]{1,0:T(8,128)(2,1)S(1)} %dynamic-slice_bitcast_fusion.11), channel_id=1, source_target_pairs={{0,24},{4,28},{8,16},{12,20},{16,8},{20,12},{24,0},{28,4},{1,25},{... | collective-permute-start | bytes 983048 | tf_op jit(solution)/shard_map/ppermute | solution.py:90
  470.6 108.8 %collective-permute-start.16 = (bf16[512,1024]{1,0:T(8,128)(2,1)S(1)}, bf16[512,1024]{1,0:T(8,128)(2,1)S(1)}, u32[]{:S(2)}, u32[]{:S(2)}) collective-permute-start(bf16[512,1024]{1,0:T(8,128)(2,1)S(1)} %copy-done.14), channel_id=1, source_target_pairs={{0,1},{1,0},{2,3},{3,2},{4,5},{5,4},{6,7},{7,6},{8,9},{9,8},{10,11... | collective-permute-start | bytes 3145736 | tf_op jit(solution)/shard_map/ppermute | solution.py:55
  477.2 46.6 %collective-permute-start.59 = (bf16[320,1024]{1,0:T(8,128)(2,1)S(1)}, bf16[320,1024]{1,0:T(8,128)(2,1)S(1)}, u32[]{:S(2)}, u32[]{:S(2)}) collective-permute-start(bf16[320,1024]{1,0:T(8,128)(2,1)S(1)} %dynamic-slice_bitcast_fusion.4), channel_id=1, source_target_pairs={{0,8},{4,12},{8,0},{12,4},{16,24},{20,28},{24,16},{28,20},{1,9},{5... | collective-permute-start | bytes 1966088 | tf_op jit(solution)/shard_map/ppermute | solution.py:90
  491.9 22.9 %collective-permute-start.82 = (bf16[160,1024]{1,0:T(8,128)(2,1)S(1)}, bf16[160,1024]{1,0:T(8,128)(2,1)S(1)}, u32[]{:S(2)}, u32[]{:S(2)}) collective-permute-start(bf16[160,1024]{1,0:T(8,128)(2,1)S(1)} %maximum_select_fusion.22), channel_id=1, source_target_pairs={{0,24},{4,28},{8,16},{12,20},{16,8},{20,12},{24,0},{28,4},{1,25},{... | collective-permute-start | bytes 983048 | tf_op jit(solution)/shard_map/ppermute | solution.py:90
  514.8 66.7 %collective-permute-start.20 = (bf16[512,1024]{1,0:T(8,128)(2,1)S(1)}, bf16[512,1024]{1,0:T(8,128)(2,1)S(1)}, u32[]{:S(2)}, u32[]{:S(2)}) collective-permute-start(bf16[512,1024]{1,0:T(8,128)(2,1)S(1)} %add_convert_fusion.2), channel_id=1, source_target_pairs={{0,2},{1,3},{2,0},{3,1},{4,6},{5,7},{6,4},{7,5},{8,10},{9,11},{10,... | collective-permute-start | bytes 3145736 | tf_op jit(solution)/shard_map/ppermute | solution.py:55
  523.8 22.4 %collective-permute-start.88 = (bf16[192,1024]{1,0:T(8,128)(2,1)S(1)}, bf16[192,1024]{1,0:T(8,128)(2,1)S(1)}, u32[]{:S(2)}, u32[]{:S(2)}) collective-permute-start(bf16[192,1024]{1,0:T(8,128)(2,1)S(1)} %maximum_select_fusion.18), channel_id=1, source_target_pairs={{0,4},{4,0},{8,12},{12,8},{16,20},{20,16},{24,28},{28,24},{1,5},{5... | collective-permute-start | bytes 1179656 | tf_op jit(solution)/shard_map/ppermute | solution.py:90
  531.9 66.9 %collective-permute-start.83 = (bf16[320,1024]{1,0:T(8,128)(2,1)S(1)}, bf16[320,1024]{1,0:T(8,128)(2,1)S(1)}, u32[]{:S(2)}, u32[]{:S(2)}) collective-permute-start(bf16[320,1024]{1,0:T(8,128)(2,1)S(1)} %maximum_select_fusion.13), channel_id=1, source_target_pairs={{0,8},{4,12},{8,0},{12,4},{16,24},{20,28},{24,16},{28,20},{1,9},{5... | collective-permute-start | bytes 1966088 | tf_op jit(solution)/shard_map/ppermute | solution.py:90
  546.2 54.8 %collective-permute-start.77 = (bf16[320,1024]{1,0:T(8,128)(2,1)S(1)}, bf16[320,1024]{1,0:T(8,128)(2,1)S(1)}, u32[]{:S(2)}, u32[]{:S(2)}) collective-permute-start(bf16[320,1024]{1,0:T(8,128)(2,1)S(1)} %maximum_select_fusion.12), channel_id=1, source_target_pairs={{0,4},{4,0},{8,12},{12,8},{16,20},{20,16},{24,28},{28,24},{1,5},{5... | collective-permute-start | bytes 1966088 | tf_op jit(solution)/shard_map/ppermute | solution.py:90
  596.6 32.9 %collective-permute-start.22 = (bf16[512,256]{1,0:T(8,128)(2,1)S(1)}, bf16[512,256]{1,0:T(8,128)(2,1)S(1)}, u32[]{:S(2)}, u32[]{:S(2)}) collective-permute-start(bf16[512,256]{1,0:T(8,128)(2,1)S(1)} %convolution_convert_fusion.11), channel_id=1, source_target_pairs={{0,2},{1,3},{2,0},{3,1},{4,6},{5,7},{6,4},{7,5},{8,10},{9,11},{10,... | collective-permute-start | bytes 786440 | tf_op jit(solution)/shard_map/ppermute | solution.py:55
  597.4 33.6 %collective-permute-start.23 = (bf16[512,256]{1,0:T(8,128)(2,1)S(1)}, bf16[512,256]{1,0:T(8,128)(2,1)S(1)}, u32[]{:S(2)}, u32[]{:S(2)}) collective-permute-start(bf16[512,256]{1,0:T(8,128)(2,1)S(1)} %convolution_convert_fusion.10), channel_id=1, source_target_pairs={{0,3},{1,2},{2,1},{3,0},{4,7},{5,6},{6,5},{7,4},{8,11},{9,10},{10,... | collective-permute-start | bytes 786440 | tf_op jit(solution)/shard_map/ppermute | solution.py:55
  605.2 117.1 %collective-permute-start.89 = (bf16[384,1024]{1,0:T(8,128)(2,1)S(1)}, bf16[384,1024]{1,0:T(8,128)(2,1)S(1)}, u32[]{:S(2)}, u32[]{:S(2)}) collective-permute-start(bf16[384,1024]{1,0:T(8,128)(2,1)S(1)} %maximum_select_fusion.9), channel_id=1, source_target_pairs={{0,24},{4,28},{8,16},{12,20},{16,8},{20,12},{24,0},{28,4},{1,25},{... | collective-permute-start | bytes 2359304 | tf_op jit(solution)/shard_map/ppermute | solution.py:90
  609.3 107.8 %collective-permute-start.43 = (bf16[256,1024]{1,0:T(8,128)(2,1)S(1)}, bf16[256,1024]{1,0:T(8,128)(2,1)S(1)}, u32[]{:S(2)}, u32[]{:S(2)}) collective-permute-start(bf16[256,1024]{1,0:T(8,128)(2,1)S(1)} %convolution_convert_fusion.6), channel_id=1, source_target_pairs={{0,1},{1,0},{2,3},{3,2},{4,5},{5,4},{6,7},{7,6},{8,9},{9,8},{10,11... | collective-permute-start | bytes 1572872 | tf_op jit(solution)/shard_map/ppermute | solution.py:55
  609.3 97.5 %collective-permute-start.68 = (bf16[96,1024]{1,0:T(8,128)(2,1)S(1)}, bf16[96,1024]{1,0:T(8,128)(2,1)S(1)}, u32[]{:S(2)}, u32[]{:S(2)}) collective-permute-start(bf16[96,1024]{1,0:T(8,128)(2,1)S(1)} %dynamic-slice_bitcast_fusion.17), channel_id=1, source_target_pairs={{0,8},{4,12},{8,0},{12,4},{16,24},{20,28},{24,16},{28,20},{1,9},{5... | collective-permute-start | bytes 589832 | tf_op jit(solution)/shard_map/ppermute | solution.py:90
  629.4 89.7 %collective-permute-start.63 = (bf16[160,1024]{1,0:T(8,128)(2,1)S(1)}, bf16[160,1024]{1,0:T(8,128)(2,1)S(1)}, u32[]{:S(2)}, u32[]{:S(2)}) collective-permute-start(bf16[160,1024]{1,0:T(8,128)(2,1)S(1)} %maximum_select_fusion.20), channel_id=1, source_target_pairs={{0,24},{4,28},{8,16},{12,20},{16,8},{20,12},{24,0},{28,4},{1,25},{... | collective-permute-start | bytes 983048 | tf_op jit(solution)/shard_map/ppermute | solution.py:90
  631.0 90.3 %collective-permute-start.56 = (bf16[160,1024]{1,0:T(8,128)(2,1)S(1)}, bf16[160,1024]{1,0:T(8,128)(2,1)S(1)}, u32[]{:S(2)}, u32[]{:S(2)}) collective-permute-start(bf16[160,1024]{1,0:T(8,128)(2,1)S(1)} %maximum_select_fusion.19), channel_id=1, source_target_pairs={{0,8},{4,12},{8,0},{12,4},{16,24},{20,28},{24,16},{28,20},{1,9},{5... | collective-permute-start | bytes 983048 | tf_op jit(solution)/shard_map/ppermute | solution.py:90
  721.3 31.4 %collective-permute-start.42 = (bf16[256,1024]{1,0:T(8,128)(2,1)}, bf16[256,1024]{1,0:T(8,128)(2,1)}, u32[]{:S(2)}, u32[]{:S(2)}) collective-permute-start(bf16[256,1024]{1,0:T(8,128)(2,1)} %convolution_convert_fusion.8), channel_id=1, source_target_pairs={{0,1},{1,0},{2,3},{3,2},{4,5},{5,4},{6,7},{7,6},{8,9},{9,8},{10,11... | collective-permute-start | bytes 1572872 | tf_op jit(solution)/shard_map/ppermute | solution.py:55
  722.4 91.9 %collective-permute-start.25 = (bf16[512,1024]{1,0:T(8,128)(2,1)}, bf16[512,1024]{1,0:T(8,128)(2,1)}, u32[]{:S(2)}, u32[]{:S(2)}) collective-permute-start(bf16[512,1024]{1,0:T(8,128)(2,1)} %convolution_convert_fusion), channel_id=1, source_target_pairs={{0,1},{1,0},{2,3},{3,2},{4,5},{5,4},{6,7},{7,6},{8,9},{9,8},{10,11... | collective-permute-start | bytes 3145736 | tf_op jit(solution)/shard_map/ppermute | solution.py:55
  749.6 141.2 %collective-permute-start.24 = (bf16[512,1024]{1,0:T(8,128)(2,1)}, bf16[512,1024]{1,0:T(8,128)(2,1)}, u32[]{:S(2)}, u32[]{:S(2)}) collective-permute-start(bf16[512,1024]{1,0:T(8,128)(2,1)} %convolution_convert_fusion.2), channel_id=1, source_target_pairs={{0,1},{1,0},{2,3},{3,2},{4,5},{5,4},{6,7},{7,6},{8,9},{9,8},{10,11... | collective-permute-start | bytes 3145736 | tf_op jit(solution)/shard_map/ppermute | solution.py:55
  751.4 34.7 %collective-permute-start.64 = (bf16[320,1024]{1,0:T(8,128)(2,1)S(1)}, bf16[320,1024]{1,0:T(8,128)(2,1)S(1)}, u32[]{:S(2)}, u32[]{:S(2)}) collective-permute-start(bf16[320,1024]{1,0:T(8,128)(2,1)S(1)} %copy-done.40), channel_id=1, source_target_pairs={{0,8},{4,12},{8,0},{12,4},{16,24},{20,28},{24,16},{28,20},{1,9},{5... | collective-permute-start | bytes 1966088 | tf_op jit(solution)/shard_map/ppermute | solution.py:90
  752.7 35.7 %collective-permute-start.57 = (bf16[320,1024]{1,0:T(8,128)(2,1)S(1)}, bf16[320,1024]{1,0:T(8,128)(2,1)S(1)}, u32[]{:S(2)}, u32[]{:S(2)}) collective-permute-start(bf16[320,1024]{1,0:T(8,128)(2,1)S(1)} %copy-done.41), channel_id=1, source_target_pairs={{0,4},{4,0},{8,12},{12,8},{16,20},{20,16},{24,28},{28,24},{1,5},{5... | collective-permute-start | bytes 1966088 | tf_op jit(solution)/shard_map/ppermute | solution.py:90
  783.8 62.2 %collective-permute-start.71 = (bf16[384,1024]{1,0:T(8,128)(2,1)S(1)}, bf16[384,1024]{1,0:T(8,128)(2,1)S(1)}, u32[]{:S(2)}, u32[]{:S(2)}) collective-permute-start(bf16[384,1024]{1,0:T(8,128)(2,1)S(1)} %maximum_select_fusion.8), channel_id=1, source_target_pairs={{0,24},{4,28},{8,16},{12,20},{16,8},{20,12},{24,0},{28,4},{1,25},{... | collective-permute-start | bytes 2359304 | tf_op jit(solution)/shard_map/ppermute | solution.py:90
  786.1 32.0 %collective-permute-start.45 = (bf16[192,1024]{1,0:T(8,128)(2,1)S(1)}, bf16[192,1024]{1,0:T(8,128)(2,1)S(1)}, u32[]{:S(2)}, u32[]{:S(2)}) collective-permute-start(bf16[192,1024]{1,0:T(8,128)(2,1)S(1)} %dynamic-slice_bitcast_fusion.9), channel_id=1, source_target_pairs={{0,24},{4,28},{8,16},{12,20},{16,8},{20,12},{24,0},{28,4},{1,25},{... | collective-permute-start | bytes 1179656 | tf_op jit(solution)/shard_map/ppermute | solution.py:90
  788.4 25.3 %collective-permute-start.34 = (bf16[64,1024]{1,0:T(8,128)(2,1)S(1)}, bf16[64,1024]{1,0:T(8,128)(2,1)S(1)}, u32[]{:S(2)}, u32[]{:S(2)}) collective-permute-start(bf16[64,1024]{1,0:T(8,128)(2,1)S(1)} %maximum_select_fusion.26), channel_id=1, source_target_pairs={{0,8},{4,12},{8,0},{12,4},{16,24},{20,28},{24,16},{28,20},{1,9},{5... | collective-permute-start | bytes 393224 | tf_op jit(solution)/shard_map/ppermute | solution.py:90
  818.1 72.7 %collective-permute-start.26 = (bf16[512,1024]{1,0:T(8,128)(2,1)}, bf16[512,1024]{1,0:T(8,128)(2,1)}, u32[]{:S(2)}, u32[]{:S(2)}) collective-permute-start(bf16[512,1024]{1,0:T(8,128)(2,1)} %add_convert_fusion), channel_id=1, source_target_pairs={{0,2},{1,3},{2,0},{3,1},{4,6},{5,7},{6,4},{7,5},{8,10},{9,11},{10,... | collective-permute-start | bytes 3145736 | tf_op jit(solution)/shard_map/ppermute | solution.py:55
  830.9 23.5 %collective-permute-start.47 = (bf16[48,1024]{1,0:T(8,128)(2,1)S(1)}, bf16[48,1024]{1,0:T(8,128)(2,1)S(1)}, u32[]{:S(2)}, u32[]{:S(2)}) collective-permute-start(bf16[48,1024]{1,0:T(8,128)(2,1)S(1)} %dynamic-slice_bitcast_fusion.25), channel_id=1, source_target_pairs={{0,8},{4,12},{8,0},{12,4},{16,24},{20,28},{24,16},{28,20},{1,9},{5... | collective-permute-start | bytes 294920 | tf_op jit(solution)/shard_map/ppermute | solution.py:90
  861.1 25.7 %collective-permute-start.49 = (bf16[96,1024]{1,0:T(8,128)(2,1)S(1)}, bf16[96,1024]{1,0:T(8,128)(2,1)S(1)}, u32[]{:S(2)}, u32[]{:S(2)}) collective-permute-start(bf16[96,1024]{1,0:T(8,128)(2,1)S(1)} %maximum_select_fusion.25), channel_id=1, source_target_pairs={{0,4},{4,0},{8,12},{12,8},{16,20},{20,16},{24,28},{28,24},{1,5},{5... | collective-permute-start | bytes 589832 | tf_op jit(solution)/shard_map/ppermute | solution.py:90
  861.2 28.7 %collective-permute-start.40 = (bf16[96,1024]{1,0:T(8,128)(2,1)S(1)}, bf16[96,1024]{1,0:T(8,128)(2,1)S(1)}, u32[]{:S(2)}, u32[]{:S(2)}) collective-permute-start(bf16[96,1024]{1,0:T(8,128)(2,1)S(1)} %maximum_select_fusion.24), channel_id=1, source_target_pairs={{0,24},{4,28},{8,16},{12,20},{16,8},{20,12},{24,0},{28,4},{1,25},{... | collective-permute-start | bytes 589832 | tf_op jit(solution)/shard_map/ppermute | solution.py:90
  887.6 54.7 %collective-permute-start.50 = (bf16[192,1024]{1,0:T(8,128)(2,1)}, bf16[192,1024]{1,0:T(8,128)(2,1)}, u32[]{:S(2)}, u32[]{:S(2)}) collective-permute-start(bf16[192,1024]{1,0:T(8,128)(2,1)} %maximum_select_fusion.16), channel_id=1, source_target_pairs={{0,24},{4,28},{8,16},{12,20},{16,8},{20,12},{24,0},{28,4},{1,25},{... | collective-permute-start | bytes 1179656 | tf_op jit(solution)/shard_map/ppermute | solution.py:90
  890.8 54.3 %collective-permute-start.41 = (bf16[192,1024]{1,0:T(8,128)(2,1)}, bf16[192,1024]{1,0:T(8,128)(2,1)}, u32[]{:S(2)}, u32[]{:S(2)}) collective-permute-start(bf16[192,1024]{1,0:T(8,128)(2,1)} %maximum_select_fusion.15), channel_id=1, source_target_pairs={{0,8},{4,12},{8,0},{12,4},{16,24},{20,28},{24,16},{28,20},{1,9},{5... | collective-permute-start | bytes 1179656 | tf_op jit(solution)/shard_map/ppermute | solution.py:90
  (130 other events, 1997.8 us)
Sparse Core Ops, SparseCore 0:
  100.3 71.3 all-gather.2

commit v2 on v1

--- a/solution.py
+++ b/solution.py
@@ -16,10 +16,12 @@
 N_SHARD = 4
 OWN_HEADS = HEADS // N_SHARD
 OWN = OWN_HEADS * HEAD_DIM
+PAIR = 2
 TILE = 256
 NEG = -1e30
 
 epsilon = 1e-05
+LIGHT = pl.CostEstimate(flops=2**20, bytes_accessed=2**16, transcendentals=0)
 f32 = jnp.float32
 bf16 = jnp.bfloat16
 
@@ -51,23 +53,31 @@
     return lax.dot_general(a, b, (((0,), (0,)), ((), ())), preferred_element_type=f32)
 
 
+def tie(value, after):
+    return lax.optimization_barrier((value, after))[0]
+
+
 def swap(value, mask):
     return lax.ppermute(value, "shard", [(i, i ^ mask) for i in range(N_SHARD)])
 
 
-def gather_blocks(value):
-    far = swap(value, 2)
-    near = swap(value, 1)
-    return (value, near, far, swap(far, 1))
-
-
 def exchange_blocks(blocks):
     return (blocks[0], swap(blocks[1], 1), swap(blocks[2], 2), swap(blocks[3], 3))
 
 
+def in_order(side, own, other):
+    return jnp.where(side == 0, jnp.stack([own, other]), jnp.stack([other, own]))
+
+
+def gather_small(value, me):
+    pair = in_order(me & 1, value, swap(value, 1))
+    both = in_order(me >> 1, pair, swap(pair, 2))
+    return both.reshape((N_SHARD,) + value.shape)
+
+
 def scatter_far(block_two, block_three):
     near = swap(block_three, 1)
-    return swap((block_two.astype(f32) + near.astype(f32)).astype(bf16), 2)
+    return (block_two.astype(f32) + near.astype(f32)).astype(bf16)
 
 
 def scatter_near(block_zero, block_one, far):
@@ -75,65 +85,115 @@
     return block_zero.astype(f32) + near.astype(f32) + far.astype(f32)
 
 
-def rep_masks(count):
-    masks = []
-    step = 1
-    while step < count:
-        masks.append(step)
-        step *= 2
-    if count == 8:
-        return [(1, (1,)), (2, (2, 4)), (6, (4,))]
-    return [(m, (m,)) for m in masks]
-
-
-def rep_pair(value, mask, count):
+def rep_swap(value, mask, count):
     return lax.ppermute(value, "rep", [(i, i ^ mask) for i in range(count)])
 
 
-def rep_side(bits):
-    index = lax.axis_index("rep")
-    side = jnp.zeros((), jnp.int32)
-    for bit in bits:
-        side = side ^ ((index & bit) // bit)
-    return side
-
-
-def rep_sum_part(value, turn, count):
-    dims = rep_masks(count)
-    turn = turn % len(dims)
-    dims = dims[turn:] + dims[:turn]
-    sides = [rep_side(bits) for unused, bits in dims]
-    for (mask, unused), side in zip(dims, sides):
-        half = value.shape[0] // 2
-        split = value.reshape(2, half, value.shape[1])
-        send = lax.dynamic_index_in_dim(split, 1 - side, 0, keepdims=False)
-        keep = lax.dynamic_index_in_dim(split, side, 0, keepdims=False)
-        other = rep_pair(send, mask, count)
-        value = (keep.astype(f32) + other.astype(f32)).astype(bf16)
-    for (mask, unused), side in reversed(list(zip(dims, sides))):
-        other = rep_pair(value, mask, count)
-        value = jnp.where(
-            side == 0,
-            jnp.concatenate([value, other], axis=0),
-            jnp.concatenate([other, value], axis=0),
-        )
-    return value
-
-
-def rep_sum(value, parts, count):
-    if count == 1:
-        return value
-    if count & (count - 1) or value.shape[0] % (16 * count):
-        return lax.psum(value, "rep")
-    unit = 16 * count
-    total = value.shape[0] // unit
-    parts = min(parts, total)
-    sizes = [(total // parts + (1 if p >= parts - total % parts else 0)) * unit for p in range(parts)]
-    pieces, start = [], 0
-    for turn, size in enumerate(sizes):
-        pieces.append(rep_sum_part(value[start : start + size], turn, count))
-        start += size
-    return jnp.concatenate(pieces, axis=0)
+QUARTERS = 4
+ORDERS = ((1, 2), (2, 1))
+
+
+def added(value, other, token):
+    return (value.astype(f32) + tie(other, token).astype(f32)).astype(bf16)
+
+
+def rep_sum_steps(quarters, count, middle):
+    place = lax.axis_index("rep") & (QUARTERS - 1)
+    sent = [jnp.stack([q(place ^ a), q(place ^ a ^ b)]) for q, (a, b) in zip(quarters, ORDERS)]
+    others = [rep_swap(v, a, count) for v, (a, b) in zip(sent, ORDERS)]
+    token = yield sent
+    stay = [added(q(place), other[0], token) for q, other in zip(quarters, others)]
+    sent = [
+        added(q(place ^ b), other[1], token)
+        for q, other, (a, b) in zip(quarters, others, ORDERS)
+    ]
+    others = [rep_swap(v, b, count) for v, (a, b) in zip(sent, ORDERS)]
+    token = yield sent
+    values = [added(v, other, token) for v, other in zip(stay, others)]
+    mask = QUARTERS
+    while mask < count:
+        both = jnp.stack(values)
+        other = rep_swap(both, mask, count)
+        token = yield both
+        values = [added(v, other[p], token) for p, v in enumerate(values)]
+        mask *= 2
+    values = yield from middle(values)
+    others = [rep_swap(v, b, count) for v, (a, b) in zip(values, ORDERS)]
+    token = yield values
+    others = [tie(other, token) for other in others]
+    sent = [jnp.stack([v, other]) for v, other in zip(values, others)]
+    lasts = [rep_swap(v, a, count) for v, (a, b) in zip(sent, ORDERS)]
+    token = yield sent
+    return [(v, other, tie(last, token)) for v, other, last in zip(values, others, lasts)]
+
+
+def rep_places():
+    place = lax.axis_index("rep").astype(jnp.int32) & (QUARTERS - 1)
+    return jnp.stack([place ^ mask for a, b in ORDERS for mask in (0, b, a, a ^ b)])
+
+
+def middle_none(values):
+    yield from ()
+    return values
+
+
+class Steps:
+    def __init__(self, steps):
+        self.steps = steps
+        self.result = None
+        self.sent = next(steps)
+
+    def step(self, token):
+        if self.result is not None:
+            return token
+        try:
+            self.sent = self.steps.send(token)
+        except StopIteration as end:
+            self.result = end.value
+        return self.sent
+
+    def finish(self, token):
+        while self.result is None:
+            self.step(token)
+        return self.result
+
+
+def project_kernel(facts, tok_a, tok_b, w0, w1, w2, w3, first, qkv, weight, params, gains):
+    me = facts[0]
+    part, columns = weight.shape[0] // N_SHARD, weight.shape[1]
+    for j, block in enumerate((w0, w1, w2, w3)):
+        at = (me ^ j) * part
+        weight[pl.ds(pl.multiple_of(at, part), part), :] = block[0:part, :]
+        gains[:, pl.ds(pl.multiple_of(at, part), part)] = block[part : part + 8, 0:part].astype(f32)
+    params[...] = gains[...]
+    for half, tok in enumerate((tok_a, tok_b)):
+        for start in range(0, tok.shape[0], TILE):
+            normed = layer_norm(tok[start : start + TILE, :].astype(f32))[0]
+            low = (normed * gains[0:1, :] + gains[1:2, :]).astype(bf16)
+            rows = slice(half * tok.shape[0] + start, half * tok.shape[0] + start + TILE)
+            first[rows, :] = low
+            qkv[rows, :] = dot_nn(low, weight[...]).astype(bf16)
+
+
+def project(facts, tok_a, tok_b, blocks):
+    rows, width = tok_a.shape
+    columns = blocks[0].shape[1]
+    vmem = pl.BlockSpec(memory_space=pltpu.VMEM)
+    return pl.pallas_call(
+        project_kernel,
+        out_shape=(
+            jax.ShapeDtypeStruct((2 * rows, width), bf16),
+            jax.ShapeDtypeStruct((2 * rows, columns), bf16),
+            jax.ShapeDtypeStruct((width, columns), bf16),
+            jax.ShapeDtypeStruct((8, width), f32),
+        ),
+        in_specs=[pl.BlockSpec(memory_space=pltpu.SMEM)] + [vmem] * 6,
+        out_specs=(vmem,) * 4,
+        scratch_shapes=[pltpu.VMEM((8, width), f32)],
+        compiler_params=pltpu.CompilerParams(vmem_limit_bytes=32 * 2**20),
+        cost_estimate=LIGHT,
+        name="project",
+    )(facts, tok_a, tok_b, *blocks)
 
 
 def visible_tile(key_block, query_block, starts):
@@ -242,23 +302,23 @@
             pltpu.VMEM((8, TILE), f32),
         ],
         compiler_params=pltpu.CompilerParams(vmem_limit_bytes=48 * 2**20),
-        cost_estimate=pl.CostEstimate(
-            flops=rows * rows * OWN * 8, bytes_accessed=rows * OWN * 10, transcendentals=rows * rows * 2
-        ),
+        cost_estimate=LIGHT,
         name="attend",
     )(facts, near, far)
 
 
 def attend_back_kernel(
-    blocks, facts, near, far, mixed, g0, g1, g2, g3, logs, grads,
+    blocks, pair, facts, near, far, mixed, g0, g1, g2, g3, logs, grads,
     q_own, k_own, v_own, k_turned, g_own, q_heads, g_heads, deltas, q_grad, k_grad, v_grad, k_heads, v_heads,
 ):
     me = facts[0]
     starts = [facts[1 + i] for i in range(facts.shape[0] - 1)]
-    lanes = head_lanes(TILE)
+    wide = PAIR * HEAD_DIM
+    lane = pair * wide
+    lanes = lax.broadcasted_iota(jnp.int32, (TILE, wide), 1) // HEAD_DIM
     pick = (
-        lax.broadcasted_iota(jnp.int32, (8, OWN), 1) // HEAD_DIM
-        == lax.broadcasted_iota(jnp.int32, (8, OWN), 0)
+        lax.broadcasted_iota(jnp.int32, (8, wide), 1) // HEAD_DIM
+        == lax.broadcasted_iota(jnp.int32, (8, wide), 0)
     ).astype(f32)
     for j in range(N_SHARD):
         src = near if j < 2 else far
@@ -267,18 +327,20 @@
         for half in range(2):
             rows = slice(base + half * TILE, base + (half + 1) * TILE)
             at = (me ^ j) * 2 + half
-            q_tile = src[rows, 0:OWN] * jnp.asarray(HEAD_DIM**-0.5, bf16)
-            k_tile = src[rows, OWN : 2 * OWN]
-            g_tile = grad_src[half * TILE : (half + 1) * TILE, :]
-            o_tile = mixed[j * 2 * TILE + half * TILE : j * 2 * TILE + (half + 1) * TILE, :]
+            q_tile = src[rows, lane : lane + wide] * jnp.asarray(HEAD_DIM**-0.5, bf16)
+            k_tile = src[rows, OWN + lane : OWN + lane + wide]
+            g_tile = grad_src[half * TILE : (half + 1) * TILE, lane : lane + wide]
+            o_rows = slice(j * 2 * TILE + half * TILE, j * 2 * TILE + (half + 1) * TILE)
+            o_tile = mixed[o_rows, lane : lane + wide]
             q_own[at] = q_tile
             k_own[at] = k_tile
-            v_own[at] = src[rows, 2 * OWN : 3 * OWN]
+            v_own[at] = src[rows, 2 * OWN + lane : 2 * OWN + lane + wide]
             k_turned[at] = k_tile.astype(f32).T.astype(bf16)
             g_own[at] = g_tile
-            for h in range(OWN_HEADS):
-                q_heads[at, h * TILE : (h + 1) * TILE, :] = jnp.where(lanes == h, q_tile, jnp.zeros_like(q_tile))
-                g_heads[at, h * TILE : (h + 1) * TILE, :] = jnp.where(lanes == h, g_tile, jnp.zeros_like(g_tile))
+            for h in range(PAIR):
+                place = slice(h * TILE, (h + 1) * TILE)
+                q_heads[at, place, :] = jnp.where(lanes == h, q_tile, jnp.zeros_like(q_tile))
+                g_heads[at, place, :] = jnp.where(lanes == h, g_tile, jnp.zeros_like(g_tile))
             both = g_tile.astype(f32) * o_tile.astype(f32)
             deltas[at] = lax.dot_general(
                 pick, both, (((1,), (1,)), ((), ())),
@@ -289,7 +351,7 @@
     def key_block(j, unused):
         k_j = k_own[j]
         v_j = v_own[j]
-        for h in range(OWN_HEADS):
+        for h in range(PAIR):
             k_heads[h * TILE : (h + 1) * TILE, :] = jnp.where(lanes == h, k_j, jnp.zeros_like(k_j))
             v_heads[h * TILE : (h + 1) * TILE, :] = jnp.where(lanes == h, v_j, jnp.zeros_like(v_j))
         k_grad[...] = jnp.zeros_like(k_grad)
@@ -302,10 +364,11 @@
             seen = visible_tile(j, i, starts) if masked else None
             softs = []
             scored = []
-            for h in range(OWN_HEADS):
+            for h in range(PAIR):
                 rows = slice(h * TILE, (h + 1) * TILE)
+                at = pair * PAIR + h
                 scores = dot_nt(k_heads[rows, :], q_i)
-                soft = jnp.exp(scores - logs[i, h : h + 1, :])
+                soft = jnp.exp(scores - logs[i, at : at + 1, :])
                 if masked:
                     soft = jnp.where(seen, soft, 0.0)
                 grad_soft = dot_nt(v_heads[rows, :], g_i)
@@ -328,50 +391,49 @@
         query_block(j, True)
         lax.fori_loop(j + 1, blocks, plain, 0)
         place = pl.multiple_of(((j // 2) ^ me) * (2 * TILE) + (j % 2) * TILE, TILE)
-        grads[pl.ds(place, TILE), OWN : 2 * OWN] = k_grad[...].astype(bf16)
-        grads[pl.ds(place, TILE), 2 * OWN : 3 * OWN] = v_grad[...].astype(bf16)
+        grads[pl.ds(place, TILE), wide : 2 * wide] = k_grad[...].astype(bf16)
+        grads[pl.ds(place, TILE), 2 * wide : 3 * wide] = v_grad[...].astype(bf16)
         return unused
 
     lax.fori_loop(0, blocks, key_block, 0)
 
     def write_query(i, unused):
         place = pl.multiple_of(((i // 2) ^ me) * (2 * TILE) + (i % 2) * TILE, TILE)
-        grads[pl.ds(place, TILE), 0:OWN] = (q_grad[i] * HEAD_DIM**-0.5).T.astype(bf16)
+        grads[pl.ds(place, TILE), 0:wide] = (q_grad[i] * HEAD_DIM**-0.5).T.astype(bf16)
         return unused
 
     lax.fori_loop(0, blocks, write_query, 0)
 
 
-def attend_back(facts, near, far, mixed, grad_blocks, logs):
+def attend_back(pair, facts, near, far, mixed, grad_blocks, logs):
     rows = near.shape[0] + far.shape[0]
     blocks = rows // TILE
+    wide = PAIR * HEAD_DIM
     vmem = pl.BlockSpec(memory_space=pltpu.VMEM)
     tile = lambda n, m, kind: pltpu.VMEM((n, m), kind)
     stack = lambda n, m, kind: pltpu.VMEM((blocks, n, m), kind)
     return pl.pallas_call(
-        functools.partial(attend_back_kernel, blocks),
-        out_shape=jax.ShapeDtypeStruct((rows, 3 * OWN), bf16),
+        functools.partial(attend_back_kernel, blocks, pair),
+        out_shape=jax.ShapeDtypeStruct((rows, 3 * wide), bf16),
         in_specs=[pl.BlockSpec(memory_space=pltpu.SMEM)] + [vmem] * 8,
         out_specs=vmem,
         scratch_shapes=[
-            stack(TILE, OWN, bf16),
-            stack(TILE, OWN, bf16),
-            stack(TILE, OWN, bf16),
-            stack(OWN, TILE, bf16),
-            stack(TILE, OWN, bf16),
-            stack(OWN_HEADS * TILE, OWN, bf16),
-            stack(OWN_HEADS * TILE, OWN, bf16),
+            stack(TILE, wide, bf16),
+            stack(TILE, wide, bf16),
+            stack(TILE, wide, bf16),
+            stack(wide, TILE, bf16),
+            stack(TILE, wide, bf16),
+            stack(PAIR * TILE, wide, bf16),
+            stack(PAIR * TILE, wide, bf16),
             stack(8, TILE, f32),
-            stack(OWN, TILE, f32),
-            tile(TILE, OWN, f32),
-            tile(TILE, OWN, f32),
-            tile(OWN_HEADS * TILE, OWN, bf16),
-            tile(OWN_HEADS * TILE, OWN, bf16),
+            stack(wide, TILE, f32),
+            tile(TILE, wide, f32),
+            tile(TILE, wide, f32),
+            tile(PAIR * TILE, wide, bf16),
+            tile(PAIR * TILE, wide, bf16),
         ],
-        compiler_params=pltpu.CompilerParams(vmem_limit_bytes=56 * 2**20),
-        cost_estimate=pl.CostEstimate(
-            flops=rows * rows * OWN * 20, bytes_accessed=rows * OWN * 20, transcendentals=rows * rows * 2
-        ),
+        compiler_params=pltpu.CompilerParams(vmem_limit_bytes=48 * 2**20),
+        cost_estimate=LIGHT,
         name="attend_back",
     )(facts, near, far, mixed, *grad_blocks, logs)
 
@@ -483,9 +545,7 @@
             jax.ShapeDtypeStruct((rows, width), bf16),
         ),
         compiler_params=pltpu.CompilerParams(vmem_limit_bytes=40 * 2**20),
-        cost_estimate=pl.CostEstimate(
-            flops=2 * rows * width * inner * 4, bytes_accessed=4 * width * inner * 2, transcendentals=0
-        ),
+        cost_estimate=LIGHT,
         name="experts",
     )(counts, rows_a, rows_b, w_in, in_bias, w_back)
 
@@ -509,11 +569,89 @@
             jax.ShapeDtypeStruct((rows, width), bf16),
         ),
         compiler_params=pltpu.CompilerParams(vmem_limit_bytes=40 * 2**20),
-        cost_estimate=pl.CostEstimate(
-            flops=2 * rows * width * inner * 4, bytes_accessed=4 * width * inner * 2, transcendentals=0
-        ),
+        cost_estimate=LIGHT,
         name="experts_back",
     )(counts, rows_a, rows_b, hidden, w_in, w_back)
+
+
+def place_experts_kernel(facts, *refs):
+    blocks, out = refs[:6], refs[6]
+    expert, turn = pl.program_id(0), pl.program_id(1)
+
+    def write(block):
+        owners, rows, width = block.shape[-3:]
+        for j in range(owners):
+            at = pl.multiple_of((facts[0] ^ j) * width, width) if owners > 1 else 0
+            out[0, :, pl.ds(at, width)] = (block[0, j] if len(block.shape) == 4 else block[j]).astype(f32)
+
+    for part in range(2):
+        for source, block in enumerate(blocks[3 * part : 3 * part + 3]):
+
+            @pl.when((expert == part) & (jnp.minimum(turn, 2) == source))
+            def _():
+                write(block)
+
+
+def place_experts(me, parts):
+    owners, rows, width = parts[0][0].shape
+    whole = pl.BlockSpec((owners, rows, width), lambda e, t, s: (0, 0, 0))
+
+    def last(part):
+        return pl.BlockSpec(
+            (1, owners, rows, width),
+            lambda e, t, s: (jnp.clip((e - part) * QUARTERS + t - 2, 0, 1), 0, 0, 0),
+        )
+
+    return pl.pallas_call(
+        place_experts_kernel,
+        grid_spec=pltpu.PrefetchScalarGridSpec(
+            num_scalar_prefetch=1,
+            grid=(2, QUARTERS),
+            in_specs=[whole, whole, last(0), whole, whole, last(1)],
+            out_specs=pl.BlockSpec(
+                (1, rows, owners * width), lambda e, t, s: (e, s[1 + e * QUARTERS + t], 0)
+            ),
+        ),
+        out_shape=jax.ShapeDtypeStruct((2, QUARTERS * rows, owners * width), f32),
+        compiler_params=pltpu.CompilerParams(vmem_limit_bytes=24 * 2**20),
+        cost_estimate=LIGHT,
+        name="place_experts",
+    )(jnp.concatenate([me[None], rep_places()]), *[b for p in parts for b in p])
+
+
+def place_attention_kernel(facts, *refs):
+    blocks, qkv_out, whole_out = refs[:6], refs[6], refs[7]
+    rows = qkv_out.shape[0] // (2 * QUARTERS)
+    for part in range(2):
+        own, second, last = blocks[3 * part : 3 * part + 3]
+        for turn in range(QUARTERS):
+            block = (own, second, last.at[0], last.at[1])[turn]
+            segment = part * QUARTERS + facts[1 + part * QUARTERS + turn]
+            to = pl.ds(pl.multiple_of(segment * rows, rows), rows)
+            for c in range(3):
+                for j in range(N_SHARD):
+                    at = pl.multiple_of(c * N_SHARD * OWN + (facts[0] ^ j) * OWN, OWN)
+                    start = (c * N_SHARD + j) * rows
+                    qkv_out[to, pl.ds(at, OWN)] = block[start : start + rows, :].astype(f32)
+            for x in range(N_SHARD):
+                start = (3 * N_SHARD + x) * rows
+                whole_out[to, x * OWN : (x + 1) * OWN] = block[start : start + rows, :].astype(f32)
+
+
+def place_attention(me, parts, rows):
+    vmem = pl.BlockSpec(memory_space=pltpu.VMEM)
+    return pl.pallas_call(
+        place_attention_kernel,
+        out_shape=(
+            jax.ShapeDtypeStruct((rows, 3 * N_SHARD * OWN), f32),
+            jax.ShapeDtypeStruct((rows, N_SHARD * OWN), f32),
+        ),
+        in_specs=[pl.BlockSpec(memory_space=pltpu.SMEM)] + [vmem] * 6,
+        out_specs=(vmem, vmem),
+        compiler_params=pltpu.CompilerParams(vmem_limit_bytes=24 * 2**20),
+        cost_estimate=LIGHT,
+        name="place_attention",
+    )(jnp.concatenate([me[None], rep_places()]), *[b for p in parts for b in p])
 
 
 def shards(
@@ -542,9 +680,40 @@
     me = lax.axis_index("shard").astype(jnp.int32)
     rep_at = lax.axis_index("rep")
     inner = w_back.shape[1]
+    shard_width = ln1_gain.shape[0]
+    seg_rows = shard_width // n_rep
     facts = jnp.concatenate([me[None], piece_starts[0]])
 
-    tok_blocks = gather_blocks(tokens)
+    packed = jnp.concatenate(
+        [
+            jnp.stack([ln1_gain, ln1_bias, out_bias, ln2_gain, ln2_bias]),
+            back_bias,
+            jnp.zeros((1, shard_width), bf16),
+        ],
+        axis=0,
+    )
+    packed = jnp.concatenate([packed, jnp.zeros((8, 3 * OWN - shard_width), bf16)], axis=1)
+    qkv_sends = [
+            jnp.concatenate(
+                [
+                    jnp.concatenate(
+                        [
+                            lax.dynamic_slice_in_dim(w_qkv, c * D + (me ^ j) * OWN, OWN, axis=1)
+                            for c in range(3)
+                        ],
+                        axis=1,
+                    ),
+                    packed,
+                ],
+                axis=0,
+            )
+            for j in range(N_SHARD)
+    ]
+    over = swap(jnp.stack(qkv_sends[2:]), 3)
+    tok_far = swap(tokens, 2)
+    near = swap(qkv_sends[1], 1)
+    tok_near = swap(tokens, 1)
+    qkv_blocks = (qkv_sends[0], near, swap(over[0], 1), over[1])
 
     expert_of = jnp.take(hash_table, token_ids)
     places = jnp.arange(local_rows, dtype=jnp.int32)
@@ -552,62 +721,55 @@
     slot_of = jnp.sum(earlier.astype(jnp.int32), axis=1)
     kept = slot_of < CAP
     is_late = expert_of > 0
-    late_count = jnp.sum(is_late.astype(jnp.int32))
-    own_counts = jnp.stack(
-        [jnp.minimum(local_rows - late_count, CAP), jnp.minimum(late_count, CAP)]
-    )
-    sorted_at = jnp.where(kept, slot_of + jnp.where(is_late, own_counts[0], 0), -1)
+    early_count = jnp.minimum(local_rows - jnp.sum(is_late.astype(jnp.int32)), CAP)
+    sorted_at = jnp.where(kept, slot_of + jnp.where(is_late, early_count, 0), -1)
     sorter = (sorted_at[None, :] == places[:, None]).astype(bf16)
-
     counted = valid_mask.astype(f32)
-    own_count = jnp.sum(counted)
-    shard_width = ln1_gain.shape[0]
-    lasts = jnp.zeros((1, shard_width), f32)
-    lasts = lasts.at[0, 0].set(own_counts[0].astype(f32)).at[0, 1].set(own_count)
-    packed = jnp.concatenate(
-        [
-            jnp.stack([v.astype(f32) for v in (ln1_gain, ln1_bias, out_bias, ln2_gain, ln2_bias)]),
-            back_bias.astype(f32),
-            lasts,
-        ],
-        axis=0,
-    )
-    everyone = lax.all_gather(packed, ("rep", "shard"), axis=0).reshape(
-        n_rep, N_SHARD, 8, shard_width
-    )
-    count_all = jnp.sum(everyone[:, :, 7, 1])
-    mine = lax.dynamic_index_in_dim(everyone, rep_at, 0, keepdims=False)
-    rows_of = mine[:, :7].transpose(1, 0, 2).reshape(7, N_SHARD * shard_width)
+    own_facts = jnp.stack([early_count.astype(f32), jnp.sum(counted)])
+    own_facts = jnp.broadcast_to(own_facts[:, None], (2, 128))
+    shared = gather_small(own_facts, me)
+    count_all = jnp.sum(shared[:, 1], axis=0, keepdims=True)
+    for bit in range(n_rep.bit_length() - 1):
+        count_all = count_all + rep_swap(count_all, 1 << bit, n_rep)
+    count_all = count_all[0, 0]
+    indices = jnp.arange(N_SHARD, dtype=jnp.int32)
+    borders = jnp.sum(
+        jnp.where((indices ^ me)[:, None] == indices[None, :], shared[:, 0, 0][None, :], 0.0), axis=1
+    ).astype(jnp.int32)
+    counts_near, counts_far = borders[:2, None], borders[2:, None]
+
+    first_near, qkv_near, qkv_weight, rows_of = project(facts, tokens, tok_near, qkv_blocks)
     gain_one, bias_one, out_shift, gain_two, bias_two = [rows_of[i] for i in range(5)]
     back_shift = rows_of[5:7]
-    borders = jnp.take(mine[:, 7, 0], me ^ jnp.arange(N_SHARD, dtype=jnp.int32)).astype(jnp.int32)
-    counts_near, counts_far = borders[:2, None], borders[2:, None]
-
-    heads_in = w_qkv.reshape(shard_width, 3, N_SHARD, OWN)
-    qkv_weight = lax.all_to_all(heads_in, "shard", split_axis=2, concat_axis=0, tiled=True)
-    qkv_weight = qkv_weight.reshape(D, 3 * OWN)
-    slice_width = inner // n_rep
-    thin = lax.dynamic_index_in_dim(
-        w_in.reshape(EXPERTS, shard_width, N_SHARD, n_rep, slice_width), rep_at, 3, keepdims=False
-    )
-    thin = lax.all_to_all(thin, "shard", split_axis=2, concat_axis=1, tiled=True)
-    in_weight = lax.all_gather(thin.reshape(EXPERTS, D, slice_width), "rep", axis=0)
-    in_weight = in_weight.transpose(1, 2, 0, 3).reshape(EXPERTS, D, inner)
-    out_blocks = gather_blocks(w_out)
+    tok_both = swap(tok_far, 1)
+    first_far, qkv_far = project(facts, tie(tok_far, qkv_near), tok_both, qkv_blocks)[:2]
 
     def first_rows(block):
         normed, inverse = layer_norm(block.astype(f32))
         return (normed * gain_one + bias_one).astype(bf16), normed, inverse
 
-    first_near = jnp.concatenate([first_rows(tok_blocks[0])[0], first_rows(tok_blocks[1])[0]], axis=0)
-    first_far = jnp.concatenate([first_rows(tok_blocks[2])[0], first_rows(tok_blocks[3])[0]], axis=0)
-    qkv_near = dot_nn(first_near, qkv_weight).astype(bf16)
-    qkv_far = dot_nn(first_far, qkv_weight).astype(bf16)
-
+    thin = lax.dynamic_slice_in_dim(w_in, rep_at * seg_rows, seg_rows, axis=1)
+    thin = tie(thin, (tok_far, over))
+    thin_blocks = exchange_blocks(
+        [lax.dynamic_slice_in_dim(thin, (me ^ j) * inner, inner, axis=2) for j in range(N_SHARD)]
+    )
+    thin = in_order(
+        me >> 1,
+        in_order(me & 1, thin_blocks[0], thin_blocks[1]),
+        in_order(me & 1, thin_blocks[2], thin_blocks[3]),
+    ).reshape(N_SHARD, EXPERTS, seg_rows, inner)
+    thin = lax.all_gather(thin.transpose(1, 0, 2, 3), "rep", axis=0)
+    in_weight = thin.transpose(1, 2, 0, 3, 4).reshape(EXPERTS, D, inner)
+    w_out = tie(w_out, tok_far)
+    out_far = swap(w_out, 2)
+    out_blocks = (w_out, swap(w_out, 1), out_far, swap(out_far, 1))
+
+    facts = tie(facts, (count_all, borders))
     mixed, logs = attend(facts, qkv_near, qkv_far)
     mixed_blocks = exchange_blocks(
         [mixed[j * local_rows : (j + 1) * local_rows] for j in range(N_SHARD)]
     )
+    mixed_blocks = mixed_blocks[:2] + lax.optimization_barrier(mixed_blocks[2:] + (in_weight,))[:2]
     tok_rows = tokens.astype(f32)
     branch = dot_nn(mixed_blocks[0], out_blocks[0])
     for j in range(1, N_SHARD):
@@ -616,11 +778,14 @@
     normed_two, inverse_two = layer_norm(middle)
     second_in = (normed_two * gain_two + bias_two).astype(bf16)
     sorted_in = dot_nn(sorter, second_in).astype(bf16)
-    rows_in = gather_blocks(sorted_in)
+    in_far = swap(sorted_in, 2)
+    in_near = swap(sorted_in, 1)
     bias_in = in_bias.astype(f32)
-    hidden_near, out0, out1 = run_experts(counts_near, rows_in[0], rows_in[1], in_weight, bias_in, w_back)
-    hidden_far, out2, out3 = run_experts(counts_far, rows_in[2], rows_in[3], in_weight, bias_in, w_back)
-    summed = scatter_near(out0, out1, scatter_far(out2, out3))
+    hidden_near, out0, out1 = run_experts(counts_near, sorted_in, in_near, in_weight, bias_in, w_back)
+    in_far = tie(in_far, out0)
+    in_both = swap(in_far, 1)
+    hidden_far, out2, out3 = run_experts(counts_far, in_far, in_both, in_weight, bias_in, w_back)
+    summed = scatter_near(out0, out1, swap(scatter_far(out2, out3), 2))
     picked = dot_tn(sorter, summed.astype(bf16))
     picked = picked + jnp.where(is_late[:, None], back_shift[1], back_shift[0])
     final = middle + jnp.where(kept[:, None], picked, 0.0)
@@ -630,104 +795,190 @@
     grad_low = grad_final.astype(bf16)
 
     sorted_grad = dot_nn(sorter, grad_low).astype(bf16)
-    rows_grad = gather_blocks(sorted_grad)
+    grad_far = swap(sorted_grad, 2)
+    grad_near = swap(sorted_grad, 1)
     pre_near, gin0, gin1 = run_experts_back(
-        counts_near, rows_grad[0], rows_grad[1], hidden_near, in_weight, w_back
+        counts_near, sorted_grad, grad_near, hidden_near, in_weight, w_back
     )
+    grad_far = tie(grad_far, gin0)
+    grad_both = swap(grad_far, 1)
     pre_far, gin2, gin3 = run_experts_back(
-        counts_far, rows_grad[2], rows_grad[3], hidden_far, in_weight, w_back
+        counts_far, grad_far, grad_both, hidden_far, in_weight, w_back
     )
-    summed_grad = scatter_near(gin0, gin1, scatter_far(gin2, gin3))
+    send_second = scatter_far(gin2, gin3)
+    far_second = swap(send_second, 2)
+
+    early = (jnp.arange(local_rows, dtype=jnp.int32)[None, :] < tie(borders, send_second)[:, None]).reshape(-1)
+    masks = [early[:, None], ~early[:, None]]
+    hidden_all = jnp.concatenate([hidden_near, hidden_far], axis=0)
+    grad_all = jnp.concatenate([sorted_grad, grad_near, grad_far, grad_both], axis=0)
+    back_grads = [dot_tn(jnp.where(m, hidden_all, 0), grad_all).astype(bf16) for m in masks]
+    back_rows = EXPERTS * inner
+    part = lambda a, i: lax.dynamic_index_in_dim(a, i, 1, keepdims=False)
+    quarter_of = lambda a: lambda i: part(a, i)
+    back_parts = [g.reshape(1, QUARTERS, inner // QUARTERS, D) for g in back_grads]
+    back_sum = Steps(rep_sum_steps([quarter_of(g) for g in back_parts], n_rep, middle_none))
+    pre_all = tie(jnp.concatenate([pre_near, pre_far], axis=0), back_sum.sent)
+    in_all = jnp.concatenate([sorted_in, in_near, in_far, in_both], axis=0)
+    in_grads = [dot_tn(in_all, jnp.where(m, pre_all, 0)).astype(bf16) for m in masks]
+    quarter_rows = shard_width // QUARTERS
+    in_parts = [g.reshape(N_SHARD, QUARTERS, quarter_rows, inner) for g in in_grads]
+
+    def middle_in(values):
+        blocks = [
+            jnp.concatenate(
+                [lax.dynamic_index_in_dim(v, me ^ j, 0, keepdims=False) for v in values], axis=0
+            )
+            for j in range(N_SHARD)
+        ]
+        moved = exchange_blocks(blocks)
+        token = yield blocks
+        moved = jnp.stack([tie(m, token) for m in moved])
+        rows = values[0].shape[1]
+        return [moved[:, p * rows : (p + 1) * rows] for p in range(len(values))]
+
+    experts_sum = Steps(rep_sum_steps([quarter_of(g) for g in in_parts], n_rep, middle_in))
+
+    far_second = tie(far_second, back_sum.step(experts_sum.sent))
+    summed_grad = scatter_near(gin0, gin1, far_second)
     grad_second = dot_tn(sorter, summed_grad.astype(bf16))
-
-    early = (jnp.arange(local_rows, dtype=jnp.int32)[None, :] < borders[:, None]).reshape(-1)
-    hidden_all = jnp.concatenate([hidden_near, hidden_far], axis=0)
-    pre_all = jnp.concatenate([pre_near, pre_far], axis=0)
-    in_all = jnp.concatenate(rows_in, axis=0)
-    grad_all = jnp.concatenate(rows_grad, axis=0)
-    masks = [early[:, None], ~early[:, None]]
-    back_grad = jnp.concatenate(
-        [dot_tn(jnp.where(m, hidden_all, 0), grad_all).astype(bf16) for m in masks], axis=0
-    )
-    in_grad = [dot_tn(in_all, jnp.where(m, pre_all, 0)).astype(bf16) for m in masks]
-    in_shift_grad = jnp.stack([jnp.sum(jnp.where(m, pre_all.astype(f32), 0), axis=0) for m in masks])
-    back_grad = rep_sum(back_grad, 3, n_rep)
-
     grad_gain_two = jnp.sum(grad_second * normed_two, axis=0)
     grad_bias_two = jnp.sum(grad_second, axis=0)
     grad_middle = grad_final + norm_back(grad_second, normed_two, inverse_two, gain_two)
     grad_branch = grad_middle.astype(bf16)
     grad_out_shift = jnp.sum(grad_branch.astype(f32), axis=0)
-    grad_mixed = exchange_blocks([dot_nt(grad_branch, w).astype(bf16) for w in out_blocks])
-
-    grad_qkv = attend_back(facts, qkv_near, qkv_far, mixed, grad_mixed, logs)
-
-    def row_block(array, j, size):
-        return lax.dynamic_slice_in_dim(array, (me ^ j) * size, size, axis=0)
-
-    in_parts = exchange_blocks(
-        [
-            jnp.concatenate([row_block(g, j, shard_width) for g in in_grad], axis=0)
-            for j in range(N_SHARD)
+    grad_mixed_own = [dot_nt(grad_branch, w).astype(bf16) for w in out_blocks]
+    grad_mixed = exchange_blocks(grad_mixed_own)
+    out_parts = [dot_tn(b, tie(grad_branch, grad_mixed_own)).astype(bf16) for b in mixed_blocks]
+    grad_mixed = lax.optimization_barrier((grad_mixed, out_parts))[0]
+    sent = experts_sum.step((back_sum.step(grad_mixed_own), grad_mixed))
+
+    half_grads = []
+    near_tied = tie(qkv_near, sent)
+    for pair in range(OWN_HEADS // PAIR):
+        half_grads.append(attend_back(pair, facts, near_tied, qkv_far, mixed, grad_mixed, logs))
+        if pair == 0:
+            out_send = tie(scatter_far(out_parts[2], out_parts[3]), half_grads[0])
+            out_far_sum = swap(out_send, 2)
+            sent = (out_send, back_sum.step(experts_sum.step(half_grads[-1])))
+        else:
+            sent = experts_sum.step(back_sum.step(half_grads[-1]))
+        near_tied = tie(qkv_near, sent)
+
+    weight_halves = [
+        jnp.concatenate(
+            [
+                qkv_weight[:, c * OWN + p * PAIR * HEAD_DIM : c * OWN + (p + 1) * PAIR * HEAD_DIM]
+                for c in range(3)
+            ],
+            axis=1,
+        )
+        for p in range(OWN_HEADS // PAIR)
+    ]
+
+    def first_grad(j, token):
+        rows = slice(j * local_rows, (j + 1) * local_rows)
+        total = dot_nt(half_grads[0][rows], tie(weight_halves[0], token))
+        for g, w in zip(half_grads[1:], weight_halves[1:]):
+            total = total + dot_nt(g[rows], w)
+        return total.astype(bf16)
+
+    first2, first3 = first_grad(2, sent), first_grad(3, sent)
+    send_first = scatter_far(first2, first3)
+    far_first = swap(send_first, 2)
+
+    sent = send_first
+    first_all = tie(jnp.concatenate([first_near, first_far], axis=0), sent)
+    half_weights = [dot_tn(first_all, g).astype(bf16) for g in half_grads]
+    out_far_sum = tie(out_far_sum, half_grads[-1])
+    out_grad = scatter_near(out_parts[0], out_parts[1], out_far_sum).astype(bf16)
+    wide = PAIR * HEAD_DIM
+    part_rows = quarter_rows // 2
+    by_owner = [h.reshape(N_SHARD, 2, QUARTERS, part_rows, 3 * wide) for h in half_weights]
+    out_quarters = out_grad.reshape(2, QUARTERS, part_rows, D)
+
+    def last_quarter(p):
+        def quarter(i):
+            pieces = [part(h[:, p], i) for h in by_owner]
+            rows = [
+                jnp.concatenate([g[:, :, c * wide : (c + 1) * wide] for g in pieces], axis=2)
+                for c in range(3)
+            ]
+            whole = lax.dynamic_index_in_dim(out_quarters[p], i, 0, keepdims=False)
+            rows += [whole[:, x * OWN : (x + 1) * OWN] for x in range(N_SHARD)]
+            return jnp.concatenate([r.reshape(-1, OWN) for r in rows], axis=0)
+
+        return quarter
+
+    def middle_last(values):
+        rest = 3 * N_SHARD * part_rows
+        moving = [
+            v[:rest].reshape(3, N_SHARD, part_rows, OWN).transpose(1, 0, 2, 3).reshape(N_SHARD, -1, OWN)
+            for v in values
         ]
-    )
-    in_parts = rep_sum(jnp.concatenate(in_parts, axis=0), 3, n_rep)
-
-    out_parts = [dot_tn(b, grad_branch).astype(bf16) for b in mixed_blocks]
-    out_grad = scatter_near(
-        out_parts[0], out_parts[1], scatter_far(out_parts[2], out_parts[3])
-    ).astype(bf16)
-
-    first_grads = [
-        dot_nt(grad_qkv[j * local_rows : (j + 1) * local_rows], qkv_weight).astype(bf16)
-        for j in range(N_SHARD)
-    ]
-    grad_first = scatter_near(first_grads[0], first_grads[1], scatter_far(first_grads[2], first_grads[3]))
-    first_all = jnp.concatenate([first_near, first_far], axis=0)
-    qkv_grad = dot_tn(first_all, grad_qkv).astype(bf16)
-    qkv_parts = exchange_blocks([row_block(qkv_grad, j, shard_width) for j in range(N_SHARD)])
-    qkv_parts = jnp.concatenate(qkv_parts, axis=0)
-    last_rows = jnp.concatenate([qkv_parts.reshape(-1, D), out_grad], axis=0)
-    last_rows = rep_sum(last_rows, 3, n_rep)
-    split_at = last_rows.shape[0] - out_grad.shape[0]
-    qkv_parts = last_rows[:split_at].reshape(N_SHARD, shard_width, 3, OWN)
-    out_grad = last_rows[split_at:].astype(f32)
-
-    first_in, normed_one, inverse_one = first_rows(tokens)
+        moved = yield from middle_in(moving)
+        return [
+            jnp.concatenate(
+                [m.reshape(N_SHARD, 3, part_rows, OWN).transpose(1, 0, 2, 3).reshape(rest, OWN), v[rest:]],
+                axis=0,
+            )
+            for m, v in zip(moved, values)
+        ]
+
+    last_sum = Steps(rep_sum_steps([last_quarter(0), last_quarter(1)], n_rep, middle_last))
+    sent = last_sum.sent
+    first0, first1 = first_grad(0, sent), first_grad(1, sent)
+    sent = experts_sum.step((first0, first1))
+    grad_first = scatter_near(first0, first1, tie(far_first, sent))
+    first_in, normed_one, inverse_one = first_rows(tie(tokens, sent))
     grad_gain_one = jnp.sum(grad_first * normed_one, axis=0)
     grad_bias_one = jnp.sum(grad_first, axis=0)
     input_grad = grad_middle + norm_back(grad_first, normed_one, inverse_one, gain_one)
 
     by_expert = jnp.stack([(kept & ~is_late), (kept & is_late)]).astype(bf16)
     grad_back_shift = dot_nn(by_expert, grad_low)
+    in_shift_grad = jnp.concatenate(
+        [dot_nn(m.astype(bf16).reshape(1, -1), pre_all) for m in masks], axis=0
+    )
     small = jnp.concatenate(
         [
             jnp.stack([grad_gain_one, grad_bias_one, grad_out_shift, grad_gain_two, grad_bias_two]),
             grad_back_shift,
+            jnp.zeros((1, D), f32),
         ],
         axis=0,
     )
-    small = lax.psum(small, ("rep", "shard"))
+    small = small + swap(small, 1)
+    small = small + swap(small, 2)
     small = lax.dynamic_slice_in_dim(small, me * shard_width, shard_width, axis=1)
-    in_shift_grad = lax.psum(in_shift_grad, "rep")
-
-    order = me ^ jnp.arange(N_SHARD, dtype=jnp.int32)
-    in_grad = jnp.take(in_parts.reshape(N_SHARD, EXPERTS, shard_width, inner), order, axis=0)
-    in_grad = in_grad.transpose(1, 2, 0, 3).reshape(EXPERTS, shard_width, N_SHARD * inner)
-    qkv_grad = jnp.take(qkv_parts, order, axis=0).transpose(1, 2, 0, 3)
+    small = jnp.concatenate([small, in_shift_grad.reshape(-1, shard_width)], axis=0)
+    sent = last_sum.step(experts_sum.step((input_grad, small)))
+    sent = last_sum.step(sent)
+    back_grad = place_experts(me, back_sum.finish(sent))
+    sent = last_sum.step(back_grad)
+    small = small + tie(rep_swap(small, 1, n_rep), sent)
+    in_grad = place_experts(me, experts_sum.finish(small))
+    sent = last_sum.step(in_grad)
+    bit = 2
+    while bit < n_rep:
+        small = small + tie(rep_swap(small, bit, n_rep), sent)
+        sent = last_sum.step(small)
+        bit *= 2
+    in_shift_grad = small[8:].reshape(EXPERTS, inner)
+    qkv_grad, out_grad = place_attention(me, last_sum.finish(small), shard_width)
     return (
         final.astype(bf16),
         input_grad,
         small[0],
         small[1],
-        qkv_grad.reshape(shard_width, 3 * D).astype(f32),
+        qkv_grad,
         out_grad,
         small[2],
         small[3],
         small[4],
-        in_grad.astype(f32),
+        in_grad,
         in_shift_grad,
-        back_grad.reshape(EXPERTS, inner, D).astype(f32),
+        back_grad,
         small[5:7],
     )
 

time: 977 us -> 638 us (0.65)
  blocking collectives: 121 us -> 0 us
  starting transfers between devices: 155 us -> 66.6 us
  waiting for transfers between devices: 262 us -> 191 us
  other arithmetic: 83.1 us -> 41.4 us
  local copies, waits for them, and re-layouts: 94.2 us -> 61.6 us
  Pallas kernels: 158 us -> 181 us
    ppermute x54 -> x33, starting transfers between devices: 128 us -> 39.6 us  [rep_swap(): return lax.ppermute(value, 'rep', [(i, i ^ mask) for i in range(count)])]
    ppermute x54 -> x33, waiting for transfers between devices: 155 us -> 83.8 us  [rep_swap(): return lax.ppermute(value, 'rep', [(i, i ^ mask) for i in range(count)])]
    psum x2 -> x0, blocking collectives: 70.8 us -> none  [the longest x1 40.9 us: shards(): small = lax.psum(small, ('rep', 'shard'))]
    all_gather x1 -> x0, blocking collectives: 50.1 us -> none  [shards(): lax.all_gather(packed, ('rep', 'shard'), axis=0)]
    pallas_call x1 -> x7, Pallas kernels: 63.9 us -> 88.1 us  [the longest x2 63.6 us: attend_back(): pl.pallas_call(functools.partial(attend_back_kernel, blocks, pair), out_s...]
    convert_element_type x37 -> x21, other arithmetic: 32.5 us -> 10.5 us  [the longest x16 7.13 us: added(): return (value.astype(f32) + tie(other, token).astype(f32)).astype(bf16)]
    select_n x29 -> x7, other arithmetic: 18.3 us -> 0.16 us  [the longest x6 0.15 us: in_order(): jnp.where(side == 0, jnp.stack([own, other]), jnp.stack([other, own]))]
    all_to_all x2 -> x0, waiting for transfers between devices: 16.3 us -> none  [the longest x1 16.3 us: shards(): lax.all_to_all(heads_in, 'shard', split_axis=2, concat_axis=0, tiled=True)]
  transfers between devices with their start and end apart: 93 -> 80, of which waited for: 29 -> 36; matrix products, arithmetic and copies ran while one was open for 22% -> 21% of each run, Pallas kernels for 15% -> 24%
where the time goes in v2:
time: 638 us; the launch traced here: 629 us
  waiting for transfers between devices  191 us (30%)
  Pallas kernels  181 us (28%)
  matrix products  69.7 us (11%)
  starting transfers between devices  66.6 us (10%)
  local copies, waits for them, and re-layouts  61.6 us (10%)
  other arithmetic  41.4 us (6%)
  between operations  17.9 us (3%)
    ppermute x46, waiting for transfers between devices, swap(): return lax.ppermute(value, 'shard', [(i, i ^ mask) for i in range(N_SHARD)])  107 us
    ppermute x33, waiting for transfers between devices, rep_swap(): return lax.ppermute(value, 'rep', [(i, i ^ mask) for i in range(count)])  83.8 us
    pallas_call x2, Pallas kernels, attend_back(): pl.pallas_call(functools.partial(attend_back_kernel, blocks, pair), out_s...  63.6 us
    dot_general x12, matrix products, dot_tn(): lax.dot_general(a, b, (((0,), (0,)), ((), ())), preferred_element_type=f32)  46.3 us
    pallas_call x1, Pallas kernels, attend(): pl.pallas_call(functools.partial(attend_kernel, blocks), out_shape=(jax.S...  42.1 us
    ppermute x33, starting transfers between devices, rep_swap(): return lax.ppermute(value, 'rep', [(i, i ^ mask) for i in range(count)])  39.6 us
    unnamed x265, local copies, waits for them, and re-layouts  27.9 us
    ppermute x46, starting transfers between devices, swap(): return lax.ppermute(value, 'shard', [(i, i ^ mask) for i in range(N_SHARD)])  27 us
  transfers between devices with their start and end apart: 80, of which 36 were waited for; matrix products, arithmetic and copies ran while one was open for 21% of the time, Pallas kernels for 24%

profile of v2, /device:TPU:0, one launch (start us, length us, event | category | flops | bytes accessed | tf_op | source)
XLA Modules:
  0.0 629.0 jit_solution(4312589342145927348)
XLA Ops:
  7.2 3.0 collective-permute-start.9
  18.0 32.3 %collective-permute-done.7 = bf16[2,264,768]{2,1,0:T(8,128)(2,1)S(1)} collective-permute-done((bf16[2,264,768]{2,1,0:T(8,128)(2,1)S(1)}, bf16[2,264,768]{2,1,0:T(8,128)(2,1)S(1)}, u32[]{:S(2)}, u32[]{:S(2)}) %collective-permute-start.7) | collective-permute-done | bytes 811040 | tf_op jit(solution)/shard_map/ppermute | solution.py:61
  52.6 3.6 collective-permute-done.17
  56.2 3.0 collective-permute-done.16
  60.2 3.1 gather_fusion
  78.8 2.6 collective-permute-start.4
  85.5 3.1 project.2
  90.7 5.5 collective-permute-done.18
  96.2 4.2 project.3
  101.7 42.1 %attend.1 = (bf16[2048,256]{1,0:T(8,128)(2,1)S(1)}, f32[8,8,256]{2,1,0:T(8,128)S(1)}) custom-call(s32[3]{0:T(128)S(1)} %pad_add_fusion.facts, bf16[1024,768]{1,0:T(8,128)(2,1)S(1)} %get-tuple-element.156.near, bf16[1024,768]{1,0:T(8,128)(2,1)S(1)} %get-tuple-element.110.far), custom_call_target="tpu_custom_call" | custom-call | flops 1048576 | bytes 65536 | tf_op jit(solution)/shard_map/attend/pallas_call | solution.py:288
  146.9 2.8 fusion.80
  152.3 5.2 copy.84
  171.1 12.8 %experts.2 = (bf16[1024,1024]{1,0:T(8,128)(2,1)S(1)}, bf16[512,1024]{1,0:T(8,128)(2,1)S(1)}, bf16[512,1024]{1,0:T(8,128)(2,1)}) custom-call(s32[2,1]{1,0:T(2,128)S(1)} %copy.85.counts, bf16[512,1024]{1,0:T(8,128)(2,1)} %convolution_convert_fusion.1.rows_a, bf16[512,1024]{1,0:T(8,128)(2,1)} %collective-permute-done.20.rows_b, ...), custom_call_target="tpu_custom_call" | custom-call | flops 1048576 | bytes 65536 | tf_op jit(solution)/shard_map/experts/pallas_call | solution.py:533
  186.3 5.5 collective-permute-done.22.rows_a
  191.9 2.9 collective-permute-done.23.rows_b
  197.0 12.5 %experts.3 = (bf16[1024,1024]{1,0:T(8,128)(2,1)S(1)}, bf16[512,1024]{1,0:T(8,128)(2,1)S(1)}, bf16[512,1024]{1,0:T(8,128)(2,1)S(1)}) custom-call(s32[2,1]{1,0:T(2,128)S(1)} %copy.86.counts, bf16[512,1024]{1,0:T(8,128)(2,1)} %collective-permute-done.22.rows_a, bf16[512,1024]{1,0:T(8,128)(2,1)} %collective-permute-done.23.rows_b, ...), custom_call_target="tpu_custom_call" | custom-call | flops 1048576 | bytes 65536 | tf_op jit(solution)/shard_map/experts/pallas_call | solution.py:533
  216.3 24.2 %collective-permute-done.25 = bf16[512,1024]{1,0:T(8,128)(2,1)} collective-permute-done((bf16[512,1024]{1,0:T(8,128)(2,1)}, bf16[512,1024]{1,0:T(8,128)(2,1)}, u32[]{:S(2)}, u32[]{:S(2)}) %collective-permute-start.25) | collective-permute-done | bytes 1048608 | tf_op jit(solution)/shard_map/ppermute | solution.py:61
  240.5 5.6 multiply_add_fusion.1
  249.6 12.5 %experts_back.2 = (bf16[1024,1024]{1,0:T(8,128)(2,1)S(1)}, bf16[512,1024]{1,0:T(8,128)(2,1)S(1)}, bf16[512,1024]{1,0:T(8,128)(2,1)S(1)}) custom-call(s32[2,1]{1,0:T(2,128)S(1)} %copy.85.counts, bf16[512,1024]{1,0:T(8,128)(2,1)S(1)} %convolution_convert_fusion.rows_a, bf16[512,1024]{1,0:T(8,128)(2,1)S(1)} %collective-permute-done.26.rows_b, ...), custom_call_target="tpu_custom_call" | custom-call | flops 1048576 | bytes 65536 | tf_op jit(solution)/shard_map/experts_back/pallas_call | solution.py:557
  265.4 7.2 %collective-permute-done.28.rows_a = bf16[512,1024]{1,0:T(8,128)(2,1)} collective-permute-done((bf16[512,1024]{1,0:T(8,128)(2,1)S(1)}, bf16[512,1024]{1,0:T(8,128)(2,1)}, u32[]{:S(2)}, u32[]{:S(2)}) %collective-permute-start.28) | collective-permute-done | bytes 1048608 | tf_op jit(solution)/shard_map/ppermute | solution.py:61
  272.7 2.4 fusion.103
  277.8 13.0 %experts_back.3 = (bf16[1024,1024]{1,0:T(8,128)(2,1)S(1)}, bf16[512,1024]{1,0:T(8,128)(2,1)S(1)}, bf16[512,1024]{1,0:T(8,128)(2,1)S(1)}) custom-call(s32[2,1]{1,0:T(2,128)S(1)} %copy.86.counts, bf16[512,1024]{1,0:T(8,128)(2,1)} %collective-permute-done.28.rows_a, bf16[512,1024]{1,0:T(8,128)(2,1)} %collective-permute-done.29.rows_b, ...), custom_call_target="tpu_custom_call" | custom-call | flops 1048576 | bytes 65536 | tf_op jit(solution)/shard_map/experts_back/pallas_call | solution.py:557
  291.3 2.5 pad_maximum_fusion.3
  301.7 6.2 fusion.27
  308.1 3.9 collective-permute-start.32
  312.0 6.2 fusion.30
  320.0 7.2 %fusion.33 = bf16[1024,1024]{1,0:T(8,128)(2,1)S(1)} fusion(bf16[2048,1024]{1,0:T(8,128)(2,1)S(1)} %pad_maximum_fusion.2, pred[2048]{0:T(1024)(128)(4,1)S(1)} %bitcast.435, bf16[512,1024]{1,0:T(8,128)(2,1)} %collective-permute-done.23.rows_b, bf16[512,1024]{1,0:T(8,128)(2,1)} %collective-permute-done.22.rows_a, ...), kind=kOutput, calls=%fused_computation.56 | convolution fusion | flops 4314890240 | bytes 10487808 | tf_op jit(solution)/shard_map/dot_general | solution.py:53
  329.7 6.8 %fusion.36 = bf16[1024,1024]{1,0:T(8,128)(2,1)S(1)} fusion(bf16[2048,1024]{1,0:T(8,128)(2,1)S(1)} %pad_maximum_fusion.2, pred[2048]{0:T(1024)(128)(4,1)S(1)} %not.15, bf16[512,1024]{1,0:T(8,128)(2,1)} %collective-permute-done.23.rows_b, bf16[512,1024]{1,0:T(8,128)(2,1)} %collective-permute-done.22.rows_a, ...), kind=kOutput, calls=%fused_computation.57 | convolution fusion | flops 4314890240 | bytes 10487808 | tf_op jit(solution)/shard_map/dot_general | solution.py:53
  337.4 5.9 collective-permute-done.33
  346.9 3.4 multiply_reduce_fusion
  371.6 6.1 collective-permute-done.39.g3
  388.6 31.8 %attend_back.2 = bf16[2048,384]{1,0:T(8,128)(2,1)S(1)} custom-call(s32[3]{0:T(128)S(1)} %pad_add_fusion.facts, bf16[1024,768]{1,0:T(8,128)(2,1)S(1)} %get-tuple-element.156.near, bf16[1024,768]{1,0:T(8,128)(2,1)} %copy-done.7, bf16[2048,256]{1,0:T(8,128)(2,1)S(1)} %copy-done.9, bf16[512,256]{1,0:T(8,128)(2,1)S(1)} %convolution_convert_fusion.11.g0, ...), custom_call_target="tpu_custom_call" | custom-call | flops 1048576 | bytes 65536 | tf_op jit(solution)/shard_map/attend_back/pallas_call | solution.py:415
  426.1 3.4 collective-permute-start.43
  433.6 31.9 %attend_back.3 = bf16[2048,384]{1,0:T(8,128)(2,1)S(1)} custom-call(s32[3]{0:T(128)S(1)} %pad_add_fusion.facts, bf16[1024,768]{1,0:T(8,128)(2,1)S(1)} %get-tuple-element.156.near, bf16[1024,768]{1,0:T(8,128)(2,1)} %copy-done.7, bf16[2048,256]{1,0:T(8,128)(2,1)S(1)} %copy-done.9, bf16[512,256]{1,0:T(8,128)(2,1)S(1)} %convolution_convert_fusion.11.g0, ...), custom_call_target="tpu_custom_call" | custom-call | flops 1048576 | bytes 65536 | tf_op jit(solution)/shard_map/attend_back/pallas_call | solution.py:415
  469.6 5.8 collective-permute-done.43
  485.4 2.4 convolution_convert_fusion.2
  500.3 6.1 collective-permute-done.63
  507.3 10.4 %collective-permute-done.59 = bf16[2,512,256]{2,1,0:T(8,128)(2,1)S(1)} collective-permute-done((bf16[2,512,256]{2,1,0:T(8,128)(2,1)S(1)}, bf16[2,512,256]{2,1,0:T(8,128)(2,1)S(1)}, u32[]{:S(2)}, u32[]{:S(2)}) %collective-permute-start.59) | collective-permute-done | bytes 524320 | tf_op jit(solution)/shard_map/ppermute | solution.py:89
  527.5 4.9 fusion.20
  532.4 9.7 %collective-permute-done.60.refs_1_ = bf16[4,64,1024]{2,1,0:T(8,128)(2,1)} collective-permute-done((bf16[4,64,1024]{2,1,0:T(8,128)(2,1)S(1)}, bf16[4,64,1024]{2,1,0:T(8,128)(2,1)}, u32[]{:S(2)}, u32[]{:S(2)}) %collective-permute-start.60) | collective-permute-done | bytes 524320 | tf_op jit(solution)/shard_map/ppermute | solution.py:89
  547.8 5.3 collective-permute-done.62
  559.8 7.9 %place_experts.2 = f32[2,1024,1024]{2,1,0:T(8,128)} custom-call(s32[9]{0:T(128)S(1)} %concatenate.293.facts, bf16[1,256,1024]{2,1,0:T(8,128)(2,1)S(1)} %add_convert_fusion.18.refs_0_, bf16[1,256,1024]{2,1,0:T(8,128)(2,1)S(1)} %copy-done.20, bf16[2,1,256,1024]{3,2,1,0:T(8,128)(2,1)} %collective-permute-done.66.refs_2_, bf16[1,256,1024]{2,1,0:T(8,128)(2,1)S(1)} %copy-done.16, ...), custom_call_target="tpu_custom_call" | custom-call | flops 1048576 | bytes 65536 | tf_op jit(solution)/shard_map/place_experts/pallas_call | solution.py:605
  567.7 11.1 %collective-permute-done.65 = bf16[2,512,256]{2,1,0:T(8,128)(2,1)} collective-permute-done((bf16[2,512,256]{2,1,0:T(8,128)(2,1)}, bf16[2,512,256]{2,1,0:T(8,128)(2,1)}, u32[]{:S(2)}, u32[]{:S(2)}) %collective-permute-start.65) | collective-permute-done | bytes 524320 | tf_op jit(solution)/shard_map/ppermute | solution.py:89
  582.5 8.2 %collective-permute-done.70.refs_5_ = bf16[2,4,64,1024]{3,2,1,0:T(8,128)(2,1)S(1)} collective-permute-done((bf16[2,4,64,1024]{3,2,1,0:T(8,128)(2,1)}, bf16[2,4,64,1024]{3,2,1,0:T(8,128)(2,1)S(1)}, u32[]{:S(2)}, u32[]{:S(2)}) %collective-permute-start.70) | collective-permute-done | bytes 1048608 | tf_op jit(solution)/shard_map/ppermute | solution.py:89
  590.7 6.4 %place_experts.3 = f32[2,256,4096]{2,1,0:T(8,128)} custom-call(s32[9]{0:T(128)S(1)} %concatenate.293.facts, bf16[4,64,1024]{2,1,0:T(8,128)(2,1)S(1)} %get-tuple-element.246.refs_0_, bf16[4,64,1024]{2,1,0:T(8,128)(2,1)} %collective-permute-done.60.refs_1_, bf16[2,4,64,1024]{3,2,1,0:T(8,128)(2,1)S(1)} %collective-permute-done.69.refs_2_, ...), custom_call_target="tpu_custom_call" | custom-call | flops 1048576 | bytes 65536 | tf_op jit(solution)/shard_map/place_experts/pallas_call | solution.py:605
  601.1 5.8 collective-permute-done.68
  610.6 5.7 collective-permute-done.74
  618.8 2.9 place_attention.1
  (645 shorter events, 194.2 us)
Async XLA Ops:
  7.2 145.1 %all-gather.3.cloned.1.call-start = ((), (), s32[]{:S(2)}) async-start(), calls=%async_computation | async-start | bytes 4718592 | tf_op jit(solution)/shard_map/all_gather | solution.py:761
  7.2 43.0 %collective-permute-start.9 = (bf16[512,1024]{1,0:T(8,128)(2,1)}, bf16[512,1024]{1,0:T(8,128)(2,1)}, u32[]{:S(2)}, u32[]{:S(2)}) collective-permute-start(bf16[512,1024]{1,0:T(8,128)(2,1)} %tok_a.1), channel_id=1, source_target_pairs={{0,2},{1,3},{2,0},{3,1},{4,6},{5,7},{6,4},{7,5},{8,10},{9,11},{10,... | collective-permute-start | bytes 3145736 | tf_op jit(solution)/shard_map/ppermute | solution.py:61
  16.8 33.5 %collective-permute-start.7 = (bf16[2,264,768]{2,1,0:T(8,128)(2,1)S(1)}, bf16[2,264,768]{2,1,0:T(8,128)(2,1)S(1)}, u32[]{:S(2)}, u32[]{:S(2)}) collective-permute-start(bf16[2,264,768]{2,1,0:T(8,128)(2,1)S(1)} %pad_maximum_fusion.15), channel_id=1, source_target_pairs={{0,3},{1,2},{2,1},{3,0},{4,7},{5,6},{6,5},{7,4},{8,11},{9,10},{10,... | collective-permute-start | bytes 2433032 | tf_op jit(solution)/shard_map/ppermute | solution.py:61
  76.9 19.4 %collective-permute-start.10 = (bf16[512,1024]{1,0:T(8,128)(2,1)}, bf16[512,1024]{1,0:T(8,128)(2,1)S(1)}, u32[]{:S(2)}, u32[]{:S(2)}) collective-permute-start(bf16[512,1024]{1,0:T(8,128)(2,1)} %collective-permute-done.9.tok_a), channel_id=1, source_target_pairs={{0,1},{1,0},{2,3},{3,2},{4,5},{5,4},{6,7},{7,6},{8,9},{9,8},{10,11... | collective-permute-start | bytes 3145736 | tf_op jit(solution)/shard_map/ppermute | solution.py:61
  83.3 12.9 %collective-permute-start.18 = (bf16[256,1024]{1,0:T(8,128)(2,1)}, bf16[256,1024]{1,0:T(8,128)(2,1)}, u32[]{:S(2)}, u32[]{:S(2)}) collective-permute-start(bf16[256,1024]{1,0:T(8,128)(2,1)} %param.28), channel_id=1, source_target_pairs={{0,2},{1,3},{2,0},{3,1},{4,6},{5,7},{6,4},{7,5},{8,10},{9,11},{10,... | collective-permute-start | bytes 1572872 | tf_op jit(solution)/shard_map/ppermute | solution.py:61
  85.5 64.2 %collective-permute-start.12 = (bf16[256,1024]{1,0:T(8,128)(2,1)}, bf16[256,1024]{1,0:T(8,128)(2,1)S(1)}, u32[]{:S(2)}, u32[]{:S(2)}) collective-permute-start(bf16[256,1024]{1,0:T(8,128)(2,1)} %param.28), channel_id=1, source_target_pairs={{0,1},{1,0},{2,3},{3,2},{4,5},{5,4},{6,7},{7,6},{8,9},{9,8},{10,11... | collective-permute-start | bytes 1572872 | tf_op jit(solution)/shard_map/ppermute | solution.py:61
  96.2 65.1 %collective-permute-start.19 = (bf16[256,1024]{1,0:T(8,128)(2,1)}, bf16[256,1024]{1,0:T(8,128)(2,1)}, u32[]{:S(2)}, u32[]{:S(2)}) collective-permute-start(bf16[256,1024]{1,0:T(8,128)(2,1)} %collective-permute-done.18), channel_id=1, source_target_pairs={{0,1},{1,0},{2,3},{3,2},{4,5},{5,4},{6,7},{7,6},{8,9},{9,8},{10,11... | collective-permute-start | bytes 1572872 | tf_op jit(solution)/shard_map/ppermute | solution.py:61
  145.3 12.2 %collective-permute-start.14 = (bf16[512,256]{1,0:T(8,128)(2,1)}, bf16[512,256]{1,0:T(8,128)(2,1)S(1)}, u32[]{:S(2)}, u32[]{:S(2)}) collective-permute-start(bf16[512,256]{1,0:T(8,128)(2,1)} %get-tuple-element.260), channel_id=1, source_target_pairs={{0,3},{1,2},{2,1},{3,0},{4,7},{5,6},{6,5},{7,4},{8,11},{9,10},{10,... | collective-permute-start | bytes 786440 | tf_op jit(solution)/shard_map/ppermute | solution.py:61
  146.1 13.6 %collective-permute-start.13 = (bf16[512,256]{1,0:T(8,128)(2,1)}, bf16[512,256]{1,0:T(8,128)(2,1)S(1)}, u32[]{:S(2)}, u32[]{:S(2)}) collective-permute-start(bf16[512,256]{1,0:T(8,128)(2,1)} %get-tuple-element.261), channel_id=1, source_target_pairs={{0,2},{1,3},{2,0},{3,1},{4,6},{5,7},{6,4},{7,5},{8,10},{9,11},{10,... | collective-permute-start | bytes 786440 | tf_op jit(solution)/shard_map/ppermute | solution.py:61
  165.9 25.9 %collective-permute-start.22 = (bf16[512,1024]{1,0:T(8,128)(2,1)}, bf16[512,1024]{1,0:T(8,128)(2,1)}, u32[]{:S(2)}, u32[]{:S(2)}) collective-permute-start(bf16[512,1024]{1,0:T(8,128)(2,1)} %convolution_convert_fusion.1.rows_a), channel_id=1, source_target_pairs={{0,2},{1,3},{2,0},{3,1},{4,6},{5,7},{6,4},{7,5},{8,10},{9,11},{10,... | collective-permute-start | bytes 3145736 | tf_op jit(solution)/shard_map/ppermute | solution.py:61
  215.0 25.5 %collective-permute-start.25 = (bf16[512,1024]{1,0:T(8,128)(2,1)}, bf16[512,1024]{1,0:T(8,128)(2,1)}, u32[]{:S(2)}, u32[]{:S(2)}) collective-permute-start(bf16[512,1024]{1,0:T(8,128)(2,1)} %add_convert_fusion.8), channel_id=1, source_target_pairs={{0,2},{1,3},{2,0},{3,1},{4,6},{5,7},{6,4},{7,5},{8,10},{9,11},{10,... | collective-permute-start | bytes 3145736 | tf_op jit(solution)/shard_map/ppermute | solution.py:61
  246.9 25.7 %collective-permute-start.28 = (bf16[512,1024]{1,0:T(8,128)(2,1)S(1)}, bf16[512,1024]{1,0:T(8,128)(2,1)}, u32[]{:S(2)}, u32[]{:S(2)}) collective-permute-start(bf16[512,1024]{1,0:T(8,128)(2,1)S(1)} %convolution_convert_fusion.rows_a), channel_id=1, source_target_pairs={{0,2},{1,3},{2,0},{3,1},{4,6},{5,7},{6,4},{7,5},{8,10},{9,11},{10,... | collective-permute-start | bytes 3145736 | tf_op jit(solution)/shard_map/ppermute | solution.py:61
  295.8 50.2 %collective-permute-start.27 = (bf16[512,1024]{1,0:T(8,128)(2,1)S(1)}, bf16[512,1024]{1,0:T(8,128)(2,1)}, u32[]{:S(2)}, u32[]{:S(2)}) collective-permute-start(bf16[512,1024]{1,0:T(8,128)(2,1)S(1)} %copy-done.43), channel_id=1, source_target_pairs={{0,1},{1,0},{2,3},{3,2},{4,5},{5,4},{6,7},{7,6},{8,9},{9,8},{10,11... | collective-permute-start | bytes 3145736 | tf_op jit(solution)/shard_map/ppermute | solution.py:61
  299.6 46.4 %collective-permute-start.31 = (bf16[512,1024]{1,0:T(8,128)(2,1)S(1)}, bf16[512,1024]{1,0:T(8,128)(2,1)}, u32[]{:S(2)}, u32[]{:S(2)}) collective-permute-start(bf16[512,1024]{1,0:T(8,128)(2,1)S(1)} %add_convert_fusion.6), channel_id=1, source_target_pairs={{0,2},{1,3},{2,0},{3,1},{4,6},{5,7},{6,4},{7,5},{8,10},{9,11},{10,... | collective-permute-start | bytes 3145736 | tf_op jit(solution)/shard_map/ppermute | solution.py:61
  308.1 36.9 %collective-permute-start.32 = (bf16[2,1,256,1024]{3,2,1,0:T(8,128)(2,1)S(1)}, bf16[2,1,256,1024]{3,2,1,0:T(8,128)(2,1)S(1)}, u32[]{:S(2)}, u32[]{:S(2)}) collective-permute-start(bf16[2,1,256,1024]{3,2,1,0:T(8,128)(2,1)S(1)} %pad_maximum_fusion.4), channel_id=1, source_target_pairs={{0,4},{4,0},{8,12},{12,8},{16,20},{20,16},{24,28},{28,24},{1,5},{5... | collective-permute-start | bytes 3145736 | tf_op jit(solution)/shard_map/ppermute | solution.py:89
  318.4 24.9 %collective-permute-start.33 = (bf16[2,1,256,1024]{3,2,1,0:T(8,128)(2,1)S(1)}, bf16[2,1,256,1024]{3,2,1,0:T(8,128)(2,1)S(1)}, u32[]{:S(2)}, u32[]{:S(2)}) collective-permute-start(bf16[2,1,256,1024]{3,2,1,0:T(8,128)(2,1)S(1)} %pad_maximum_fusion.5), channel_id=1, source_target_pairs={{0,8},{4,12},{8,0},{12,4},{16,24},{20,28},{24,16},{28,20},{1,9},{5... | collective-permute-start | bytes 3145736 | tf_op jit(solution)/shard_map/ppermute | solution.py:89
  328.7 36.4 %collective-permute-start.34 = (bf16[2,4,64,1024]{3,2,1,0:T(8,128)(2,1)}, bf16[2,4,64,1024]{3,2,1,0:T(8,128)(2,1)}, u32[]{:S(2)}, u32[]{:S(2)}) collective-permute-start(bf16[2,4,64,1024]{3,2,1,0:T(8,128)(2,1)} %pad_maximum_fusion.6), channel_id=1, source_target_pairs={{0,4},{4,0},{8,12},{12,8},{16,20},{20,16},{24,28},{28,24},{1,5},{5... | collective-permute-start | bytes 3145736 | tf_op jit(solution)/shard_map/ppermute | solution.py:89
  343.3 26.1 %collective-permute-start.41 = (bf16[2,4,64,1024]{3,2,1,0:T(8,128)(2,1)S(1)}, bf16[2,4,64,1024]{3,2,1,0:T(8,128)(2,1)S(1)}, u32[]{:S(2)}, u32[]{:S(2)}) collective-permute-start(bf16[2,4,64,1024]{3,2,1,0:T(8,128)(2,1)S(1)} %pad_maximum_fusion.7), channel_id=1, source_target_pairs={{0,8},{4,12},{8,0},{12,4},{16,24},{20,28},{24,16},{28,20},{1,9},{5... | collective-permute-start | bytes 3145736 | tf_op jit(solution)/shard_map/ppermute | solution.py:89
  345.3 33.3 %collective-permute-start.35 = (bf16[1,256,1024]{2,1,0:T(8,128)(2,1)S(1)}, bf16[1,256,1024]{2,1,0:T(8,128)(2,1)S(1)}, u32[]{:S(2)}, u32[]{:S(2)}) collective-permute-start(bf16[1,256,1024]{2,1,0:T(8,128)(2,1)S(1)} %fusion.47), channel_id=1, source_target_pairs={{0,8},{4,12},{8,0},{12,4},{16,24},{20,28},{24,16},{28,20},{1,9},{5... | collective-permute-start | bytes 1572872 | tf_op jit(solution)/shard_map/ppermute | solution.py:89
  354.7 15.6 %collective-permute-start.37 = (bf16[512,256]{1,0:T(8,128)(2,1)S(1)}, bf16[512,256]{1,0:T(8,128)(2,1)S(1)}, u32[]{:S(2)}, u32[]{:S(2)}) collective-permute-start(bf16[512,256]{1,0:T(8,128)(2,1)S(1)} %convolution_convert_fusion.10), channel_id=1, source_target_pairs={{0,1},{1,0},{2,3},{3,2},{4,5},{5,4},{6,7},{7,6},{8,9},{9,8},{10,11... | collective-permute-start | bytes 786440 | tf_op jit(solution)/shard_map/ppermute | solution.py:61
  356.3 15.3 %collective-permute-start.38 = (bf16[512,256]{1,0:T(8,128)(2,1)S(1)}, bf16[512,256]{1,0:T(8,128)(2,1)S(1)}, u32[]{:S(2)}, u32[]{:S(2)}) collective-permute-start(bf16[512,256]{1,0:T(8,128)(2,1)S(1)} %convolution_convert_fusion.9), channel_id=1, source_target_pairs={{0,2},{1,3},{2,0},{3,1},{4,6},{5,7},{6,4},{7,5},{8,10},{9,11},{10,... | collective-permute-start | bytes 786440 | tf_op jit(solution)/shard_map/ppermute | solution.py:61
  365.1 14.0 %collective-permute-start.36 = (bf16[1,256,1024]{2,1,0:T(8,128)(2,1)S(1)}, bf16[1,256,1024]{2,1,0:T(8,128)(2,1)S(1)}, u32[]{:S(2)}, u32[]{:S(2)}) collective-permute-start(bf16[1,256,1024]{2,1,0:T(8,128)(2,1)S(1)} %fusion.46), channel_id=1, source_target_pairs={{0,4},{4,0},{8,12},{12,8},{16,20},{20,16},{24,28},{28,24},{1,5},{5... | collective-permute-start | bytes 1572872 | tf_op jit(solution)/shard_map/ppermute | solution.py:89
  370.3 50.1 %collective-permute-start.46 = (bf16[256,1024]{1,0:T(8,128)(2,1)}, bf16[256,1024]{1,0:T(8,128)(2,1)}, u32[]{:S(2)}, u32[]{:S(2)}) collective-permute-start(bf16[256,1024]{1,0:T(8,128)(2,1)} %convolution_convert_fusion.4), channel_id=1, source_target_pairs={{0,1},{1,0},{2,3},{3,2},{4,5},{5,4},{6,7},{7,6},{8,9},{9,8},{10,11... | collective-permute-start | bytes 1572872 | tf_op jit(solution)/shard_map/ppermute | solution.py:61
  380.8 48.6 %collective-permute-start.44 = (bf16[2,1,256,1024]{3,2,1,0:T(8,128)(2,1)}, bf16[2,1,256,1024]{3,2,1,0:T(8,128)(2,1)}, u32[]{:S(2)}, u32[]{:S(2)}) collective-permute-start(bf16[2,1,256,1024]{3,2,1,0:T(8,128)(2,1)} %pad_maximum_fusion.8), channel_id=1, source_target_pairs={{0,16},{4,20},{8,24},{12,28},{16,0},{20,4},{24,8},{28,12},{1,17},{... | collective-permute-start | bytes 3145736 | tf_op jit(solution)/shard_map/ppermute | solution.py:89
  382.8 40.1 %collective-permute-start.40 = (bf16[4,64,1024]{2,1,0:T(8,128)(2,1)}, bf16[4,64,1024]{2,1,0:T(8,128)(2,1)}, u32[]{:S(2)}, u32[]{:S(2)}) collective-permute-start(bf16[4,64,1024]{2,1,0:T(8,128)(2,1)} %fusion.42), channel_id=1, source_target_pairs={{0,8},{4,12},{8,0},{12,4},{16,24},{20,28},{24,16},{28,20},{1,9},{5... | collective-permute-start | bytes 1572872 | tf_op jit(solution)/shard_map/ppermute | solution.py:89
  385.1 37.8 %collective-permute-start.42 = (bf16[4,64,1024]{2,1,0:T(8,128)(2,1)}, bf16[4,64,1024]{2,1,0:T(8,128)(2,1)}, u32[]{:S(2)}, u32[]{:S(2)}) collective-permute-start(bf16[4,64,1024]{2,1,0:T(8,128)(2,1)} %fusion.41), channel_id=1, source_target_pairs={{0,4},{4,0},{8,12},{12,8},{16,20},{20,16},{24,28},{28,24},{1,5},{5... | collective-permute-start | bytes 1572872 | tf_op jit(solution)/shard_map/ppermute | solution.py:89
  386.4 79.1 %collective-permute-start.49 = (bf16[256,1024]{1,0:T(8,128)(2,1)}, bf16[256,1024]{1,0:T(8,128)(2,1)S(1)}, u32[]{:S(2)}, u32[]{:S(2)}) collective-permute-start(bf16[256,1024]{1,0:T(8,128)(2,1)} %convolution_convert_fusion.6), channel_id=1, source_target_pairs={{0,1},{1,0},{2,3},{3,2},{4,5},{5,4},{6,7},{7,6},{8,9},{9,8},{10,11... | collective-permute-start | bytes 1572872 | tf_op jit(solution)/shard_map/ppermute | solution.py:61
  421.7 43.8 %collective-permute-start.50 = (bf16[256,1024]{1,0:T(8,128)(2,1)S(1)}, bf16[256,1024]{1,0:T(8,128)(2,1)S(1)}, u32[]{:S(2)}, u32[]{:S(2)}) collective-permute-start(bf16[256,1024]{1,0:T(8,128)(2,1)S(1)} %add_convert_fusion.17), channel_id=1, source_target_pairs={{0,2},{1,3},{2,0},{3,1},{4,6},{5,7},{6,4},{7,5},{8,10},{9,11},{10,... | collective-permute-start | bytes 1572872 | tf_op jit(solution)/shard_map/ppermute | solution.py:61
  426.1 49.4 %collective-permute-start.43 = (bf16[2,4,64,1024]{3,2,1,0:T(8,128)(2,1)S(1)}, bf16[2,4,64,1024]{3,2,1,0:T(8,128)(2,1)S(1)}, u32[]{:S(2)}, u32[]{:S(2)}) collective-permute-start(bf16[2,4,64,1024]{3,2,1,0:T(8,128)(2,1)S(1)} %pad_maximum_fusion.9), channel_id=1, source_target_pairs={{0,16},{4,20},{8,24},{12,28},{16,0},{20,4},{24,8},{28,12},{1,17},{... | collective-permute-start | bytes 3145736 | tf_op jit(solution)/shard_map/ppermute | solution.py:89
  431.0 36.3 %collective-permute-start.45 = (bf16[1,256,1024]{2,1,0:T(8,128)(2,1)S(1)}, bf16[1,256,1024]{2,1,0:T(8,128)(2,1)S(1)}, u32[]{:S(2)}, u32[]{:S(2)}) collective-permute-start(bf16[1,256,1024]{2,1,0:T(8,128)(2,1)S(1)} %add_convert_fusion.18.refs_0_), channel_id=1, source_target_pairs={{0,8},{4,12},{8,0},{12,4},{16,24},{20,28},{24,16},{28,20},{1,9},{5... | collective-permute-start | bytes 1572872 | tf_op jit(solution)/shard_map/ppermute | solution.py:89
  432.5 34.9 %collective-permute-start.47 = (bf16[1,256,1024]{2,1,0:T(8,128)(2,1)S(1)}, bf16[1,256,1024]{2,1,0:T(8,128)(2,1)S(1)}, u32[]{:S(2)}, u32[]{:S(2)}) collective-permute-start(bf16[1,256,1024]{2,1,0:T(8,128)(2,1)S(1)} %add_convert_fusion.16.refs_3_), channel_id=1, source_target_pairs={{0,4},{4,0},{8,12},{12,8},{16,20},{20,16},{24,28},{28,24},{1,5},{5... | collective-permute-start | bytes 1572872 | tf_op jit(solution)/shard_map/ppermute | solution.py:89
  480.2 79.5 %collective-permute-start.66 = (bf16[2,1,256,1024]{3,2,1,0:T(8,128)(2,1)}, bf16[2,1,256,1024]{3,2,1,0:T(8,128)(2,1)}, u32[]{:S(2)}, u32[]{:S(2)}) collective-permute-start(bf16[2,1,256,1024]{3,2,1,0:T(8,128)(2,1)} %pad_maximum_fusion.10), channel_id=1, source_target_pairs={{0,4},{4,0},{8,12},{12,8},{16,20},{20,16},{24,28},{28,24},{1,5},{5... | collective-permute-start | bytes 3145736 | tf_op jit(solution)/shard_map/ppermute | solution.py:89
  482.5 14.4 %collective-permute-start.51 = (bf16[128,1024]{1,0:T(8,128)(2,1)S(1)}, bf16[128,1024]{1,0:T(8,128)(2,1)S(1)}, u32[]{:S(2)}, u32[]{:S(2)}) collective-permute-start(bf16[128,1024]{1,0:T(8,128)(2,1)S(1)} %pad_maximum_fusion.29), channel_id=1, source_target_pairs={{0,1},{1,0},{2,3},{3,2},{4,5},{5,4},{6,7},{7,6},{8,9},{9,8},{10,11... | collective-permute-start | bytes 786440 | tf_op jit(solution)/shard_map/ppermute | solution.py:61
  483.7 13.2 %collective-permute-start.52 = (bf16[128,1024]{1,0:T(8,128)(2,1)S(1)}, bf16[128,1024]{1,0:T(8,128)(2,1)S(1)}, u32[]{:S(2)}, u32[]{:S(2)}) collective-permute-start(bf16[128,1024]{1,0:T(8,128)(2,1)S(1)} %pad_maximum_fusion.30), channel_id=1, source_target_pairs={{0,2},{1,3},{2,0},{3,1},{4,6},{5,7},{6,4},{7,5},{8,10},{9,11},{10,... | collective-permute-start | bytes 786440 | tf_op jit(solution)/shard_map/ppermute | solution.py:61
  492.5 13.8 %collective-permute-start.63 = (bf16[2,512,256]{2,1,0:T(8,128)(2,1)S(1)}, bf16[2,512,256]{2,1,0:T(8,128)(2,1)S(1)}, u32[]{:S(2)}, u32[]{:S(2)}) collective-permute-start(bf16[2,512,256]{2,1,0:T(8,128)(2,1)S(1)} %pad_maximum_fusion.23), channel_id=1, source_target_pairs={{0,8},{4,12},{8,0},{12,4},{16,24},{20,28},{24,16},{28,20},{1,9},{5... | collective-permute-start | bytes 1572872 | tf_op jit(solution)/shard_map/ppermute | solution.py:89
  494.4 23.3 %collective-permute-start.59 = (bf16[2,512,256]{2,1,0:T(8,128)(2,1)S(1)}, bf16[2,512,256]{2,1,0:T(8,128)(2,1)S(1)}, u32[]{:S(2)}, u32[]{:S(2)}) collective-permute-start(bf16[2,512,256]{2,1,0:T(8,128)(2,1)S(1)} %pad_maximum_fusion.22), channel_id=1, source_target_pairs={{0,4},{4,0},{8,12},{12,8},{16,20},{20,16},{24,28},{28,24},{1,5},{5... | collective-permute-start | bytes 1572872 | tf_op jit(solution)/shard_map/ppermute | solution.py:89
  496.9 25.6 %collective-permute-start.54 = (bf16[512,1024]{1,0:T(8,128)(2,1)S(1)}, bf16[512,1024]{1,0:T(8,128)(2,1)S(1)}, u32[]{:S(2)}, u32[]{:S(2)}) collective-permute-start(bf16[512,1024]{1,0:T(8,128)(2,1)S(1)} %add_convert_fusion), channel_id=1, source_target_pairs={{0,1},{1,0},{2,3},{3,2},{4,5},{5,4},{6,7},{7,6},{8,9},{9,8},{10,11... | collective-permute-start | bytes 3145736 | tf_op jit(solution)/shard_map/ppermute | solution.py:61
  496.9 25.6 %collective-permute-start.55 = (bf16[512,1024]{1,0:T(8,128)(2,1)S(1)}, bf16[512,1024]{1,0:T(8,128)(2,1)S(1)}, u32[]{:S(2)}, u32[]{:S(2)}) collective-permute-start(bf16[512,1024]{1,0:T(8,128)(2,1)S(1)} %add_convert_fusion.2), channel_id=1, source_target_pairs={{0,2},{1,3},{2,0},{3,1},{4,6},{5,7},{6,4},{7,5},{8,10},{9,11},{10,... | collective-permute-start | bytes 3145736 | tf_op jit(solution)/shard_map/ppermute | solution.py:61
  506.3 52.7 %collective-permute-start.67 = (bf16[2,1,256,1024]{3,2,1,0:T(8,128)(2,1)}, bf16[2,1,256,1024]{3,2,1,0:T(8,128)(2,1)}, u32[]{:S(2)}, u32[]{:S(2)}) collective-permute-start(bf16[2,1,256,1024]{3,2,1,0:T(8,128)(2,1)} %pad_maximum_fusion.11), channel_id=1, source_target_pairs={{0,8},{4,12},{8,0},{12,4},{16,24},{20,28},{24,16},{28,20},{1,9},{5... | collective-permute-start | bytes 3145736 | tf_op jit(solution)/shard_map/ppermute | solution.py:89
  517.7 14.7 %collective-permute-start.61 = (bf16[4,64,1024]{2,1,0:T(8,128)(2,1)S(1)}, bf16[4,64,1024]{2,1,0:T(8,128)(2,1)}, u32[]{:S(2)}, u32[]{:S(2)}) collective-permute-start(bf16[4,64,1024]{2,1,0:T(8,128)(2,1)S(1)} %get-tuple-element.245.refs_3_), channel_id=1, source_target_pairs={{0,4},{4,0},{8,12},{12,8},{16,20},{20,16},{24,28},{28,24},{1,5},{5... | collective-permute-start | bytes 1572872 | tf_op jit(solution)/shard_map/ppermute | solution.py:89
  522.5 19.6 %collective-permute-start.60 = (bf16[4,64,1024]{2,1,0:T(8,128)(2,1)S(1)}, bf16[4,64,1024]{2,1,0:T(8,128)(2,1)}, u32[]{:S(2)}, u32[]{:S(2)}) collective-permute-start(bf16[4,64,1024]{2,1,0:T(8,128)(2,1)S(1)} %get-tuple-element.246.refs_0_), channel_id=1, source_target_pairs={{0,8},{4,12},{8,0},{12,4},{16,24},{20,28},{24,16},{28,20},{1,9},{5... | collective-permute-start | bytes 1572872 | tf_op jit(solution)/shard_map/ppermute | solution.py:89
  555.1 23.8 %collective-permute-start.65 = (bf16[2,512,256]{2,1,0:T(8,128)(2,1)}, bf16[2,512,256]{2,1,0:T(8,128)(2,1)}, u32[]{:S(2)}, u32[]{:S(2)}) collective-permute-start(bf16[2,512,256]{2,1,0:T(8,128)(2,1)} %pad_maximum_fusion.24), channel_id=1, source_target_pairs={{0,16},{4,20},{8,24},{12,28},{16,0},{20,4},{24,8},{28,12},{1,17},{... | collective-permute-start | bytes 1572872 | tf_op jit(solution)/shard_map/ppermute | solution.py:89
  557.1 24.5 %collective-permute-start.58 = (f32[16,256]{1,0:T(8,128)S(1)}, f32[16,256]{1,0:T(8,128)S(1)}, u32[]{:S(2)}, u32[]{:S(2)}) collective-permute-start(f32[16,256]{1,0:T(8,128)S(1)} %pad_maximum_fusion.62), channel_id=1, source_target_pairs={{0,4},{4,0},{8,12},{12,8},{16,20},{20,16},{24,28},{28,24},{1,5},{5... | collective-permute-start | bytes 49160 | tf_op jit(solution)/shard_map/ppermute | solution.py:89
  558.2 32.5 %collective-permute-start.70 = (bf16[2,4,64,1024]{3,2,1,0:T(8,128)(2,1)}, bf16[2,4,64,1024]{3,2,1,0:T(8,128)(2,1)S(1)}, u32[]{:S(2)}, u32[]{:S(2)}) collective-permute-start(bf16[2,4,64,1024]{3,2,1,0:T(8,128)(2,1)} %pad_maximum_fusion.14), channel_id=1, source_target_pairs={{0,8},{4,12},{8,0},{12,4},{16,24},{20,28},{24,16},{28,20},{1,9},{5... | collective-permute-start | bytes 3145736 | tf_op jit(solution)/shard_map/ppermute | solution.py:89
  559.0 31.8 %collective-permute-start.69 = (bf16[2,4,64,1024]{3,2,1,0:T(8,128)(2,1)}, bf16[2,4,64,1024]{3,2,1,0:T(8,128)(2,1)S(1)}, u32[]{:S(2)}, u32[]{:S(2)}) collective-permute-start(bf16[2,4,64,1024]{3,2,1,0:T(8,128)(2,1)} %pad_maximum_fusion.13), channel_id=1, source_target_pairs={{0,4},{4,0},{8,12},{12,8},{16,20},{20,16},{24,28},{28,24},{1,5},{5... | collective-permute-start | bytes 3145736 | tf_op jit(solution)/shard_map/ppermute | solution.py:89
  580.4 16.7 %collective-permute-start.71 = (bf16[192,256]{1,0:T(8,128)(2,1)S(1)}, bf16[192,256]{1,0:T(8,128)(2,1)S(1)}, u32[]{:S(2)}, u32[]{:S(2)}) collective-permute-start(bf16[192,256]{1,0:T(8,128)(2,1)S(1)} %pad_maximum_fusion.35), channel_id=1, source_target_pairs={{0,1},{1,0},{2,3},{3,2},{4,5},{5,4},{6,7},{7,6},{8,9},{9,8},{10,11... | collective-permute-start | bytes 294920 | tf_op jit(solution)/shard_map/ppermute | solution.py:61
  580.5 16.6 %collective-permute-start.72 = (bf16[192,256]{1,0:T(8,128)(2,1)S(1)}, bf16[192,256]{1,0:T(8,128)(2,1)S(1)}, u32[]{:S(2)}, u32[]{:S(2)}) collective-permute-start(bf16[192,256]{1,0:T(8,128)(2,1)S(1)} %pad_maximum_fusion.36), channel_id=1, source_target_pairs={{0,2},{1,3},{2,0},{3,1},{4,6},{5,7},{6,4},{7,5},{8,10},{9,11},{10,... | collective-permute-start | bytes 294920 | tf_op jit(solution)/shard_map/ppermute | solution.py:61
  581.7 15.4 %collective-permute-start.73 = (bf16[192,256]{1,0:T(8,128)(2,1)S(1)}, bf16[192,256]{1,0:T(8,128)(2,1)S(1)}, u32[]{:S(2)}, u32[]{:S(2)}) collective-permute-start(bf16[192,256]{1,0:T(8,128)(2,1)S(1)} %pad_maximum_fusion.37), channel_id=1, source_target_pairs={{0,3},{1,2},{2,1},{3,0},{4,7},{5,6},{6,5},{7,4},{8,11},{9,10},{10,... | collective-permute-start | bytes 294920 | tf_op jit(solution)/shard_map/ppermute | solution.py:61
  (141 other events, 1164.6 us)
Sparse Core Ops, SparseCore 0:
  60.3 74.3 all-gather.2

commit v3 on v2

--- a/solution.py
+++ b/solution.py
@@ -17,6 +17,7 @@
 OWN_HEADS = HEADS // N_SHARD
 OWN = OWN_HEADS * HEAD_DIM
 PAIR = 2
+CHUNKS = 1
 TILE = 256
 NEG = -1e30
 
@@ -67,12 +68,6 @@
 
 def in_order(side, own, other):
     return jnp.where(side == 0, jnp.stack([own, other]), jnp.stack([other, own]))
-
-
-def gather_small(value, me):
-    pair = in_order(me & 1, value, swap(value, 1))
-    both = in_order(me >> 1, pair, swap(pair, 2))
-    return both.reshape((N_SHARD,) + value.shape)
 
 
 def scatter_far(block_two, block_three):
@@ -150,6 +145,7 @@
             self.sent = self.steps.send(token)
         except StopIteration as end:
             self.result = end.value
+            return token
         return self.sent
 
     def finish(self, token):
@@ -446,72 +442,62 @@
     return border, late
 
 
-def expert_kernel(tiles, counts, rows_a, rows_b, w_in, in_bias, w_back, hidden, out_a, out_b, held):
+def take_rows(step, tiles, rows_a, rows_b, taken):
+    @pl.when(step < tiles)
+    def _():
+        taken[...] = rows_a[...]
+
+    @pl.when(step >= tiles)
+    def _():
+        taken[...] = rows_b[...]
+
+
+def give_rows(step, tiles, given, out_a, out_b):
+    @pl.when(step < tiles)
+    def _():
+        out_a[...] = given[...]
+
+    @pl.when(step >= tiles)
+    def _():
+        out_b[...] = given[...]
+
+
+def by_expert_rows(border, late, work, out):
+    @pl.when(border > 0)
+    def _():
+        out[...] = work(0)
+
+    @pl.when(border < TILE)
+    def _():
+        out[...] = jnp.where(late, work(1), out[...])
+
+
+def expert_kernel(tiles, counts, rows_a, rows_b, w_in, in_bias, w_back, hidden, out_a, out_b, taken, given):
     step = pl.program_id(0)
     border, late = expert_tile(counts, step, tiles)
-
-    def work(rows, out):
-        @pl.when(border > 0)
-        def _():
-            held[...] = jnp.maximum(dot_nn(rows[...], w_in[0]) + in_bias[0:1, :], 0.0).astype(bf16)
-
-        @pl.when(border < TILE)
-        def _():
-            one = jnp.maximum(dot_nn(rows[...], w_in[1]) + in_bias[1:2, :], 0.0).astype(bf16)
-            held[...] = jnp.where(late, one, held[...])
-
-        hidden[...] = held[...]
-
-        @pl.when(border > 0)
-        def _():
-            out[...] = dot_nn(held[...], w_back[0]).astype(bf16)
-
-        @pl.when(border < TILE)
-        def _():
-            out[...] = jnp.where(late, dot_nn(held[...], w_back[1]).astype(bf16), out[...])
-
-    @pl.when(step < tiles)
-    def _():
-        work(rows_a, out_a)
-
-    @pl.when(step >= tiles)
-    def _():
-        work(rows_b, out_b)
-
-
-def expert_back_kernel(tiles, counts, rows_a, rows_b, hidden, w_in, w_back, grad_pre, out_a, out_b, held):
+    take_rows(step, tiles, rows_a, rows_b, taken)
+    by_expert_rows(
+        border,
+        late,
+        lambda e: jnp.maximum(dot_nn(taken[...], w_in[e]) + in_bias[e : e + 1, :], 0.0).astype(bf16),
+        hidden,
+    )
+    by_expert_rows(border, late, lambda e: dot_nn(hidden[...], w_back[e]).astype(bf16), given)
+    give_rows(step, tiles, given, out_a, out_b)
+
+
+def expert_back_kernel(tiles, counts, rows_a, rows_b, hidden, w_in, w_back, grad_pre, out_a, out_b, taken, given):
     step = pl.program_id(0)
     border, late = expert_tile(counts, step, tiles)
-
-    def work(rows, out):
-        alive = hidden[...] > 0
-
-        @pl.when(border > 0)
-        def _():
-            held[...] = jnp.where(alive, dot_nt(rows[...], w_back[0]), 0.0).astype(bf16)
-
-        @pl.when(border < TILE)
-        def _():
-            one = jnp.where(alive, dot_nt(rows[...], w_back[1]), 0.0).astype(bf16)
-            held[...] = jnp.where(late, one, held[...])
-
-        grad_pre[...] = held[...]
-
-        @pl.when(border > 0)
-        def _():
-            out[...] = dot_nt(held[...], w_in[0]).astype(bf16)
-
-        @pl.when(border < TILE)
-        def _():
-            out[...] = jnp.where(late, dot_nt(held[...], w_in[1]).astype(bf16), out[...])
-
-    @pl.when(step < tiles)
-    def _():
-        work(rows_a, out_a)
-
-    @pl.when(step >= tiles)
-    def _():
-        work(rows_b, out_b)
+    take_rows(step, tiles, rows_a, rows_b, taken)
+    by_expert_rows(
+        border,
+        late,
+        lambda e: jnp.where(hidden[...] > 0, dot_nt(taken[...], w_back[e]), 0.0).astype(bf16),
+        grad_pre,
+    )
+    by_expert_rows(border, late, lambda e: dot_nt(grad_pre[...], w_in[e]).astype(bf16), given)
+    give_rows(step, tiles, given, out_a, out_b)
 
 
 def expert_specs(rows, width, inner):
@@ -537,7 +523,7 @@
             grid=(2 * tiles,),
             in_specs=[first, second, in_spec, bias_spec, back_spec],
             out_specs=[both, first, second],
-            scratch_shapes=[pltpu.VMEM((TILE, inner), bf16)],
+            scratch_shapes=[pltpu.VMEM((TILE, width), bf16)] * 2,
         ),
         out_shape=(
             jax.ShapeDtypeStruct((2 * rows, inner), bf16),
@@ -561,7 +547,7 @@
             grid=(2 * tiles,),
             in_specs=[first, second, both, in_spec, back_spec],
             out_specs=[both, first, second],
-            scratch_shapes=[pltpu.VMEM((TILE, inner), bf16)],
+            scratch_shapes=[pltpu.VMEM((TILE, width), bf16)] * 2,
         ),
         out_shape=(
             jax.ShapeDtypeStruct((2 * rows, inner), bf16),
@@ -684,6 +670,18 @@
     seg_rows = shard_width // n_rep
     facts = jnp.concatenate([me[None], piece_starts[0]])
 
+    expert_of = jnp.take(hash_table, token_ids)
+    places = jnp.arange(local_rows, dtype=jnp.int32)
+    earlier = (expert_of[:, None] == expert_of[None, :]) & (places[None, :] < places[:, None])
+    slot_of = jnp.sum(earlier.astype(jnp.int32), axis=1)
+    kept = slot_of < CAP
+    is_late = expert_of > 0
+    early_count = jnp.minimum(local_rows - jnp.sum(is_late.astype(jnp.int32)), CAP)
+    sorted_at = jnp.where(kept, slot_of + jnp.where(is_late, early_count, 0), -1)
+    sorter = (sorted_at[None, :] == places[:, None]).astype(bf16)
+    counted = valid_mask.astype(f32)
+    own_facts = jnp.stack([early_count.astype(f32), jnp.sum(valid_mask).astype(f32)])
+
     packed = jnp.concatenate(
         [
             jnp.stack([ln1_gain, ln1_bias, out_bias, ln2_gain, ln2_bias]),
@@ -711,48 +709,27 @@
     ]
     over = swap(jnp.stack(qkv_sends[2:]), 3)
     tok_far = swap(tokens, 2)
+    thin = lax.dynamic_slice_in_dim(w_in, rep_at * seg_rows, seg_rows, axis=1)
+    thin_sends = [lax.dynamic_slice_in_dim(thin, (me ^ j) * inner, inner, axis=2) for j in range(N_SHARD)]
+    over = tie(over, thin_sends)
     near = swap(qkv_sends[1], 1)
     tok_near = swap(tokens, 1)
+    tok_both = swap(tok_far, 1)
     qkv_blocks = (qkv_sends[0], near, swap(over[0], 1), over[1])
-
-    expert_of = jnp.take(hash_table, token_ids)
-    places = jnp.arange(local_rows, dtype=jnp.int32)
-    earlier = (expert_of[:, None] == expert_of[None, :]) & (places[None, :] < places[:, None])
-    slot_of = jnp.sum(earlier.astype(jnp.int32), axis=1)
-    kept = slot_of < CAP
-    is_late = expert_of > 0
-    early_count = jnp.minimum(local_rows - jnp.sum(is_late.astype(jnp.int32)), CAP)
-    sorted_at = jnp.where(kept, slot_of + jnp.where(is_late, early_count, 0), -1)
-    sorter = (sorted_at[None, :] == places[:, None]).astype(bf16)
-    counted = valid_mask.astype(f32)
-    own_facts = jnp.stack([early_count.astype(f32), jnp.sum(counted)])
-    own_facts = jnp.broadcast_to(own_facts[:, None], (2, 128))
-    shared = gather_small(own_facts, me)
-    count_all = jnp.sum(shared[:, 1], axis=0, keepdims=True)
-    for bit in range(n_rep.bit_length() - 1):
-        count_all = count_all + rep_swap(count_all, 1 << bit, n_rep)
-    count_all = count_all[0, 0]
-    indices = jnp.arange(N_SHARD, dtype=jnp.int32)
-    borders = jnp.sum(
-        jnp.where((indices ^ me)[:, None] == indices[None, :], shared[:, 0, 0][None, :], 0.0), axis=1
-    ).astype(jnp.int32)
-    counts_near, counts_far = borders[:2, None], borders[2:, None]
-
-    first_near, qkv_near, qkv_weight, rows_of = project(facts, tokens, tok_near, qkv_blocks)
+    thin_blocks = exchange_blocks(tie(thin_sends, (tok_both, qkv_blocks[2])))
+
+    first_near, qkv_near, qkv_weight, rows_of = project(
+        tie(facts, (tok_both, own_facts, sorter)), tokens, tok_near, qkv_blocks
+    )
     gain_one, bias_one, out_shift, gain_two, bias_two = [rows_of[i] for i in range(5)]
     back_shift = rows_of[5:7]
-    tok_both = swap(tok_far, 1)
     first_far, qkv_far = project(facts, tie(tok_far, qkv_near), tok_both, qkv_blocks)[:2]
 
     def first_rows(block):
         normed, inverse = layer_norm(block.astype(f32))
         return (normed * gain_one + bias_one).astype(bf16), normed, inverse
 
-    thin = lax.dynamic_slice_in_dim(w_in, rep_at * seg_rows, seg_rows, axis=1)
-    thin = tie(thin, (tok_far, over))
-    thin_blocks = exchange_blocks(
-        [lax.dynamic_slice_in_dim(thin, (me ^ j) * inner, inner, axis=2) for j in range(N_SHARD)]
-    )
+    thin_blocks = tie(thin_blocks, qkv_near)
     thin = in_order(
         me >> 1,
         in_order(me & 1, thin_blocks[0], thin_blocks[1]),
@@ -762,14 +739,25 @@
     in_weight = thin.transpose(1, 2, 0, 3, 4).reshape(EXPERTS, D, inner)
     w_out = tie(w_out, tok_far)
     out_far = swap(w_out, 2)
+
+    own_facts = jnp.broadcast_to(tie(own_facts, qkv_far)[:, None], (2, 128))
+    shared = jnp.stack(exchange_blocks([own_facts] * N_SHARD))
+    borders = shared[:, 0, 0].astype(jnp.int32)
+    counts_near = borders[:2, None]
+    chunk = local_rows // CHUNKS
+    counts_far = [borders[2:, None] - h * chunk for h in range(CHUNKS)]
+
+    mixed, logs = attend(facts, qkv_near, qkv_far)
+    count_all = jnp.sum(shared[:, 1], axis=0, keepdims=True)
+    for bit in range(n_rep.bit_length() - 1):
+        count_all = count_all + rep_swap(count_all, 1 << bit, n_rep)
+    count_all = count_all[0, 0]
+    out_far = tie(out_far, mixed)
     out_blocks = (w_out, swap(w_out, 1), out_far, swap(out_far, 1))
-
-    facts = tie(facts, (count_all, borders))
-    mixed, logs = attend(facts, qkv_near, qkv_far)
     mixed_blocks = exchange_blocks(
         [mixed[j * local_rows : (j + 1) * local_rows] for j in range(N_SHARD)]
     )
-    mixed_blocks = mixed_blocks[:2] + lax.optimization_barrier(mixed_blocks[2:] + (in_weight,))[:2]
+    mixed_blocks = mixed_blocks[:2] + lax.optimization_barrier(mixed_blocks[2:] + (borders,))[:2]
     tok_rows = tokens.astype(f32)
     branch = dot_nn(mixed_blocks[0], out_blocks[0])
     for j in range(1, N_SHARD):
@@ -778,14 +766,23 @@
     normed_two, inverse_two = layer_norm(middle)
     second_in = (normed_two * gain_two + bias_two).astype(bf16)
     sorted_in = dot_nn(sorter, second_in).astype(bf16)
-    in_far = swap(sorted_in, 2)
+    half_of = lambda value, h: value[h * chunk : (h + 1) * chunk]
+    in_far = [swap(half_of(sorted_in, h), 2) for h in range(CHUNKS)]
     in_near = swap(sorted_in, 1)
     bias_in = in_bias.astype(f32)
     hidden_near, out0, out1 = run_experts(counts_near, sorted_in, in_near, in_weight, bias_in, w_back)
-    in_far = tie(in_far, out0)
-    in_both = swap(in_far, 1)
-    hidden_far, out2, out3 = run_experts(counts_far, in_far, in_both, in_weight, bias_in, w_back)
-    summed = scatter_near(out0, out1, swap(scatter_far(out2, out3), 2))
+    token = out0
+    in_both, hidden_far, far_sums = [], [], []
+    for h in range(CHUNKS):
+        in_far[h] = tie(in_far[h], token)
+        in_both.append(swap(in_far[h], 1))
+        hidden, out2, out3 = run_experts(
+            counts_far[h], in_far[h], in_both[h], in_weight, bias_in, w_back
+        )
+        hidden_far.append(hidden)
+        token = scatter_far(out2, out3)
+        far_sums.append(swap(token, 2))
+    summed = scatter_near(out0, out1, jnp.concatenate(far_sums, axis=0))
     picked = dot_tn(sorter, summed.astype(bf16))
     picked = picked + jnp.where(is_late[:, None], back_shift[1], back_shift[0])
     final = middle + jnp.where(kept[:, None], picked, 0.0)
@@ -795,31 +792,47 @@
     grad_low = grad_final.astype(bf16)
 
     sorted_grad = dot_nn(sorter, grad_low).astype(bf16)
-    grad_far = swap(sorted_grad, 2)
+    grad_far = [swap(half_of(sorted_grad, h), 2) for h in range(CHUNKS)]
     grad_near = swap(sorted_grad, 1)
     pre_near, gin0, gin1 = run_experts_back(
         counts_near, sorted_grad, grad_near, hidden_near, in_weight, w_back
     )
-    grad_far = tie(grad_far, gin0)
-    grad_both = swap(grad_far, 1)
-    pre_far, gin2, gin3 = run_experts_back(
-        counts_far, grad_far, grad_both, hidden_far, in_weight, w_back
-    )
-    send_second = scatter_far(gin2, gin3)
-    far_second = swap(send_second, 2)
-
-    early = (jnp.arange(local_rows, dtype=jnp.int32)[None, :] < tie(borders, send_second)[:, None]).reshape(-1)
+    token = gin0
+    grad_both, pre_far, far_second = [], [], []
+    for h in range(CHUNKS):
+        grad_far[h] = tie(grad_far[h], token)
+        grad_both.append(swap(grad_far[h], 1))
+        pre, gin2, gin3 = run_experts_back(
+            counts_far[h], grad_far[h], grad_both[h], hidden_far[h], in_weight, w_back
+        )
+        pre_far.append(pre)
+        token = scatter_far(gin2, gin3)
+        far_second.append(swap(token, 2))
+    send_second = token
+
+    bounds = tie(borders, send_second)
+    tile_rows = jnp.arange(TILE, dtype=jnp.int32)
+    starts = range(0, chunk, TILE)
+    tiles = [bounds[j] - h for j in range(2) for h in range(0, local_rows, TILE)]
+    tiles += [
+        bounds[j] - h * chunk - start for h in range(CHUNKS) for j in range(2, N_SHARD) for start in starts
+    ]
+    early = jnp.concatenate([tile_rows < bound for bound in tiles])
     masks = [early[:, None], ~early[:, None]]
-    hidden_all = jnp.concatenate([hidden_near, hidden_far], axis=0)
-    grad_all = jnp.concatenate([sorted_grad, grad_near, grad_far, grad_both], axis=0)
-    back_grads = [dot_tn(jnp.where(m, hidden_all, 0), grad_all).astype(bf16) for m in masks]
+    in_tile_order = lambda own, near, far, both: jnp.concatenate(
+        [own, near] + [half for pair in zip(far, both) for half in pair], axis=0
+    )
+    hidden_all = jnp.concatenate([hidden_near] + hidden_far, axis=0)
+    grad_all = in_tile_order(sorted_grad, grad_near, grad_far, grad_both)
+    back_grads = [dot_tn(jnp.where(masks[0], hidden_all, 0), grad_all).astype(bf16)]
+    back_grads.append(dot_tn(jnp.where(masks[1], hidden_all, 0), grad_all).astype(bf16))
     back_rows = EXPERTS * inner
     part = lambda a, i: lax.dynamic_index_in_dim(a, i, 1, keepdims=False)
     quarter_of = lambda a: lambda i: part(a, i)
     back_parts = [g.reshape(1, QUARTERS, inner // QUARTERS, D) for g in back_grads]
     back_sum = Steps(rep_sum_steps([quarter_of(g) for g in back_parts], n_rep, middle_none))
-    pre_all = tie(jnp.concatenate([pre_near, pre_far], axis=0), back_sum.sent)
-    in_all = jnp.concatenate([sorted_in, in_near, in_far, in_both], axis=0)
+    pre_all = tie(jnp.concatenate([pre_near] + pre_far, axis=0), back_sum.sent)
+    in_all = in_tile_order(sorted_in, in_near, in_far, in_both)
     in_grads = [dot_tn(in_all, jnp.where(m, pre_all, 0)).astype(bf16) for m in masks]
     quarter_rows = shard_width // QUARTERS
     in_parts = [g.reshape(N_SHARD, QUARTERS, quarter_rows, inner) for g in in_grads]
@@ -840,7 +853,7 @@
     experts_sum = Steps(rep_sum_steps([quarter_of(g) for g in in_parts], n_rep, middle_in))
 
     far_second = tie(far_second, back_sum.step(experts_sum.sent))
-    summed_grad = scatter_near(gin0, gin1, far_second)
+    summed_grad = scatter_near(gin0, gin1, jnp.concatenate(far_second, axis=0))
     grad_second = dot_tn(sorter, summed_grad.astype(bf16))
     grad_gain_two = jnp.sum(grad_second * normed_two, axis=0)
     grad_bias_two = jnp.sum(grad_second, axis=0)
@@ -860,7 +873,8 @@
         if pair == 0:
             out_send = tie(scatter_far(out_parts[2], out_parts[3]), half_grads[0])
             out_far_sum = swap(out_send, 2)
-            sent = (out_send, back_sum.step(experts_sum.step(half_grads[-1])))
+            sent = experts_sum.step(half_grads[-1])
+            sent = (out_send, sent, back_sum.step(sent))
         else:
             sent = experts_sum.step(back_sum.step(half_grads[-1]))
         near_tied = tie(qkv_near, sent)
@@ -929,6 +943,10 @@
     sent = last_sum.sent
     first0, first1 = first_grad(0, sent), first_grad(1, sent)
     sent = experts_sum.step((first0, first1))
+    sent = last_sum.step(sent)
+    back_grad = place_experts(me, back_sum.finish(sent))
+    sent = last_sum.step(back_grad)
+    sent = experts_sum.step(sent)
     grad_first = scatter_near(first0, first1, tie(far_first, sent))
     first_in, normed_one, inverse_one = first_rows(tie(tokens, sent))
     grad_gain_one = jnp.sum(grad_first * normed_one, axis=0)
@@ -952,20 +970,16 @@
     small = small + swap(small, 2)
     small = lax.dynamic_slice_in_dim(small, me * shard_width, shard_width, axis=1)
     small = jnp.concatenate([small, in_shift_grad.reshape(-1, shard_width)], axis=0)
-    sent = last_sum.step(experts_sum.step((input_grad, small)))
-    sent = last_sum.step(sent)
-    back_grad = place_experts(me, back_sum.finish(sent))
-    sent = last_sum.step(back_grad)
-    small = small + tie(rep_swap(small, 1, n_rep), sent)
-    in_grad = place_experts(me, experts_sum.finish(small))
-    sent = last_sum.step(in_grad)
-    bit = 2
+    sent = last_sum.step((input_grad, small))
+    bit = 1
     while bit < n_rep:
         small = small + tie(rep_swap(small, bit, n_rep), sent)
-        sent = last_sum.step(small)
+        sent = small
         bit *= 2
+    sent = last_sum.step(sent)
+    in_grad = place_experts(me, experts_sum.finish(sent))
     in_shift_grad = small[8:].reshape(EXPERTS, inner)
-    qkv_grad, out_grad = place_attention(me, last_sum.finish(small), shard_width)
+    qkv_grad, out_grad = place_attention(me, last_sum.finish(in_grad), shard_width)
     return (
         final.astype(bf16),
         input_grad,

time: 638 us -> 616 us (0.966)
  waiting for transfers between devices: 191 us -> 177 us
  matrix products: 69.7 us -> 58.6 us
    ppermute x33, waiting for transfers between devices: 83.8 us -> 72.1 us  [rep_swap(): return lax.ppermute(value, 'rep', [(i, i ^ mask) for i in range(count)])]
    ppermute x46 -> x47, waiting for transfers between devices: 107 us -> 105 us  [swap(): return lax.ppermute(value, 'shard', [(i, i ^ mask) for i in range(N_SHARD)])]
    unnamed x265 -> x258, local copies, waits for them, and re-layouts: 27.9 us -> 28.7 us
    ppermute x46 -> x47, starting transfers between devices: 27 us -> 26.4 us  [swap(): return lax.ppermute(value, 'shard', [(i, i ^ mask) for i in range(N_SHARD)])]
  transfers between devices with their start and end apart: 80 -> 81, of which waited for: 36 -> 35; matrix products, arithmetic and copies ran while one was open for 21% -> 20% of each run, Pallas kernels for 24% -> 25%
where the time goes in v3:
time: 616 us; the launch traced here: 607 us
  Pallas kernels  182 us (30%)
  waiting for transfers between devices  177 us (29%)
  starting transfers between devices  69.6 us (11%)
  matrix products  58.6 us (10%)
  local copies, waits for them, and re-layouts  56.7 us (9%)
  other arithmetic  41.5 us (7%)
  between operations  21.2 us (3%)
    ppermute x47, waiting for transfers between devices, swap(): return lax.ppermute(value, 'shard', [(i, i ^ mask) for i in range(N_SHARD)])  105 us
    ppermute x33, waiting for transfers between devices, rep_swap(): return lax.ppermute(value, 'rep', [(i, i ^ mask) for i in range(count)])  72.1 us
    pallas_call x2, Pallas kernels, attend_back(): pl.pallas_call(functools.partial(attend_back_kernel, blocks, pair), out_s...  63.9 us
    dot_general x12, matrix products, dot_tn(): lax.dot_general(a, b, (((0,), (0,)), ((), ())), preferred_element_type=f32)  44.3 us
    ppermute x33, starting transfers between devices, rep_swap(): return lax.ppermute(value, 'rep', [(i, i ^ mask) for i in range(count)])  43.1 us
    pallas_call x1, Pallas kernels, attend(): pl.pallas_call(functools.partial(attend_kernel, blocks), out_shape=(jax.S...  42.4 us
    unnamed x258, local copies, waits for them, and re-layouts  28.7 us
    ppermute x47, starting transfers between devices, swap(): return lax.ppermute(value, 'shard', [(i, i ^ mask) for i in range(N_SHARD)])  26.4 us
  transfers between devices with their start and end apart: 81, of which 35 were waited for; matrix products, arithmetic and copies ran while one was open for 20% of the time, Pallas kernels for 25%

profile of v3, /device:TPU:0, one launch (start us, length us, event | category | flops | bytes accessed | tf_op | source)
XLA Modules:
  0.0 607.0 jit_solution(4015348658741200278)
XLA Ops:
  7.2 3.0 collective-permute-start
  18.2 3.1 gather_fusion
  21.4 13.2 %collective-permute-done.tok_a = bf16[512,1024]{1,0:T(8,128)(2,1)} collective-permute-done((bf16[512,1024]{1,0:T(8,128)(2,1)}, bf16[512,1024]{1,0:T(8,128)(2,1)}, u32[]{:S(2)}, u32[]{:S(2)}) %collective-permute-start) | collective-permute-done | bytes 1048608 | tf_op jit(solution)/shard_map/ppermute | solution.py:62
  36.9 13.5 %collective-permute-done.4 = bf16[2,264,768]{2,1,0:T(8,128)(2,1)} collective-permute-done((bf16[2,264,768]{2,1,0:T(8,128)(2,1)}, bf16[2,264,768]{2,1,0:T(8,128)(2,1)}, u32[]{:S(2)}, u32[]{:S(2)}) %collective-permute-start.4) | collective-permute-done | bytes 811040 | tf_op jit(solution)/shard_map/ppermute | solution.py:62
  62.2 3.8 project.2
  76.0 4.2 project.3
  83.6 42.4 %attend.1 = (bf16[2048,256]{1,0:T(8,128)(2,1)S(1)}, f32[8,8,256]{2,1,0:T(8,128)S(1)}) custom-call(s32[3]{0:T(128)S(1)} %pad_add_fusion.facts, bf16[1024,768]{1,0:T(8,128)(2,1)S(1)} %get-tuple-element.176.near, bf16[1024,768]{1,0:T(8,128)(2,1)S(1)} %get-tuple-element.121.far), custom_call_target="tpu_custom_call" | custom-call | flops 1048576 | bytes 65536 | tf_op jit(solution)/shard_map/attend/pallas_call | solution.py:284
  129.9 5.1 collective-permute-done.9
  135.0 6.2 %collective-permute-done.8 = bf16[512,256]{1,0:T(8,128)(2,1)S(1)} collective-permute-done((bf16[512,256]{1,0:T(8,128)(2,1)S(1)}, bf16[512,256]{1,0:T(8,128)(2,1)S(1)}, u32[]{:S(2)}, u32[]{:S(2)}) %collective-permute-start.8) | collective-permute-done | bytes 262176 | tf_op jit(solution)/shard_map/ppermute | solution.py:62
  146.2 3.0 copy.84
  149.2 13.2 %experts.2 = (bf16[1024,1024]{1,0:T(8,128)(2,1)S(1)}, bf16[512,1024]{1,0:T(8,128)(2,1)S(1)}, bf16[512,1024]{1,0:T(8,128)(2,1)S(1)}) custom-call(s32[2,1]{1,0:T(2,128)S(1)} %bitcast.348, bf16[512,1024]{1,0:T(8,128)(2,1)} %convolution_convert_fusion.1.rows_a, bf16[512,1024]{1,0:T(8,128)(2,1)} %collective-permute-done.15.rows_b, ...), custom_call_target="tpu_custom_call" | custom-call | flops 1048576 | bytes 65536 | tf_op jit(solution)/shard_map/experts/pallas_call | solution.py:519
  162.4 8.9 %collective-permute-done.20.rows_a = bf16[512,1024]{1,0:T(8,128)(2,1)} collective-permute-done((bf16[512,1024]{1,0:T(8,128)(2,1)}, bf16[512,1024]{1,0:T(8,128)(2,1)}, u32[]{:S(2)}, u32[]{:S(2)}) %collective-permute-start.20) | collective-permute-done | bytes 1048608 | tf_op jit(solution)/shard_map/ppermute | solution.py:62
  171.3 2.9 collective-permute-done.21.rows_b
  174.1 12.2 %experts.3 = (bf16[1024,1024]{1,0:T(8,128)(2,1)S(1)}, bf16[512,1024]{1,0:T(8,128)(2,1)S(1)}, bf16[512,1024]{1,0:T(8,128)(2,1)S(1)}) custom-call(s32[2,1]{1,0:T(2,128)S(1)} %bitcast.346, bf16[512,1024]{1,0:T(8,128)(2,1)} %collective-permute-done.20.rows_a, bf16[512,1024]{1,0:T(8,128)(2,1)S(1)} %collective-permute-done.21.rows_b, ...), custom_call_target="tpu_custom_call" | custom-call | flops 1048576 | bytes 65536 | tf_op jit(solution)/shard_map/experts/pallas_call | solution.py:519
  190.1 4.0 collective-permute-start.24
  199.2 3.0 collective-permute-start.26
  203.9 11.0 %collective-permute-done.23 = bf16[512,1024]{1,0:T(8,128)(2,1)S(1)} collective-permute-done((bf16[512,1024]{1,0:T(8,128)(2,1)S(1)}, bf16[512,1024]{1,0:T(8,128)(2,1)S(1)}, u32[]{:S(2)}, u32[]{:S(2)}) %collective-permute-start.23) | collective-permute-done | bytes 1048608 | tf_op jit(solution)/shard_map/ppermute | solution.py:62
  220.7 13.4 %experts_back.2 = (bf16[1024,1024]{1,0:T(8,128)(2,1)S(1)}, bf16[512,1024]{1,0:T(8,128)(2,1)S(1)}, bf16[512,1024]{1,0:T(8,128)(2,1)}) custom-call(s32[2,1]{1,0:T(2,128)S(1)} %bitcast.349, bf16[512,1024]{1,0:T(8,128)(2,1)S(1)} %convolution_convert_fusion.rows_a, bf16[512,1024]{1,0:T(8,128)(2,1)S(1)} %collective-permute-done.27.rows_b, ...), custom_call_target="tpu_custom_call" | custom-call | flops 1048576 | bytes 65536 | tf_op jit(solution)/shard_map/experts_back/pallas_call | solution.py:543
  236.4 7.3 %collective-permute-done.29.rows_a = bf16[512,1024]{1,0:T(8,128)(2,1)} collective-permute-done((bf16[512,1024]{1,0:T(8,128)(2,1)S(1)}, bf16[512,1024]{1,0:T(8,128)(2,1)}, u32[]{:S(2)}, u32[]{:S(2)}) %collective-permute-start.29) | collective-permute-done | bytes 1048608 | tf_op jit(solution)/shard_map/ppermute | solution.py:62
  246.3 4.4 pad_maximum_fusion.3
  250.7 12.9 %experts_back.3 = (bf16[1024,1024]{1,0:T(8,128)(2,1)S(1)}, bf16[512,1024]{1,0:T(8,128)(2,1)S(1)}, bf16[512,1024]{1,0:T(8,128)(2,1)S(1)}) custom-call(s32[2,1]{1,0:T(2,128)S(1)} %bitcast.347, bf16[512,1024]{1,0:T(8,128)(2,1)} %collective-permute-done.29.rows_a, bf16[512,1024]{1,0:T(8,128)(2,1)} %collective-permute-done.30.rows_b, ...), custom_call_target="tpu_custom_call" | custom-call | flops 1048576 | bytes 65536 | tf_op jit(solution)/shard_map/experts_back/pallas_call | solution.py:543
  267.3 2.8 copy-done.18
  270.1 2.5 pad_maximum_fusion.2
  282.4 8.2 %fusion.27 = bf16[1024,1024]{1,0:T(8,128)(2,1)S(1)} fusion(bf16[2048,1024]{1,0:T(8,128)(2,1)} %copy-done.74, pred[2048]{0:T(1024)(128)(4,1)S(1)} %dynamic-update-slice.65, bf16[512,1024]{1,0:T(8,128)(2,1)} %collective-permute-done.30.rows_b, bf16[512,1024]{1,0:T(8,128)(2,1)} %collective-permute-done.29.rows_a, bf16[512,1024]{1,0:T(8,128)(2,1)} %copy-done.28, ...), kind=kOutput, calls=%fused_computation.54 | convolution fusion | flops 4314890240 | bytes 10487808 | tf_op jit(solution)/shard_map/dot_general | solution.py:54
  290.8 4.0 collective-permute-start.33
  294.8 6.5 %fusion.30 = bf16[1024,1024]{1,0:T(8,128)(2,1)S(1)} fusion(bf16[2048,1024]{1,0:T(8,128)(2,1)S(1)} %copy-done.75, pred[2048]{0:T(1024)(128)(4,1)S(1)} %not.15, bf16[512,1024]{1,0:T(8,128)(2,1)} %collective-permute-done.30.rows_b, bf16[512,1024]{1,0:T(8,128)(2,1)} %collective-permute-done.29.rows_a, bf16[512,1024]{1,0:T(8,128)(2,1)S(1)} %copy-done.29, ...), kind=kOutput, calls=%fused_computation.55 | convolution fusion | flops 4314890240 | bytes 10487808 | tf_op jit(solution)/shard_map/dot_general | solution.py:54
  303.2 7.0 %fusion.33 = bf16[1024,1024]{1,0:T(8,128)(2,1)S(1)} fusion(bf16[2048,1024]{1,0:T(8,128)(2,1)S(1)} %copy-done.43, pred[2048]{0:T(1024)(128)(4,1)S(1)} %dynamic-update-slice.65, bf16[512,1024]{1,0:T(8,128)(2,1)S(1)} %copy-done.27, bf16[512,1024]{1,0:T(8,128)(2,1)} %collective-permute-done.20.rows_a, bf16[512,1024]{1,0:T(8,128)(2,1)} %collective-permute-done.15.rows_b, ...), kind=kOutput, calls=%fused_computation.56 | convolution fusion | flops 4314890240 | bytes 10487808 | tf_op jit(solution)/shard_map/dot_general | solution.py:54
  311.8 6.6 %fusion.36 = bf16[1024,1024]{1,0:T(8,128)(2,1)S(1)} fusion(bf16[2048,1024]{1,0:T(8,128)(2,1)S(1)} %copy-done.43, pred[2048]{0:T(1024)(128)(4,1)S(1)} %not.15, bf16[512,1024]{1,0:T(8,128)(2,1)S(1)} %copy-done.27, bf16[512,1024]{1,0:T(8,128)(2,1)} %collective-permute-done.20.rows_a, bf16[512,1024]{1,0:T(8,128)(2,1)} %collective-permute-done.15.rows_b, ...), kind=kOutput, calls=%fused_computation.57 | convolution fusion | flops 4314890240 | bytes 10487808 | tf_op jit(solution)/shard_map/dot_general | solution.py:54
  319.3 6.8 %collective-permute-done.34 = bf16[2,1,256,1024]{3,2,1,0:T(8,128)(2,1)S(1)} collective-permute-done((bf16[2,1,256,1024]{3,2,1,0:T(8,128)(2,1)S(1)}, bf16[2,1,256,1024]{3,2,1,0:T(8,128)(2,1)S(1)}, u32[]{:S(2)}, u32[]{:S(2)}) %collective-permute-start.34) | collective-permute-done | bytes 1048608 | tf_op jit(solution)/shard_map/ppermute | solution.py:84
  329.9 2.9 multiply_reduce_fusion
  347.6 4.6 collective-permute-done.42
  354.8 5.8 collective-permute-done.40.g3
  362.6 2.7 collective-permute-start.45
  373.6 31.9 %attend_back.2 = bf16[2048,384]{1,0:T(8,128)(2,1)S(1)} custom-call(s32[3]{0:T(128)S(1)} %pad_add_fusion.facts, bf16[1024,768]{1,0:T(8,128)(2,1)S(1)} %get-tuple-element.176.near, bf16[1024,768]{1,0:T(8,128)(2,1)} %copy-done.5, bf16[2048,256]{1,0:T(8,128)(2,1)S(1)} %copy-done.7, bf16[512,256]{1,0:T(8,128)(2,1)S(1)} %convolution_convert_fusion.11.g0, ...), custom_call_target="tpu_custom_call" | custom-call | flops 1048576 | bytes 65536 | tf_op jit(solution)/shard_map/attend_back/pallas_call | solution.py:411
  416.1 32.0 %attend_back.3 = bf16[2048,384]{1,0:T(8,128)(2,1)S(1)} custom-call(s32[3]{0:T(128)S(1)} %pad_add_fusion.facts, bf16[1024,768]{1,0:T(8,128)(2,1)S(1)} %get-tuple-element.176.near, bf16[1024,768]{1,0:T(8,128)(2,1)} %copy-done.5, bf16[2048,256]{1,0:T(8,128)(2,1)S(1)} %copy-done.7, bf16[512,256]{1,0:T(8,128)(2,1)S(1)} %convolution_convert_fusion.11.g0, ...), custom_call_target="tpu_custom_call" | custom-call | flops 1048576 | bytes 65536 | tf_op jit(solution)/shard_map/attend_back/pallas_call | solution.py:411
  450.1 10.1 %collective-permute-done.44 = bf16[2,4,64,1024]{3,2,1,0:T(8,128)(2,1)S(1)} collective-permute-done((bf16[2,4,64,1024]{3,2,1,0:T(8,128)(2,1)S(1)}, bf16[2,4,64,1024]{3,2,1,0:T(8,128)(2,1)S(1)}, u32[]{:S(2)}, u32[]{:S(2)}) %collective-permute-start.44) | collective-permute-done | bytes 1048608 | tf_op jit(solution)/shard_map/ppermute | solution.py:84
  478.1 3.2 collective-permute-done.53
  484.3 18.0 %collective-permute-done.56 = bf16[2,512,256]{2,1,0:T(8,128)(2,1)S(1)} collective-permute-done((bf16[2,512,256]{2,1,0:T(8,128)(2,1)S(1)}, bf16[2,512,256]{2,1,0:T(8,128)(2,1)S(1)}, u32[]{:S(2)}, u32[]{:S(2)}) %collective-permute-start.56) | collective-permute-done | bytes 524320 | tf_op jit(solution)/shard_map/ppermute | solution.py:84
  506.8 5.1 place_experts.2
  512.0 6.8 %collective-permute-done.61 = bf16[512,256]{1,0:T(8,128)(2,1)S(1)} collective-permute-done((bf16[512,256]{1,0:T(8,128)(2,1)S(1)}, bf16[512,256]{1,0:T(8,128)(2,1)S(1)}, u32[]{:S(2)}, u32[]{:S(2)}) %collective-permute-start.61) | collective-permute-done | bytes 262176 | tf_op jit(solution)/shard_map/ppermute | solution.py:84
  526.2 17.3 %collective-permute-done.64 = bf16[512,1024]{1,0:T(8,128)(2,1)S(1)} collective-permute-done((bf16[512,1024]{1,0:T(8,128)(2,1)S(1)}, bf16[512,1024]{1,0:T(8,128)(2,1)S(1)}, u32[]{:S(2)}, u32[]{:S(2)}) %collective-permute-start.64) | collective-permute-done | bytes 1048608 | tf_op jit(solution)/shard_map/ppermute | solution.py:62
  546.8 4.9 fusion.20
  555.5 3.7 collective-permute-done.69
  561.1 2.8 collective-permute-done.70
  564.7 4.3 collective-permute-done.73
  571.0 7.9 %place_experts.3 = f32[2,256,4096]{2,1,0:T(8,128)} custom-call(s32[9]{0:T(128)S(1)} %concatenate.278.facts, bf16[4,64,1024]{2,1,0:T(8,128)(2,1)S(1)} %get-tuple-element.272.refs_0_, bf16[4,64,1024]{2,1,0:T(8,128)(2,1)S(1)} %collective-permute-done.55.refs_1_, bf16[2,4,64,1024]{3,2,1,0:T(8,128)(2,1)} %collective-permute-done.75.refs_2_, ...), custom_call_target="tpu_custom_call" | custom-call | flops 1048576 | bytes 65536 | tf_op jit(solution)/shard_map/place_experts/pallas_call | solution.py:591
  584.0 9.4 %collective-permute-done.79.refs_5_ = bf16[2,512,256]{2,1,0:T(8,128)(2,1)S(1)} collective-permute-done((bf16[2,512,256]{2,1,0:T(8,128)(2,1)S(1)}, bf16[2,512,256]{2,1,0:T(8,128)(2,1)S(1)}, u32[]{:S(2)}, u32[]{:S(2)}) %collective-permute-start.79) | collective-permute-done | bytes 524320 | tf_op jit(solution)/shard_map/ppermute | solution.py:84
  596.8 2.9 place_attention.1
  (644 shorter events, 174.7 us)
Async XLA Ops:
  7.2 139.0 %all-gather.3.cloned.1.call-start = ((), (), s32[]{:S(2)}) async-start(), calls=%async_computation | async-start | bytes 4718592 | tf_op jit(solution)/shard_map/all_gather | solution.py:738
  7.2 27.3 %collective-permute-start = (bf16[512,1024]{1,0:T(8,128)(2,1)}, bf16[512,1024]{1,0:T(8,128)(2,1)}, u32[]{:S(2)}, u32[]{:S(2)}) collective-permute-start(bf16[512,1024]{1,0:T(8,128)(2,1)} %tok_a.1), channel_id=1, source_target_pairs={{0,2},{1,3},{2,0},{3,1},{4,6},{5,7},{6,4},{7,5},{8,10},{9,11},{10,... | collective-permute-start | bytes 3145736 | tf_op jit(solution)/shard_map/ppermute | solution.py:62
  17.7 32.7 %collective-permute-start.4 = (bf16[2,264,768]{2,1,0:T(8,128)(2,1)}, bf16[2,264,768]{2,1,0:T(8,128)(2,1)}, u32[]{:S(2)}, u32[]{:S(2)}) collective-permute-start(bf16[2,264,768]{2,1,0:T(8,128)(2,1)} %pad_maximum_fusion.15), channel_id=1, source_target_pairs={{0,3},{1,2},{2,1},{3,0},{4,7},{5,6},{6,5},{7,4},{8,11},{9,10},{10,... | collective-permute-start | bytes 2433032 | tf_op jit(solution)/shard_map/ppermute | solution.py:62
  17.7 42.5 %collective-permute-start.2 = (bf16[512,1024]{1,0:T(8,128)(2,1)S(1)}, bf16[512,1024]{1,0:T(8,128)(2,1)}, u32[]{:S(2)}, u32[]{:S(2)}) collective-permute-start(bf16[512,1024]{1,0:T(8,128)(2,1)S(1)} %copy-done.4), channel_id=1, source_target_pairs={{0,1},{1,0},{2,3},{3,2},{4,5},{5,4},{6,7},{7,6},{8,9},{9,8},{10,11... | collective-permute-start | bytes 3145736 | tf_op jit(solution)/shard_map/ppermute | solution.py:62
  17.9 41.6 %collective-permute-start.3 = (bf16[264,768]{1,0:T(8,128)(2,1)}, bf16[264,768]{1,0:T(8,128)(2,1)S(1)}, u32[]{:S(2)}, u32[]{:S(2)}) collective-permute-start(bf16[264,768]{1,0:T(8,128)(2,1)} %get-tuple-element.409), channel_id=1, source_target_pairs={{0,1},{1,0},{2,3},{3,2},{4,5},{5,4},{6,7},{7,6},{8,9},{9,8},{10,11... | collective-permute-start | bytes 1216520 | tf_op jit(solution)/shard_map/ppermute | solution.py:62
  34.6 19.7 %collective-permute-start.1 = (bf16[512,1024]{1,0:T(8,128)(2,1)}, bf16[512,1024]{1,0:T(8,128)(2,1)S(1)}, u32[]{:S(2)}, u32[]{:S(2)}) collective-permute-start(bf16[512,1024]{1,0:T(8,128)(2,1)} %collective-permute-done.tok_a), channel_id=1, source_target_pairs={{0,1},{1,0},{2,3},{3,2},{4,5},{5,4},{6,7},{7,6},{8,9},{9,8},{10,11... | collective-permute-start | bytes 3145736 | tf_op jit(solution)/shard_map/ppermute | solution.py:62
  70.9 56.1 %collective-permute-start.13 = (bf16[256,1024]{1,0:T(8,128)(2,1)}, bf16[256,1024]{1,0:T(8,128)(2,1)S(1)}, u32[]{:S(2)}, u32[]{:S(2)}) collective-permute-start(bf16[256,1024]{1,0:T(8,128)(2,1)} %param.28), channel_id=1, source_target_pairs={{0,2},{1,3},{2,0},{3,1},{4,6},{5,7},{6,4},{7,5},{8,10},{9,11},{10,... | collective-permute-start | bytes 1572872 | tf_op jit(solution)/shard_map/ppermute | solution.py:62
  72.4 69.2 %collective-permute-start.7 = (bf16[256,1024]{1,0:T(8,128)(2,1)}, bf16[256,1024]{1,0:T(8,128)(2,1)S(1)}, u32[]{:S(2)}, u32[]{:S(2)}) collective-permute-start(bf16[256,1024]{1,0:T(8,128)(2,1)} %param.28), channel_id=1, source_target_pairs={{0,1},{1,0},{2,3},{3,2},{4,5},{5,4},{6,7},{7,6},{8,9},{9,8},{10,11... | collective-permute-start | bytes 1572872 | tf_op jit(solution)/shard_map/ppermute | solution.py:62
  81.7 45.8 %collective-permute-start.12 = (f32[2,128]{1,0:T(2,128)S(1)}, f32[2,128]{1,0:T(2,128)S(1)}, u32[]{:S(2)}, u32[]{:S(2)}) collective-permute-start(f32[2,128]{1,0:T(2,128)S(1)} %broadcast_in_dim.123), channel_id=1, source_target_pairs={{0,3},{1,2},{2,1},{3,0},{4,7},{5,6},{6,5},{7,4},{8,11},{9,10},{10,... | collective-permute-start | bytes 3080 | tf_op jit(solution)/shard_map/ppermute | solution.py:62
  82.0 47.0 %collective-permute-start.11 = (f32[2,128]{1,0:T(2,128)S(1)}, f32[2,128]{1,0:T(2,128)S(1)}, u32[]{:S(2)}, u32[]{:S(2)}) collective-permute-start(f32[2,128]{1,0:T(2,128)S(1)} %broadcast_in_dim.123), channel_id=1, source_target_pairs={{0,2},{1,3},{2,0},{3,1},{4,6},{5,7},{6,4},{7,5},{8,10},{9,11},{10,... | collective-permute-start | bytes 3080 | tf_op jit(solution)/shard_map/ppermute | solution.py:62
  83.5 45.6 %collective-permute-start.10 = (f32[2,128]{1,0:T(2,128)S(1)}, f32[2,128]{1,0:T(2,128)S(1)}, u32[]{:S(2)}, u32[]{:S(2)}) collective-permute-start(f32[2,128]{1,0:T(2,128)S(1)} %broadcast_in_dim.123), channel_id=1, source_target_pairs={{0,1},{1,0},{2,3},{3,2},{4,5},{5,4},{6,7},{7,6},{8,9},{9,8},{10,11... | collective-permute-start | bytes 3080 | tf_op jit(solution)/shard_map/ppermute | solution.py:62
  145.4 25.9 %collective-permute-start.20 = (bf16[512,1024]{1,0:T(8,128)(2,1)}, bf16[512,1024]{1,0:T(8,128)(2,1)}, u32[]{:S(2)}, u32[]{:S(2)}) collective-permute-start(bf16[512,1024]{1,0:T(8,128)(2,1)} %convolution_convert_fusion.1.rows_a), channel_id=1, source_target_pairs={{0,2},{1,3},{2,0},{3,1},{4,6},{5,7},{6,4},{7,5},{8,10},{9,11},{10,... | collective-permute-start | bytes 3145736 | tf_op jit(solution)/shard_map/ppermute | solution.py:62
  186.6 17.2 %collective-permute-start.19 = (bf16[512,1024]{1,0:T(8,128)(2,1)S(1)}, bf16[512,1024]{1,0:T(8,128)(2,1)S(1)}, u32[]{:S(2)}, u32[]{:S(2)}) collective-permute-start(bf16[512,1024]{1,0:T(8,128)(2,1)S(1)} %get-tuple-element.138), channel_id=1, source_target_pairs={{0,1},{1,0},{2,3},{3,2},{4,5},{5,4},{6,7},{7,6},{8,9},{9,8},{10,11... | collective-permute-start | bytes 3145736 | tf_op jit(solution)/shard_map/ppermute | solution.py:62
  189.6 25.3 %collective-permute-start.23 = (bf16[512,1024]{1,0:T(8,128)(2,1)S(1)}, bf16[512,1024]{1,0:T(8,128)(2,1)S(1)}, u32[]{:S(2)}, u32[]{:S(2)}) collective-permute-start(bf16[512,1024]{1,0:T(8,128)(2,1)S(1)} %add_convert_fusion.8), channel_id=1, source_target_pairs={{0,2},{1,3},{2,0},{3,1},{4,6},{5,7},{6,4},{7,5},{8,10},{9,11},{10,... | collective-permute-start | bytes 3145736 | tf_op jit(solution)/shard_map/ppermute | solution.py:62
  218.0 25.7 %collective-permute-start.29 = (bf16[512,1024]{1,0:T(8,128)(2,1)S(1)}, bf16[512,1024]{1,0:T(8,128)(2,1)}, u32[]{:S(2)}, u32[]{:S(2)}) collective-permute-start(bf16[512,1024]{1,0:T(8,128)(2,1)S(1)} %convolution_convert_fusion.rows_a), channel_id=1, source_target_pairs={{0,2},{1,3},{2,0},{3,1},{4,6},{5,7},{6,4},{7,5},{8,10},{9,11},{10,... | collective-permute-start | bytes 3145736 | tf_op jit(solution)/shard_map/ppermute | solution.py:62
  267.3 61.1 %collective-permute-start.28 = (bf16[512,1024]{1,0:T(8,128)(2,1)}, bf16[512,1024]{1,0:T(8,128)(2,1)}, u32[]{:S(2)}, u32[]{:S(2)}) collective-permute-start(bf16[512,1024]{1,0:T(8,128)(2,1)} %get-tuple-element.144), channel_id=1, source_target_pairs={{0,1},{1,0},{2,3},{3,2},{4,5},{5,4},{6,7},{7,6},{8,9},{9,8},{10,11... | collective-permute-start | bytes 3145736 | tf_op jit(solution)/shard_map/ppermute | solution.py:62
  279.9 48.5 %collective-permute-start.32 = (bf16[512,1024]{1,0:T(8,128)(2,1)}, bf16[512,1024]{1,0:T(8,128)(2,1)}, u32[]{:S(2)}, u32[]{:S(2)}) collective-permute-start(bf16[512,1024]{1,0:T(8,128)(2,1)} %add_convert_fusion.6), channel_id=1, source_target_pairs={{0,2},{1,3},{2,0},{3,1},{4,6},{5,7},{6,4},{7,5},{8,10},{9,11},{10,... | collective-permute-start | bytes 3145736 | tf_op jit(solution)/shard_map/ppermute | solution.py:62
  290.8 37.1 %collective-permute-start.33 = (bf16[2,1,256,1024]{3,2,1,0:T(8,128)(2,1)S(1)}, bf16[2,1,256,1024]{3,2,1,0:T(8,128)(2,1)S(1)}, u32[]{:S(2)}, u32[]{:S(2)}) collective-permute-start(bf16[2,1,256,1024]{3,2,1,0:T(8,128)(2,1)S(1)} %pad_maximum_fusion.4), channel_id=1, source_target_pairs={{0,4},{4,0},{8,12},{12,8},{16,20},{20,16},{24,28},{28,24},{1,5},{5... | collective-permute-start | bytes 3145736 | tf_op jit(solution)/shard_map/ppermute | solution.py:84
  301.5 24.6 %collective-permute-start.34 = (bf16[2,1,256,1024]{3,2,1,0:T(8,128)(2,1)S(1)}, bf16[2,1,256,1024]{3,2,1,0:T(8,128)(2,1)S(1)}, u32[]{:S(2)}, u32[]{:S(2)}) collective-permute-start(bf16[2,1,256,1024]{3,2,1,0:T(8,128)(2,1)S(1)} %pad_maximum_fusion.5), channel_id=1, source_target_pairs={{0,8},{4,12},{8,0},{12,4},{16,24},{20,28},{24,16},{28,20},{1,9},{5... | collective-permute-start | bytes 3145736 | tf_op jit(solution)/shard_map/ppermute | solution.py:84
  310.5 34.5 %collective-permute-start.35 = (bf16[2,4,64,1024]{3,2,1,0:T(8,128)(2,1)S(1)}, bf16[2,4,64,1024]{3,2,1,0:T(8,128)(2,1)S(1)}, u32[]{:S(2)}, u32[]{:S(2)}) collective-permute-start(bf16[2,4,64,1024]{3,2,1,0:T(8,128)(2,1)S(1)} %pad_maximum_fusion.6), channel_id=1, source_target_pairs={{0,4},{4,0},{8,12},{12,8},{16,20},{20,16},{24,28},{28,24},{1,5},{5... | collective-permute-start | bytes 3145736 | tf_op jit(solution)/shard_map/ppermute | solution.py:84
  326.1 26.1 %collective-permute-start.42 = (bf16[2,4,64,1024]{3,2,1,0:T(8,128)(2,1)S(1)}, bf16[2,4,64,1024]{3,2,1,0:T(8,128)(2,1)S(1)}, u32[]{:S(2)}, u32[]{:S(2)}) collective-permute-start(bf16[2,4,64,1024]{3,2,1,0:T(8,128)(2,1)S(1)} %pad_maximum_fusion.7), channel_id=1, source_target_pairs={{0,8},{4,12},{8,0},{12,4},{16,24},{20,28},{24,16},{28,20},{1,9},{5... | collective-permute-start | bytes 3145736 | tf_op jit(solution)/shard_map/ppermute | solution.py:84
  335.8 25.0 %collective-permute-start.36 = (bf16[1,256,1024]{2,1,0:T(8,128)(2,1)S(1)}, bf16[1,256,1024]{2,1,0:T(8,128)(2,1)S(1)}, u32[]{:S(2)}, u32[]{:S(2)}) collective-permute-start(bf16[1,256,1024]{2,1,0:T(8,128)(2,1)S(1)} %fusion.47), channel_id=1, source_target_pairs={{0,8},{4,12},{8,0},{12,4},{16,24},{20,28},{24,16},{28,20},{1,9},{5... | collective-permute-start | bytes 1572872 | tf_op jit(solution)/shard_map/ppermute | solution.py:84
  336.7 16.4 %collective-permute-start.38 = (bf16[512,256]{1,0:T(8,128)(2,1)S(1)}, bf16[512,256]{1,0:T(8,128)(2,1)S(1)}, u32[]{:S(2)}, u32[]{:S(2)}) collective-permute-start(bf16[512,256]{1,0:T(8,128)(2,1)S(1)} %convolution_convert_fusion.10), channel_id=1, source_target_pairs={{0,1},{1,0},{2,3},{3,2},{4,5},{5,4},{6,7},{7,6},{8,9},{9,8},{10,11... | collective-permute-start | bytes 786440 | tf_op jit(solution)/shard_map/ppermute | solution.py:62
  336.8 18.0 %collective-permute-start.39 = (bf16[512,256]{1,0:T(8,128)(2,1)S(1)}, bf16[512,256]{1,0:T(8,128)(2,1)S(1)}, u32[]{:S(2)}, u32[]{:S(2)}) collective-permute-start(bf16[512,256]{1,0:T(8,128)(2,1)S(1)} %convolution_convert_fusion.9), channel_id=1, source_target_pairs={{0,2},{1,3},{2,0},{3,1},{4,6},{5,7},{6,4},{7,5},{8,10},{9,11},{10,... | collective-permute-start | bytes 786440 | tf_op jit(solution)/shard_map/ppermute | solution.py:62
  345.0 15.9 %collective-permute-start.37 = (bf16[1,256,1024]{2,1,0:T(8,128)(2,1)S(1)}, bf16[1,256,1024]{2,1,0:T(8,128)(2,1)S(1)}, u32[]{:S(2)}, u32[]{:S(2)}) collective-permute-start(bf16[1,256,1024]{2,1,0:T(8,128)(2,1)S(1)} %fusion.46), channel_id=1, source_target_pairs={{0,4},{4,0},{8,12},{12,8},{16,20},{20,16},{24,28},{28,24},{1,5},{5... | collective-permute-start | bytes 1572872 | tf_op jit(solution)/shard_map/ppermute | solution.py:84
  353.1 52.4 %collective-permute-start.47 = (bf16[256,1024]{1,0:T(8,128)(2,1)}, bf16[256,1024]{1,0:T(8,128)(2,1)}, u32[]{:S(2)}, u32[]{:S(2)}) collective-permute-start(bf16[256,1024]{1,0:T(8,128)(2,1)} %convolution_convert_fusion.4), channel_id=1, source_target_pairs={{0,1},{1,0},{2,3},{3,2},{4,5},{5,4},{6,7},{7,6},{8,9},{9,8},{10,11... | collective-permute-start | bytes 1572872 | tf_op jit(solution)/shard_map/ppermute | solution.py:62
  362.6 51.0 %collective-permute-start.45 = (bf16[2,1,256,1024]{3,2,1,0:T(8,128)(2,1)}, bf16[2,1,256,1024]{3,2,1,0:T(8,128)(2,1)}, u32[]{:S(2)}, u32[]{:S(2)}) collective-permute-start(bf16[2,1,256,1024]{3,2,1,0:T(8,128)(2,1)} %pad_maximum_fusion.8), channel_id=1, source_target_pairs={{0,16},{4,20},{8,24},{12,28},{16,0},{20,4},{24,8},{28,12},{1,17},{... | collective-permute-start | bytes 3145736 | tf_op jit(solution)/shard_map/ppermute | solution.py:84
  366.3 42.1 %collective-permute-start.41 = (bf16[4,64,1024]{2,1,0:T(8,128)(2,1)}, bf16[4,64,1024]{2,1,0:T(8,128)(2,1)}, u32[]{:S(2)}, u32[]{:S(2)}) collective-permute-start(bf16[4,64,1024]{2,1,0:T(8,128)(2,1)} %fusion.42), channel_id=1, source_target_pairs={{0,8},{4,12},{8,0},{12,4},{16,24},{20,28},{24,16},{28,20},{1,9},{5... | collective-permute-start | bytes 1572872 | tf_op jit(solution)/shard_map/ppermute | solution.py:84
  369.1 39.3 %collective-permute-start.43 = (bf16[4,64,1024]{2,1,0:T(8,128)(2,1)}, bf16[4,64,1024]{2,1,0:T(8,128)(2,1)}, u32[]{:S(2)}, u32[]{:S(2)}) collective-permute-start(bf16[4,64,1024]{2,1,0:T(8,128)(2,1)} %fusion.41), channel_id=1, source_target_pairs={{0,4},{4,0},{8,12},{12,8},{16,20},{20,16},{24,28},{28,24},{1,5},{5... | collective-permute-start | bytes 1572872 | tf_op jit(solution)/shard_map/ppermute | solution.py:84
  371.3 76.8 %collective-permute-start.50 = (bf16[256,1024]{1,0:T(8,128)(2,1)}, bf16[256,1024]{1,0:T(8,128)(2,1)S(1)}, u32[]{:S(2)}, u32[]{:S(2)}) collective-permute-start(bf16[256,1024]{1,0:T(8,128)(2,1)} %convolution_convert_fusion.6), channel_id=1, source_target_pairs={{0,1},{1,0},{2,3},{3,2},{4,5},{5,4},{6,7},{7,6},{8,9},{9,8},{10,11... | collective-permute-start | bytes 1572872 | tf_op jit(solution)/shard_map/ppermute | solution.py:62
  406.8 41.3 %collective-permute-start.51 = (bf16[256,1024]{1,0:T(8,128)(2,1)S(1)}, bf16[256,1024]{1,0:T(8,128)(2,1)S(1)}, u32[]{:S(2)}, u32[]{:S(2)}) collective-permute-start(bf16[256,1024]{1,0:T(8,128)(2,1)S(1)} %add_convert_fusion.17), channel_id=1, source_target_pairs={{0,2},{1,3},{2,0},{3,1},{4,6},{5,7},{6,4},{7,5},{8,10},{9,11},{10,... | collective-permute-start | bytes 1572872 | tf_op jit(solution)/shard_map/ppermute | solution.py:62
  411.5 48.7 %collective-permute-start.44 = (bf16[2,4,64,1024]{3,2,1,0:T(8,128)(2,1)S(1)}, bf16[2,4,64,1024]{3,2,1,0:T(8,128)(2,1)S(1)}, u32[]{:S(2)}, u32[]{:S(2)}) collective-permute-start(bf16[2,4,64,1024]{3,2,1,0:T(8,128)(2,1)S(1)} %pad_maximum_fusion.9), channel_id=1, source_target_pairs={{0,16},{4,20},{8,24},{12,28},{16,0},{20,4},{24,8},{28,12},{1,17},{... | collective-permute-start | bytes 3145736 | tf_op jit(solution)/shard_map/ppermute | solution.py:84
  415.1 34.8 %collective-permute-start.46 = (bf16[1,256,1024]{2,1,0:T(8,128)(2,1)S(1)}, bf16[1,256,1024]{2,1,0:T(8,128)(2,1)S(1)}, u32[]{:S(2)}, u32[]{:S(2)}) collective-permute-start(bf16[1,256,1024]{2,1,0:T(8,128)(2,1)S(1)} %add_convert_fusion.18.refs_0_), channel_id=1, source_target_pairs={{0,8},{4,12},{8,0},{12,4},{16,24},{20,28},{24,16},{28,20},{1,9},{5... | collective-permute-start | bytes 1572872 | tf_op jit(solution)/shard_map/ppermute | solution.py:84
  415.8 34.1 %collective-permute-start.48 = (bf16[1,256,1024]{2,1,0:T(8,128)(2,1)S(1)}, bf16[1,256,1024]{2,1,0:T(8,128)(2,1)S(1)}, u32[]{:S(2)}, u32[]{:S(2)}) collective-permute-start(bf16[1,256,1024]{2,1,0:T(8,128)(2,1)S(1)} %add_convert_fusion.16.refs_3_), channel_id=1, source_target_pairs={{0,4},{4,0},{8,12},{12,8},{16,20},{20,16},{24,28},{28,24},{1,5},{5... | collective-permute-start | bytes 1572872 | tf_op jit(solution)/shard_map/ppermute | solution.py:84
  465.1 41.5 %collective-permute-start.58 = (bf16[2,1,256,1024]{3,2,1,0:T(8,128)(2,1)S(1)}, bf16[2,1,256,1024]{3,2,1,0:T(8,128)(2,1)S(1)}, u32[]{:S(2)}, u32[]{:S(2)}) collective-permute-start(bf16[2,1,256,1024]{3,2,1,0:T(8,128)(2,1)S(1)} %pad_maximum_fusion.10), channel_id=1, source_target_pairs={{0,4},{4,0},{8,12},{12,8},{16,20},{20,16},{24,28},{28,24},{1,5},{5... | collective-permute-start | bytes 3145736 | tf_op jit(solution)/shard_map/ppermute | solution.py:84
  466.9 37.6 %collective-permute-start.60 = (bf16[2,1,256,1024]{3,2,1,0:T(8,128)(2,1)S(1)}, bf16[2,1,256,1024]{3,2,1,0:T(8,128)(2,1)S(1)}, u32[]{:S(2)}, u32[]{:S(2)}) collective-permute-start(bf16[2,1,256,1024]{3,2,1,0:T(8,128)(2,1)S(1)} %pad_maximum_fusion.11), channel_id=1, source_target_pairs={{0,8},{4,12},{8,0},{12,4},{16,24},{20,28},{24,16},{28,20},{1,9},{5... | collective-permute-start | bytes 3145736 | tf_op jit(solution)/shard_map/ppermute | solution.py:84
  466.9 16.3 %collective-permute-start.52 = (bf16[128,1024]{1,0:T(8,128)(2,1)S(1)}, bf16[128,1024]{1,0:T(8,128)(2,1)S(1)}, u32[]{:S(2)}, u32[]{:S(2)}) collective-permute-start(bf16[128,1024]{1,0:T(8,128)(2,1)S(1)} %pad_maximum_fusion.29), channel_id=1, source_target_pairs={{0,1},{1,0},{2,3},{3,2},{4,5},{5,4},{6,7},{7,6},{8,9},{9,8},{10,11... | collective-permute-start | bytes 786440 | tf_op jit(solution)/shard_map/ppermute | solution.py:62
  477.8 24.5 %collective-permute-start.56 = (bf16[2,512,256]{2,1,0:T(8,128)(2,1)S(1)}, bf16[2,512,256]{2,1,0:T(8,128)(2,1)S(1)}, u32[]{:S(2)}, u32[]{:S(2)}) collective-permute-start(bf16[2,512,256]{2,1,0:T(8,128)(2,1)S(1)} %pad_maximum_fusion.22), channel_id=1, source_target_pairs={{0,4},{4,0},{8,12},{12,8},{16,20},{20,16},{24,28},{28,24},{1,5},{5... | collective-permute-start | bytes 1572872 | tf_op jit(solution)/shard_map/ppermute | solution.py:84
  481.3 22.1 %collective-permute-start.59 = (bf16[2,512,256]{2,1,0:T(8,128)(2,1)S(1)}, bf16[2,512,256]{2,1,0:T(8,128)(2,1)S(1)}, u32[]{:S(2)}, u32[]{:S(2)}) collective-permute-start(bf16[2,512,256]{2,1,0:T(8,128)(2,1)S(1)} %pad_maximum_fusion.23), channel_id=1, source_target_pairs={{0,8},{4,12},{8,0},{12,4},{16,24},{20,28},{24,16},{28,20},{1,9},{5... | collective-permute-start | bytes 1572872 | tf_op jit(solution)/shard_map/ppermute | solution.py:84
  483.9 36.5 %collective-permute-start.62 = (bf16[4,64,1024]{2,1,0:T(8,128)(2,1)S(1)}, bf16[4,64,1024]{2,1,0:T(8,128)(2,1)S(1)}, u32[]{:S(2)}, u32[]{:S(2)}) collective-permute-start(bf16[4,64,1024]{2,1,0:T(8,128)(2,1)S(1)} %get-tuple-element.271.refs_3_), channel_id=1, source_target_pairs={{0,4},{4,0},{8,12},{12,8},{16,20},{20,16},{24,28},{28,24},{1,5},{5... | collective-permute-start | bytes 1572872 | tf_op jit(solution)/shard_map/ppermute | solution.py:84
  503.5 15.8 %collective-permute-start.57 = (bf16[512,256]{1,0:T(8,128)(2,1)S(1)}, bf16[512,256]{1,0:T(8,128)(2,1)S(1)}, u32[]{:S(2)}, u32[]{:S(2)}) collective-permute-start(bf16[512,256]{1,0:T(8,128)(2,1)S(1)} %add_convert_fusion.29), channel_id=1, source_target_pairs={{0,8},{4,12},{8,0},{12,4},{16,24},{20,28},{24,16},{28,20},{1,9},{5... | collective-permute-start | bytes 786440 | tf_op jit(solution)/shard_map/ppermute | solution.py:84
  503.9 14.9 %collective-permute-start.61 = (bf16[512,256]{1,0:T(8,128)(2,1)S(1)}, bf16[512,256]{1,0:T(8,128)(2,1)S(1)}, u32[]{:S(2)}, u32[]{:S(2)}) collective-permute-start(bf16[512,256]{1,0:T(8,128)(2,1)S(1)} %add_convert_fusion.28), channel_id=1, source_target_pairs={{0,4},{4,0},{8,12},{12,8},{16,20},{20,16},{24,28},{28,24},{1,5},{5... | collective-permute-start | bytes 786440 | tf_op jit(solution)/shard_map/ppermute | solution.py:84
  504.5 17.9 %collective-permute-start.55 = (bf16[4,64,1024]{2,1,0:T(8,128)(2,1)S(1)}, bf16[4,64,1024]{2,1,0:T(8,128)(2,1)S(1)}, u32[]{:S(2)}, u32[]{:S(2)}) collective-permute-start(bf16[4,64,1024]{2,1,0:T(8,128)(2,1)S(1)} %get-tuple-element.272.refs_0_), channel_id=1, source_target_pairs={{0,8},{4,12},{8,0},{12,4},{16,24},{20,28},{24,16},{28,20},{1,9},{5... | collective-permute-start | bytes 1572872 | tf_op jit(solution)/shard_map/ppermute | solution.py:84
  506.6 36.9 %collective-permute-start.63 = (bf16[512,1024]{1,0:T(8,128)(2,1)S(1)}, bf16[512,1024]{1,0:T(8,128)(2,1)S(1)}, u32[]{:S(2)}, u32[]{:S(2)}) collective-permute-start(bf16[512,1024]{1,0:T(8,128)(2,1)S(1)} %add_convert_fusion), channel_id=1, source_target_pairs={{0,1},{1,0},{2,3},{3,2},{4,5},{5,4},{6,7},{7,6},{8,9},{9,8},{10,11... | collective-permute-start | bytes 3145736 | tf_op jit(solution)/shard_map/ppermute | solution.py:62
  518.7 24.8 %collective-permute-start.64 = (bf16[512,1024]{1,0:T(8,128)(2,1)S(1)}, bf16[512,1024]{1,0:T(8,128)(2,1)S(1)}, u32[]{:S(2)}, u32[]{:S(2)}) collective-permute-start(bf16[512,1024]{1,0:T(8,128)(2,1)S(1)} %add_convert_fusion.2), channel_id=1, source_target_pairs={{0,2},{1,3},{2,0},{3,1},{4,6},{5,7},{6,4},{7,5},{8,10},{9,11},{10,... | collective-permute-start | bytes 3145736 | tf_op jit(solution)/shard_map/ppermute | solution.py:62
  520.4 33.1 %collective-permute-start.68 = (bf16[2,512,256]{2,1,0:T(8,128)(2,1)}, bf16[2,512,256]{2,1,0:T(8,128)(2,1)}, u32[]{:S(2)}, u32[]{:S(2)}) collective-permute-start(bf16[2,512,256]{2,1,0:T(8,128)(2,1)} %pad_maximum_fusion.24), channel_id=1, source_target_pairs={{0,16},{4,20},{8,24},{12,28},{16,0},{20,4},{24,8},{28,12},{1,17},{... | collective-permute-start | bytes 1572872 | tf_op jit(solution)/shard_map/ppermute | solution.py:84
  523.4 47.5 %collective-permute-start.76 = (bf16[2,4,64,1024]{3,2,1,0:T(8,128)(2,1)}, bf16[2,4,64,1024]{3,2,1,0:T(8,128)(2,1)}, u32[]{:S(2)}, u32[]{:S(2)}) collective-permute-start(bf16[2,4,64,1024]{3,2,1,0:T(8,128)(2,1)} %pad_maximum_fusion.14), channel_id=1, source_target_pairs={{0,8},{4,12},{8,0},{12,4},{16,24},{20,28},{24,16},{28,20},{1,9},{5... | collective-permute-start | bytes 3145736 | tf_op jit(solution)/shard_map/ppermute | solution.py:84
  525.1 45.8 %collective-permute-start.75 = (bf16[2,4,64,1024]{3,2,1,0:T(8,128)(2,1)}, bf16[2,4,64,1024]{3,2,1,0:T(8,128)(2,1)}, u32[]{:S(2)}, u32[]{:S(2)}) collective-permute-start(bf16[2,4,64,1024]{3,2,1,0:T(8,128)(2,1)} %pad_maximum_fusion.13), channel_id=1, source_target_pairs={{0,4},{4,0},{8,12},{12,8},{16,20},{20,16},{24,28},{28,24},{1,5},{5... | collective-permute-start | bytes 3145736 | tf_op jit(solution)/shard_map/ppermute | solution.py:84
  (135 other events, 1344.3 us)
Sparse Core Ops, SparseCore 0:
  71.0 75.1 all-gather.2

commit v4 on v3

--- a/solution.py
+++ b/solution.py
@@ -192,13 +192,13 @@
     )(facts, tok_a, tok_b, *blocks)
 
 
-def visible_tile(key_block, query_block, starts):
-    key_pos = key_block * TILE + lax.broadcasted_iota(jnp.int32, (TILE, TILE), 0)
-    query_pos = query_block * TILE + lax.broadcasted_iota(jnp.int32, (TILE, TILE), 1)
+def visible_tile(key_start, query_start, keys, queries, starts):
+    key_pos = key_start + lax.broadcasted_iota(jnp.int32, (keys, queries), 0)
+    query_pos = query_start + lax.broadcasted_iota(jnp.int32, (keys, queries), 1)
     seen = key_pos <= query_pos
+    low = jnp.minimum(key_pos, query_pos)
+    high = jnp.maximum(key_pos, query_pos)
     for start in starts:
-        low = jnp.minimum(key_pos, query_pos)
-        high = jnp.maximum(key_pos, query_pos)
         seen = seen | ((low >= start) & (high < start + PIECE_LEN))
     return seen
 
@@ -214,19 +214,20 @@
     return lax.broadcasted_iota(jnp.int32, (rows, OWN), 1) // HEAD_DIM
 
 
+WIDE = 2 * TILE
+
+
 def attend_kernel(blocks, facts, near, far, mixed, logs, q_own, k_own, v_turned, acc, top, total):
     me = facts[0]
     starts = [facts[1 + i] for i in range(facts.shape[0] - 1)]
     for j in range(N_SHARD):
         src = near if j < 2 else far
-        base = (j % 2) * 2 * TILE
-        for half in range(2):
-            rows = slice(base + half * TILE, base + (half + 1) * TILE)
-            at = (me ^ j) * 2 + half
-            q_own[at] = src[rows, 0:OWN] * jnp.asarray(HEAD_DIM**-0.5, bf16)
-            k_own[at] = src[rows, OWN : 2 * OWN]
-            v_turned[at] = src[rows, 2 * OWN : 3 * OWN].astype(f32).T.astype(bf16)
-    lanes = head_lanes(TILE)
+        rows = slice((j % 2) * WIDE, (j % 2 + 1) * WIDE)
+        at = me ^ j
+        q_own[at] = src[rows, 0:OWN] * jnp.asarray(HEAD_DIM**-0.5, bf16)
+        k_own[at] = src[rows, OWN : 2 * OWN]
+        v_turned[at] = src[rows, 2 * OWN : 3 * OWN].astype(f32).T.astype(bf16)
+    lanes = head_lanes(WIDE)
 
     def query_block(i, unused):
         q_i = q_own[i]
@@ -235,12 +236,12 @@
         top[...] = jnp.full_like(top, NEG)
         total[...] = jnp.zeros_like(total)
 
-        def key_block(j, masked):
-            k_j = k_own[j]
-            v_j = v_turned[j]
-            seen = visible_tile(j, i, starts) if masked else None
+        def key_pair(p, masked):
+            k_p = k_own[p]
+            v_p = v_turned[p]
+            seen = visible_tile(p * WIDE, i * WIDE, WIDE, WIDE, starts) if masked else None
             for h in range(OWN_HEADS):
-                scores = dot_nt(k_j, q_heads[h])
+                scores = dot_nt(k_p, q_heads[h])
                 if masked:
                     scores = jnp.where(seen, scores, NEG)
                 old_top = top[h : h + 1, :]
@@ -251,30 +252,29 @@
                 total[h : h + 1, :] = total[h : h + 1, :] * fade + jnp.sum(
                     raised, axis=0, keepdims=True
                 )
-                part = dot_nn(v_j[h * HEAD_DIM : (h + 1) * HEAD_DIM, :], raised.astype(bf16))
                 rows = slice(h * HEAD_DIM, (h + 1) * HEAD_DIM)
-                acc[rows, :] = acc[rows, :] * fade + part
-
-        def plain(j, unused):
-            key_block(j, False)
+                acc[rows, :] = acc[rows, :] * fade + dot_nn(v_p[rows, :], raised.astype(bf16))
+
+        def plain(p, unused):
+            key_pair(p, False)
             return unused
 
+        def edge(p, unused):
+            key_pair(p, True)
+            return unused
+
         lax.fori_loop(0, i, plain, 0)
-        key_block(i, True)
-
-        @pl.when((i + 1 < blocks) & crosses((i + 1) * TILE, starts))
-        def _():
-            key_block(i + 1, True)
+        more = (i + 1 < blocks // 2) & crosses((i + 1) * WIDE, starts)
+        lax.fori_loop(i, i + 1 + more.astype(jnp.int32), edge, 0)
 
         for h in range(OWN_HEADS):
             rows = slice(h * HEAD_DIM, (h + 1) * HEAD_DIM)
             acc[rows, :] = acc[rows, :] / total[h : h + 1, :]
-        place = ((i // 2) ^ me) * (2 * TILE) + (i % 2) * TILE
-        mixed[pl.ds(pl.multiple_of(place, TILE), TILE), :] = acc[...].T.astype(bf16)
+        mixed[pl.ds(pl.multiple_of((i ^ me) * WIDE, WIDE), WIDE), :] = acc[...].T.astype(bf16)
         logs[i] = top[...] + jnp.log(jnp.maximum(total[...], 1e-30))
         return unused
 
-    lax.fori_loop(0, blocks, query_block, 0)
+    lax.fori_loop(0, blocks // 2, query_block, 0)
 
 
 def attend(facts, near, far):
@@ -285,17 +285,17 @@
         functools.partial(attend_kernel, blocks),
         out_shape=(
             jax.ShapeDtypeStruct((rows, OWN), bf16),
-            jax.ShapeDtypeStruct((blocks, 8, TILE), f32),
+            jax.ShapeDtypeStruct((blocks // 2, 8, WIDE), f32),
         ),
         in_specs=[pl.BlockSpec(memory_space=pltpu.SMEM), vmem, vmem],
         out_specs=(vmem, vmem),
         scratch_shapes=[
-            pltpu.VMEM((blocks, TILE, OWN), bf16),
-            pltpu.VMEM((blocks, TILE, OWN), bf16),
-            pltpu.VMEM((blocks, OWN, TILE), bf16),
-            pltpu.VMEM((OWN, TILE), f32),
-            pltpu.VMEM((8, TILE), f32),
-            pltpu.VMEM((8, TILE), f32),
+            pltpu.VMEM((blocks // 2, WIDE, OWN), bf16),
+            pltpu.VMEM((blocks // 2, WIDE, OWN), bf16),
+            pltpu.VMEM((blocks // 2, OWN, WIDE), bf16),
+            pltpu.VMEM((OWN, WIDE), f32),
+            pltpu.VMEM((8, WIDE), f32),
+            pltpu.VMEM((8, WIDE), f32),
         ],
         compiler_params=pltpu.CompilerParams(vmem_limit_bytes=48 * 2**20),
         cost_estimate=LIGHT,
@@ -319,86 +319,89 @@
     for j in range(N_SHARD):
         src = near if j < 2 else far
         grad_src = (g0, g1, g2, g3)[j]
-        base = (j % 2) * 2 * TILE
+        at = me ^ j
         for half in range(2):
-            rows = slice(base + half * TILE, base + (half + 1) * TILE)
-            at = (me ^ j) * 2 + half
+            base = (j % 2) * WIDE + half * TILE
+            rows = slice(base, base + TILE)
+            to = slice(half * TILE, (half + 1) * TILE)
             q_tile = src[rows, lane : lane + wide] * jnp.asarray(HEAD_DIM**-0.5, bf16)
             k_tile = src[rows, OWN + lane : OWN + lane + wide]
-            g_tile = grad_src[half * TILE : (half + 1) * TILE, lane : lane + wide]
-            o_rows = slice(j * 2 * TILE + half * TILE, j * 2 * TILE + (half + 1) * TILE)
-            o_tile = mixed[o_rows, lane : lane + wide]
-            q_own[at] = q_tile
-            k_own[at] = k_tile
-            v_own[at] = src[rows, 2 * OWN + lane : 2 * OWN + lane + wide]
-            k_turned[at] = k_tile.astype(f32).T.astype(bf16)
-            g_own[at] = g_tile
+            g_tile = grad_src[to, lane : lane + wide]
+            o_tile = mixed[j * WIDE + half * TILE : j * WIDE + (half + 1) * TILE, lane : lane + wide]
+            q_own[at, to, :] = q_tile
+            k_own[at, to, :] = k_tile
+            v_own[at, to, :] = src[rows, 2 * OWN + lane : 2 * OWN + lane + wide]
+            k_turned[at, :, to] = k_tile.astype(f32).T.astype(bf16)
+            g_own[at, to, :] = g_tile
             for h in range(PAIR):
-                place = slice(h * TILE, (h + 1) * TILE)
+                place = slice(h * WIDE + half * TILE, h * WIDE + (half + 1) * TILE)
                 q_heads[at, place, :] = jnp.where(lanes == h, q_tile, jnp.zeros_like(q_tile))
                 g_heads[at, place, :] = jnp.where(lanes == h, g_tile, jnp.zeros_like(g_tile))
             both = g_tile.astype(f32) * o_tile.astype(f32)
-            deltas[at] = lax.dot_general(
+            deltas[at, :, to] = lax.dot_general(
                 pick, both, (((1,), (1,)), ((), ())),
                 precision=lax.Precision.HIGHEST, preferred_element_type=f32,
             )
     q_grad[...] = jnp.zeros_like(q_grad)
+    wide_lanes = lax.broadcasted_iota(jnp.int32, (WIDE, wide), 1) // HEAD_DIM
 
     def key_block(j, unused):
         k_j = k_own[j]
         v_j = v_own[j]
         for h in range(PAIR):
-            k_heads[h * TILE : (h + 1) * TILE, :] = jnp.where(lanes == h, k_j, jnp.zeros_like(k_j))
-            v_heads[h * TILE : (h + 1) * TILE, :] = jnp.where(lanes == h, v_j, jnp.zeros_like(v_j))
+            rows = slice(h * WIDE, (h + 1) * WIDE)
+            k_heads[rows, :] = jnp.where(wide_lanes == h, k_j, jnp.zeros_like(k_j))
+            v_heads[rows, :] = jnp.where(wide_lanes == h, v_j, jnp.zeros_like(v_j))
         k_grad[...] = jnp.zeros_like(k_grad)
         v_grad[...] = jnp.zeros_like(v_grad)
 
-        def query_block(i, masked):
-            q_i = q_own[i]
-            g_i = g_own[i]
+        def query_pair(p, masked):
+            q_p = q_own[p]
+            g_p = g_own[p]
             kt = k_turned[j]
-            seen = visible_tile(j, i, starts) if masked else None
+            seen = visible_tile(j * WIDE, p * WIDE, WIDE, WIDE, starts) if masked else None
             softs = []
             scored = []
             for h in range(PAIR):
-                rows = slice(h * TILE, (h + 1) * TILE)
+                rows = slice(h * WIDE, (h + 1) * WIDE)
                 at = pair * PAIR + h
-                scores = dot_nt(k_heads[rows, :], q_i)
-                soft = jnp.exp(scores - logs[i, at : at + 1, :])
+                scores = dot_nt(k_heads[rows, :], q_p)
+                soft = jnp.exp(scores - logs[p, at : at + 1, :])
                 if masked:
                     soft = jnp.where(seen, soft, 0.0)
-                grad_soft = dot_nt(v_heads[rows, :], g_i)
-                grad_scores = (soft * (grad_soft - deltas[i, h : h + 1, :])).astype(bf16)
+                grad_soft = dot_nt(v_heads[rows, :], g_p)
+                grad_scores = (soft * (grad_soft - deltas[p, h : h + 1, :])).astype(bf16)
                 softs.append(soft.astype(bf16))
                 scored.append(grad_scores)
                 head = slice(h * HEAD_DIM, (h + 1) * HEAD_DIM)
-                q_grad[i, head, :] += dot_nn(kt[head, :], grad_scores)
-            v_grad[...] += dot_nn(jnp.concatenate(softs, axis=1), g_heads[i])
-            k_grad[...] += dot_nn(jnp.concatenate(scored, axis=1), q_heads[i])
-
-        def plain(i, unused):
-            query_block(i, False)
+                q_grad[p, head, :] += dot_nn(kt[head, :], grad_scores)
+            v_grad[...] += dot_nn(jnp.concatenate(softs, axis=1), g_heads[p])
+            k_grad[...] += dot_nn(jnp.concatenate(scored, axis=1), q_heads[p])
+
+        def plain(p, unused):
+            query_pair(p, False)
             return unused
 
-        @pl.when((j > 0) & crosses(j * TILE, starts))
-        def _():
-            query_block(j - 1, True)
-
-        query_block(j, True)
-        lax.fori_loop(j + 1, blocks, plain, 0)
-        place = pl.multiple_of(((j // 2) ^ me) * (2 * TILE) + (j % 2) * TILE, TILE)
-        grads[pl.ds(place, TILE), wide : 2 * wide] = k_grad[...].astype(bf16)
-        grads[pl.ds(place, TILE), 2 * wide : 3 * wide] = v_grad[...].astype(bf16)
+        def edge(p, unused):
+            query_pair(p, True)
+            return unused
+
+        less = (j > 0) & crosses(j * WIDE, starts)
+        lax.fori_loop(j - less.astype(jnp.int32), j + 1, edge, 0)
+        lax.fori_loop(j + 1, blocks // 2, plain, 0)
+        place = pl.multiple_of((j ^ me) * WIDE, WIDE)
+        grads[pl.ds(place, WIDE), wide : 2 * wide] = k_grad[...].astype(bf16)
+        grads[pl.ds(place, WIDE), 2 * wide : 3 * wide] = v_grad[...].astype(bf16)
         return unused
 
-    lax.fori_loop(0, blocks, key_block, 0)
-
-    def write_query(i, unused):
-        place = pl.multiple_of(((i // 2) ^ me) * (2 * TILE) + (i % 2) * TILE, TILE)
-        grads[pl.ds(place, TILE), 0:wide] = (q_grad[i] * HEAD_DIM**-0.5).T.astype(bf16)
+    lax.fori_loop(0, blocks // 2, key_block, 0)
+
+    def write_query(p, unused):
+        place = pl.multiple_of((p ^ me) * WIDE, WIDE)
+        grads[pl.ds(place, WIDE), 0:wide] = (q_grad[p] * HEAD_DIM**-0.5).T.astype(bf16)
         return unused
 
-    lax.fori_loop(0, blocks, write_query, 0)
+    lax.fori_loop(0, blocks // 2, write_query, 0)
 
 
 def attend_back(pair, facts, near, far, mixed, grad_blocks, logs):
@@ -407,26 +410,26 @@
     wide = PAIR * HEAD_DIM
     vmem = pl.BlockSpec(memory_space=pltpu.VMEM)
     tile = lambda n, m, kind: pltpu.VMEM((n, m), kind)
-    stack = lambda n, m, kind: pltpu.VMEM((blocks, n, m), kind)
+    double = lambda n, m, kind: pltpu.VMEM((blocks // 2, n, m), kind)
     return pl.pallas_call(
         functools.partial(attend_back_kernel, blocks, pair),
         out_shape=jax.ShapeDtypeStruct((rows, 3 * wide), bf16),
         in_specs=[pl.BlockSpec(memory_space=pltpu.SMEM)] + [vmem] * 8,
         out_specs=vmem,
         scratch_shapes=[
-            stack(TILE, wide, bf16),
-            stack(TILE, wide, bf16),
-            stack(TILE, wide, bf16),
-            stack(wide, TILE, bf16),
-            stack(TILE, wide, bf16),
-            stack(PAIR * TILE, wide, bf16),
-            stack(PAIR * TILE, wide, bf16),
-            stack(8, TILE, f32),
-            stack(wide, TILE, f32),
-            tile(TILE, wide, f32),
-            tile(TILE, wide, f32),
-            tile(PAIR * TILE, wide, bf16),
-            tile(PAIR * TILE, wide, bf16),
+            double(WIDE, wide, bf16),
+            double(WIDE, wide, bf16),
+            double(WIDE, wide, bf16),
+            double(wide, WIDE, bf16),
+            double(WIDE, wide, bf16),
+            double(PAIR * WIDE, wide, bf16),
+            double(PAIR * WIDE, wide, bf16),
+            double(8, WIDE, f32),
+            double(wide, WIDE, f32),
+            tile(WIDE, wide, f32),
+            tile(WIDE, wide, f32),
+            tile(PAIR * WIDE, wide, bf16),
+            tile(PAIR * WIDE, wide, bf16),
         ],
         compiler_params=pltpu.CompilerParams(vmem_limit_bytes=48 * 2**20),
         cost_estimate=LIGHT,

time: 616 us -> 612 us (level)
  waiting for transfers between devices: 177 us -> 212 us
  Pallas kernels: 182 us -> 151 us
  starting transfers between devices: 69.6 us -> 59.4 us
    ppermute x33, waiting for transfers between devices: 72.1 us -> 105 us  [rep_swap(): return lax.ppermute(value, 'rep', [(i, i ^ mask) for i in range(count)])]
    pallas_call x2, Pallas kernels: 63.9 us -> 45.9 us  [attend_back(): pl.pallas_call(functools.partial(attend_back_kernel, blocks, pair), out_s...]
    pallas_call x1, Pallas kernels: 42.4 us -> 29.2 us  [attend(): pl.pallas_call(functools.partial(attend_kernel, blocks), out_shape=(jax.S...]
    all_gather x1, waiting for transfers between devices: 0.26 us -> 13.3 us  [shards(): thin = lax.all_gather(thin.transpose(1, 0, 2, 3), 'rep', axis=0)]
    ppermute x33, starting transfers between devices: 43.1 us -> 31 us  [rep_swap(): return lax.ppermute(value, 'rep', [(i, i ^ mask) for i in range(count)])]
    ppermute x47, waiting for transfers between devices: 105 us -> 93.3 us  [swap(): return lax.ppermute(value, 'shard', [(i, i ^ mask) for i in range(N_SHARD)])]
  transfers between devices with their start and end apart: 81 -> 81, of which waited for: 35 -> 33; matrix products, arithmetic and copies ran while one was open for 20% -> 20% of each run, Pallas kernels for 25% -> 20%
where the time goes in v4:
time: 612 us; the launch traced here: 601 us
  waiting for transfers between devices  212 us (35%)
  Pallas kernels  151 us (25%)
  starting transfers between devices  59.4 us (10%)
  matrix products  58.6 us (10%)
  local copies, waits for them, and re-layouts  57.4 us (9%)
  other arithmetic  41.4 us (7%)
  between operations  21.3 us (3%)
    ppermute x33, waiting for transfers between devices, rep_swap(): return lax.ppermute(value, 'rep', [(i, i ^ mask) for i in range(count)])  105 us
    ppermute x47, waiting for transfers between devices, swap(): return lax.ppermute(value, 'shard', [(i, i ^ mask) for i in range(N_SHARD)])  93.3 us
    pallas_call x2, Pallas kernels, attend_back(): pl.pallas_call(functools.partial(attend_back_kernel, blocks, pair), out_s...  45.9 us
    dot_general x12, matrix products, dot_tn(): lax.dot_general(a, b, (((0,), (0,)), ((), ())), preferred_element_type=f32)  44.3 us
    ppermute x33, starting transfers between devices, rep_swap(): return lax.ppermute(value, 'rep', [(i, i ^ mask) for i in range(count)])  31 us
    unnamed x258, local copies, waits for them, and re-layouts  29.5 us
    pallas_call x1, Pallas kernels, attend(): pl.pallas_call(functools.partial(attend_kernel, blocks), out_shape=(jax.S...  29.2 us
    ppermute x47, starting transfers between devices, swap(): return lax.ppermute(value, 'shard', [(i, i ^ mask) for i in range(N_SHARD)])  28.4 us
  transfers between devices with their start and end apart: 81, of which 33 were waited for; matrix products, arithmetic and copies ran while one was open for 20% of the time, Pallas kernels for 20%

profile of v4, /device:TPU:0, one launch (start us, length us, event | category | flops | bytes accessed | tf_op | source)
XLA Modules:
  0.0 600.7 jit_solution(16963404798710605760)
XLA Ops:
  7.2 3.0 collective-permute-start
  18.2 3.1 gather_fusion
  21.4 13.2 %collective-permute-done.tok_a = bf16[512,1024]{1,0:T(8,128)(2,1)} collective-permute-done((bf16[512,1024]{1,0:T(8,128)(2,1)}, bf16[512,1024]{1,0:T(8,128)(2,1)}, u32[]{:S(2)}, u32[]{:S(2)}) %collective-permute-start) | collective-permute-done | bytes 1048608 | tf_op jit(solution)/shard_map/ppermute | solution.py:62
  36.9 13.5 %collective-permute-done.4 = bf16[2,264,768]{2,1,0:T(8,128)(2,1)} collective-permute-done((bf16[2,264,768]{2,1,0:T(8,128)(2,1)}, bf16[2,264,768]{2,1,0:T(8,128)(2,1)}, u32[]{:S(2)}, u32[]{:S(2)}) %collective-permute-start.4) | collective-permute-done | bytes 811040 | tf_op jit(solution)/shard_map/ppermute | solution.py:62
  62.2 3.8 project.2
  76.0 4.2 project.3
  83.6 29.2 %attend.1 = (bf16[2048,256]{1,0:T(8,128)(2,1)S(1)}, f32[4,8,512]{2,1,0:T(8,128)S(1)}) custom-call(s32[3]{0:T(128)S(1)} %pad_add_fusion.facts, bf16[1024,768]{1,0:T(8,128)(2,1)S(1)} %get-tuple-element.176.near, bf16[1024,768]{1,0:T(8,128)(2,1)S(1)} %get-tuple-element.121.far), custom_call_target="tpu_custom_call" | custom-call | flops 1048576 | bytes 65536 | tf_op jit(solution)/shard_map/attend/pallas_call | solution.py:284
  116.7 5.1 collective-permute-done.9
  121.8 6.2 %collective-permute-done.8 = bf16[512,256]{1,0:T(8,128)(2,1)S(1)} collective-permute-done((bf16[512,256]{1,0:T(8,128)(2,1)S(1)}, bf16[512,256]{1,0:T(8,128)(2,1)S(1)}, u32[]{:S(2)}, u32[]{:S(2)}) %collective-permute-start.8) | collective-permute-done | bytes 262176 | tf_op jit(solution)/shard_map/ppermute | solution.py:62
  132.7 13.3 %all-gather.3.cloned.1.call-done = bf16[16,4,32,1024]{3,2,1,0:T(8,128)(2,1)} async-done(((bf16[2,4,32,1024]{3,2,1,0:T(8,128)(2,1)}), bf16[16,4,32,1024]{3,2,1,0:T(8,128)(2,1)}) %all-gather.3.cloned.1.call-update) | async-done | bytes 4194320 | tf_op jit(solution)/shard_map/all_gather | solution.py:741
  146.0 3.0 copy.84
  149.0 13.2 %experts.2 = (bf16[1024,1024]{1,0:T(8,128)(2,1)S(1)}, bf16[512,1024]{1,0:T(8,128)(2,1)S(1)}, bf16[512,1024]{1,0:T(8,128)(2,1)S(1)}) custom-call(s32[2,1]{1,0:T(2,128)S(1)} %bitcast.348, bf16[512,1024]{1,0:T(8,128)(2,1)} %convolution_convert_fusion.1.rows_a, bf16[512,1024]{1,0:T(8,128)(2,1)} %collective-permute-done.15.rows_b, ...), custom_call_target="tpu_custom_call" | custom-call | flops 1048576 | bytes 65536 | tf_op jit(solution)/shard_map/experts/pallas_call | solution.py:522
  162.3 2.9 collective-permute-done.21.rows_b
  165.2 12.2 %experts.3 = (bf16[1024,1024]{1,0:T(8,128)(2,1)S(1)}, bf16[512,1024]{1,0:T(8,128)(2,1)S(1)}, bf16[512,1024]{1,0:T(8,128)(2,1)S(1)}) custom-call(s32[2,1]{1,0:T(2,128)S(1)} %bitcast.346, bf16[512,1024]{1,0:T(8,128)(2,1)} %collective-permute-done.20.rows_a, bf16[512,1024]{1,0:T(8,128)(2,1)S(1)} %collective-permute-done.21.rows_b, ...), custom_call_target="tpu_custom_call" | custom-call | flops 1048576 | bytes 65536 | tf_op jit(solution)/shard_map/experts/pallas_call | solution.py:522
  182.8 3.0 collective-permute-done.24
  186.6 2.7 collective-permute-done.25
  190.9 2.8 collective-permute-done.26
  193.9 12.0 %collective-permute-done.23 = bf16[512,1024]{1,0:T(8,128)(2,1)S(1)} collective-permute-done((bf16[512,1024]{1,0:T(8,128)(2,1)S(1)}, bf16[512,1024]{1,0:T(8,128)(2,1)S(1)}, u32[]{:S(2)}, u32[]{:S(2)}) %collective-permute-start.23) | collective-permute-done | bytes 1048608 | tf_op jit(solution)/shard_map/ppermute | solution.py:62
  211.7 13.7 %experts_back.2 = (bf16[1024,1024]{1,0:T(8,128)(2,1)S(1)}, bf16[512,1024]{1,0:T(8,128)(2,1)S(1)}, bf16[512,1024]{1,0:T(8,128)(2,1)}) custom-call(s32[2,1]{1,0:T(2,128)S(1)} %bitcast.349, bf16[512,1024]{1,0:T(8,128)(2,1)S(1)} %convolution_convert_fusion.rows_a, bf16[512,1024]{1,0:T(8,128)(2,1)S(1)} %collective-permute-done.27.rows_b, ...), custom_call_target="tpu_custom_call" | custom-call | flops 1048576 | bytes 65536 | tf_op jit(solution)/shard_map/experts_back/pallas_call | solution.py:546
  227.7 7.1 %collective-permute-done.29.rows_a = bf16[512,1024]{1,0:T(8,128)(2,1)} collective-permute-done((bf16[512,1024]{1,0:T(8,128)(2,1)S(1)}, bf16[512,1024]{1,0:T(8,128)(2,1)}, u32[]{:S(2)}, u32[]{:S(2)}) %collective-permute-start.29) | collective-permute-done | bytes 1048608 | tf_op jit(solution)/shard_map/ppermute | solution.py:62
  237.3 4.4 pad_maximum_fusion.3
  241.7 12.9 %experts_back.3 = (bf16[1024,1024]{1,0:T(8,128)(2,1)S(1)}, bf16[512,1024]{1,0:T(8,128)(2,1)S(1)}, bf16[512,1024]{1,0:T(8,128)(2,1)S(1)}) custom-call(s32[2,1]{1,0:T(2,128)S(1)} %bitcast.347, bf16[512,1024]{1,0:T(8,128)(2,1)} %collective-permute-done.29.rows_a, bf16[512,1024]{1,0:T(8,128)(2,1)} %collective-permute-done.30.rows_b, ...), custom_call_target="tpu_custom_call" | custom-call | flops 1048576 | bytes 65536 | tf_op jit(solution)/shard_map/experts_back/pallas_call | solution.py:546
  258.3 2.8 copy-done.18
  261.1 2.5 pad_maximum_fusion.2
  274.3 8.2 %fusion.27 = bf16[1024,1024]{1,0:T(8,128)(2,1)S(1)} fusion(bf16[2048,1024]{1,0:T(8,128)(2,1)} %copy-done.74, pred[2048]{0:T(1024)(128)(4,1)S(1)} %dynamic-update-slice.65, bf16[512,1024]{1,0:T(8,128)(2,1)} %collective-permute-done.30.rows_b, bf16[512,1024]{1,0:T(8,128)(2,1)} %collective-permute-done.29.rows_a, bf16[512,1024]{1,0:T(8,128)(2,1)} %copy-done.28, ...), kind=kOutput, calls=%fused_computation.54 | convolution fusion | flops 4314890240 | bytes 10487808 | tf_op jit(solution)/shard_map/dot_general | solution.py:54
  284.1 6.5 %fusion.30 = bf16[1024,1024]{1,0:T(8,128)(2,1)S(1)} fusion(bf16[2048,1024]{1,0:T(8,128)(2,1)S(1)} %copy-done.75, pred[2048]{0:T(1024)(128)(4,1)S(1)} %not.15, bf16[512,1024]{1,0:T(8,128)(2,1)} %collective-permute-done.30.rows_b, bf16[512,1024]{1,0:T(8,128)(2,1)} %collective-permute-done.29.rows_a, bf16[512,1024]{1,0:T(8,128)(2,1)S(1)} %copy-done.29, ...), kind=kOutput, calls=%fused_computation.55 | convolution fusion | flops 4314890240 | bytes 10487808 | tf_op jit(solution)/shard_map/dot_general | solution.py:54
  291.8 7.1 %fusion.33 = bf16[1024,1024]{1,0:T(8,128)(2,1)S(1)} fusion(bf16[2048,1024]{1,0:T(8,128)(2,1)S(1)} %copy-done.43, pred[2048]{0:T(1024)(128)(4,1)S(1)} %dynamic-update-slice.65, bf16[512,1024]{1,0:T(8,128)(2,1)S(1)} %copy-done.27, bf16[512,1024]{1,0:T(8,128)(2,1)} %collective-permute-done.20.rows_a, bf16[512,1024]{1,0:T(8,128)(2,1)} %collective-permute-done.15.rows_b, ...), kind=kOutput, calls=%fused_computation.56 | convolution fusion | flops 4314890240 | bytes 10487808 | tf_op jit(solution)/shard_map/dot_general | solution.py:54
  299.9 6.6 %fusion.36 = bf16[1024,1024]{1,0:T(8,128)(2,1)S(1)} fusion(bf16[2048,1024]{1,0:T(8,128)(2,1)S(1)} %copy-done.43, pred[2048]{0:T(1024)(128)(4,1)S(1)} %not.15, bf16[512,1024]{1,0:T(8,128)(2,1)S(1)} %copy-done.27, bf16[512,1024]{1,0:T(8,128)(2,1)} %collective-permute-done.20.rows_a, bf16[512,1024]{1,0:T(8,128)(2,1)} %collective-permute-done.15.rows_b, ...), kind=kOutput, calls=%fused_computation.57 | convolution fusion | flops 4314890240 | bytes 10487808 | tf_op jit(solution)/shard_map/dot_general | solution.py:54
  307.4 8.3 %collective-permute-done.34 = bf16[2,1,256,1024]{3,2,1,0:T(8,128)(2,1)S(1)} collective-permute-done((bf16[2,1,256,1024]{3,2,1,0:T(8,128)(2,1)S(1)}, bf16[2,1,256,1024]{3,2,1,0:T(8,128)(2,1)S(1)}, u32[]{:S(2)}, u32[]{:S(2)}) %collective-permute-start.34) | collective-permute-done | bytes 1048608 | tf_op jit(solution)/shard_map/ppermute | solution.py:84
  318.6 2.9 multiply_reduce_fusion
  335.3 6.5 %collective-permute-done.42 = bf16[2,4,64,1024]{3,2,1,0:T(8,128)(2,1)S(1)} collective-permute-done((bf16[2,4,64,1024]{3,2,1,0:T(8,128)(2,1)S(1)}, bf16[2,4,64,1024]{3,2,1,0:T(8,128)(2,1)S(1)}, u32[]{:S(2)}, u32[]{:S(2)}) %collective-permute-start.42) | collective-permute-done | bytes 1048608 | tf_op jit(solution)/shard_map/ppermute | solution.py:84
  343.4 6.1 %collective-permute-done.40.g3 = bf16[512,256]{1,0:T(8,128)(2,1)S(1)} collective-permute-done((bf16[512,256]{1,0:T(8,128)(2,1)S(1)}, bf16[512,256]{1,0:T(8,128)(2,1)S(1)}, u32[]{:S(2)}, u32[]{:S(2)}) %collective-permute-start.40) | collective-permute-done | bytes 262176 | tf_op jit(solution)/shard_map/ppermute | solution.py:62
  360.0 22.9 %attend_back.2 = bf16[2048,384]{1,0:T(8,128)(2,1)S(1)} custom-call(s32[3]{0:T(128)S(1)} %pad_add_fusion.facts, bf16[1024,768]{1,0:T(8,128)(2,1)S(1)} %get-tuple-element.176.near, bf16[1024,768]{1,0:T(8,128)(2,1)} %copy-done.5, bf16[2048,256]{1,0:T(8,128)(2,1)S(1)} %copy-done.7, bf16[512,256]{1,0:T(8,128)(2,1)S(1)} %convolution_convert_fusion.11.g0, ...), custom_call_target="tpu_custom_call" | custom-call | flops 1048576 | bytes 65536 | tf_op jit(solution)/shard_map/attend_back/pallas_call | solution.py:414
  389.6 2.5 collective-permute-start.44
  392.2 30.1 %collective-permute-done.45 = bf16[2,1,256,1024]{3,2,1,0:T(8,128)(2,1)} collective-permute-done((bf16[2,1,256,1024]{3,2,1,0:T(8,128)(2,1)}, bf16[2,1,256,1024]{3,2,1,0:T(8,128)(2,1)}, u32[]{:S(2)}, u32[]{:S(2)}) %collective-permute-start.45) | collective-permute-done | bytes 1048608 | tf_op jit(solution)/shard_map/ppermute | solution.py:84
  424.6 23.0 %attend_back.3 = bf16[2048,384]{1,0:T(8,128)(2,1)S(1)} custom-call(s32[3]{0:T(128)S(1)} %pad_add_fusion.facts, bf16[1024,768]{1,0:T(8,128)(2,1)S(1)} %get-tuple-element.176.near, bf16[1024,768]{1,0:T(8,128)(2,1)} %copy-done.5, bf16[2048,256]{1,0:T(8,128)(2,1)S(1)} %copy-done.7, bf16[512,256]{1,0:T(8,128)(2,1)S(1)} %convolution_convert_fusion.11.g0, ...), custom_call_target="tpu_custom_call" | custom-call | flops 1048576 | bytes 65536 | tf_op jit(solution)/shard_map/attend_back/pallas_call | solution.py:414
  449.5 5.9 collective-permute-done.46.refs_1_
  480.4 17.3 %collective-permute-done.56 = bf16[2,512,256]{2,1,0:T(8,128)(2,1)S(1)} collective-permute-done((bf16[2,512,256]{2,1,0:T(8,128)(2,1)S(1)}, bf16[2,512,256]{2,1,0:T(8,128)(2,1)S(1)}, u32[]{:S(2)}, u32[]{:S(2)}) %collective-permute-start.56) | collective-permute-done | bytes 524320 | tf_op jit(solution)/shard_map/ppermute | solution.py:84
  501.7 5.1 place_experts.2
  506.8 7.3 %collective-permute-done.61 = bf16[512,256]{1,0:T(8,128)(2,1)S(1)} collective-permute-done((bf16[512,256]{1,0:T(8,128)(2,1)S(1)}, bf16[512,256]{1,0:T(8,128)(2,1)S(1)}, u32[]{:S(2)}, u32[]{:S(2)}) %collective-permute-start.61) | collective-permute-done | bytes 262176 | tf_op jit(solution)/shard_map/ppermute | solution.py:84
  523.1 16.4 %collective-permute-done.64 = bf16[512,1024]{1,0:T(8,128)(2,1)S(1)} collective-permute-done((bf16[512,1024]{1,0:T(8,128)(2,1)S(1)}, bf16[512,1024]{1,0:T(8,128)(2,1)S(1)}, u32[]{:S(2)}, u32[]{:S(2)}) %collective-permute-start.64) | collective-permute-done | bytes 1048608 | tf_op jit(solution)/shard_map/ppermute | solution.py:62
  543.9 4.9 fusion.20
  552.6 3.7 collective-permute-done.69
  556.8 4.2 collective-permute-done.70
  561.7 3.3 collective-permute-done.73
  566.8 7.9 %place_experts.3 = f32[2,256,4096]{2,1,0:T(8,128)} custom-call(s32[9]{0:T(128)S(1)} %concatenate.278.facts, bf16[4,64,1024]{2,1,0:T(8,128)(2,1)S(1)} %get-tuple-element.272.refs_0_, bf16[4,64,1024]{2,1,0:T(8,128)(2,1)S(1)} %collective-permute-done.55.refs_1_, bf16[2,4,64,1024]{3,2,1,0:T(8,128)(2,1)} %collective-permute-done.75.refs_2_, ...), custom_call_target="tpu_custom_call" | custom-call | flops 1048576 | bytes 65536 | tf_op jit(solution)/shard_map/place_experts/pallas_call | solution.py:594
  580.0 8.5 %collective-permute-done.79.refs_5_ = bf16[2,512,256]{2,1,0:T(8,128)(2,1)S(1)} collective-permute-done((bf16[2,512,256]{2,1,0:T(8,128)(2,1)S(1)}, bf16[2,512,256]{2,1,0:T(8,128)(2,1)S(1)}, u32[]{:S(2)}, u32[]{:S(2)}) %collective-permute-start.79) | collective-permute-done | bytes 524320 | tf_op jit(solution)/shard_map/ppermute | solution.py:84
  590.6 2.9 place_attention.1
  (644 shorter events, 171.9 us)
Async XLA Ops:
  7.2 138.8 %all-gather.3.cloned.1.call-start = ((), (), s32[]{:S(2)}) async-start(), calls=%async_computation | async-start | bytes 4718592 | tf_op jit(solution)/shard_map/all_gather | solution.py:741
  7.2 27.3 %collective-permute-start = (bf16[512,1024]{1,0:T(8,128)(2,1)}, bf16[512,1024]{1,0:T(8,128)(2,1)}, u32[]{:S(2)}, u32[]{:S(2)}) collective-permute-start(bf16[512,1024]{1,0:T(8,128)(2,1)} %tok_a.1), channel_id=1, source_target_pairs={{0,2},{1,3},{2,0},{3,1},{4,6},{5,7},{6,4},{7,5},{8,10},{9,11},{10,... | collective-permute-start | bytes 3145736 | tf_op jit(solution)/shard_map/ppermute | solution.py:62
  17.7 32.7 %collective-permute-start.4 = (bf16[2,264,768]{2,1,0:T(8,128)(2,1)}, bf16[2,264,768]{2,1,0:T(8,128)(2,1)}, u32[]{:S(2)}, u32[]{:S(2)}) collective-permute-start(bf16[2,264,768]{2,1,0:T(8,128)(2,1)} %pad_maximum_fusion.15), channel_id=1, source_target_pairs={{0,3},{1,2},{2,1},{3,0},{4,7},{5,6},{6,5},{7,4},{8,11},{9,10},{10,... | collective-permute-start | bytes 2433032 | tf_op jit(solution)/shard_map/ppermute | solution.py:62
  17.7 42.5 %collective-permute-start.2 = (bf16[512,1024]{1,0:T(8,128)(2,1)S(1)}, bf16[512,1024]{1,0:T(8,128)(2,1)}, u32[]{:S(2)}, u32[]{:S(2)}) collective-permute-start(bf16[512,1024]{1,0:T(8,128)(2,1)S(1)} %copy-done.4), channel_id=1, source_target_pairs={{0,1},{1,0},{2,3},{3,2},{4,5},{5,4},{6,7},{7,6},{8,9},{9,8},{10,11... | collective-permute-start | bytes 3145736 | tf_op jit(solution)/shard_map/ppermute | solution.py:62
  17.9 41.6 %collective-permute-start.3 = (bf16[264,768]{1,0:T(8,128)(2,1)}, bf16[264,768]{1,0:T(8,128)(2,1)S(1)}, u32[]{:S(2)}, u32[]{:S(2)}) collective-permute-start(bf16[264,768]{1,0:T(8,128)(2,1)} %get-tuple-element.409), channel_id=1, source_target_pairs={{0,1},{1,0},{2,3},{3,2},{4,5},{5,4},{6,7},{7,6},{8,9},{9,8},{10,11... | collective-permute-start | bytes 1216520 | tf_op jit(solution)/shard_map/ppermute | solution.py:62
  34.6 19.7 %collective-permute-start.1 = (bf16[512,1024]{1,0:T(8,128)(2,1)}, bf16[512,1024]{1,0:T(8,128)(2,1)S(1)}, u32[]{:S(2)}, u32[]{:S(2)}) collective-permute-start(bf16[512,1024]{1,0:T(8,128)(2,1)} %collective-permute-done.tok_a), channel_id=1, source_target_pairs={{0,1},{1,0},{2,3},{3,2},{4,5},{5,4},{6,7},{7,6},{8,9},{9,8},{10,11... | collective-permute-start | bytes 3145736 | tf_op jit(solution)/shard_map/ppermute | solution.py:62
  70.9 42.9 %collective-permute-start.13 = (bf16[256,1024]{1,0:T(8,128)(2,1)}, bf16[256,1024]{1,0:T(8,128)(2,1)S(1)}, u32[]{:S(2)}, u32[]{:S(2)}) collective-permute-start(bf16[256,1024]{1,0:T(8,128)(2,1)} %param.28), channel_id=1, source_target_pairs={{0,2},{1,3},{2,0},{3,1},{4,6},{5,7},{6,4},{7,5},{8,10},{9,11},{10,... | collective-permute-start | bytes 1572872 | tf_op jit(solution)/shard_map/ppermute | solution.py:62
  72.4 56.0 %collective-permute-start.7 = (bf16[256,1024]{1,0:T(8,128)(2,1)}, bf16[256,1024]{1,0:T(8,128)(2,1)S(1)}, u32[]{:S(2)}, u32[]{:S(2)}) collective-permute-start(bf16[256,1024]{1,0:T(8,128)(2,1)} %param.28), channel_id=1, source_target_pairs={{0,1},{1,0},{2,3},{3,2},{4,5},{5,4},{6,7},{7,6},{8,9},{9,8},{10,11... | collective-permute-start | bytes 1572872 | tf_op jit(solution)/shard_map/ppermute | solution.py:62
  81.7 32.6 %collective-permute-start.12 = (f32[2,128]{1,0:T(2,128)S(1)}, f32[2,128]{1,0:T(2,128)S(1)}, u32[]{:S(2)}, u32[]{:S(2)}) collective-permute-start(f32[2,128]{1,0:T(2,128)S(1)} %broadcast_in_dim.123), channel_id=1, source_target_pairs={{0,3},{1,2},{2,1},{3,0},{4,7},{5,6},{6,5},{7,4},{8,11},{9,10},{10,... | collective-permute-start | bytes 3080 | tf_op jit(solution)/shard_map/ppermute | solution.py:62
  82.0 33.9 %collective-permute-start.11 = (f32[2,128]{1,0:T(2,128)S(1)}, f32[2,128]{1,0:T(2,128)S(1)}, u32[]{:S(2)}, u32[]{:S(2)}) collective-permute-start(f32[2,128]{1,0:T(2,128)S(1)} %broadcast_in_dim.123), channel_id=1, source_target_pairs={{0,2},{1,3},{2,0},{3,1},{4,6},{5,7},{6,4},{7,5},{8,10},{9,11},{10,... | collective-permute-start | bytes 3080 | tf_op jit(solution)/shard_map/ppermute | solution.py:62
  83.5 32.5 %collective-permute-start.10 = (f32[2,128]{1,0:T(2,128)S(1)}, f32[2,128]{1,0:T(2,128)S(1)}, u32[]{:S(2)}, u32[]{:S(2)}) collective-permute-start(f32[2,128]{1,0:T(2,128)S(1)} %broadcast_in_dim.123), channel_id=1, source_target_pairs={{0,1},{1,0},{2,3},{3,2},{4,5},{5,4},{6,7},{7,6},{8,9},{9,8},{10,11... | collective-permute-start | bytes 3080 | tf_op jit(solution)/shard_map/ppermute | solution.py:62
  132.2 16.8 %collective-permute-start.15 = (bf16[512,1024]{1,0:T(8,128)(2,1)}, bf16[512,1024]{1,0:T(8,128)(2,1)}, u32[]{:S(2)}, u32[]{:S(2)}) collective-permute-start(bf16[512,1024]{1,0:T(8,128)(2,1)} %convolution_convert_fusion.1.rows_a), channel_id=1, source_target_pairs={{0,1},{1,0},{2,3},{3,2},{4,5},{5,4},{6,7},{7,6},{8,9},{9,8},{10,11... | collective-permute-start | bytes 3145736 | tf_op jit(solution)/shard_map/ppermute | solution.py:62
  132.2 30.0 %collective-permute-start.20 = (bf16[512,1024]{1,0:T(8,128)(2,1)}, bf16[512,1024]{1,0:T(8,128)(2,1)}, u32[]{:S(2)}, u32[]{:S(2)}) collective-permute-start(bf16[512,1024]{1,0:T(8,128)(2,1)} %convolution_convert_fusion.1.rows_a), channel_id=1, source_target_pairs={{0,2},{1,3},{2,0},{3,1},{4,6},{5,7},{6,4},{7,5},{8,10},{9,11},{10,... | collective-permute-start | bytes 3145736 | tf_op jit(solution)/shard_map/ppermute | solution.py:62
  177.7 16.2 %collective-permute-start.19 = (bf16[512,1024]{1,0:T(8,128)(2,1)S(1)}, bf16[512,1024]{1,0:T(8,128)(2,1)S(1)}, u32[]{:S(2)}, u32[]{:S(2)}) collective-permute-start(bf16[512,1024]{1,0:T(8,128)(2,1)S(1)} %get-tuple-element.138), channel_id=1, source_target_pairs={{0,1},{1,0},{2,3},{3,2},{4,5},{5,4},{6,7},{7,6},{8,9},{9,8},{10,11... | collective-permute-start | bytes 3145736 | tf_op jit(solution)/shard_map/ppermute | solution.py:62
  180.6 25.3 %collective-permute-start.23 = (bf16[512,1024]{1,0:T(8,128)(2,1)S(1)}, bf16[512,1024]{1,0:T(8,128)(2,1)S(1)}, u32[]{:S(2)}, u32[]{:S(2)}) collective-permute-start(bf16[512,1024]{1,0:T(8,128)(2,1)S(1)} %add_convert_fusion.8), channel_id=1, source_target_pairs={{0,2},{1,3},{2,0},{3,1},{4,6},{5,7},{6,4},{7,5},{8,10},{9,11},{10,... | collective-permute-start | bytes 3145736 | tf_op jit(solution)/shard_map/ppermute | solution.py:62
  209.0 25.7 %collective-permute-start.29 = (bf16[512,1024]{1,0:T(8,128)(2,1)S(1)}, bf16[512,1024]{1,0:T(8,128)(2,1)}, u32[]{:S(2)}, u32[]{:S(2)}) collective-permute-start(bf16[512,1024]{1,0:T(8,128)(2,1)S(1)} %convolution_convert_fusion.rows_a), channel_id=1, source_target_pairs={{0,2},{1,3},{2,0},{3,1},{4,6},{5,7},{6,4},{7,5},{8,10},{9,11},{10,... | collective-permute-start | bytes 3145736 | tf_op jit(solution)/shard_map/ppermute | solution.py:62
  258.3 58.9 %collective-permute-start.28 = (bf16[512,1024]{1,0:T(8,128)(2,1)}, bf16[512,1024]{1,0:T(8,128)(2,1)}, u32[]{:S(2)}, u32[]{:S(2)}) collective-permute-start(bf16[512,1024]{1,0:T(8,128)(2,1)} %get-tuple-element.144), channel_id=1, source_target_pairs={{0,1},{1,0},{2,3},{3,2},{4,5},{5,4},{6,7},{7,6},{8,9},{9,8},{10,11... | collective-permute-start | bytes 3145736 | tf_op jit(solution)/shard_map/ppermute | solution.py:62
  270.9 46.3 %collective-permute-start.32 = (bf16[512,1024]{1,0:T(8,128)(2,1)}, bf16[512,1024]{1,0:T(8,128)(2,1)}, u32[]{:S(2)}, u32[]{:S(2)}) collective-permute-start(bf16[512,1024]{1,0:T(8,128)(2,1)} %add_convert_fusion.6), channel_id=1, source_target_pairs={{0,2},{1,3},{2,0},{3,1},{4,6},{5,7},{6,4},{7,5},{8,10},{9,11},{10,... | collective-permute-start | bytes 3145736 | tf_op jit(solution)/shard_map/ppermute | solution.py:62
  282.8 33.8 %collective-permute-start.33 = (bf16[2,1,256,1024]{3,2,1,0:T(8,128)(2,1)S(1)}, bf16[2,1,256,1024]{3,2,1,0:T(8,128)(2,1)S(1)}, u32[]{:S(2)}, u32[]{:S(2)}) collective-permute-start(bf16[2,1,256,1024]{3,2,1,0:T(8,128)(2,1)S(1)} %pad_maximum_fusion.4), channel_id=1, source_target_pairs={{0,4},{4,0},{8,12},{12,8},{16,20},{20,16},{24,28},{28,24},{1,5},{5... | collective-permute-start | bytes 3145736 | tf_op jit(solution)/shard_map/ppermute | solution.py:84
  290.8 24.9 %collective-permute-start.34 = (bf16[2,1,256,1024]{3,2,1,0:T(8,128)(2,1)S(1)}, bf16[2,1,256,1024]{3,2,1,0:T(8,128)(2,1)S(1)}, u32[]{:S(2)}, u32[]{:S(2)}) collective-permute-start(bf16[2,1,256,1024]{3,2,1,0:T(8,128)(2,1)S(1)} %pad_maximum_fusion.5), channel_id=1, source_target_pairs={{0,8},{4,12},{8,0},{12,4},{16,24},{20,28},{24,16},{28,20},{1,9},{5... | collective-permute-start | bytes 3145736 | tf_op jit(solution)/shard_map/ppermute | solution.py:84
  299.1 34.5 %collective-permute-start.35 = (bf16[2,4,64,1024]{3,2,1,0:T(8,128)(2,1)S(1)}, bf16[2,4,64,1024]{3,2,1,0:T(8,128)(2,1)S(1)}, u32[]{:S(2)}, u32[]{:S(2)}) collective-permute-start(bf16[2,4,64,1024]{3,2,1,0:T(8,128)(2,1)S(1)} %pad_maximum_fusion.6), channel_id=1, source_target_pairs={{0,4},{4,0},{8,12},{12,8},{16,20},{20,16},{24,28},{28,24},{1,5},{5... | collective-permute-start | bytes 3145736 | tf_op jit(solution)/shard_map/ppermute | solution.py:84
  315.7 26.1 %collective-permute-start.42 = (bf16[2,4,64,1024]{3,2,1,0:T(8,128)(2,1)S(1)}, bf16[2,4,64,1024]{3,2,1,0:T(8,128)(2,1)S(1)}, u32[]{:S(2)}, u32[]{:S(2)}) collective-permute-start(bf16[2,4,64,1024]{3,2,1,0:T(8,128)(2,1)S(1)} %pad_maximum_fusion.7), channel_id=1, source_target_pairs={{0,8},{4,12},{8,0},{12,4},{16,24},{20,28},{24,16},{28,20},{1,9},{5... | collective-permute-start | bytes 3145736 | tf_op jit(solution)/shard_map/ppermute | solution.py:84
  324.6 26.2 %collective-permute-start.36 = (bf16[1,256,1024]{2,1,0:T(8,128)(2,1)S(1)}, bf16[1,256,1024]{2,1,0:T(8,128)(2,1)S(1)}, u32[]{:S(2)}, u32[]{:S(2)}) collective-permute-start(bf16[1,256,1024]{2,1,0:T(8,128)(2,1)S(1)} %fusion.47), channel_id=1, source_target_pairs={{0,8},{4,12},{8,0},{12,4},{16,24},{20,28},{24,16},{28,20},{1,9},{5... | collective-permute-start | bytes 1572872 | tf_op jit(solution)/shard_map/ppermute | solution.py:84
  326.3 16.4 %collective-permute-start.38 = (bf16[512,256]{1,0:T(8,128)(2,1)S(1)}, bf16[512,256]{1,0:T(8,128)(2,1)S(1)}, u32[]{:S(2)}, u32[]{:S(2)}) collective-permute-start(bf16[512,256]{1,0:T(8,128)(2,1)S(1)} %convolution_convert_fusion.10), channel_id=1, source_target_pairs={{0,1},{1,0},{2,3},{3,2},{4,5},{5,4},{6,7},{7,6},{8,9},{9,8},{10,11... | collective-permute-start | bytes 786440 | tf_op jit(solution)/shard_map/ppermute | solution.py:62
  326.4 17.0 %collective-permute-start.39 = (bf16[512,256]{1,0:T(8,128)(2,1)S(1)}, bf16[512,256]{1,0:T(8,128)(2,1)S(1)}, u32[]{:S(2)}, u32[]{:S(2)}) collective-permute-start(bf16[512,256]{1,0:T(8,128)(2,1)S(1)} %convolution_convert_fusion.9), channel_id=1, source_target_pairs={{0,2},{1,3},{2,0},{3,1},{4,6},{5,7},{6,4},{7,5},{8,10},{9,11},{10,... | collective-permute-start | bytes 786440 | tf_op jit(solution)/shard_map/ppermute | solution.py:62
  333.6 17.3 %collective-permute-start.37 = (bf16[1,256,1024]{2,1,0:T(8,128)(2,1)S(1)}, bf16[1,256,1024]{2,1,0:T(8,128)(2,1)S(1)}, u32[]{:S(2)}, u32[]{:S(2)}) collective-permute-start(bf16[1,256,1024]{2,1,0:T(8,128)(2,1)S(1)} %fusion.46), channel_id=1, source_target_pairs={{0,4},{4,0},{8,12},{12,8},{16,20},{20,16},{24,28},{28,24},{1,5},{5... | collective-permute-start | bytes 1572872 | tf_op jit(solution)/shard_map/ppermute | solution.py:84
  342.7 40.2 %collective-permute-start.47 = (bf16[256,1024]{1,0:T(8,128)(2,1)}, bf16[256,1024]{1,0:T(8,128)(2,1)}, u32[]{:S(2)}, u32[]{:S(2)}) collective-permute-start(bf16[256,1024]{1,0:T(8,128)(2,1)} %convolution_convert_fusion.4), channel_id=1, source_target_pairs={{0,1},{1,0},{2,3},{3,2},{4,5},{5,4},{6,7},{7,6},{8,9},{9,8},{10,11... | collective-permute-start | bytes 1572872 | tf_op jit(solution)/shard_map/ppermute | solution.py:62
  352.6 69.7 %collective-permute-start.45 = (bf16[2,1,256,1024]{3,2,1,0:T(8,128)(2,1)}, bf16[2,1,256,1024]{3,2,1,0:T(8,128)(2,1)}, u32[]{:S(2)}, u32[]{:S(2)}) collective-permute-start(bf16[2,1,256,1024]{3,2,1,0:T(8,128)(2,1)} %pad_maximum_fusion.8), channel_id=1, source_target_pairs={{0,16},{4,20},{8,24},{12,28},{16,0},{20,4},{24,8},{28,12},{1,17},{... | collective-permute-start | bytes 3145736 | tf_op jit(solution)/shard_map/ppermute | solution.py:84
  355.2 31.3 %collective-permute-start.41 = (bf16[4,64,1024]{2,1,0:T(8,128)(2,1)}, bf16[4,64,1024]{2,1,0:T(8,128)(2,1)}, u32[]{:S(2)}, u32[]{:S(2)}) collective-permute-start(bf16[4,64,1024]{2,1,0:T(8,128)(2,1)} %fusion.42), channel_id=1, source_target_pairs={{0,8},{4,12},{8,0},{12,4},{16,24},{20,28},{24,16},{28,20},{1,9},{5... | collective-permute-start | bytes 1572872 | tf_op jit(solution)/shard_map/ppermute | solution.py:84
  356.7 28.1 %collective-permute-start.43 = (bf16[4,64,1024]{2,1,0:T(8,128)(2,1)}, bf16[4,64,1024]{2,1,0:T(8,128)(2,1)}, u32[]{:S(2)}, u32[]{:S(2)}) collective-permute-start(bf16[4,64,1024]{2,1,0:T(8,128)(2,1)} %fusion.41), channel_id=1, source_target_pairs={{0,4},{4,0},{8,12},{12,8},{16,20},{20,16},{24,28},{28,24},{1,5},{5... | collective-permute-start | bytes 1572872 | tf_op jit(solution)/shard_map/ppermute | solution.py:84
  357.7 89.9 %collective-permute-start.50 = (bf16[256,1024]{1,0:T(8,128)(2,1)}, bf16[256,1024]{1,0:T(8,128)(2,1)S(1)}, u32[]{:S(2)}, u32[]{:S(2)}) collective-permute-start(bf16[256,1024]{1,0:T(8,128)(2,1)} %convolution_convert_fusion.6), channel_id=1, source_target_pairs={{0,1},{1,0},{2,3},{3,2},{4,5},{5,4},{6,7},{7,6},{8,9},{9,8},{10,11... | collective-permute-start | bytes 1572872 | tf_op jit(solution)/shard_map/ppermute | solution.py:62
  384.2 63.4 %collective-permute-start.51 = (bf16[256,1024]{1,0:T(8,128)(2,1)S(1)}, bf16[256,1024]{1,0:T(8,128)(2,1)S(1)}, u32[]{:S(2)}, u32[]{:S(2)}) collective-permute-start(bf16[256,1024]{1,0:T(8,128)(2,1)S(1)} %add_convert_fusion.17), channel_id=1, source_target_pairs={{0,2},{1,3},{2,0},{3,1},{4,6},{5,7},{6,4},{7,5},{8,10},{9,11},{10,... | collective-permute-start | bytes 1572872 | tf_op jit(solution)/shard_map/ppermute | solution.py:62
  389.6 66.0 %collective-permute-start.44 = (bf16[2,4,64,1024]{3,2,1,0:T(8,128)(2,1)S(1)}, bf16[2,4,64,1024]{3,2,1,0:T(8,128)(2,1)S(1)}, u32[]{:S(2)}, u32[]{:S(2)}) collective-permute-start(bf16[2,4,64,1024]{3,2,1,0:T(8,128)(2,1)S(1)} %pad_maximum_fusion.9), channel_id=1, source_target_pairs={{0,16},{4,20},{8,24},{12,28},{16,0},{20,4},{24,8},{28,12},{1,17},{... | collective-permute-start | bytes 3145736 | tf_op jit(solution)/shard_map/ppermute | solution.py:84
  423.8 31.6 %collective-permute-start.46 = (bf16[1,256,1024]{2,1,0:T(8,128)(2,1)S(1)}, bf16[1,256,1024]{2,1,0:T(8,128)(2,1)S(1)}, u32[]{:S(2)}, u32[]{:S(2)}) collective-permute-start(bf16[1,256,1024]{2,1,0:T(8,128)(2,1)S(1)} %add_convert_fusion.18.refs_0_), channel_id=1, source_target_pairs={{0,8},{4,12},{8,0},{12,4},{16,24},{20,28},{24,16},{28,20},{1,9},{5... | collective-permute-start | bytes 1572872 | tf_op jit(solution)/shard_map/ppermute | solution.py:84
  424.1 31.3 %collective-permute-start.48 = (bf16[1,256,1024]{2,1,0:T(8,128)(2,1)S(1)}, bf16[1,256,1024]{2,1,0:T(8,128)(2,1)S(1)}, u32[]{:S(2)}, u32[]{:S(2)}) collective-permute-start(bf16[1,256,1024]{2,1,0:T(8,128)(2,1)S(1)} %add_convert_fusion.16.refs_3_), channel_id=1, source_target_pairs={{0,4},{4,0},{8,12},{12,8},{16,20},{20,16},{24,28},{28,24},{1,5},{5... | collective-permute-start | bytes 1572872 | tf_op jit(solution)/shard_map/ppermute | solution.py:84
  460.4 41.0 %collective-permute-start.58 = (bf16[2,1,256,1024]{3,2,1,0:T(8,128)(2,1)S(1)}, bf16[2,1,256,1024]{3,2,1,0:T(8,128)(2,1)S(1)}, u32[]{:S(2)}, u32[]{:S(2)}) collective-permute-start(bf16[2,1,256,1024]{3,2,1,0:T(8,128)(2,1)S(1)} %pad_maximum_fusion.10), channel_id=1, source_target_pairs={{0,4},{4,0},{8,12},{12,8},{16,20},{20,16},{24,28},{28,24},{1,5},{5... | collective-permute-start | bytes 3145736 | tf_op jit(solution)/shard_map/ppermute | solution.py:84
  461.1 38.5 %collective-permute-start.60 = (bf16[2,1,256,1024]{3,2,1,0:T(8,128)(2,1)S(1)}, bf16[2,1,256,1024]{3,2,1,0:T(8,128)(2,1)S(1)}, u32[]{:S(2)}, u32[]{:S(2)}) collective-permute-start(bf16[2,1,256,1024]{3,2,1,0:T(8,128)(2,1)S(1)} %pad_maximum_fusion.11), channel_id=1, source_target_pairs={{0,8},{4,12},{8,0},{12,4},{16,24},{20,28},{24,16},{28,20},{1,9},{5... | collective-permute-start | bytes 3145736 | tf_op jit(solution)/shard_map/ppermute | solution.py:84
  461.1 16.9 %collective-permute-start.52 = (bf16[128,1024]{1,0:T(8,128)(2,1)S(1)}, bf16[128,1024]{1,0:T(8,128)(2,1)S(1)}, u32[]{:S(2)}, u32[]{:S(2)}) collective-permute-start(bf16[128,1024]{1,0:T(8,128)(2,1)S(1)} %pad_maximum_fusion.29), channel_id=1, source_target_pairs={{0,1},{1,0},{2,3},{3,2},{4,5},{5,4},{6,7},{7,6},{8,9},{9,8},{10,11... | collective-permute-start | bytes 786440 | tf_op jit(solution)/shard_map/ppermute | solution.py:62
  472.4 25.3 %collective-permute-start.56 = (bf16[2,512,256]{2,1,0:T(8,128)(2,1)S(1)}, bf16[2,512,256]{2,1,0:T(8,128)(2,1)S(1)}, u32[]{:S(2)}, u32[]{:S(2)}) collective-permute-start(bf16[2,512,256]{2,1,0:T(8,128)(2,1)S(1)} %pad_maximum_fusion.22), channel_id=1, source_target_pairs={{0,4},{4,0},{8,12},{12,8},{16,20},{20,16},{24,28},{28,24},{1,5},{5... | collective-permute-start | bytes 1572872 | tf_op jit(solution)/shard_map/ppermute | solution.py:84
  476.0 21.7 %collective-permute-start.59 = (bf16[2,512,256]{2,1,0:T(8,128)(2,1)S(1)}, bf16[2,512,256]{2,1,0:T(8,128)(2,1)S(1)}, u32[]{:S(2)}, u32[]{:S(2)}) collective-permute-start(bf16[2,512,256]{2,1,0:T(8,128)(2,1)S(1)} %pad_maximum_fusion.23), channel_id=1, source_target_pairs={{0,8},{4,12},{8,0},{12,4},{16,24},{20,28},{24,16},{28,20},{1,9},{5... | collective-permute-start | bytes 1572872 | tf_op jit(solution)/shard_map/ppermute | solution.py:84
  478.8 38.7 %collective-permute-start.62 = (bf16[4,64,1024]{2,1,0:T(8,128)(2,1)S(1)}, bf16[4,64,1024]{2,1,0:T(8,128)(2,1)S(1)}, u32[]{:S(2)}, u32[]{:S(2)}) collective-permute-start(bf16[4,64,1024]{2,1,0:T(8,128)(2,1)S(1)} %get-tuple-element.271.refs_3_), channel_id=1, source_target_pairs={{0,4},{4,0},{8,12},{12,8},{16,20},{20,16},{24,28},{28,24},{1,5},{5... | collective-permute-start | bytes 1572872 | tf_op jit(solution)/shard_map/ppermute | solution.py:84
  497.8 18.6 %collective-permute-start.57 = (bf16[512,256]{1,0:T(8,128)(2,1)S(1)}, bf16[512,256]{1,0:T(8,128)(2,1)S(1)}, u32[]{:S(2)}, u32[]{:S(2)}) collective-permute-start(bf16[512,256]{1,0:T(8,128)(2,1)S(1)} %add_convert_fusion.29), channel_id=1, source_target_pairs={{0,8},{4,12},{8,0},{12,4},{16,24},{20,28},{24,16},{28,20},{1,9},{5... | collective-permute-start | bytes 786440 | tf_op jit(solution)/shard_map/ppermute | solution.py:84
  499.6 17.9 %collective-permute-start.55 = (bf16[4,64,1024]{2,1,0:T(8,128)(2,1)S(1)}, bf16[4,64,1024]{2,1,0:T(8,128)(2,1)S(1)}, u32[]{:S(2)}, u32[]{:S(2)}) collective-permute-start(bf16[4,64,1024]{2,1,0:T(8,128)(2,1)S(1)} %get-tuple-element.272.refs_0_), channel_id=1, source_target_pairs={{0,8},{4,12},{8,0},{12,4},{16,24},{20,28},{24,16},{28,20},{1,9},{5... | collective-permute-start | bytes 1572872 | tf_op jit(solution)/shard_map/ppermute | solution.py:84
  501.4 38.0 %collective-permute-start.63 = (bf16[512,1024]{1,0:T(8,128)(2,1)S(1)}, bf16[512,1024]{1,0:T(8,128)(2,1)S(1)}, u32[]{:S(2)}, u32[]{:S(2)}) collective-permute-start(bf16[512,1024]{1,0:T(8,128)(2,1)S(1)} %add_convert_fusion), channel_id=1, source_target_pairs={{0,1},{1,0},{2,3},{3,2},{4,5},{5,4},{6,7},{7,6},{8,9},{9,8},{10,11... | collective-permute-start | bytes 3145736 | tf_op jit(solution)/shard_map/ppermute | solution.py:62
  514.1 25.3 %collective-permute-start.64 = (bf16[512,1024]{1,0:T(8,128)(2,1)S(1)}, bf16[512,1024]{1,0:T(8,128)(2,1)S(1)}, u32[]{:S(2)}, u32[]{:S(2)}) collective-permute-start(bf16[512,1024]{1,0:T(8,128)(2,1)S(1)} %add_convert_fusion.2), channel_id=1, source_target_pairs={{0,2},{1,3},{2,0},{3,1},{4,6},{5,7},{6,4},{7,5},{8,10},{9,11},{10,... | collective-permute-start | bytes 3145736 | tf_op jit(solution)/shard_map/ppermute | solution.py:62
  517.5 31.9 %collective-permute-start.68 = (bf16[2,512,256]{2,1,0:T(8,128)(2,1)}, bf16[2,512,256]{2,1,0:T(8,128)(2,1)}, u32[]{:S(2)}, u32[]{:S(2)}) collective-permute-start(bf16[2,512,256]{2,1,0:T(8,128)(2,1)} %pad_maximum_fusion.24), channel_id=1, source_target_pairs={{0,16},{4,20},{8,24},{12,28},{16,0},{20,4},{24,8},{28,12},{1,17},{... | collective-permute-start | bytes 1572872 | tf_op jit(solution)/shard_map/ppermute | solution.py:84
  518.6 48.1 %collective-permute-start.76 = (bf16[2,4,64,1024]{3,2,1,0:T(8,128)(2,1)}, bf16[2,4,64,1024]{3,2,1,0:T(8,128)(2,1)}, u32[]{:S(2)}, u32[]{:S(2)}) collective-permute-start(bf16[2,4,64,1024]{3,2,1,0:T(8,128)(2,1)} %pad_maximum_fusion.14), channel_id=1, source_target_pairs={{0,8},{4,12},{8,0},{12,4},{16,24},{20,28},{24,16},{28,20},{1,9},{5... | collective-permute-start | bytes 3145736 | tf_op jit(solution)/shard_map/ppermute | solution.py:84
  521.8 44.9 %collective-permute-start.75 = (bf16[2,4,64,1024]{3,2,1,0:T(8,128)(2,1)}, bf16[2,4,64,1024]{3,2,1,0:T(8,128)(2,1)}, u32[]{:S(2)}, u32[]{:S(2)}) collective-permute-start(bf16[2,4,64,1024]{3,2,1,0:T(8,128)(2,1)} %pad_maximum_fusion.13), channel_id=1, source_target_pairs={{0,4},{4,0},{8,12},{12,8},{16,20},{20,16},{24,28},{28,24},{1,5},{5... | collective-permute-start | bytes 3145736 | tf_op jit(solution)/shard_map/ppermute | solution.py:84
  (135 other events, 1327.1 us)
Sparse Core Ops, SparseCore 0:
  71.0 74.9 all-gather.2

commit v5 on v4

--- a/solution.py
+++ b/solution.py
@@ -980,7 +980,9 @@
         sent = small
         bit *= 2
     sent = last_sum.step(sent)
-    in_grad = place_experts(me, experts_sum.finish(sent))
+    in_done = experts_sum.finish(sent)
+    sent = last_sum.step(in_done)
+    in_grad = place_experts(me, tie(in_done, sent))
     in_shift_grad = small[8:].reshape(EXPERTS, inner)
     qkv_grad, out_grad = place_attention(me, last_sum.finish(in_grad), shard_width)
     return (

time: 612 us -> 613 us (level)
  starting transfers between devices: 59.4 us -> 68.2 us
  waiting for transfers between devices: 212 us -> 205 us
    ppermute x33, waiting for transfers between devices: 105 us -> 96.5 us  [rep_swap(): return lax.ppermute(value, 'rep', [(i, i ^ mask) for i in range(count)])]
    ppermute x33, starting transfers between devices: 31 us -> 39.3 us  [rep_swap(): return lax.ppermute(value, 'rep', [(i, i ^ mask) for i in range(count)])]
  transfers between devices with their start and end apart: 81 -> 81, of which waited for: 33 -> 37; matrix products, arithmetic and copies ran while one was open for 20% -> 21% of each run, Pallas kernels for 20% -> 20%
where the time goes in v5:
time: 613 us; the launch traced here: 603 us
  waiting for transfers between devices  205 us (33%)
  Pallas kernels  152 us (25%)
  starting transfers between devices  68.2 us (11%)
  matrix products  58.6 us (10%)
  local copies, waits for them, and re-layouts  55.4 us (9%)
  other arithmetic  43.1 us (7%)
  between operations  21.2 us (3%)
    ppermute x33, waiting for transfers between devices, rep_swap(): return lax.ppermute(value, 'rep', [(i, i ^ mask) for i in range(count)])  96.5 us
    ppermute x47, waiting for transfers between devices, swap(): return lax.ppermute(value, 'shard', [(i, i ^ mask) for i in range(N_SHARD)])  95 us
    pallas_call x2, Pallas kernels, attend_back(): pl.pallas_call(functools.partial(attend_back_kernel, blocks, pair), out_s...  45.9 us
    dot_general x12, matrix products, dot_tn(): lax.dot_general(a, b, (((0,), (0,)), ((), ())), preferred_element_type=f32)  44.3 us
    ppermute x33, starting transfers between devices, rep_swap(): return lax.ppermute(value, 'rep', [(i, i ^ mask) for i in range(count)])  39.3 us
    pallas_call x1, Pallas kernels, attend(): pl.pallas_call(functools.partial(attend_kernel, blocks), out_shape=(jax.S...  29.2 us
    ppermute x47, starting transfers between devices, swap(): return lax.ppermute(value, 'shard', [(i, i ^ mask) for i in range(N_SHARD)])  28.9 us
    unnamed x258, local copies, waits for them, and re-layouts  27.4 us
  transfers between devices with their start and end apart: 81, of which 37 were waited for; matrix products, arithmetic and copies ran while one was open for 21% of the time, Pallas kernels for 20%

profile of v5, /device:TPU:0, one launch (start us, length us, event | category | flops | bytes accessed | tf_op | source)
XLA Modules:
  0.0 603.4 jit_solution(10225429639532658811)
XLA Ops:
  7.2 3.0 collective-permute-start
  18.2 3.1 gather_fusion
  21.4 13.2 %collective-permute-done.tok_a = bf16[512,1024]{1,0:T(8,128)(2,1)} collective-permute-done((bf16[512,1024]{1,0:T(8,128)(2,1)}, bf16[512,1024]{1,0:T(8,128)(2,1)}, u32[]{:S(2)}, u32[]{:S(2)}) %collective-permute-start) | collective-permute-done | bytes 1048608 | tf_op jit(solution)/shard_map/ppermute | solution.py:62
  36.9 13.5 %collective-permute-done.4 = bf16[2,264,768]{2,1,0:T(8,128)(2,1)} collective-permute-done((bf16[2,264,768]{2,1,0:T(8,128)(2,1)}, bf16[2,264,768]{2,1,0:T(8,128)(2,1)}, u32[]{:S(2)}, u32[]{:S(2)}) %collective-permute-start.4) | collective-permute-done | bytes 811040 | tf_op jit(solution)/shard_map/ppermute | solution.py:62
  62.2 3.8 project.2
  76.0 4.2 project.3
  83.6 29.2 %attend.1 = (bf16[2048,256]{1,0:T(8,128)(2,1)S(1)}, f32[4,8,512]{2,1,0:T(8,128)S(1)}) custom-call(s32[3]{0:T(128)S(1)} %pad_add_fusion.facts, bf16[1024,768]{1,0:T(8,128)(2,1)S(1)} %get-tuple-element.182.near, bf16[1024,768]{1,0:T(8,128)(2,1)S(1)} %get-tuple-element.127.far), custom_call_target="tpu_custom_call" | custom-call | flops 1048576 | bytes 65536 | tf_op jit(solution)/shard_map/attend/pallas_call | solution.py:284
  116.7 5.1 collective-permute-done.9
  121.8 6.2 %collective-permute-done.8 = bf16[512,256]{1,0:T(8,128)(2,1)S(1)} collective-permute-done((bf16[512,256]{1,0:T(8,128)(2,1)S(1)}, bf16[512,256]{1,0:T(8,128)(2,1)S(1)}, u32[]{:S(2)}, u32[]{:S(2)}) %collective-permute-start.8) | collective-permute-done | bytes 262176 | tf_op jit(solution)/shard_map/ppermute | solution.py:62
  132.7 13.3 %all-gather.3.cloned.1.call-done = bf16[16,4,32,1024]{3,2,1,0:T(8,128)(2,1)} async-done(((bf16[2,4,32,1024]{3,2,1,0:T(8,128)(2,1)}), bf16[16,4,32,1024]{3,2,1,0:T(8,128)(2,1)}) %all-gather.3.cloned.1.call-update) | async-done | bytes 4194320 | tf_op jit(solution)/shard_map/all_gather | solution.py:741
  146.0 3.0 copy.84
  149.0 13.3 %experts.2 = (bf16[1024,1024]{1,0:T(8,128)(2,1)S(1)}, bf16[512,1024]{1,0:T(8,128)(2,1)S(1)}, bf16[512,1024]{1,0:T(8,128)(2,1)S(1)}) custom-call(s32[2,1]{1,0:T(2,128)S(1)} %bitcast.348, bf16[512,1024]{1,0:T(8,128)(2,1)} %convolution_convert_fusion.1.rows_a, bf16[512,1024]{1,0:T(8,128)(2,1)} %collective-permute-done.15.rows_b, ...), custom_call_target="tpu_custom_call" | custom-call | flops 1048576 | bytes 65536 | tf_op jit(solution)/shard_map/experts/pallas_call | solution.py:522
  162.4 2.9 collective-permute-done.21.rows_b
  165.3 12.3 %experts.3 = (bf16[1024,1024]{1,0:T(8,128)(2,1)S(1)}, bf16[512,1024]{1,0:T(8,128)(2,1)S(1)}, bf16[512,1024]{1,0:T(8,128)(2,1)S(1)}) custom-call(s32[2,1]{1,0:T(2,128)S(1)} %bitcast.346, bf16[512,1024]{1,0:T(8,128)(2,1)} %collective-permute-done.20.rows_a, bf16[512,1024]{1,0:T(8,128)(2,1)S(1)} %collective-permute-done.21.rows_b, ...), custom_call_target="tpu_custom_call" | custom-call | flops 1048576 | bytes 65536 | tf_op jit(solution)/shard_map/experts/pallas_call | solution.py:522
  183.0 3.0 collective-permute-done.24
  191.1 3.1 collective-permute-done.26
  194.3 11.8 %collective-permute-done.23 = bf16[512,1024]{1,0:T(8,128)(2,1)S(1)} collective-permute-done((bf16[512,1024]{1,0:T(8,128)(2,1)S(1)}, bf16[512,1024]{1,0:T(8,128)(2,1)S(1)}, u32[]{:S(2)}, u32[]{:S(2)}) %collective-permute-start.23) | collective-permute-done | bytes 1048608 | tf_op jit(solution)/shard_map/ppermute | solution.py:62
  211.9 13.8 %experts_back.2 = (bf16[1024,1024]{1,0:T(8,128)(2,1)S(1)}, bf16[512,1024]{1,0:T(8,128)(2,1)S(1)}, bf16[512,1024]{1,0:T(8,128)(2,1)}) custom-call(s32[2,1]{1,0:T(2,128)S(1)} %bitcast.349, bf16[512,1024]{1,0:T(8,128)(2,1)S(1)} %convolution_convert_fusion.rows_a, bf16[512,1024]{1,0:T(8,128)(2,1)S(1)} %collective-permute-done.27.rows_b, ...), custom_call_target="tpu_custom_call" | custom-call | flops 1048576 | bytes 65536 | tf_op jit(solution)/shard_map/experts_back/pallas_call | solution.py:546
  228.0 6.9 %collective-permute-done.29.rows_a = bf16[512,1024]{1,0:T(8,128)(2,1)} collective-permute-done((bf16[512,1024]{1,0:T(8,128)(2,1)S(1)}, bf16[512,1024]{1,0:T(8,128)(2,1)}, u32[]{:S(2)}, u32[]{:S(2)}) %collective-permute-start.29) | collective-permute-done | bytes 1048608 | tf_op jit(solution)/shard_map/ppermute | solution.py:62
  237.5 4.4 pad_maximum_fusion.3
  241.9 13.1 %experts_back.3 = (bf16[1024,1024]{1,0:T(8,128)(2,1)S(1)}, bf16[512,1024]{1,0:T(8,128)(2,1)S(1)}, bf16[512,1024]{1,0:T(8,128)(2,1)S(1)}) custom-call(s32[2,1]{1,0:T(2,128)S(1)} %bitcast.347, bf16[512,1024]{1,0:T(8,128)(2,1)} %collective-permute-done.29.rows_a, bf16[512,1024]{1,0:T(8,128)(2,1)} %collective-permute-done.30.rows_b, ...), custom_call_target="tpu_custom_call" | custom-call | flops 1048576 | bytes 65536 | tf_op jit(solution)/shard_map/experts_back/pallas_call | solution.py:546
  258.7 2.8 copy-done.18
  274.7 8.2 %fusion.27 = bf16[1024,1024]{1,0:T(8,128)(2,1)S(1)} fusion(bf16[2048,1024]{1,0:T(8,128)(2,1)} %copy-done.74, pred[2048]{0:T(1024)(128)(4,1)S(1)} %dynamic-update-slice.65, bf16[512,1024]{1,0:T(8,128)(2,1)} %collective-permute-done.30.rows_b, bf16[512,1024]{1,0:T(8,128)(2,1)} %collective-permute-done.29.rows_a, bf16[512,1024]{1,0:T(8,128)(2,1)} %copy-done.28, ...), kind=kOutput, calls=%fused_computation.54 | convolution fusion | flops 4314890240 | bytes 10487808 | tf_op jit(solution)/shard_map/dot_general | solution.py:54
  284.4 6.5 %fusion.30 = bf16[1024,1024]{1,0:T(8,128)(2,1)S(1)} fusion(bf16[2048,1024]{1,0:T(8,128)(2,1)S(1)} %copy-done.75, pred[2048]{0:T(1024)(128)(4,1)S(1)} %not.15, bf16[512,1024]{1,0:T(8,128)(2,1)} %collective-permute-done.30.rows_b, bf16[512,1024]{1,0:T(8,128)(2,1)} %collective-permute-done.29.rows_a, bf16[512,1024]{1,0:T(8,128)(2,1)S(1)} %copy-done.29, ...), kind=kOutput, calls=%fused_computation.55 | convolution fusion | flops 4314890240 | bytes 10487808 | tf_op jit(solution)/shard_map/dot_general | solution.py:54
  291.2 3.1 collective-permute-start.34
  294.3 7.0 %fusion.33 = bf16[1024,1024]{1,0:T(8,128)(2,1)S(1)} fusion(bf16[2048,1024]{1,0:T(8,128)(2,1)S(1)} %copy-done.43, pred[2048]{0:T(1024)(128)(4,1)S(1)} %dynamic-update-slice.65, bf16[512,1024]{1,0:T(8,128)(2,1)S(1)} %copy-done.27, bf16[512,1024]{1,0:T(8,128)(2,1)} %collective-permute-done.20.rows_a, bf16[512,1024]{1,0:T(8,128)(2,1)} %collective-permute-done.15.rows_b, ...), kind=kOutput, calls=%fused_computation.56 | convolution fusion | flops 4314890240 | bytes 10487808 | tf_op jit(solution)/shard_map/dot_general | solution.py:54
  302.8 6.6 %fusion.36 = bf16[1024,1024]{1,0:T(8,128)(2,1)S(1)} fusion(bf16[2048,1024]{1,0:T(8,128)(2,1)S(1)} %copy-done.43, pred[2048]{0:T(1024)(128)(4,1)S(1)} %not.15, bf16[512,1024]{1,0:T(8,128)(2,1)S(1)} %copy-done.27, bf16[512,1024]{1,0:T(8,128)(2,1)} %collective-permute-done.20.rows_a, bf16[512,1024]{1,0:T(8,128)(2,1)} %collective-permute-done.15.rows_b, ...), kind=kOutput, calls=%fused_computation.57 | convolution fusion | flops 4314890240 | bytes 10487808 | tf_op jit(solution)/shard_map/dot_general | solution.py:54
  310.3 6.7 %collective-permute-done.34 = bf16[2,1,256,1024]{3,2,1,0:T(8,128)(2,1)S(1)} collective-permute-done((bf16[2,1,256,1024]{3,2,1,0:T(8,128)(2,1)S(1)}, bf16[2,1,256,1024]{3,2,1,0:T(8,128)(2,1)S(1)}, u32[]{:S(2)}, u32[]{:S(2)}) %collective-permute-start.34) | collective-permute-done | bytes 1048608 | tf_op jit(solution)/shard_map/ppermute | solution.py:84
  320.9 2.9 multiply_reduce_fusion
  338.6 4.6 collective-permute-done.42
  345.8 5.9 collective-permute-done.40.g3
  362.2 22.9 %attend_back.2 = bf16[2048,384]{1,0:T(8,128)(2,1)S(1)} custom-call(s32[3]{0:T(128)S(1)} %pad_add_fusion.facts, bf16[1024,768]{1,0:T(8,128)(2,1)S(1)} %get-tuple-element.182.near, bf16[1024,768]{1,0:T(8,128)(2,1)} %copy-done.5, bf16[2048,256]{1,0:T(8,128)(2,1)S(1)} %copy-done.7, bf16[512,256]{1,0:T(8,128)(2,1)S(1)} %convolution_convert_fusion.11.g0, ...), custom_call_target="tpu_custom_call" | custom-call | flops 1048576 | bytes 65536 | tf_op jit(solution)/shard_map/attend_back/pallas_call | solution.py:414
  391.3 4.9 collective-permute-start.44
  396.2 29.9 %collective-permute-done.45 = bf16[2,1,256,1024]{3,2,1,0:T(8,128)(2,1)} collective-permute-done((bf16[2,1,256,1024]{3,2,1,0:T(8,128)(2,1)}, bf16[2,1,256,1024]{3,2,1,0:T(8,128)(2,1)}, u32[]{:S(2)}, u32[]{:S(2)}) %collective-permute-start.45) | collective-permute-done | bytes 1048608 | tf_op jit(solution)/shard_map/ppermute | solution.py:84
  429.7 23.0 %attend_back.3 = bf16[2048,384]{1,0:T(8,128)(2,1)S(1)} custom-call(s32[3]{0:T(128)S(1)} %pad_add_fusion.facts, bf16[1024,768]{1,0:T(8,128)(2,1)S(1)} %get-tuple-element.182.near, bf16[1024,768]{1,0:T(8,128)(2,1)} %copy-done.5, bf16[2048,256]{1,0:T(8,128)(2,1)S(1)} %copy-done.7, bf16[512,256]{1,0:T(8,128)(2,1)S(1)} %convolution_convert_fusion.11.g0, ...), custom_call_target="tpu_custom_call" | custom-call | flops 1048576 | bytes 65536 | tf_op jit(solution)/shard_map/attend_back/pallas_call | solution.py:414
  454.5 4.0 collective-permute-done.46.refs_1_
  477.4 3.2 collective-permute-done.53
  482.8 18.0 %collective-permute-done.56 = bf16[2,512,256]{2,1,0:T(8,128)(2,1)S(1)} collective-permute-done((bf16[2,512,256]{2,1,0:T(8,128)(2,1)S(1)}, bf16[2,512,256]{2,1,0:T(8,128)(2,1)S(1)}, u32[]{:S(2)}, u32[]{:S(2)}) %collective-permute-start.56) | collective-permute-done | bytes 524320 | tf_op jit(solution)/shard_map/ppermute | solution.py:84
  505.1 5.1 place_experts.2
  510.2 7.0 %collective-permute-done.61 = bf16[512,256]{1,0:T(8,128)(2,1)S(1)} collective-permute-done((bf16[512,256]{1,0:T(8,128)(2,1)S(1)}, bf16[512,256]{1,0:T(8,128)(2,1)S(1)}, u32[]{:S(2)}, u32[]{:S(2)}) %collective-permute-start.61) | collective-permute-done | bytes 262176 | tf_op jit(solution)/shard_map/ppermute | solution.py:84
  525.3 16.7 %collective-permute-done.64 = bf16[512,1024]{1,0:T(8,128)(2,1)S(1)} collective-permute-done((bf16[512,1024]{1,0:T(8,128)(2,1)S(1)}, bf16[512,1024]{1,0:T(8,128)(2,1)S(1)}, u32[]{:S(2)}, u32[]{:S(2)}) %collective-permute-start.64) | collective-permute-done | bytes 1048608 | tf_op jit(solution)/shard_map/ppermute | solution.py:62
  545.1 4.9 fusion.20
  554.9 2.6 collective-permute-done.69
  559.3 2.8 collective-permute-done.70
  562.8 4.2 collective-permute-done.73
  570.6 4.9 collective-permute-done.78.refs_4_
  582.0 7.9 %place_experts.3 = f32[2,256,4096]{2,1,0:T(8,128)} custom-call(s32[9]{0:T(128)S(1)} %concatenate.278.facts, bf16[4,64,1024]{2,1,0:T(8,128)(2,1)S(1)} %get-tuple-element.223.refs_0_, bf16[4,64,1024]{2,1,0:T(8,128)(2,1)S(1)} %collective-permute-done.55.refs_1_, bf16[2,4,64,1024]{3,2,1,0:T(8,128)(2,1)} %collective-permute-done.75.refs_2_, ...), custom_call_target="tpu_custom_call" | custom-call | flops 1048576 | bytes 65536 | tf_op jit(solution)/shard_map/place_experts/pallas_call | solution.py:594
  592.6 3.5 place_attention.1
  (644 shorter events, 180.3 us)
Async XLA Ops:
  7.2 138.8 %all-gather.3.cloned.1.call-start = ((), (), s32[]{:S(2)}) async-start(), calls=%async_computation | async-start | bytes 4718592 | tf_op jit(solution)/shard_map/all_gather | solution.py:741
  7.2 27.3 %collective-permute-start = (bf16[512,1024]{1,0:T(8,128)(2,1)}, bf16[512,1024]{1,0:T(8,128)(2,1)}, u32[]{:S(2)}, u32[]{:S(2)}) collective-permute-start(bf16[512,1024]{1,0:T(8,128)(2,1)} %tok_a.1), channel_id=1, source_target_pairs={{0,2},{1,3},{2,0},{3,1},{4,6},{5,7},{6,4},{7,5},{8,10},{9,11},{10,... | collective-permute-start | bytes 3145736 | tf_op jit(solution)/shard_map/ppermute | solution.py:62
  17.7 32.7 %collective-permute-start.4 = (bf16[2,264,768]{2,1,0:T(8,128)(2,1)}, bf16[2,264,768]{2,1,0:T(8,128)(2,1)}, u32[]{:S(2)}, u32[]{:S(2)}) collective-permute-start(bf16[2,264,768]{2,1,0:T(8,128)(2,1)} %pad_maximum_fusion.15), channel_id=1, source_target_pairs={{0,3},{1,2},{2,1},{3,0},{4,7},{5,6},{6,5},{7,4},{8,11},{9,10},{10,... | collective-permute-start | bytes 2433032 | tf_op jit(solution)/shard_map/ppermute | solution.py:62
  17.7 42.5 %collective-permute-start.2 = (bf16[512,1024]{1,0:T(8,128)(2,1)S(1)}, bf16[512,1024]{1,0:T(8,128)(2,1)}, u32[]{:S(2)}, u32[]{:S(2)}) collective-permute-start(bf16[512,1024]{1,0:T(8,128)(2,1)S(1)} %copy-done.4), channel_id=1, source_target_pairs={{0,1},{1,0},{2,3},{3,2},{4,5},{5,4},{6,7},{7,6},{8,9},{9,8},{10,11... | collective-permute-start | bytes 3145736 | tf_op jit(solution)/shard_map/ppermute | solution.py:62
  17.9 41.6 %collective-permute-start.3 = (bf16[264,768]{1,0:T(8,128)(2,1)}, bf16[264,768]{1,0:T(8,128)(2,1)S(1)}, u32[]{:S(2)}, u32[]{:S(2)}) collective-permute-start(bf16[264,768]{1,0:T(8,128)(2,1)} %get-tuple-element.421), channel_id=1, source_target_pairs={{0,1},{1,0},{2,3},{3,2},{4,5},{5,4},{6,7},{7,6},{8,9},{9,8},{10,11... | collective-permute-start | bytes 1216520 | tf_op jit(solution)/shard_map/ppermute | solution.py:62
  34.6 19.7 %collective-permute-start.1 = (bf16[512,1024]{1,0:T(8,128)(2,1)}, bf16[512,1024]{1,0:T(8,128)(2,1)S(1)}, u32[]{:S(2)}, u32[]{:S(2)}) collective-permute-start(bf16[512,1024]{1,0:T(8,128)(2,1)} %collective-permute-done.tok_a), channel_id=1, source_target_pairs={{0,1},{1,0},{2,3},{3,2},{4,5},{5,4},{6,7},{7,6},{8,9},{9,8},{10,11... | collective-permute-start | bytes 3145736 | tf_op jit(solution)/shard_map/ppermute | solution.py:62
  70.9 42.9 %collective-permute-start.13 = (bf16[256,1024]{1,0:T(8,128)(2,1)}, bf16[256,1024]{1,0:T(8,128)(2,1)S(1)}, u32[]{:S(2)}, u32[]{:S(2)}) collective-permute-start(bf16[256,1024]{1,0:T(8,128)(2,1)} %param.28), channel_id=1, source_target_pairs={{0,2},{1,3},{2,0},{3,1},{4,6},{5,7},{6,4},{7,5},{8,10},{9,11},{10,... | collective-permute-start | bytes 1572872 | tf_op jit(solution)/shard_map/ppermute | solution.py:62
  72.4 56.0 %collective-permute-start.7 = (bf16[256,1024]{1,0:T(8,128)(2,1)}, bf16[256,1024]{1,0:T(8,128)(2,1)S(1)}, u32[]{:S(2)}, u32[]{:S(2)}) collective-permute-start(bf16[256,1024]{1,0:T(8,128)(2,1)} %param.28), channel_id=1, source_target_pairs={{0,1},{1,0},{2,3},{3,2},{4,5},{5,4},{6,7},{7,6},{8,9},{9,8},{10,11... | collective-permute-start | bytes 1572872 | tf_op jit(solution)/shard_map/ppermute | solution.py:62
  81.7 32.6 %collective-permute-start.12 = (f32[2,128]{1,0:T(2,128)S(1)}, f32[2,128]{1,0:T(2,128)S(1)}, u32[]{:S(2)}, u32[]{:S(2)}) collective-permute-start(f32[2,128]{1,0:T(2,128)S(1)} %broadcast_in_dim.123), channel_id=1, source_target_pairs={{0,3},{1,2},{2,1},{3,0},{4,7},{5,6},{6,5},{7,4},{8,11},{9,10},{10,... | collective-permute-start | bytes 3080 | tf_op jit(solution)/shard_map/ppermute | solution.py:62
  82.0 33.9 %collective-permute-start.11 = (f32[2,128]{1,0:T(2,128)S(1)}, f32[2,128]{1,0:T(2,128)S(1)}, u32[]{:S(2)}, u32[]{:S(2)}) collective-permute-start(f32[2,128]{1,0:T(2,128)S(1)} %broadcast_in_dim.123), channel_id=1, source_target_pairs={{0,2},{1,3},{2,0},{3,1},{4,6},{5,7},{6,4},{7,5},{8,10},{9,11},{10,... | collective-permute-start | bytes 3080 | tf_op jit(solution)/shard_map/ppermute | solution.py:62
  83.5 32.5 %collective-permute-start.10 = (f32[2,128]{1,0:T(2,128)S(1)}, f32[2,128]{1,0:T(2,128)S(1)}, u32[]{:S(2)}, u32[]{:S(2)}) collective-permute-start(f32[2,128]{1,0:T(2,128)S(1)} %broadcast_in_dim.123), channel_id=1, source_target_pairs={{0,1},{1,0},{2,3},{3,2},{4,5},{5,4},{6,7},{7,6},{8,9},{9,8},{10,11... | collective-permute-start | bytes 3080 | tf_op jit(solution)/shard_map/ppermute | solution.py:62
  132.2 16.8 %collective-permute-start.15 = (bf16[512,1024]{1,0:T(8,128)(2,1)}, bf16[512,1024]{1,0:T(8,128)(2,1)}, u32[]{:S(2)}, u32[]{:S(2)}) collective-permute-start(bf16[512,1024]{1,0:T(8,128)(2,1)} %convolution_convert_fusion.1.rows_a), channel_id=1, source_target_pairs={{0,1},{1,0},{2,3},{3,2},{4,5},{5,4},{6,7},{7,6},{8,9},{9,8},{10,11... | collective-permute-start | bytes 3145736 | tf_op jit(solution)/shard_map/ppermute | solution.py:62
  132.2 30.1 %collective-permute-start.20 = (bf16[512,1024]{1,0:T(8,128)(2,1)}, bf16[512,1024]{1,0:T(8,128)(2,1)}, u32[]{:S(2)}, u32[]{:S(2)}) collective-permute-start(bf16[512,1024]{1,0:T(8,128)(2,1)} %convolution_convert_fusion.1.rows_a), channel_id=1, source_target_pairs={{0,2},{1,3},{2,0},{3,1},{4,6},{5,7},{6,4},{7,5},{8,10},{9,11},{10,... | collective-permute-start | bytes 3145736 | tf_op jit(solution)/shard_map/ppermute | solution.py:62
  177.8 16.4 %collective-permute-start.19 = (bf16[512,1024]{1,0:T(8,128)(2,1)S(1)}, bf16[512,1024]{1,0:T(8,128)(2,1)S(1)}, u32[]{:S(2)}, u32[]{:S(2)}) collective-permute-start(bf16[512,1024]{1,0:T(8,128)(2,1)S(1)} %get-tuple-element.144), channel_id=1, source_target_pairs={{0,1},{1,0},{2,3},{3,2},{4,5},{5,4},{6,7},{7,6},{8,9},{9,8},{10,11... | collective-permute-start | bytes 3145736 | tf_op jit(solution)/shard_map/ppermute | solution.py:62
  180.8 25.3 %collective-permute-start.23 = (bf16[512,1024]{1,0:T(8,128)(2,1)S(1)}, bf16[512,1024]{1,0:T(8,128)(2,1)S(1)}, u32[]{:S(2)}, u32[]{:S(2)}) collective-permute-start(bf16[512,1024]{1,0:T(8,128)(2,1)S(1)} %add_convert_fusion.8), channel_id=1, source_target_pairs={{0,2},{1,3},{2,0},{3,1},{4,6},{5,7},{6,4},{7,5},{8,10},{9,11},{10,... | collective-permute-start | bytes 3145736 | tf_op jit(solution)/shard_map/ppermute | solution.py:62
  209.2 25.7 %collective-permute-start.29 = (bf16[512,1024]{1,0:T(8,128)(2,1)S(1)}, bf16[512,1024]{1,0:T(8,128)(2,1)}, u32[]{:S(2)}, u32[]{:S(2)}) collective-permute-start(bf16[512,1024]{1,0:T(8,128)(2,1)S(1)} %convolution_convert_fusion.rows_a), channel_id=1, source_target_pairs={{0,2},{1,3},{2,0},{3,1},{4,6},{5,7},{6,4},{7,5},{8,10},{9,11},{10,... | collective-permute-start | bytes 3145736 | tf_op jit(solution)/shard_map/ppermute | solution.py:62
  258.6 60.8 %collective-permute-start.28 = (bf16[512,1024]{1,0:T(8,128)(2,1)}, bf16[512,1024]{1,0:T(8,128)(2,1)}, u32[]{:S(2)}, u32[]{:S(2)}) collective-permute-start(bf16[512,1024]{1,0:T(8,128)(2,1)} %get-tuple-element.150), channel_id=1, source_target_pairs={{0,1},{1,0},{2,3},{3,2},{4,5},{5,4},{6,7},{7,6},{8,9},{9,8},{10,11... | collective-permute-start | bytes 3145736 | tf_op jit(solution)/shard_map/ppermute | solution.py:62
  271.2 48.2 %collective-permute-start.32 = (bf16[512,1024]{1,0:T(8,128)(2,1)}, bf16[512,1024]{1,0:T(8,128)(2,1)}, u32[]{:S(2)}, u32[]{:S(2)}) collective-permute-start(bf16[512,1024]{1,0:T(8,128)(2,1)} %add_convert_fusion.6), channel_id=1, source_target_pairs={{0,2},{1,3},{2,0},{3,1},{4,6},{5,7},{6,4},{7,5},{8,10},{9,11},{10,... | collective-permute-start | bytes 3145736 | tf_op jit(solution)/shard_map/ppermute | solution.py:62
  283.1 35.7 %collective-permute-start.33 = (bf16[2,1,256,1024]{3,2,1,0:T(8,128)(2,1)S(1)}, bf16[2,1,256,1024]{3,2,1,0:T(8,128)(2,1)S(1)}, u32[]{:S(2)}, u32[]{:S(2)}) collective-permute-start(bf16[2,1,256,1024]{3,2,1,0:T(8,128)(2,1)S(1)} %pad_maximum_fusion.4), channel_id=1, source_target_pairs={{0,4},{4,0},{8,12},{12,8},{16,20},{20,16},{24,28},{28,24},{1,5},{5... | collective-permute-start | bytes 3145736 | tf_op jit(solution)/shard_map/ppermute | solution.py:84
  291.2 25.9 %collective-permute-start.34 = (bf16[2,1,256,1024]{3,2,1,0:T(8,128)(2,1)S(1)}, bf16[2,1,256,1024]{3,2,1,0:T(8,128)(2,1)S(1)}, u32[]{:S(2)}, u32[]{:S(2)}) collective-permute-start(bf16[2,1,256,1024]{3,2,1,0:T(8,128)(2,1)S(1)} %pad_maximum_fusion.5), channel_id=1, source_target_pairs={{0,8},{4,12},{8,0},{12,4},{16,24},{20,28},{24,16},{28,20},{1,9},{5... | collective-permute-start | bytes 3145736 | tf_op jit(solution)/shard_map/ppermute | solution.py:84
  301.5 34.4 %collective-permute-start.35 = (bf16[2,4,64,1024]{3,2,1,0:T(8,128)(2,1)S(1)}, bf16[2,4,64,1024]{3,2,1,0:T(8,128)(2,1)S(1)}, u32[]{:S(2)}, u32[]{:S(2)}) collective-permute-start(bf16[2,4,64,1024]{3,2,1,0:T(8,128)(2,1)S(1)} %pad_maximum_fusion.6), channel_id=1, source_target_pairs={{0,4},{4,0},{8,12},{12,8},{16,20},{20,16},{24,28},{28,24},{1,5},{5... | collective-permute-start | bytes 3145736 | tf_op jit(solution)/shard_map/ppermute | solution.py:84
  317.0 26.1 %collective-permute-start.42 = (bf16[2,4,64,1024]{3,2,1,0:T(8,128)(2,1)S(1)}, bf16[2,4,64,1024]{3,2,1,0:T(8,128)(2,1)S(1)}, u32[]{:S(2)}, u32[]{:S(2)}) collective-permute-start(bf16[2,4,64,1024]{3,2,1,0:T(8,128)(2,1)S(1)} %pad_maximum_fusion.7), channel_id=1, source_target_pairs={{0,8},{4,12},{8,0},{12,4},{16,24},{20,28},{24,16},{28,20},{1,9},{5... | collective-permute-start | bytes 3145736 | tf_op jit(solution)/shard_map/ppermute | solution.py:84
  326.9 25.3 %collective-permute-start.36 = (bf16[1,256,1024]{2,1,0:T(8,128)(2,1)S(1)}, bf16[1,256,1024]{2,1,0:T(8,128)(2,1)S(1)}, u32[]{:S(2)}, u32[]{:S(2)}) collective-permute-start(bf16[1,256,1024]{2,1,0:T(8,128)(2,1)S(1)} %fusion.47), channel_id=1, source_target_pairs={{0,8},{4,12},{8,0},{12,4},{16,24},{20,28},{24,16},{28,20},{1,9},{5... | collective-permute-start | bytes 1572872 | tf_op jit(solution)/shard_map/ppermute | solution.py:84
  327.7 16.4 %collective-permute-start.38 = (bf16[512,256]{1,0:T(8,128)(2,1)S(1)}, bf16[512,256]{1,0:T(8,128)(2,1)S(1)}, u32[]{:S(2)}, u32[]{:S(2)}) collective-permute-start(bf16[512,256]{1,0:T(8,128)(2,1)S(1)} %convolution_convert_fusion.10), channel_id=1, source_target_pairs={{0,1},{1,0},{2,3},{3,2},{4,5},{5,4},{6,7},{7,6},{8,9},{9,8},{10,11... | collective-permute-start | bytes 786440 | tf_op jit(solution)/shard_map/ppermute | solution.py:62
  327.8 18.0 %collective-permute-start.39 = (bf16[512,256]{1,0:T(8,128)(2,1)S(1)}, bf16[512,256]{1,0:T(8,128)(2,1)S(1)}, u32[]{:S(2)}, u32[]{:S(2)}) collective-permute-start(bf16[512,256]{1,0:T(8,128)(2,1)S(1)} %convolution_convert_fusion.9), channel_id=1, source_target_pairs={{0,2},{1,3},{2,0},{3,1},{4,6},{5,7},{6,4},{7,5},{8,10},{9,11},{10,... | collective-permute-start | bytes 786440 | tf_op jit(solution)/shard_map/ppermute | solution.py:62
  335.9 16.3 %collective-permute-start.37 = (bf16[1,256,1024]{2,1,0:T(8,128)(2,1)S(1)}, bf16[1,256,1024]{2,1,0:T(8,128)(2,1)S(1)}, u32[]{:S(2)}, u32[]{:S(2)}) collective-permute-start(bf16[1,256,1024]{2,1,0:T(8,128)(2,1)S(1)} %fusion.46), channel_id=1, source_target_pairs={{0,4},{4,0},{8,12},{12,8},{16,20},{20,16},{24,28},{28,24},{1,5},{5... | collective-permute-start | bytes 1572872 | tf_op jit(solution)/shard_map/ppermute | solution.py:84
  344.1 40.9 %collective-permute-start.47 = (bf16[256,1024]{1,0:T(8,128)(2,1)}, bf16[256,1024]{1,0:T(8,128)(2,1)}, u32[]{:S(2)}, u32[]{:S(2)}) collective-permute-start(bf16[256,1024]{1,0:T(8,128)(2,1)} %convolution_convert_fusion.4), channel_id=1, source_target_pairs={{0,1},{1,0},{2,3},{3,2},{4,5},{5,4},{6,7},{7,6},{8,9},{9,8},{10,11... | collective-permute-start | bytes 1572872 | tf_op jit(solution)/shard_map/ppermute | solution.py:62
  353.9 72.2 %collective-permute-start.45 = (bf16[2,1,256,1024]{3,2,1,0:T(8,128)(2,1)}, bf16[2,1,256,1024]{3,2,1,0:T(8,128)(2,1)}, u32[]{:S(2)}, u32[]{:S(2)}) collective-permute-start(bf16[2,1,256,1024]{3,2,1,0:T(8,128)(2,1)} %pad_maximum_fusion.8), channel_id=1, source_target_pairs={{0,16},{4,20},{8,24},{12,28},{16,0},{20,4},{24,8},{28,12},{1,17},{... | collective-permute-start | bytes 3145736 | tf_op jit(solution)/shard_map/ppermute | solution.py:84
  355.5 32.6 %collective-permute-start.41 = (bf16[4,64,1024]{2,1,0:T(8,128)(2,1)}, bf16[4,64,1024]{2,1,0:T(8,128)(2,1)}, u32[]{:S(2)}, u32[]{:S(2)}) collective-permute-start(bf16[4,64,1024]{2,1,0:T(8,128)(2,1)} %fusion.42), channel_id=1, source_target_pairs={{0,8},{4,12},{8,0},{12,4},{16,24},{20,28},{24,16},{28,20},{1,9},{5... | collective-permute-start | bytes 1572872 | tf_op jit(solution)/shard_map/ppermute | solution.py:84
  357.4 30.6 %collective-permute-start.43 = (bf16[4,64,1024]{2,1,0:T(8,128)(2,1)}, bf16[4,64,1024]{2,1,0:T(8,128)(2,1)}, u32[]{:S(2)}, u32[]{:S(2)}) collective-permute-start(bf16[4,64,1024]{2,1,0:T(8,128)(2,1)} %fusion.41), channel_id=1, source_target_pairs={{0,4},{4,0},{8,12},{12,8},{16,20},{20,16},{24,28},{28,24},{1,5},{5... | collective-permute-start | bytes 1572872 | tf_op jit(solution)/shard_map/ppermute | solution.py:84
  359.9 92.8 %collective-permute-start.50 = (bf16[256,1024]{1,0:T(8,128)(2,1)}, bf16[256,1024]{1,0:T(8,128)(2,1)S(1)}, u32[]{:S(2)}, u32[]{:S(2)}) collective-permute-start(bf16[256,1024]{1,0:T(8,128)(2,1)} %convolution_convert_fusion.6), channel_id=1, source_target_pairs={{0,1},{1,0},{2,3},{3,2},{4,5},{5,4},{6,7},{7,6},{8,9},{9,8},{10,11... | collective-permute-start | bytes 1572872 | tf_op jit(solution)/shard_map/ppermute | solution.py:62
  386.4 66.3 %collective-permute-start.51 = (bf16[256,1024]{1,0:T(8,128)(2,1)S(1)}, bf16[256,1024]{1,0:T(8,128)(2,1)S(1)}, u32[]{:S(2)}, u32[]{:S(2)}) collective-permute-start(bf16[256,1024]{1,0:T(8,128)(2,1)S(1)} %add_convert_fusion.17), channel_id=1, source_target_pairs={{0,2},{1,3},{2,0},{3,1},{4,6},{5,7},{6,4},{7,5},{8,10},{9,11},{10,... | collective-permute-start | bytes 1572872 | tf_op jit(solution)/shard_map/ppermute | solution.py:62
  391.3 67.5 %collective-permute-start.44 = (bf16[2,4,64,1024]{3,2,1,0:T(8,128)(2,1)S(1)}, bf16[2,4,64,1024]{3,2,1,0:T(8,128)(2,1)S(1)}, u32[]{:S(2)}, u32[]{:S(2)}) collective-permute-start(bf16[2,4,64,1024]{3,2,1,0:T(8,128)(2,1)S(1)} %pad_maximum_fusion.9), channel_id=1, source_target_pairs={{0,16},{4,20},{8,24},{12,28},{16,0},{20,4},{24,8},{28,12},{1,17},{... | collective-permute-start | bytes 3145736 | tf_op jit(solution)/shard_map/ppermute | solution.py:84
  427.6 30.9 %collective-permute-start.46 = (bf16[1,256,1024]{2,1,0:T(8,128)(2,1)S(1)}, bf16[1,256,1024]{2,1,0:T(8,128)(2,1)S(1)}, u32[]{:S(2)}, u32[]{:S(2)}) collective-permute-start(bf16[1,256,1024]{2,1,0:T(8,128)(2,1)S(1)} %add_convert_fusion.18.refs_0_), channel_id=1, source_target_pairs={{0,8},{4,12},{8,0},{12,4},{16,24},{20,28},{24,16},{28,20},{1,9},{5... | collective-permute-start | bytes 1572872 | tf_op jit(solution)/shard_map/ppermute | solution.py:84
  427.9 30.6 %collective-permute-start.48 = (bf16[1,256,1024]{2,1,0:T(8,128)(2,1)S(1)}, bf16[1,256,1024]{2,1,0:T(8,128)(2,1)S(1)}, u32[]{:S(2)}, u32[]{:S(2)}) collective-permute-start(bf16[1,256,1024]{2,1,0:T(8,128)(2,1)S(1)} %add_convert_fusion.16.refs_3_), channel_id=1, source_target_pairs={{0,4},{4,0},{8,12},{12,8},{16,20},{20,16},{24,28},{28,24},{1,5},{5... | collective-permute-start | bytes 1572872 | tf_op jit(solution)/shard_map/ppermute | solution.py:84
  463.5 41.3 %collective-permute-start.58 = (bf16[2,1,256,1024]{3,2,1,0:T(8,128)(2,1)S(1)}, bf16[2,1,256,1024]{3,2,1,0:T(8,128)(2,1)S(1)}, u32[]{:S(2)}, u32[]{:S(2)}) collective-permute-start(bf16[2,1,256,1024]{3,2,1,0:T(8,128)(2,1)S(1)} %pad_maximum_fusion.10), channel_id=1, source_target_pairs={{0,4},{4,0},{8,12},{12,8},{16,20},{20,16},{24,28},{28,24},{1,5},{5... | collective-permute-start | bytes 3145736 | tf_op jit(solution)/shard_map/ppermute | solution.py:84
  465.1 38.8 %collective-permute-start.60 = (bf16[2,1,256,1024]{3,2,1,0:T(8,128)(2,1)S(1)}, bf16[2,1,256,1024]{3,2,1,0:T(8,128)(2,1)S(1)}, u32[]{:S(2)}, u32[]{:S(2)}) collective-permute-start(bf16[2,1,256,1024]{3,2,1,0:T(8,128)(2,1)S(1)} %pad_maximum_fusion.11), channel_id=1, source_target_pairs={{0,8},{4,12},{8,0},{12,4},{16,24},{20,28},{24,16},{28,20},{1,9},{5... | collective-permute-start | bytes 3145736 | tf_op jit(solution)/shard_map/ppermute | solution.py:84
  466.3 15.1 %collective-permute-start.52 = (bf16[128,1024]{1,0:T(8,128)(2,1)S(1)}, bf16[128,1024]{1,0:T(8,128)(2,1)S(1)}, u32[]{:S(2)}, u32[]{:S(2)}) collective-permute-start(bf16[128,1024]{1,0:T(8,128)(2,1)S(1)} %pad_maximum_fusion.29), channel_id=1, source_target_pairs={{0,1},{1,0},{2,3},{3,2},{4,5},{5,4},{6,7},{7,6},{8,9},{9,8},{10,11... | collective-permute-start | bytes 786440 | tf_op jit(solution)/shard_map/ppermute | solution.py:62
  477.2 23.6 %collective-permute-start.56 = (bf16[2,512,256]{2,1,0:T(8,128)(2,1)S(1)}, bf16[2,512,256]{2,1,0:T(8,128)(2,1)S(1)}, u32[]{:S(2)}, u32[]{:S(2)}) collective-permute-start(bf16[2,512,256]{2,1,0:T(8,128)(2,1)S(1)} %pad_maximum_fusion.22), channel_id=1, source_target_pairs={{0,4},{4,0},{8,12},{12,8},{16,20},{20,16},{24,28},{28,24},{1,5},{5... | collective-permute-start | bytes 1572872 | tf_op jit(solution)/shard_map/ppermute | solution.py:84
  480.6 21.1 %collective-permute-start.59 = (bf16[2,512,256]{2,1,0:T(8,128)(2,1)S(1)}, bf16[2,512,256]{2,1,0:T(8,128)(2,1)S(1)}, u32[]{:S(2)}, u32[]{:S(2)}) collective-permute-start(bf16[2,512,256]{2,1,0:T(8,128)(2,1)S(1)} %pad_maximum_fusion.23), channel_id=1, source_target_pairs={{0,8},{4,12},{8,0},{12,4},{16,24},{20,28},{24,16},{28,20},{1,9},{5... | collective-permute-start | bytes 1572872 | tf_op jit(solution)/shard_map/ppermute | solution.py:84
  482.2 36.3 %collective-permute-start.62 = (bf16[4,64,1024]{2,1,0:T(8,128)(2,1)S(1)}, bf16[4,64,1024]{2,1,0:T(8,128)(2,1)S(1)}, u32[]{:S(2)}, u32[]{:S(2)}) collective-permute-start(bf16[4,64,1024]{2,1,0:T(8,128)(2,1)S(1)} %get-tuple-element.226.refs_3_), channel_id=1, source_target_pairs={{0,4},{4,0},{8,12},{12,8},{16,20},{20,16},{24,28},{28,24},{1,5},{5... | collective-permute-start | bytes 1572872 | tf_op jit(solution)/shard_map/ppermute | solution.py:84
  501.8 15.6 %collective-permute-start.57 = (bf16[512,256]{1,0:T(8,128)(2,1)S(1)}, bf16[512,256]{1,0:T(8,128)(2,1)S(1)}, u32[]{:S(2)}, u32[]{:S(2)}) collective-permute-start(bf16[512,256]{1,0:T(8,128)(2,1)S(1)} %add_convert_fusion.29), channel_id=1, source_target_pairs={{0,8},{4,12},{8,0},{12,4},{16,24},{20,28},{24,16},{28,20},{1,9},{5... | collective-permute-start | bytes 786440 | tf_op jit(solution)/shard_map/ppermute | solution.py:84
  503.9 16.7 %collective-permute-start.55 = (bf16[4,64,1024]{2,1,0:T(8,128)(2,1)S(1)}, bf16[4,64,1024]{2,1,0:T(8,128)(2,1)S(1)}, u32[]{:S(2)}, u32[]{:S(2)}) collective-permute-start(bf16[4,64,1024]{2,1,0:T(8,128)(2,1)S(1)} %get-tuple-element.223.refs_0_), channel_id=1, source_target_pairs={{0,8},{4,12},{8,0},{12,4},{16,24},{20,28},{24,16},{28,20},{1,9},{5... | collective-permute-start | bytes 1572872 | tf_op jit(solution)/shard_map/ppermute | solution.py:84
  504.8 37.2 %collective-permute-start.63 = (bf16[512,1024]{1,0:T(8,128)(2,1)S(1)}, bf16[512,1024]{1,0:T(8,128)(2,1)S(1)}, u32[]{:S(2)}, u32[]{:S(2)}) collective-permute-start(bf16[512,1024]{1,0:T(8,128)(2,1)S(1)} %add_convert_fusion), channel_id=1, source_target_pairs={{0,1},{1,0},{2,3},{3,2},{4,5},{5,4},{6,7},{7,6},{8,9},{9,8},{10,11... | collective-permute-start | bytes 3145736 | tf_op jit(solution)/shard_map/ppermute | solution.py:62
  517.2 24.8 %collective-permute-start.64 = (bf16[512,1024]{1,0:T(8,128)(2,1)S(1)}, bf16[512,1024]{1,0:T(8,128)(2,1)S(1)}, u32[]{:S(2)}, u32[]{:S(2)}) collective-permute-start(bf16[512,1024]{1,0:T(8,128)(2,1)S(1)} %add_convert_fusion.2), channel_id=1, source_target_pairs={{0,2},{1,3},{2,0},{3,1},{4,6},{5,7},{6,4},{7,5},{8,10},{9,11},{10,... | collective-permute-start | bytes 3145736 | tf_op jit(solution)/shard_map/ppermute | solution.py:62
  518.5 33.1 %collective-permute-start.68 = (bf16[2,512,256]{2,1,0:T(8,128)(2,1)}, bf16[2,512,256]{2,1,0:T(8,128)(2,1)}, u32[]{:S(2)}, u32[]{:S(2)}) collective-permute-start(bf16[2,512,256]{2,1,0:T(8,128)(2,1)} %pad_maximum_fusion.24), channel_id=1, source_target_pairs={{0,16},{4,20},{8,24},{12,28},{16,0},{20,4},{24,8},{28,12},{1,17},{... | collective-permute-start | bytes 1572872 | tf_op jit(solution)/shard_map/ppermute | solution.py:84
  521.7 48.9 %collective-permute-start.76 = (bf16[2,4,64,1024]{3,2,1,0:T(8,128)(2,1)}, bf16[2,4,64,1024]{3,2,1,0:T(8,128)(2,1)}, u32[]{:S(2)}, u32[]{:S(2)}) collective-permute-start(bf16[2,4,64,1024]{3,2,1,0:T(8,128)(2,1)} %pad_maximum_fusion.14), channel_id=1, source_target_pairs={{0,8},{4,12},{8,0},{12,4},{16,24},{20,28},{24,16},{28,20},{1,9},{5... | collective-permute-start | bytes 3145736 | tf_op jit(solution)/shard_map/ppermute | solution.py:84
  524.6 46.0 %collective-permute-start.75 = (bf16[2,4,64,1024]{3,2,1,0:T(8,128)(2,1)}, bf16[2,4,64,1024]{3,2,1,0:T(8,128)(2,1)}, u32[]{:S(2)}, u32[]{:S(2)}) collective-permute-start(bf16[2,4,64,1024]{3,2,1,0:T(8,128)(2,1)} %pad_maximum_fusion.13), channel_id=1, source_target_pairs={{0,4},{4,0},{8,12},{12,8},{16,20},{20,16},{24,28},{28,24},{1,5},{5... | collective-permute-start | bytes 3145736 | tf_op jit(solution)/shard_map/ppermute | solution.py:84
  (135 other events, 1340.8 us)
Sparse Core Ops, SparseCore 0:
  71.0 74.9 all-gather.2
